TPU v7x, 256 devices: a whole 4x4x8 slice. The times are simulated.
256 devices in a mesh: tm: 64 (over z, y, core), series: 4 (over x).
Axes of the slice: x: 4, y: 4, z: 8, core: 2. Of those that a mesh axis runs over, the one named last changes fastest.
Arguments:
- series_values: bfloat16 [4096, 32768], P('tm', 'series'), may hold values from -4 to 4
- observed: int32 [4096, 32768], P('tm', 'series'), may hold values 0 or 1
- series_factors: bfloat16 [32768, 128], P('series'), may hold values from -0.03125 to 0.03125
- time_factors: float32 [4096, 128], P('tm'), may hold values from -6 to 6
- lag_weights: float32 [25, 128], replicated, may hold values from -0.5 to 0.5
Outputs:
- time_update: float32 [4096, 128], P('tm')
- misfit: bfloat16 [4096, 32768], P(None, ('series', 'tm'))
Inputs may be any that keep to these rules, and one draw needn't show every extreme that they name: observed holds only 0 and 1.
All inputs are finite; a program needn't handle non-finite values. No bound on the sum of `observed` on one device may be relied on, other than what follows from the above.
Results may differ from a plain program's by a relative error of at most 0.005.
Values may be sent and summed in bfloat16 or wider, within the bound.
No kernel may reach another device: no remote copies, remote signals or barrier semaphores. Data moves between devices by JAX's collectives and lax.ppermute only.
A program may use at most 64 MiB of HBM per device.

v0:
```python
import jax
import jax.numpy as jnp
from jax import lax
from jax.sharding import PartitionSpec as P

SHORT = 24
SEASON = 168
ITERS = 3


data_weight = 2.0
penalty_weight = 0.5
ridge_weight = 0.2


def from_behind(block, axis, distance):
    devices = range(lax.axis_size(axis))
    route = [(i - distance, i) for i in devices if i - distance in devices]
    return lax.ppermute(block, axis, route)


def delays():
    return list(range(1, SHORT + 1)) + [SEASON]


def source_rows(time_rows, ahead):
    sources = []
    for hop_count in range(1, SEASON // time_rows + 2):
        first_row = time_rows
        last_row = 0
        for lag_steps in delays():
            shifted = (
                lag_steps - hop_count * time_rows if ahead else hop_count * time_rows - lag_steps
            )
            start_row = max(shifted, 0)
            end_row = min(shifted + time_rows, time_rows)
            if start_row < end_row:
                first_row = min(first_row, start_row)
                last_row = max(last_row, end_row)
        sources.append((hop_count, first_row, last_row))
    return sources


def behind(current, lag_weights):
    time_rows, rank_width = current.shape
    window = jnp.concatenate([jnp.zeros((SEASON, rank_width), jnp.float32), current], axis=0)
    for hop_count, first_row, last_row in source_rows(time_rows, False):
        arrived = from_behind(
            current[first_row:last_row].astype(jnp.bfloat16), "tm", hop_count
        ).astype(jnp.float32)
        placed = SEASON + first_row - hop_count * time_rows
        window = window.at[placed : placed + last_row - first_row].set(arrived)
    result = current
    for number, lag_steps in enumerate(delays()):
        result = (
            result
            - lag_weights[number] * window[SEASON - lag_steps : SEASON - lag_steps + time_rows]
        )
    return result


def ahead_of(current, lag_weights):
    time_rows, rank_width = current.shape
    window = jnp.concatenate([current, jnp.zeros((SEASON, rank_width), jnp.float32)], axis=0)
    for hop_count, first_row, last_row in source_rows(time_rows, True):
        arrived = from_behind(
            current[first_row:last_row].astype(jnp.bfloat16), "tm", -hop_count
        ).astype(jnp.float32)
        placed = hop_count * time_rows + first_row
        window = window.at[placed : placed + last_row - first_row].set(arrived)
    result = current
    for number, lag_steps in enumerate(delays()):
        result = result - lag_weights[number] * window[lag_steps : lag_steps + time_rows]
    return result


def lag_penalty(current, lag_weights):
    lagged = ahead_of(behind(current, lag_weights), lag_weights)
    return penalty_weight * lagged + ridge_weight * current


def against(left_rows, factors):
    return lax.dot_general(
        left_rows, factors, (((1,), (1,)), ((), ())), preferred_element_type=jnp.float32
    )


def project(current, series_factors, observed_on):
    fitted = against(current.astype(jnp.bfloat16), series_factors)
    masked = jnp.where(observed_on, fitted, 0.0).astype(jnp.bfloat16)
    return (fitted, jnp.dot(masked, series_factors, preferred_element_type=jnp.float32))


def series_total(partial_value):
    return lax.psum(partial_value, "series")


def time_total(value):
    return lax.psum(value, "tm")


def on_device(series_values, observed, series_factors, time_factors, lag_weights):
    observed_on = observed == 1
    kept = jnp.where(observed_on, series_values, jnp.zeros((), jnp.bfloat16))
    target = jnp.dot(kept, series_factors, preferred_element_type=jnp.float32)
    fitted, image_local = project(time_factors, series_factors, observed_on)
    penalty = lag_penalty(time_factors, lag_weights)
    residual = series_total(data_weight * (target - image_local)) - penalty
    direction = residual
    solution = time_factors
    squared = time_total(jnp.sum(residual * residual))
    for step_number in range(ITERS):
        fitted, image_local = project(direction, series_factors, observed_on)
        penalty = lag_penalty(direction, lag_weights)
        image = data_weight * series_total(image_local) + penalty
        curvature = lax.psum(jnp.sum(direction * image), "tm")
        step_size = squared / curvature
        solution = solution + step_size * direction
        residual = residual - step_size * image
        renewed = time_total(jnp.sum(residual * residual))
        direction = residual + renewed / squared * direction
        squared = renewed
    final_low = solution.astype(jnp.bfloat16)
    local_misfit = (series_values.astype(jnp.float32) - against(final_low, series_factors)).astype(
        jnp.bfloat16
    )
    misfit = lax.all_to_all(local_misfit, "tm", split_axis=1, concat_axis=0, tiled=True)
    return (solution, misfit)


def solution(mesh):
    placed = (P("tm", "series"), P("tm", "series"), P("series", None), P("tm", None), P())
    return jax.shard_map(
        on_device,
        mesh=mesh,
        in_specs=placed,
        out_specs=(P("tm", None), P(None, ("series", "tm"))),
        check_vma=False,
    )
```

profile of v0, /device:TPU:1, one launch (start us, length us, event | category | flops | bytes accessed | tf_op | source)
XLA Modules:
  0.0 854.5 jit_solution(15811981526736450724)
XLA Ops:
  0.7 0.9 convert_element_type.129
  1.6 4.1 collective-permute-start.1
  5.7 4.0 collective-permute-start
  9.8 3.2 collective-permute-start.2
  13.1 1.0 slice_bitcast_fusion.24
  14.1 1.9 broadcast_compare_fusion
  15.9 0.6 fusion.16
  16.5 1.2 fusion.11
  17.7 0.8 slice_bitcast_fusion.23
  18.6 0.1 fusion.251
  18.7 2.0 collective-permute-start.3
  20.7 13.5 %psum.70 = f32[64,128]{1,0:T(8,128)S(1)} all-reduce(f32[64,128]{1,0:T(8,128)S(1)} %fusion.11), channel_id=1, replica_groups=mesh['tm'=64,'series'=4] {'series'}, use_global_device_ids=true, to_apply=%region_0.1 | all-reduce | flops 8192 | bytes 65536 | tf_op jit(solution)/shard_map/psum | solution.py:95
  34.2 1.3 collective-permute-start.4
  35.5 1.3 collective-permute-start.5
  36.8 1.7 collective-permute-done.4
  38.6 8.2 collective-permute-done.5
  46.7 0.1 fusion.249
  46.8 1.9 collective-permute-start.6
  48.8 1.1 fusion.8
  49.9 3.3 collective-permute-start.7
  53.2 6.3 collective-permute-start.8
  59.6 0.7 collective-permute-done.8
  60.4 1.9 collective-permute-start.9
  62.4 11.2 %psum.72 = f32[64,128]{1,0:T(8,128)S(1)} all-reduce(f32[64,128]{1,0:T(8,128)S(1)} %fusion.8), channel_id=1, replica_groups=mesh['tm'=64,'series'=4] {'series'}, use_global_device_ids=true, to_apply=%region_3.4 | all-reduce | flops 8192 | bytes 65536 | tf_op jit(solution)/shard_map/psum | solution.py:95
  73.6 1.3 collective-permute-start.10
  74.9 1.3 collective-permute-start.11
  76.2 1.7 collective-permute-done.10
  78.0 7.8 collective-permute-done.11
  85.8 0.7 multiply_reduce_fusion.3
  86.5 125.2 %all-reduce.8 = (f32[]{:T(128)}, f32[]{:T(128)}) all-reduce(f32[]{:T(128)} %get-tuple-element.291, f32[]{:T(128)} %get-tuple-element.290), channel_id=1, replica_groups=mesh['tm'=64,'series'=4] {'tm'}, use_global_device_ids=true, to_apply=%region_2.3 | all-reduce | flops 2 | bytes 16 | tf_op jit(solution)/shard_map/psum | solution.py:99
  213.1 0.6 multiply_reduce_fusion.2
  213.7 129.7 %psum.74 = f32[]{:T(128)} all-reduce(f32[]{:T(128)} %get-tuple-element.304), channel_id=1, replica_groups=mesh['tm'=64,'series'=4] {'tm'}, use_global_device_ids=true, to_apply=%region_7.8 | all-reduce | flops 1 | bytes 8 | tf_op jit(solution)/shard_map/psum | solution.py:99
  344.8 1.9 collective-permute-start.12
  346.7 1.2 fusion.7
  347.9 1.3 collective-permute-start.13
  349.2 1.3 collective-permute-start.14
  350.5 0.7 collective-permute-done.14
  351.3 3.0 collective-permute-start.15
  354.3 12.6 %psum.75 = f32[64,128]{1,0:T(8,128)S(1)} all-reduce(f32[64,128]{1,0:T(8,128)S(1)} %fusion.7), channel_id=1, replica_groups=mesh['tm'=64,'series'=4] {'series'}, use_global_device_ids=true, to_apply=%region_8.9 | all-reduce | flops 8192 | bytes 65536 | tf_op jit(solution)/shard_map/psum | solution.py:95
  366.9 1.3 collective-permute-start.16
  368.2 1.3 collective-permute-start.17
  369.6 1.7 collective-permute-done.16
  371.3 7.8 collective-permute-done.17
  379.1 0.7 multiply_reduce_fusion.1
  379.8 121.6 %psum.76 = f32[]{:T(128)} all-reduce(f32[]{:T(128)} %get-tuple-element.298), channel_id=1, replica_groups=mesh['tm'=64,'series'=4] {'tm'}, use_global_device_ids=true, to_apply=%region_10.11 | all-reduce | flops 1 | bytes 8 | tf_op jit(solution)/shard_map/psum | solution.py:116
  502.7 0.6 multiply_reduce_fusion
  503.3 129.4 %psum.77 = f32[]{:T(128)} all-reduce(f32[]{:T(128)} %multiply_reduce_fusion), channel_id=1, replica_groups=mesh['tm'=64,'series'=4] {'tm'}, use_global_device_ids=true, to_apply=%region_12.13 | all-reduce | flops 1 | bytes 8 | tf_op jit(solution)/shard_map/psum | solution.py:99
  634.1 1.9 collective-permute-start.18
  636.0 1.1 fusion.6
  637.2 1.4 collective-permute-start.19
  638.6 1.3 collective-permute-start.20
  640.0 0.7 collective-permute-done.20
  640.8 3.0 collective-permute-start.21
  643.8 10.9 %psum.78 = f32[64,128]{1,0:T(8,128)S(1)} all-reduce(f32[64,128]{1,0:T(8,128)S(1)} %fusion.6), channel_id=1, replica_groups=mesh['tm'=64,'series'=4] {'series'}, use_global_device_ids=true, to_apply=%region_13.14 | all-reduce | flops 8192 | bytes 65536 | tf_op jit(solution)/shard_map/psum | solution.py:95
  654.8 1.3 collective-permute-start.22
  656.1 1.3 collective-permute-start.23
  657.4 1.7 collective-permute-done.22
  659.2 7.7 collective-permute-done.23
  666.9 0.7 fusion.24
  667.6 121.6 %psum.79 = f32[]{:T(128)} all-reduce(f32[]{:T(128)} %fusion.24), channel_id=1, replica_groups=mesh['tm'=64,'series'=4] {'tm'}, use_global_device_ids=true, to_apply=%region_15.16 | all-reduce | flops 1 | bytes 8 | tf_op jit(solution)/shard_map/psum | solution.py:116
  790.5 0.8 fusion.5
  791.4 0.3 copy.11
  791.7 61.8 %all_to_all.19 = bf16[64,64,128]{2,0,1:T(8,128)(2,1)S(1)} all-to-all(bf16[64,64,128]{2,0,1:T(8,128)(2,1)S(1)} %bitcast.72), channel_id=1, replica_groups=mesh['tm'=64,'series'=4] {'tm'}, dimensions={1} | all-to-all | bytes 2097152 | tf_op jit(solution)/shard_map/all_to_all | solution.py:127
  853.5 1.0 copy.43
  (77 shorter events, 0.6 us)
Async XLA Ops:
  0.6 15.3 %copy-start = (bf16[8192,128]{1,0:T(8,128)(2,1)S(1)}, bf16[8192,128]{1,0:T(8,128)(2,1)}, u32[]{:S(2)}) copy-start(bf16[8192,128]{1,0:T(8,128)(2,1)} %param.55) | copy-start | bytes 6291460
  0.6 15.3 %copy-start.1 = (bf16[64,8192]{1,0:T(8,128)(2,1)S(1)}, bf16[64,8192]{1,0:T(8,128)(2,1)}, u32[]{:S(2)}) copy-start(bf16[64,8192]{1,0:T(8,128)(2,1)} %param.53) | copy-start | bytes 3145732
  1.6 17.0 %collective-permute-start.1 = (bf16[24,128]{1,0:T(8,128)(2,1)S(1)}, bf16[24,128]{1,0:T(8,128)(2,1)S(1)}, u32[]{:S(2)}, u32[]{:S(2)}) collective-permute-start(bf16[24,128]{1,0:T(8,128)(2,1)S(1)} %get-tuple-element.352), channel_id=1, source_target_pairs={{0,8},{4,12},{8,16},{12,20},{16,24},{20,28},{24,32},{28,36},{32,40... | collective-permute-start | bytes 18440 | tf_op jit(solution)/shard_map/ppermute | solution.py:19
  5.7 12.8 %collective-permute-start = (bf16[24,128]{1,0:T(8,128)(2,1)S(1)}, bf16[24,128]{1,0:T(8,128)(2,1)S(1)}, u32[]{:S(2)}, u32[]{:S(2)}) collective-permute-start(bf16[24,128]{1,0:T(8,128)(2,1)S(1)} %get-tuple-element.353), channel_id=1, source_target_pairs={{0,4},{4,8},{8,12},{12,16},{16,20},{20,24},{24,28},{28,32},{32,36}... | collective-permute-start | bytes 18440 | tf_op jit(solution)/shard_map/ppermute | solution.py:19
  9.8 8.8 %collective-permute-start.2 = (bf16[40,128]{1,0:T(8,128)(2,1)S(1)}, bf16[40,128]{1,0:T(8,128)(2,1)S(1)}, u32[]{:S(2)}, u32[]{:S(2)}) collective-permute-start(bf16[40,128]{1,0:T(8,128)(2,1)S(1)} %slice.1605), channel_id=1, source_target_pairs={{0,12},{4,16},{8,20},{12,24},{16,28},{20,32},{24,36},{28,40},{32,4... | collective-permute-start | bytes 30728 | tf_op jit(solution)/shard_map/ppermute | solution.py:19
  16.5 2.0 copy-start.3
  18.7 18.1 %collective-permute-start.3 = (bf16[24,128]{1,0:T(8,128)(2,1)S(1)}, bf16[24,128]{1,0:T(8,128)(2,1)S(1)}, u32[]{:S(2)}, u32[]{:S(2)}) collective-permute-start(bf16[24,128]{1,0:T(8,128)(2,1)S(1)} %get-tuple-element.326), channel_id=1, source_target_pairs={{4,0},{8,4},{12,8},{16,12},{20,16},{24,20},{28,24},{32,28},{36,32}... | collective-permute-start | bytes 18440 | tf_op jit(solution)/shard_map/ppermute | solution.py:19
  34.2 4.4 collective-permute-start.4
  35.5 11.2 %collective-permute-start.5 = (bf16[40,128]{1,0:T(8,128)(2,1)S(1)}, bf16[40,128]{1,0:T(8,128)(2,1)S(1)}, u32[]{:S(2)}, u32[]{:S(2)}) collective-permute-start(bf16[40,128]{1,0:T(8,128)(2,1)S(1)} %slice.1633), channel_id=1, source_target_pairs={{12,0},{16,4},{20,8},{24,12},{28,16},{32,20},{36,24},{40,28},{44,3... | collective-permute-start | bytes 30728 | tf_op jit(solution)/shard_map/ppermute | solution.py:19
  46.8 12.7 %collective-permute-start.6 = (bf16[24,128]{1,0:T(8,128)(2,1)S(1)}, bf16[24,128]{1,0:T(8,128)(2,1)S(1)}, u32[]{:S(2)}, u32[]{:S(2)}) collective-permute-start(bf16[24,128]{1,0:T(8,128)(2,1)S(1)} %get-tuple-element.324), channel_id=1, source_target_pairs={{0,4},{4,8},{8,12},{12,16},{16,20},{20,24},{24,28},{28,32},{32,36}... | collective-permute-start | bytes 18440 | tf_op jit(solution)/shard_map/ppermute | solution.py:19
  49.9 9.7 %collective-permute-start.7 = (bf16[24,128]{1,0:T(8,128)(2,1)S(1)}, bf16[24,128]{1,0:T(8,128)(2,1)S(1)}, u32[]{:S(2)}, u32[]{:S(2)}) collective-permute-start(bf16[24,128]{1,0:T(8,128)(2,1)S(1)} %get-tuple-element.323), channel_id=1, source_target_pairs={{0,8},{4,12},{8,16},{12,20},{16,24},{20,28},{24,32},{28,36},{32,40... | collective-permute-start | bytes 18440 | tf_op jit(solution)/shard_map/ppermute | solution.py:19
  53.2 7.1 collective-permute-start.8
  60.4 15.7 %collective-permute-start.9 = (bf16[24,128]{1,0:T(8,128)(2,1)S(1)}, bf16[24,128]{1,0:T(8,128)(2,1)S(1)}, u32[]{:S(2)}, u32[]{:S(2)}) collective-permute-start(bf16[24,128]{1,0:T(8,128)(2,1)S(1)} %get-tuple-element.322), channel_id=1, source_target_pairs={{4,0},{8,4},{12,8},{16,12},{20,16},{24,20},{28,24},{32,28},{36,32}... | collective-permute-start | bytes 18440 | tf_op jit(solution)/shard_map/ppermute | solution.py:19
  73.6 4.4 collective-permute-start.10
  74.9 10.9 %collective-permute-start.11 = (bf16[40,128]{1,0:T(8,128)(2,1)S(1)}, bf16[40,128]{1,0:T(8,128)(2,1)S(1)}, u32[]{:S(2)}, u32[]{:S(2)}) collective-permute-start(bf16[40,128]{1,0:T(8,128)(2,1)S(1)} %slice.1689), channel_id=1, source_target_pairs={{12,0},{16,4},{20,8},{24,12},{28,16},{32,20},{36,24},{40,28},{44,3... | collective-permute-start | bytes 30728 | tf_op jit(solution)/shard_map/ppermute | solution.py:19
  344.8 5.7 collective-permute-start.12
  347.9 2.6 collective-permute-start.13
  349.2 2.1 collective-permute-start.14
  351.3 18.2 %collective-permute-start.15 = (bf16[24,128]{1,0:T(8,128)(2,1)S(1)}, bf16[24,128]{1,0:T(8,128)(2,1)S(1)}, u32[]{:S(2)}, u32[]{:S(2)}) collective-permute-start(bf16[24,128]{1,0:T(8,128)(2,1)S(1)} %get-tuple-element.318), channel_id=1, source_target_pairs={{4,0},{8,4},{12,8},{16,12},{20,16},{24,20},{28,24},{32,28},{36,32}... | collective-permute-start | bytes 18440 | tf_op jit(solution)/shard_map/ppermute | solution.py:19
  366.9 4.4 collective-permute-start.16
  368.2 10.9 %collective-permute-start.17 = (bf16[40,128]{1,0:T(8,128)(2,1)S(1)}, bf16[40,128]{1,0:T(8,128)(2,1)S(1)}, u32[]{:S(2)}, u32[]{:S(2)}) collective-permute-start(bf16[40,128]{1,0:T(8,128)(2,1)S(1)} %slice.1745), channel_id=1, source_target_pairs={{12,0},{16,4},{20,8},{24,12},{28,16},{32,20},{36,24},{40,28},{44,3... | collective-permute-start | bytes 30728 | tf_op jit(solution)/shard_map/ppermute | solution.py:19
  634.1 5.9 collective-permute-start.18
  637.2 153.3 %copy-start.2 = (bf16[64,8192]{1,0:T(8,128)(2,1)S(1)}, bf16[64,8192]{1,0:T(8,128)(2,1)}, u32[]{:S(2)}) copy-start(bf16[64,8192]{1,0:T(8,128)(2,1)} %param.53) | copy-start | bytes 3145732
  637.2 2.8 collective-permute-start.19
  638.6 2.1 collective-permute-start.20
  640.8 16.6 %collective-permute-start.21 = (bf16[24,128]{1,0:T(8,128)(2,1)S(1)}, bf16[24,128]{1,0:T(8,128)(2,1)S(1)}, u32[]{:S(2)}, u32[]{:S(2)}) collective-permute-start(bf16[24,128]{1,0:T(8,128)(2,1)S(1)} %get-tuple-element.314), channel_id=1, source_target_pairs={{4,0},{8,4},{12,8},{16,12},{20,16},{24,20},{28,24},{32,28},{36,32}... | collective-permute-start | bytes 18440 | tf_op jit(solution)/shard_map/ppermute | solution.py:19
  654.8 4.4 collective-permute-start.22
  656.1 10.8 %collective-permute-start.23 = (bf16[40,128]{1,0:T(8,128)(2,1)S(1)}, bf16[40,128]{1,0:T(8,128)(2,1)S(1)}, u32[]{:S(2)}, u32[]{:S(2)}) collective-permute-start(bf16[40,128]{1,0:T(8,128)(2,1)S(1)} %slice.1801), channel_id=1, source_target_pairs={{12,0},{16,4},{20,8},{24,12},{28,16},{32,20},{36,24},{40,28},{44,3... | collective-permute-start | bytes 30728 | tf_op jit(solution)/shard_map/ppermute | solution.py:19
  790.5 0.9 copy-start.4
where the time goes:
time: 856 us; the launch traced here: 855 us
  blocking collectives  737 us (86%)
  starting transfers between devices  52.3 us (6%)
  waiting for transfers between devices  40.7 us (5%)
    psum x3, blocking collectives, time_total(): return lax.psum(value, 'tm')  384 us
    psum x2, blocking collectives, on_device(): curvature = lax.psum(jnp.sum(direction * image), 'tm')  243 us
    all_to_all x1, blocking collectives, on_device(): lax.all_to_all(local_misfit, 'tm', split_axis=1, concat_axis=0, tiled=True)  61.8 us
    ppermute x24, starting transfers between devices, from_behind(): return lax.ppermute(block, axis, route)  52.3 us
    psum x4, blocking collectives, series_total(): return lax.psum(partial_value, 'series')  48.2 us
    ppermute x24, waiting for transfers between devices, from_behind(): return lax.ppermute(block, axis, route)  40.7 us
  transfers between devices with their start and end apart: 24, of which 11 were waited for; matrix products, arithmetic and copies ran while one was open for 1% of the time, Pallas kernels for 0%

commit v1 on v0

v1 whole, which is shorter than its diff:
```python
import jax
import jax.numpy as jnp
from jax import lax
from jax.sharding import PartitionSpec as P

SHORT = 24
SEASON = 168
LAGS = list(range(1, SHORT + 1)) + [SEASON]
data_weight = 2.0
penalty_weight = 0.5
ridge_weight = 0.2


def against(left_rows, factors):
    return lax.dot_general(
        left_rows, factors, (((1,), (1,)), ((), ())), preferred_element_type=jnp.float32
    )


def on_device(series_values, observed, series_factors, time_factors, lag_weights):
    rows, rank = time_factors.shape
    n_tm = lax.axis_size("tm")
    n_series = lax.axis_size("series")
    here = lax.axis_index("series")
    first_time = lax.axis_index("tm") * rows

    def route(steps):
        pairs = []
        for column, step in enumerate(steps):
            if step is None:
                continue
            for source in range(n_tm):
                target = source + step
                if 0 <= target < n_tm:
                    pairs.append((source * n_series + column, target * n_series + column))
        return pairs

    near_route = route([1, -1, 2, -2])
    far_route = route([3, -3, None, None])

    def fetch(field):
        near = jnp.where((here == 0) | (here == 3), field[16:64], field[0:48])
        far = jnp.where(here == 0, field[24:64], field[0:40])
        both = ("tm", "series")
        return lax.ppermute(near, both, near_route), lax.ppermute(far, both, far_route)

    def penalty_part(field, near, far):
        at = lambda column, part: jnp.where(here == column, part, 0.0)
        blank = lambda count: jnp.zeros((count, rank), jnp.float32)
        window = jnp.concatenate(
            [
                at(0, far),
                at(2, near),
                blank(32),
                at(0, near),
                at(2, field),
                at(1, near),
                blank(32),
                at(3, near),
                at(1, far),
            ],
            axis=0,
        )

        def lagged(start, count):
            result = window[SEASON + start : SEASON + start + count]
            for number, lag in enumerate(LAGS):
                begin = SEASON + start - lag
                result = result - lag_weights[number] * window[begin : begin + count]
            stamp = first_time + start + lax.broadcasted_iota(jnp.int32, (count, 1), 0)
            return jnp.where(stamp < n_tm * rows, result, 0.0)

        short = lagged(0, rows + SHORT)
        season = lagged(SEASON, rows)
        result = short[:rows]
        for number, lag in enumerate(LAGS[:-1]):
            result = result - lag_weights[number] * short[lag : lag + rows]
        return result - lag_weights[len(LAGS) - 1] * season

    def series_sum(part):
        def moved(distance):
            pairs = [(i, (i + distance) % n_series) for i in range(n_series)]
            return lax.ppermute(part, "series", pairs)

        return (part + moved(2)) + (moved(1) + moved(3))

    seen = observed == 1

    def fit(field):
        return jnp.where(seen, against(field.astype(jnp.bfloat16), series_factors), 0.0)

    def back(rows_here):
        return jnp.dot(rows_here, series_factors, preferred_element_type=jnp.float32)

    def image(field):
        near, far = fetch(field)
        local = back(fit(field).astype(jnp.bfloat16))
        part = data_weight * local + penalty_weight * penalty_part(field, near, far)
        return part

    kept = jnp.where(seen, series_values, jnp.zeros((), jnp.bfloat16))
    power0 = series_sum(data_weight * back(kept) - image(time_factors)) - ridge_weight * time_factors
    power1 = series_sum(image(power0)) + ridge_weight * power0
    power2 = series_sum(image(power1)) + ridge_weight * power1
    near, far = fetch(power2)
    fitted = fit(power2)
    share = 1.0 / n_series
    quadratic = data_weight * jnp.sum(fitted * fitted) + penalty_weight * jnp.sum(
        power2 * penalty_part(power2, near, far)
    )
    sums = [
        share * jnp.sum(power0 * power0),
        share * jnp.sum(power0 * power1),
        share * jnp.sum(power0 * power2),
        share * jnp.sum(power1 * power1),
        share * jnp.sum(power1 * power2),
        share * jnp.sum(power2 * power2),
        quadratic,
    ]
    lane = lax.broadcasted_iota(jnp.int32, (1, 128), 1)
    packed = jnp.zeros((1, 128), jnp.float32)
    for number, value in enumerate(sums):
        packed = jnp.where(lane == number, value, packed)
    everyone = n_tm * n_series
    spread = jnp.broadcast_to(packed[None], (everyone, 1, 128))
    gathered = lax.all_to_all(spread, ("tm", "series"), split_axis=0, concat_axis=0, tiled=True)
    total = jnp.sum(gathered, axis=(0, 1))
    m00, m01, m02, m11, m12, m22 = [total[number] for number in range(6)]
    m23 = total[6] + ridge_weight * m22

    alpha0 = m00 / m01
    norm1 = m00 - 2.0 * alpha0 * m01 + alpha0 * alpha0 * m11
    beta0 = norm1 / m00
    g0 = 1.0 + beta0
    curvature1 = g0 * g0 * m01 - g0 * alpha0 * (m02 + m11) + alpha0 * alpha0 * m12
    alpha1 = norm1 / curvature1
    a = -(alpha0 + alpha1 * g0)
    b = alpha0 * alpha1
    norm2 = m00 + a * a * m11 + b * b * m22 + 2.0 * (a * m01 + b * m02 + a * b * m12)
    beta1 = norm2 / norm1
    c = 1.0 + beta1 * g0
    d = a - beta1 * alpha0
    e = b
    curvature2 = (
        c * c * m01
        + c * d * (m02 + m11)
        + 2.0 * c * e * m12
        + d * d * m12
        + 2.0 * d * e * m22
        + e * e * m23
    )
    alpha2 = norm2 / curvature2
    k0 = alpha0 + alpha1 * g0 + alpha2 * c
    k1 = alpha2 * d - alpha1 * alpha0
    k2 = alpha2 * e
    solution_rows = time_factors + (k0 * power0 + k1 * power1 + k2 * power2)
    low = solution_rows.astype(jnp.bfloat16)
    local_misfit = (series_values.astype(jnp.float32) - against(low, series_factors)).astype(
        jnp.bfloat16
    )
    misfit = lax.all_to_all(local_misfit, "tm", split_axis=1, concat_axis=0, tiled=True)
    return solution_rows, misfit


def solution(mesh):
    placed = (P("tm", "series"), P("tm", "series"), P("series", None), P("tm", None), P())
    return jax.shard_map(
        on_device,
        mesh=mesh,
        in_specs=placed,
        out_specs=(P("tm", None), P(None, ("series", "tm"))),
        check_vma=False,
    )
```

time: 856 us -> 160 us (0.19)
  blocking collectives: 737 us -> 63.3 us
  waiting for transfers between devices: 40.7 us -> 15.6 us
  starting transfers between devices: 52.3 us -> 38.7 us
  between operations: 8.07 us -> 19.9 us
    psum x9 -> x0, blocking collectives: 676 us -> none  [the longest x3 384 us: time_total(): return lax.psum(value, 'tm')]
    all_to_all x0 -> x1, blocking collectives: none -> 30.9 us  [on_device(): lax.all_to_all(spread, ('tm', 'series'), split_axis=0, concat_axis=0, til...]
    all_to_all x1, blocking collectives: 61.8 us -> 32.4 us  [on_device(): lax.all_to_all(local_misfit, 'tm', split_axis=1, concat_axis=0, tiled=True)]
    ppermute x24 -> x17, waiting for transfers between devices: 40.7 us -> 15.6 us  [the longest x9 12.8 us: moved(): return lax.ppermute(part, 'series', pairs)]
    ppermute x24 -> x17, starting transfers between devices: 52.3 us -> 38.7 us  [the longest x4 26.4 us: fetch(): lax.ppermute(far, both, far_route)]
  transfers between devices with their start and end apart: 24 -> 17, of which waited for: 11 -> 12; matrix products, arithmetic and copies ran while one was open for 1% -> 4% of each run, Pallas kernels for 0% -> 0%
where the time goes in v1:
time: 160 us; the launch traced here: 159 us
  blocking collectives  63.3 us (40%)
  starting transfers between devices  38.7 us (24%)
  between operations  19.9 us (12%)
  waiting for transfers between devices  15.6 us (10%)
  matrix products  11 us (7%)
  other arithmetic  5.95 us (4%)
  local copies, waits for them, and re-layouts  4.64 us (3%)
    all_to_all x1, blocking collectives, on_device(): lax.all_to_all(local_misfit, 'tm', split_axis=1, concat_axis=0, tiled=True)  32.4 us
    all_to_all x1, blocking collectives, on_device(): lax.all_to_all(spread, ('tm', 'series'), split_axis=0, concat_axis=0, til...  30.9 us
    ppermute x4, starting transfers between devices, fetch(): lax.ppermute(far, both, far_route)  26.4 us
    ppermute x9, waiting for transfers between devices, moved(): return lax.ppermute(part, 'series', pairs)  12.8 us
    ppermute x4, starting transfers between devices, fetch(): lax.ppermute(near, both, near_route)  7.67 us
    dot_general x4, matrix products, back(): jnp.dot(rows_here, series_factors, preferred_element_type=jnp.float32)  7.64 us
    ppermute x9, starting transfers between devices, moved(): return lax.ppermute(part, 'series', pairs)  4.66 us
    dot_general x2, matrix products, against(): lax.dot_general(left_rows, factors, (((1,), (1,)), ((), ())), preferred_e...  3.38 us
  transfers between devices with their start and end apart: 17, of which 12 were waited for; matrix products, arithmetic and copies ran while one was open for 4% of the time, Pallas kernels for 0%

profile of v1, /device:TPU:1, one launch (start us, length us, event | category | flops | bytes accessed | tf_op | source)
XLA Modules:
  0.0 159.1 jit_solution(1765629895342454047)
XLA Ops:
  0.6 0.0 copy-start
  0.6 0.0 copy-start.1
  0.7 0.9 slice_select_fusion.7
  1.6 6.3 %collective-permute-start.1 = (f32[40,128]{1,0:T(8,128)S(1)}, f32[40,128]{1,0:T(8,128)S(1)}, u32[]{:S(2)}, u32[]{:S(2)}) collective-permute-start(f32[40,128]{1,0:T(8,128)S(1)} %slice_select_fusion.7), channel_id=1, source_target_pairs={{0,12},{4,16},{8,20},{12,24},{16,28},{20,32},{24,36},{28,40},{32,4... | collective-permute-start | bytes 61448 | tf_op jit(solution)/shard_map/ppermute | solution.py:45
  7.9 0.8 slice_select_fusion.3
  8.7 1.9 %collective-permute-start = (f32[48,128]{1,0:T(8,128)S(1)}, f32[48,128]{1,0:T(8,128)S(1)}, u32[]{:S(2)}, u32[]{:S(2)}) collective-permute-start(f32[48,128]{1,0:T(8,128)S(1)} %slice_select_fusion.3), channel_id=1, source_target_pairs={{0,4},{4,8},{8,12},{12,16},{16,20},{20,24},{24,28},{28,32},{32,36}... | collective-permute-start | bytes 73736 | tf_op jit(solution)/shard_map/ppermute | solution.py:45
  10.6 0.8 slice_bitcast_fusion.23
  11.5 1.0 slice_bitcast_fusion.24
  12.5 1.9 %broadcast_compare_fusion = pred[64,8192]{1,0:T(32,128)(4,1)S(1)} fusion(s32[64,8192]{1,0:T(8,128)} %param.6), kind=kLoop, calls=%fused_computation.27 | loop fusion | flops 524288 | bytes 2621440 | tf_op jit(solution)/shard_map/eq | solution.py:87
  14.4 0.0 copy-start.2
  14.4 0.8 copy-done.2
  15.2 0.0 copy-done
  15.2 0.0 copy-done.1
  15.2 0.6 convolution_multiply_fusion
  15.8 0.0 collective-permute-done.1
  15.8 0.0 collective-permute-done
  15.9 0.1 fusion.106
  16.0 2.4 %fusion.11 = f32[64,128]{1,0:T(8,128)S(1)} fusion(f32[64,128]{1,0:T(8,128)S(1)} %convolution_multiply_fusion, bf16[8192,128]{1,0:T(8,128)(2,1)S(1)} %copy-done, pred[64,8192]{1,0:T(32,128)(4,1)} %copy-done.2, f32[48,128]{1,0:T(8,128)S(1)} %get-tuple-element.27, f32[40,128]{1,0:T(8,128)S(1)} %get-tuple-element.37, f32[88,128]{1,0:T(8,128)S(1)} %fusion.106, ...), kind=kOutput, calls=%fused_computation.16 | convolution fusion | flops 270565376 | bytes 5727233 | tf_op jit(solution)/shard_map/dot_general | solution.py:93
  18.4 0.1 collective-permute-start.4
  18.5 1.5 collective-permute-start.3
  19.9 0.1 collective-permute-start.2
  20.0 1.2 collective-permute-done.4
  21.2 1.3 collective-permute-done.3
  22.6 1.7 %collective-permute-done.2 = f32[64,128]{1,0:T(8,128)S(1)} collective-permute-done((f32[64,128]{1,0:T(8,128)S(1)}, f32[64,128]{1,0:T(8,128)S(1)}, u32[]{:S(2)}, u32[]{:S(2)}) %collective-permute-start.2) | collective-permute-done | bytes 32800 | tf_op jit(solution)/shard_map/ppermute | solution.py:83
  24.3 5.4 %collective-permute-start.6 = (f32[40,128]{1,0:T(8,128)S(1)}, f32[40,128]{1,0:T(8,128)S(1)}, u32[]{:S(2)}, u32[]{:S(2)}) collective-permute-start(f32[40,128]{1,0:T(8,128)S(1)} %slice_select_fusion.6), channel_id=1, source_target_pairs={{0,12},{4,16},{8,20},{12,24},{16,28},{20,32},{24,36},{28,40},{32,4... | collective-permute-start | bytes 61448 | tf_op jit(solution)/shard_map/ppermute | solution.py:45
  29.7 1.9 %collective-permute-start.5 = (f32[48,128]{1,0:T(8,128)S(1)}, f32[48,128]{1,0:T(8,128)S(1)}, u32[]{:S(2)}, u32[]{:S(2)}) collective-permute-start(f32[48,128]{1,0:T(8,128)S(1)} %slice_select_fusion.2), channel_id=1, source_target_pairs={{0,4},{4,8},{8,12},{12,16},{16,20},{20,24},{24,28},{28,32},{32,36}... | collective-permute-start | bytes 73736 | tf_op jit(solution)/shard_map/ppermute | solution.py:45
  31.6 0.0 collective-permute-done.6
  31.6 1.1 collective-permute-done.5
  32.8 0.1 fusion.79
  32.9 2.4 %fusion.13 = f32[64,128]{1,0:T(8,128)S(1)} fusion(bf16[8192,128]{1,0:T(8,128)(2,1)S(1)} %copy-done, pred[64,8192]{1,0:T(32,128)(4,1)} %copy-done.2, f32[48,128]{1,0:T(8,128)S(1)} %get-tuple-element.23, f32[40,128]{1,0:T(8,128)S(1)} %get-tuple-element.35, f32[88,128]{1,0:T(8,128)S(1)} %fusion.79, f32[64,128]{1,0:T(8,128)S(1)} %get-tuple-element.13, ...), kind=kOutput, calls=%fused_computation.18 | convolution fusion | flops 270557184 | bytes 5694465 | tf_op jit(solution)/shard_map/dot_general | solution.py:93
  35.3 0.1 collective-permute-start.9
  35.4 1.5 collective-permute-start.8
  36.8 0.0 collective-permute-start.7
  36.8 1.3 collective-permute-done.9
  38.1 1.3 collective-permute-done.8
  39.4 1.7 %collective-permute-done.7 = f32[64,128]{1,0:T(8,128)S(1)} collective-permute-done((f32[64,128]{1,0:T(8,128)S(1)}, f32[64,128]{1,0:T(8,128)S(1)}, u32[]{:S(2)}, u32[]{:S(2)}) %collective-permute-start.7) | collective-permute-done | bytes 32800 | tf_op jit(solution)/shard_map/ppermute | solution.py:83
  41.2 7.3 %collective-permute-start.11 = (f32[40,128]{1,0:T(8,128)S(1)}, f32[40,128]{1,0:T(8,128)S(1)}, u32[]{:S(2)}, u32[]{:S(2)}) collective-permute-start(f32[40,128]{1,0:T(8,128)S(1)} %slice_select_fusion.5), channel_id=1, source_target_pairs={{0,12},{4,16},{8,20},{12,24},{16,28},{20,32},{24,36},{28,40},{32,4... | collective-permute-start | bytes 61448 | tf_op jit(solution)/shard_map/ppermute | solution.py:45
  48.5 1.9 %collective-permute-start.10 = (f32[48,128]{1,0:T(8,128)S(1)}, f32[48,128]{1,0:T(8,128)S(1)}, u32[]{:S(2)}, u32[]{:S(2)}) collective-permute-start(f32[48,128]{1,0:T(8,128)S(1)} %slice_select_fusion.1), channel_id=1, source_target_pairs={{0,4},{4,8},{8,12},{12,16},{16,20},{20,24},{24,28},{28,32},{32,36}... | collective-permute-start | bytes 73736 | tf_op jit(solution)/shard_map/ppermute | solution.py:45
  50.4 0.0 collective-permute-done.11
  50.4 1.1 collective-permute-done.10
  51.6 0.1 fusion.52
  51.7 2.4 %fusion.15 = f32[64,128]{1,0:T(8,128)S(1)} fusion(bf16[8192,128]{1,0:T(8,128)(2,1)S(1)} %copy-done, pred[64,8192]{1,0:T(32,128)(4,1)} %copy-done.2, f32[48,128]{1,0:T(8,128)S(1)} %get-tuple-element.19, f32[40,128]{1,0:T(8,128)S(1)} %get-tuple-element.33, f32[88,128]{1,0:T(8,128)S(1)} %fusion.52, f32[64,128]{1,0:T(8,128)S(1)} %get-tuple-element.11, ...), kind=kOutput, calls=%fused_computation.20 | convolution fusion | flops 270557184 | bytes 5694465 | tf_op jit(solution)/shard_map/dot_general | solution.py:93
  54.1 0.1 collective-permute-start.14
  54.2 1.5 collective-permute-start.13
  55.6 0.0 collective-permute-start.12
  55.6 1.3 collective-permute-done.14
  56.9 1.3 collective-permute-done.13
  58.2 1.7 %collective-permute-done.12 = f32[64,128]{1,0:T(8,128)S(1)} collective-permute-done((f32[64,128]{1,0:T(8,128)S(1)}, f32[64,128]{1,0:T(8,128)S(1)}, u32[]{:S(2)}, u32[]{:S(2)}) %collective-permute-start.12) | collective-permute-done | bytes 32800 | tf_op jit(solution)/shard_map/ppermute | solution.py:83
  59.9 2.5 %fusion.20 = f32[]{:T(128)} fusion(pred[64,8192]{1,0:T(32,128)(4,1)} %copy-done.2, bf16[8192,128]{1,0:T(8,128)(2,1)S(1)} %copy-done, f32[64,128]{1,0:T(8,128)S(1)} %get-tuple-element.9), kind=kOutput, calls=%fused_computation.28 | convolution fusion | flops 135798784 | bytes 2654212 | tf_op jit(solution)/shard_map/dot_general | solution.py:15
  62.5 7.4 %collective-permute-start.16 = (f32[40,128]{1,0:T(8,128)S(1)}, f32[40,128]{1,0:T(8,128)S(1)}, u32[]{:S(2)}, u32[]{:S(2)}) collective-permute-start(f32[40,128]{1,0:T(8,128)S(1)} %slice_select_fusion.4), channel_id=1, source_target_pairs={{0,12},{4,16},{8,20},{12,24},{16,28},{20,32},{24,36},{28,40},{32,4... | collective-permute-start | bytes 61448 | tf_op jit(solution)/shard_map/ppermute | solution.py:45
  69.9 0.7 multiply_reduce_fusion.5
  74.3 1.9 %collective-permute-start.15 = (f32[48,128]{1,0:T(8,128)S(1)}, f32[48,128]{1,0:T(8,128)S(1)}, u32[]{:S(2)}, u32[]{:S(2)}) collective-permute-start(f32[48,128]{1,0:T(8,128)S(1)} %slice_select_fusion), channel_id=1, source_target_pairs={{0,4},{4,8},{8,12},{12,16},{16,20},{20,24},{24,28},{28,32},{32,36}... | collective-permute-start | bytes 73736 | tf_op jit(solution)/shard_map/ppermute | solution.py:45
  76.8 0.0 collective-permute-done.16
  76.9 0.5 collective-permute-done.15
  77.4 0.1 fusion.25
  77.5 0.8 fusion.534
  79.0 0.1 broadcast_in_dim.141
  79.1 30.9 %all_to_all.24 = f32[256,1,128]{2,1,0:T(1,128)S(1)} all-to-all(f32[256,1,128]{2,1,0:T(1,128)S(1)} %broadcast_in_dim.141), channel_id=1, replica_groups=mesh['tm'=64,'series'=4] {'tm','series'}, dimensions={0} | all-to-all | bytes 262144 | tf_op jit(solution)/shard_map/all_to_all | solution.py:126
  110.0 0.7 fusion.547
  124.5 0.0 copy-start.4
  124.5 0.8 fusion.5
  125.4 0.3 copy.14
  125.7 32.4 %all_to_all.25 = bf16[64,64,128]{2,0,1:T(8,128)(2,1)S(1)} all-to-all(bf16[64,64,128]{2,0,1:T(8,128)(2,1)S(1)} %bitcast.75), channel_id=1, replica_groups=mesh['tm'=64,'series'=4] {'tm'}, dimensions={1} | all-to-all | bytes 2097152 | tf_op jit(solution)/shard_map/all_to_all | solution.py:161
  158.1 1.0 copy.22
  (30 shorter events, 0.3 us)
Async XLA Ops:
  0.6 14.6 %copy-start = (bf16[8192,128]{1,0:T(8,128)(2,1)S(1)}, bf16[8192,128]{1,0:T(8,128)(2,1)}, u32[]{:S(2)}) copy-start(bf16[8192,128]{1,0:T(8,128)(2,1)} %param.7) | copy-start | bytes 6291460
  0.6 14.6 %copy-start.1 = (bf16[64,8192]{1,0:T(8,128)(2,1)S(1)}, bf16[64,8192]{1,0:T(8,128)(2,1)}, u32[]{:S(2)}) copy-start(bf16[64,8192]{1,0:T(8,128)(2,1)} %param.5) | copy-start | bytes 3145732
  1.6 14.3 %collective-permute-start.1 = (f32[40,128]{1,0:T(8,128)S(1)}, f32[40,128]{1,0:T(8,128)S(1)}, u32[]{:S(2)}, u32[]{:S(2)}) collective-permute-start(f32[40,128]{1,0:T(8,128)S(1)} %slice_select_fusion.7), channel_id=1, source_target_pairs={{0,12},{4,16},{8,20},{12,24},{16,28},{20,32},{24,36},{28,40},{32,4... | collective-permute-start | bytes 61448 | tf_op jit(solution)/shard_map/ppermute | solution.py:45
  8.7 7.1 %collective-permute-start = (f32[48,128]{1,0:T(8,128)S(1)}, f32[48,128]{1,0:T(8,128)S(1)}, u32[]{:S(2)}, u32[]{:S(2)}) collective-permute-start(f32[48,128]{1,0:T(8,128)S(1)} %slice_select_fusion.3), channel_id=1, source_target_pairs={{0,4},{4,8},{8,12},{12,16},{16,20},{20,24},{24,28},{28,32},{32,36}... | collective-permute-start | bytes 73736 | tf_op jit(solution)/shard_map/ppermute | solution.py:45
  14.4 0.8 copy-start.2
  15.2 0.8 copy-start.3
  18.4 2.8 %collective-permute-start.4 = (f32[64,128]{1,0:T(8,128)S(1)}, f32[64,128]{1,0:T(8,128)S(1)}, u32[]{:S(2)}, u32[]{:S(2)}) collective-permute-start(f32[64,128]{1,0:T(8,128)S(1)} %fusion.11), channel_id=1, source_target_pairs={{0,3},{1,0},{2,1},{3,2},{4,7},{5,4},{6,5},{7,6},{8,11},{9,8},{10,9... | collective-permute-start | bytes 98312 | tf_op jit(solution)/shard_map/ppermute | solution.py:83
  18.5 4.1 %collective-permute-start.3 = (f32[64,128]{1,0:T(8,128)S(1)}, f32[64,128]{1,0:T(8,128)S(1)}, u32[]{:S(2)}, u32[]{:S(2)}) collective-permute-start(f32[64,128]{1,0:T(8,128)S(1)} %fusion.11), channel_id=1, source_target_pairs={{0,1},{1,2},{2,3},{3,0},{4,5},{5,6},{6,7},{7,4},{8,9},{9,10},{10,1... | collective-permute-start | bytes 98312 | tf_op jit(solution)/shard_map/ppermute | solution.py:83
  19.9 4.3 %collective-permute-start.2 = (f32[64,128]{1,0:T(8,128)S(1)}, f32[64,128]{1,0:T(8,128)S(1)}, u32[]{:S(2)}, u32[]{:S(2)}) collective-permute-start(f32[64,128]{1,0:T(8,128)S(1)} %fusion.11), channel_id=1, source_target_pairs={{0,2},{1,3},{2,0},{3,1},{4,6},{5,7},{6,4},{7,5},{8,10},{9,11},{10,... | collective-permute-start | bytes 98312 | tf_op jit(solution)/shard_map/ppermute | solution.py:83
  24.3 7.4 %collective-permute-start.6 = (f32[40,128]{1,0:T(8,128)S(1)}, f32[40,128]{1,0:T(8,128)S(1)}, u32[]{:S(2)}, u32[]{:S(2)}) collective-permute-start(f32[40,128]{1,0:T(8,128)S(1)} %slice_select_fusion.6), channel_id=1, source_target_pairs={{0,12},{4,16},{8,20},{12,24},{16,28},{20,32},{24,36},{28,40},{32,4... | collective-permute-start | bytes 61448 | tf_op jit(solution)/shard_map/ppermute | solution.py:45
  29.7 3.1 %collective-permute-start.5 = (f32[48,128]{1,0:T(8,128)S(1)}, f32[48,128]{1,0:T(8,128)S(1)}, u32[]{:S(2)}, u32[]{:S(2)}) collective-permute-start(f32[48,128]{1,0:T(8,128)S(1)} %slice_select_fusion.2), channel_id=1, source_target_pairs={{0,4},{4,8},{8,12},{12,16},{16,20},{20,24},{24,28},{28,32},{32,36}... | collective-permute-start | bytes 73736 | tf_op jit(solution)/shard_map/ppermute | solution.py:45
  35.3 2.8 %collective-permute-start.9 = (f32[64,128]{1,0:T(8,128)S(1)}, f32[64,128]{1,0:T(8,128)S(1)}, u32[]{:S(2)}, u32[]{:S(2)}) collective-permute-start(f32[64,128]{1,0:T(8,128)S(1)} %fusion.13), channel_id=1, source_target_pairs={{0,3},{1,0},{2,1},{3,2},{4,7},{5,4},{6,5},{7,6},{8,11},{9,8},{10,9... | collective-permute-start | bytes 98312 | tf_op jit(solution)/shard_map/ppermute | solution.py:83
  35.4 4.1 %collective-permute-start.8 = (f32[64,128]{1,0:T(8,128)S(1)}, f32[64,128]{1,0:T(8,128)S(1)}, u32[]{:S(2)}, u32[]{:S(2)}) collective-permute-start(f32[64,128]{1,0:T(8,128)S(1)} %fusion.13), channel_id=1, source_target_pairs={{0,1},{1,2},{2,3},{3,0},{4,5},{5,6},{6,7},{7,4},{8,9},{9,10},{10,1... | collective-permute-start | bytes 98312 | tf_op jit(solution)/shard_map/ppermute | solution.py:83
  36.8 4.3 %collective-permute-start.7 = (f32[64,128]{1,0:T(8,128)S(1)}, f32[64,128]{1,0:T(8,128)S(1)}, u32[]{:S(2)}, u32[]{:S(2)}) collective-permute-start(f32[64,128]{1,0:T(8,128)S(1)} %fusion.13), channel_id=1, source_target_pairs={{0,2},{1,3},{2,0},{3,1},{4,6},{5,7},{6,4},{7,5},{8,10},{9,11},{10,... | collective-permute-start | bytes 98312 | tf_op jit(solution)/shard_map/ppermute | solution.py:83
  41.2 9.2 %collective-permute-start.11 = (f32[40,128]{1,0:T(8,128)S(1)}, f32[40,128]{1,0:T(8,128)S(1)}, u32[]{:S(2)}, u32[]{:S(2)}) collective-permute-start(f32[40,128]{1,0:T(8,128)S(1)} %slice_select_fusion.5), channel_id=1, source_target_pairs={{0,12},{4,16},{8,20},{12,24},{16,28},{20,32},{24,36},{28,40},{32,4... | collective-permute-start | bytes 61448 | tf_op jit(solution)/shard_map/ppermute | solution.py:45
  48.5 3.1 %collective-permute-start.10 = (f32[48,128]{1,0:T(8,128)S(1)}, f32[48,128]{1,0:T(8,128)S(1)}, u32[]{:S(2)}, u32[]{:S(2)}) collective-permute-start(f32[48,128]{1,0:T(8,128)S(1)} %slice_select_fusion.1), channel_id=1, source_target_pairs={{0,4},{4,8},{8,12},{12,16},{16,20},{20,24},{24,28},{28,32},{32,36}... | collective-permute-start | bytes 73736 | tf_op jit(solution)/shard_map/ppermute | solution.py:45
  54.1 2.8 %collective-permute-start.14 = (f32[64,128]{1,0:T(8,128)S(1)}, f32[64,128]{1,0:T(8,128)S(1)}, u32[]{:S(2)}, u32[]{:S(2)}) collective-permute-start(f32[64,128]{1,0:T(8,128)S(1)} %fusion.15), channel_id=1, source_target_pairs={{0,3},{1,0},{2,1},{3,2},{4,7},{5,4},{6,5},{7,6},{8,11},{9,8},{10,9... | collective-permute-start | bytes 98312 | tf_op jit(solution)/shard_map/ppermute | solution.py:83
  54.2 4.1 %collective-permute-start.13 = (f32[64,128]{1,0:T(8,128)S(1)}, f32[64,128]{1,0:T(8,128)S(1)}, u32[]{:S(2)}, u32[]{:S(2)}) collective-permute-start(f32[64,128]{1,0:T(8,128)S(1)} %fusion.15), channel_id=1, source_target_pairs={{0,1},{1,2},{2,3},{3,0},{4,5},{5,6},{6,7},{7,4},{8,9},{9,10},{10,1... | collective-permute-start | bytes 98312 | tf_op jit(solution)/shard_map/ppermute | solution.py:83
  55.6 4.3 %collective-permute-start.12 = (f32[64,128]{1,0:T(8,128)S(1)}, f32[64,128]{1,0:T(8,128)S(1)}, u32[]{:S(2)}, u32[]{:S(2)}) collective-permute-start(f32[64,128]{1,0:T(8,128)S(1)} %fusion.15), channel_id=1, source_target_pairs={{0,2},{1,3},{2,0},{3,1},{4,6},{5,7},{6,4},{7,5},{8,10},{9,11},{10,... | collective-permute-start | bytes 98312 | tf_op jit(solution)/shard_map/ppermute | solution.py:83
  62.5 14.4 %collective-permute-start.16 = (f32[40,128]{1,0:T(8,128)S(1)}, f32[40,128]{1,0:T(8,128)S(1)}, u32[]{:S(2)}, u32[]{:S(2)}) collective-permute-start(f32[40,128]{1,0:T(8,128)S(1)} %slice_select_fusion.4), channel_id=1, source_target_pairs={{0,12},{4,16},{8,20},{12,24},{16,28},{20,32},{24,36},{28,40},{32,4... | collective-permute-start | bytes 61448 | tf_op jit(solution)/shard_map/ppermute | solution.py:45
  74.3 3.1 %collective-permute-start.15 = (f32[48,128]{1,0:T(8,128)S(1)}, f32[48,128]{1,0:T(8,128)S(1)}, u32[]{:S(2)}, u32[]{:S(2)}) collective-permute-start(f32[48,128]{1,0:T(8,128)S(1)} %slice_select_fusion), channel_id=1, source_target_pairs={{0,4},{4,8},{8,12},{12,16},{16,20},{20,24},{24,28},{28,32},{32,36}... | collective-permute-start | bytes 73736 | tf_op jit(solution)/shard_map/ppermute | solution.py:45
  124.5 0.9 copy-start.4

commit v2 on v1

v2 whole, which is shorter than its diff:
```python
import functools

import jax
import jax.numpy as jnp
from jax import lax
from jax.experimental import pallas as pl
from jax.experimental.pallas import tpu as pltpu
from jax.sharding import PartitionSpec as P

SHORT = 24
SEASON = 168
LAGS = list(range(1, SHORT + 1)) + [SEASON]
NEAR = 48
FAR = 40
data_weight = 2.0
penalty_weight = 0.5
ridge_weight = 0.2

VMEM = pl.BlockSpec(memory_space=pltpu.VMEM)
SMEM = pl.BlockSpec(memory_space=pltpu.SMEM)
SMALL = pltpu.CompilerParams(vmem_limit_bytes=2 << 20)


def against(left_rows, factors):
    return lax.dot_general(
        left_rows, factors, (((1,), (1,)), ((), ())), preferred_element_type=jnp.float32
    )


def lag_product(place_ref, field, near, far, weights_ref, window, short, last_time):
    rows, rank = field.shape
    here = place_ref[0]
    first_time = place_ref[1]
    window[...] = jnp.zeros_like(window)
    window[SEASON : SEASON + rows, :] = jnp.where(here == 2, field, 0.0)
    near_at = jnp.where(
        here == 0, 120, jnp.where(here == 1, 232, jnp.where(here == 2, 40, 312))
    )
    far_at = jnp.where(here == 1, 360, 0)
    window[pl.ds(pl.multiple_of(near_at, 8), NEAR), :] = near
    window[pl.ds(pl.multiple_of(far_at, 8), FAR), :] = far

    def weight(number):
        return weights_ref[number : number + 1, :]

    def lagged(start, count):
        base = SEASON + start
        result = window[base : base + count, :]
        for number, lag in enumerate(LAGS):
            result = result - weight(number) * window[base - lag : base - lag + count, :]
        stamp = first_time + start + lax.broadcasted_iota(jnp.int32, (count, rank), 0)
        return jnp.where(stamp < last_time, result, 0.0)

    short[...] = lagged(0, rows + SHORT)
    result = short[0:rows, :] - weight(SHORT) * lagged(SEASON, rows)
    for number in range(SHORT):
        lag = LAGS[number]
        result = result - weight(number) * short[lag : lag + rows, :]
    return result


def penalty_kernel(
    scale, last_time, place_ref, field_ref, near_ref, far_ref, weights_ref, local_ref,
    part_ref, window, short,
):
    product = lag_product(
        place_ref, field_ref[...], near_ref[...], far_ref[...], weights_ref, window, short, last_time
    )
    part_ref[...] = data_weight * local_ref[...] + scale * product


def sum_kernel(
    scale, place_ref, own_ref, first_ref, second_ref, third_ref, field_ref,
    total_ref, low_ref, near_ref, far_ref,
):
    here = place_ref[0]
    total = (own_ref[...] + second_ref[...]) + (first_ref[...] + third_ref[...])
    total = total + scale * field_ref[...]
    total_ref[...] = total
    low_ref[...] = total.astype(jnp.bfloat16)
    rows = total.shape[0]
    late = jnp.logical_or(here == 0, here == 3)
    near_ref[...] = jnp.where(late, total[rows - NEAR :], total[:NEAR])
    far_ref[...] = jnp.where(here == 0, total[rows - FAR :], total[:FAR])


def moments_kernel(
    share, last_time, place_ref, squares_ref, zero_ref, one_ref, two_ref, near_ref, far_ref,
    weights_ref, spread_ref, window, short,
):
    zero, one, two = zero_ref[...], one_ref[...], two_ref[...]
    product = lag_product(
        place_ref, two, near_ref[...], far_ref[...], weights_ref, window, short, last_time
    )

    def inner(left, right):
        return jnp.sum(jnp.sum(left * right, axis=0, keepdims=True), axis=1, keepdims=True)

    sums = [
        share * inner(zero, zero),
        share * inner(zero, one),
        share * inner(zero, two),
        share * inner(one, one),
        share * inner(one, two),
        share * inner(two, two),
        data_weight * squares_ref[0, 0] + penalty_weight * inner(two, product),
    ]
    lane = lax.broadcasted_iota(jnp.int32, (1, zero.shape[1]), 1)
    packed = jnp.zeros((1, zero.shape[1]), jnp.float32)
    for number, value in enumerate(sums):
        packed = jnp.where(lane == number, value, packed)
    spread_ref[...] = jnp.broadcast_to(packed[None], spread_ref.shape)


def update_kernel(gathered_ref, start_ref, zero_ref, one_ref, two_ref, final_ref, low_ref):
    total = jnp.sum(gathered_ref[...], axis=0)
    lane = lax.broadcasted_iota(jnp.int32, total.shape, 1)

    def pick(number):
        return jnp.sum(jnp.where(lane == number, total, 0.0), axis=1, keepdims=True)

    m00, m01, m02, m11, m12, m22, m23 = [pick(number) for number in range(7)]
    m23 = m23 + ridge_weight * m22
    alpha0 = m00 / m01
    norm1 = m00 - 2.0 * alpha0 * m01 + alpha0 * alpha0 * m11
    g0 = 1.0 + norm1 / m00
    curvature1 = g0 * g0 * m01 - g0 * alpha0 * (m02 + m11) + alpha0 * alpha0 * m12
    alpha1 = norm1 / curvature1
    a = -(alpha0 + alpha1 * g0)
    b = alpha0 * alpha1
    norm2 = m00 + a * a * m11 + b * b * m22 + 2.0 * (a * m01 + b * m02 + a * b * m12)
    beta1 = norm2 / norm1
    c = 1.0 + beta1 * g0
    d = a - beta1 * alpha0
    curvature2 = (
        c * c * m01
        + c * d * (m02 + m11)
        + 2.0 * c * b * m12
        + d * d * m12
        + 2.0 * d * b * m22
        + b * b * m23
    )
    alpha2 = norm2 / curvature2
    k0 = alpha0 + alpha1 * g0 + alpha2 * c
    k1 = alpha2 * d - alpha1 * alpha0
    k2 = alpha2 * b
    final = start_ref[...] + (k0 * zero_ref[...] + k1 * one_ref[...] + k2 * two_ref[...])
    final_ref[...] = final
    low_ref[...] = final.astype(jnp.bfloat16)


def on_device(series_values, observed, series_factors, time_factors, lag_weights):
    rows, rank = time_factors.shape
    n_tm = lax.axis_size("tm")
    n_series = lax.axis_size("series")
    everyone = n_tm * n_series
    last_time = n_tm * rows
    here = lax.axis_index("series")
    place = jnp.stack([here, lax.axis_index("tm") * rows]).astype(jnp.int32)
    field_shape = jax.ShapeDtypeStruct((rows, rank), jnp.float32)
    low_shape = jax.ShapeDtypeStruct((rows, rank), jnp.bfloat16)
    lag_scratch = [
        pltpu.VMEM((2 * SEASON + rows, rank), jnp.float32),
        pltpu.VMEM((rows + SHORT, rank), jnp.float32),
    ]

    def route(steps):
        pairs = []
        for column, step in enumerate(steps):
            if step is None:
                continue
            for source in range(n_tm):
                target = source + step
                if 0 <= target < n_tm:
                    pairs.append((source * n_series + column, target * n_series + column))
        return pairs

    near_route = route([1, -1, 2, -2])
    far_route = route([3, -3, None, None])

    def fetch(near, far):
        both = ("tm", "series")
        return lax.ppermute(near, both, near_route), lax.ppermute(far, both, far_route)

    def penalty(scale, field, near, far, local):
        return pl.pallas_call(
            functools.partial(penalty_kernel, scale, last_time),
            out_shape=field_shape,
            in_specs=[SMEM] + [VMEM] * 5,
            out_specs=VMEM,
            scratch_shapes=lag_scratch,
            compiler_params=SMALL,
        )(place, field, near, far, lag_weights, local)

    def series_sum(scale, part, field):
        def moved(distance):
            pairs = [(i, (i + distance) % n_series) for i in range(n_series)]
            return lax.ppermute(part, "series", pairs)

        return pl.pallas_call(
            functools.partial(sum_kernel, scale),
            out_shape=(
                field_shape,
                low_shape,
                jax.ShapeDtypeStruct((NEAR, rank), jnp.float32),
                jax.ShapeDtypeStruct((FAR, rank), jnp.float32),
            ),
            in_specs=[SMEM] + [VMEM] * 5,
            out_specs=(VMEM,) * 4,
            compiler_params=SMALL,
        )(place, part, moved(1), moved(2), moved(3), field)

    seen = observed == 1

    def fit(low):
        return jnp.where(seen, against(low, series_factors), 0.0)

    def back(rows_here):
        return jnp.dot(rows_here, series_factors, preferred_element_type=jnp.float32)

    late = (here == 0) | (here == 3)
    near = jnp.where(late, time_factors[rows - NEAR :], time_factors[:NEAR])
    far = jnp.where(here == 0, time_factors[rows - FAR :], time_factors[:FAR])
    near, far = fetch(near, far)
    kept = jnp.where(seen, series_values, jnp.zeros((), jnp.bfloat16))
    local = back(kept) - back(fit(time_factors.astype(jnp.bfloat16)).astype(jnp.bfloat16))
    part = penalty(-penalty_weight, time_factors, near, far, local)
    power0, low, near, far = series_sum(-ridge_weight, part, time_factors)

    def image(field, low, near, far):
        near, far = fetch(near, far)
        local = back(fit(low).astype(jnp.bfloat16))
        part = penalty(penalty_weight, field, near, far, local)
        return series_sum(ridge_weight, part, field)

    power1, low, near, far = image(power0, low, near, far)
    power2, low, near, far = image(power1, low, near, far)
    near, far = fetch(near, far)
    fitted = fit(low)
    squares = jnp.sum(fitted * fitted).reshape(1, 1)
    spread = pl.pallas_call(
        functools.partial(moments_kernel, 1.0 / n_series, last_time),
        out_shape=jax.ShapeDtypeStruct((everyone, 1, rank), jnp.float32),
        in_specs=[SMEM, SMEM] + [VMEM] * 6,
        out_specs=VMEM,
        scratch_shapes=lag_scratch,
        compiler_params=SMALL,
    )(place, squares, power0, power1, power2, near, far, lag_weights)
    gathered = lax.all_to_all(spread, ("tm", "series"), split_axis=0, concat_axis=0, tiled=True)
    final, final_low = pl.pallas_call(
        update_kernel,
        out_shape=(field_shape, low_shape),
        in_specs=[VMEM] * 5,
        out_specs=(VMEM, VMEM),
        compiler_params=SMALL,
    )(gathered, time_factors, power0, power1, power2)
    local_misfit = (series_values.astype(jnp.float32) - against(final_low, series_factors)).astype(
        jnp.bfloat16
    )
    misfit = lax.all_to_all(local_misfit, "tm", split_axis=1, concat_axis=0, tiled=True)
    return final, misfit


def solution(mesh):
    placed = (P("tm", "series"), P("tm", "series"), P("series", None), P("tm", None), P())
    return jax.shard_map(
        on_device,
        mesh=mesh,
        in_specs=placed,
        out_specs=(P("tm", None), P(None, ("series", "tm"))),
        check_vma=False,
    )
```

time: 160 us -> 132 us (0.82)
  between operations: 19.9 us -> 0.93 us
  Pallas kernels: 0 us -> 6.51 us
  matrix products: 11 us -> 6.32 us
  waiting for transfers between devices: 15.6 us -> 12 us
  local copies, waits for them, and re-layouts: 4.64 us -> 1.46 us
  other arithmetic: 5.95 us -> 3.75 us
  blocking collectives: 63.3 us -> 61.1 us
    pallas_call x0 -> x8, Pallas kernels: none -> 6.51 us  [the longest x3 2.27 us: penalty(): pl.pallas_call(functools.partial(penalty_kernel, scale, last_time), out_s...]
    dot_general x4, matrix products: 7.64 us -> 4.01 us  [back(): jnp.dot(rows_here, series_factors, preferred_element_type=jnp.float32)]
    ppermute x4, waiting for transfers between devices: 2.78 us -> 0.01 us  [fetch(): lax.ppermute(near, both, near_route)]
    all_to_all x1, blocking collectives: 30.9 us -> 28.7 us  [on_device(): lax.all_to_all(spread, ('tm', 'series'), split_axis=0, concat_axis=0, til...]
    mul x2 -> x0, local copies, waits for them, and re-layouts: 1.84 us -> none  [lagged(): result = result - lag_weights[number] * window[begin:begin + count]]
  transfers between devices with their start and end apart: 17 -> 17, of which waited for: 12 -> 9; matrix products, arithmetic and copies ran while one was open for 4% -> 6% of each run, Pallas kernels for 0% -> 0%
where the time goes in v2:
time: 132 us; the launch traced here: 131 us
  blocking collectives  61.1 us (46%)
  starting transfers between devices  39.4 us (30%)
  waiting for transfers between devices  12 us (9%)
  Pallas kernels  6.51 us (5%)
  matrix products  6.32 us (5%)
  other arithmetic  3.75 us (3%)
  local copies, waits for them, and re-layouts  1.46 us (1%)
    all_to_all x1, blocking collectives, on_device(): lax.all_to_all(local_misfit, 'tm', split_axis=1, concat_axis=0, tiled=True)  32.4 us
    all_to_all x1, blocking collectives, on_device(): lax.all_to_all(spread, ('tm', 'series'), split_axis=0, concat_axis=0, til...  28.7 us
    ppermute x4, starting transfers between devices, fetch(): lax.ppermute(far, both, far_route)  27.1 us
    ppermute x9, waiting for transfers between devices, moved(): return lax.ppermute(part, 'series', pairs)  12 us
    ppermute x4, starting transfers between devices, fetch(): lax.ppermute(near, both, near_route)  7.67 us
    ppermute x9, starting transfers between devices, moved(): return lax.ppermute(part, 'series', pairs)  4.61 us
    dot_general x4, matrix products, back(): jnp.dot(rows_here, series_factors, preferred_element_type=jnp.float32)  4.01 us
  transfers between devices with their start and end apart: 17, of which 9 were waited for; matrix products, arithmetic and copies ran while one was open for 6% of the time, Pallas kernels for 0%

profile of v2, /device:TPU:1, one launch (start us, length us, event | category | flops | bytes accessed | tf_op | source)
XLA Modules:
  0.0 131.5 jit_solution(3246589648120155566)
XLA Ops:
  0.6 0.0 copy-start
  0.7 0.9 slice_select_fusion.1
  1.5 6.2 %collective-permute-start.1 = (f32[40,128]{1,0:T(8,128)S(1)}, f32[40,128]{1,0:T(8,128)S(1)}, u32[]{:S(2)}, u32[]{:S(2)}) collective-permute-start(f32[40,128]{1,0:T(8,128)S(1)} %slice_select_fusion.1), channel_id=1, source_target_pairs={{0,12},{4,16},{8,20},{12,24},{16,28},{20,32},{24,36},{28,40},{32,4... | collective-permute-start | bytes 61448 | tf_op jit(solution)/shard_map/ppermute | solution.py:183
  7.8 0.8 slice_select_fusion
  8.6 1.9 %collective-permute-start = (f32[48,128]{1,0:T(8,128)S(1)}, f32[48,128]{1,0:T(8,128)S(1)}, u32[]{:S(2)}, u32[]{:S(2)}) collective-permute-start(f32[48,128]{1,0:T(8,128)S(1)} %slice_select_fusion), channel_id=1, source_target_pairs={{0,4},{4,8},{8,12},{12,16},{16,20},{20,24},{24,28},{28,32},{32,36}... | collective-permute-start | bytes 73736 | tf_op jit(solution)/shard_map/ppermute | solution.py:183
  10.5 0.0 copy-start.3
  10.5 2.0 %broadcast_compare_fusion = pred[64,8192]{1,0:T(32,128)(4,1)S(1)} fusion(s32[64,8192]{1,0:T(8,128)} %param.6), kind=kLoop, calls=%fused_computation.21 | loop fusion | flops 524288 | bytes 2621440 | tf_op jit(solution)/shard_map/eq | solution.py:213
  12.5 0.0 copy-done
  12.5 0.0 copy-done.3
  12.5 0.0 copy-start.1
  12.5 0.6 fusion.13
  13.1 0.2 copy-done.1
  13.3 1.1 fusion.9.local_ref
  14.4 0.1 pad_add_fusion.place_ref
  14.5 0.0 collective-permute-done.1.far_ref
  14.5 0.0 collective-permute-done.near_ref
  14.5 0.8 shard_map.68.own_ref
  15.3 0.1 collective-permute-start.4
  15.4 0.1 collective-permute-start.3
  15.5 1.4 %collective-permute-start.2 = (f32[64,128]{1,0:T(8,128)S(1)}, f32[64,128]{1,0:T(8,128)S(1)}, u32[]{:S(2)}, u32[]{:S(2)}) collective-permute-start(f32[64,128]{1,0:T(8,128)S(1)} %shard_map.68.own_ref), channel_id=1, source_target_pairs={{0,1},{1,2},{2,3},{3,0},{4,5},{5,6},{6,7},{7,4},{8,9},{9,10},{10,1... | collective-permute-start | bytes 98312 | tf_op jit(solution)/shard_map/ppermute | solution.py:198
  16.8 1.3 collective-permute-done.4.third_ref
  18.1 1.6 %collective-permute-done.3.second_ref = f32[64,128]{1,0:T(8,128)S(1)} collective-permute-done((f32[64,128]{1,0:T(8,128)S(1)}, f32[64,128]{1,0:T(8,128)S(1)}, u32[]{:S(2)}, u32[]{:S(2)}) %collective-permute-start.3) | collective-permute-done | bytes 32800 | tf_op jit(solution)/shard_map/ppermute | solution.py:198
  19.7 1.3 collective-permute-done.2.first_ref
  21.0 0.6 shard_map.69
  21.5 5.6 %collective-permute-start.6 = (f32[40,128]{1,0:T(8,128)S(1)}, f32[40,128]{1,0:T(8,128)S(1)}, u32[]{:S(2)}, u32[]{:S(2)}) collective-permute-start(f32[40,128]{1,0:T(8,128)S(1)} %get-tuple-element.18), channel_id=1, source_target_pairs={{0,12},{4,16},{8,20},{12,24},{16,28},{20,32},{24,36},{28,40},{32,4... | collective-permute-start | bytes 61448 | tf_op jit(solution)/shard_map/ppermute | solution.py:183
  27.1 1.9 %collective-permute-start.5 = (f32[48,128]{1,0:T(8,128)S(1)}, f32[48,128]{1,0:T(8,128)S(1)}, u32[]{:S(2)}, u32[]{:S(2)}) collective-permute-start(f32[48,128]{1,0:T(8,128)S(1)} %get-tuple-element.17), channel_id=1, source_target_pairs={{0,4},{4,8},{8,12},{12,16},{16,20},{20,24},{24,28},{28,32},{32,36}... | collective-permute-start | bytes 73736 | tf_op jit(solution)/shard_map/ppermute | solution.py:183
  29.0 1.1 fusion.7.local_ref
  30.2 0.0 collective-permute-done.6.far_ref
  30.2 0.0 collective-permute-done.5.near_ref
  30.2 0.8 shard_map.70.own_ref
  31.0 0.1 collective-permute-start.9
  31.1 0.2 collective-permute-start.8
  31.2 1.3 collective-permute-start.7
  32.5 1.3 collective-permute-done.9.third_ref
  33.8 1.6 %collective-permute-done.8.second_ref = f32[64,128]{1,0:T(8,128)S(1)} collective-permute-done((f32[64,128]{1,0:T(8,128)S(1)}, f32[64,128]{1,0:T(8,128)S(1)}, u32[]{:S(2)}, u32[]{:S(2)}) %collective-permute-start.8) | collective-permute-done | bytes 32800 | tf_op jit(solution)/shard_map/ppermute | solution.py:198
  35.4 0.8 collective-permute-done.7.first_ref
  36.2 0.6 shard_map.71
  36.8 7.5 %collective-permute-start.11 = (f32[40,128]{1,0:T(8,128)S(1)}, f32[40,128]{1,0:T(8,128)S(1)}, u32[]{:S(2)}, u32[]{:S(2)}) collective-permute-start(f32[40,128]{1,0:T(8,128)S(1)} %get-tuple-element.22), channel_id=1, source_target_pairs={{0,12},{4,16},{8,20},{12,24},{16,28},{20,32},{24,36},{28,40},{32,4... | collective-permute-start | bytes 61448 | tf_op jit(solution)/shard_map/ppermute | solution.py:183
  44.3 1.9 %collective-permute-start.10 = (f32[48,128]{1,0:T(8,128)S(1)}, f32[48,128]{1,0:T(8,128)S(1)}, u32[]{:S(2)}, u32[]{:S(2)}) collective-permute-start(f32[48,128]{1,0:T(8,128)S(1)} %get-tuple-element.21), channel_id=1, source_target_pairs={{0,4},{4,8},{8,12},{12,16},{16,20},{20,24},{24,28},{28,32},{32,36}... | collective-permute-start | bytes 73736 | tf_op jit(solution)/shard_map/ppermute | solution.py:183
  46.2 1.1 fusion.6.local_ref
  47.4 0.0 copy-start.4
  47.4 0.0 collective-permute-done.11.far_ref
  47.4 0.0 collective-permute-done.10.near_ref
  47.4 0.8 shard_map.72.own_ref
  48.2 0.1 collective-permute-start.14
  48.3 0.7 collective-permute-start.13
  49.0 0.8 collective-permute-start.12
  49.7 1.3 collective-permute-done.14.third_ref
  51.0 1.6 %collective-permute-done.13.second_ref = f32[64,128]{1,0:T(8,128)S(1)} collective-permute-done((f32[64,128]{1,0:T(8,128)S(1)}, f32[64,128]{1,0:T(8,128)S(1)}, u32[]{:S(2)}, u32[]{:S(2)}) %collective-permute-start.13) | collective-permute-done | bytes 32800 | tf_op jit(solution)/shard_map/ppermute | solution.py:198
  52.6 1.3 collective-permute-done.12.first_ref
  53.9 0.6 shard_map.73
  54.5 7.8 %collective-permute-start.16 = (f32[40,128]{1,0:T(8,128)S(1)}, f32[40,128]{1,0:T(8,128)S(1)}, u32[]{:S(2)}, u32[]{:S(2)}) collective-permute-start(f32[40,128]{1,0:T(8,128)S(1)} %get-tuple-element.27), channel_id=1, source_target_pairs={{0,12},{4,16},{8,20},{12,24},{16,28},{20,32},{24,36},{28,40},{32,4... | collective-permute-start | bytes 61448 | tf_op jit(solution)/shard_map/ppermute | solution.py:183
  62.2 1.9 %collective-permute-start.15 = (f32[48,128]{1,0:T(8,128)S(1)}, f32[48,128]{1,0:T(8,128)S(1)}, u32[]{:S(2)}, u32[]{:S(2)}) collective-permute-start(f32[48,128]{1,0:T(8,128)S(1)} %get-tuple-element.26), channel_id=1, source_target_pairs={{0,4},{4,8},{8,12},{12,16},{16,20},{20,24},{24,28},{28,32},{32,36}... | collective-permute-start | bytes 73736 | tf_op jit(solution)/shard_map/ppermute | solution.py:183
  64.2 1.5 %fusion.15 = f32[]{:T(128)} fusion(pred[64,8192]{1,0:T(32,128)(4,1)S(1)} %broadcast_compare_fusion, bf16[64,128]{1,0:T(8,128)(2,1)S(1)} %get-tuple-element.24, bf16[8192,128]{1,0:T(8,128)(2,1)S(1)} %copy-done), kind=kOutput, calls=%fused_computation.22 | convolution fusion | flops 135790592 | bytes 2637828 | tf_op jit(solution)/shard_map/dot_general | solution.py:25
  65.6 0.0 collective-permute-done.16.far_ref
  65.6 0.0 collective-permute-done.15.near_ref
  65.6 1.6 %shard_map.74 = f32[256,1,128]{2,1,0:T(1,128)S(1)} custom-call(s32[2]{0:T(128)S(1)} %pad_add_fusion.place_ref, f32[1,1]{1,0:T(1,128)} %bitcast.2.squares_ref, f32[64,128]{1,0:T(8,128)S(1)} %get-tuple-element.16.field_ref.zero_ref, f32[64,128]{1,0:T(8,128)S(1)} %get-tuple-element.20.field_ref.one_ref, f32[64,128]{1,0:T(8,128)S(1)} %get-tuple-element.25.two_ref, ...), custom_call_target="tpu_custom_call" | custom-call | tf_op jit(solution)/shard_map/pallas_call | solution.py:241
  67.2 28.7 %all_to_all.24.gathered_ref = f32[256,1,128]{2,1,0:T(1,128)S(1)} all-to-all(f32[256,1,128]{2,1,0:T(1,128)S(1)} %shard_map.74), channel_id=1, replica_groups=mesh['tm'=64,'series'=4] {'tm','series'}, dimensions={0} | all-to-all | bytes 262144 | tf_op jit(solution)/shard_map/all_to_all | solution.py:249
  95.9 1.0 shard_map.75
  96.9 0.0 copy-done.4
  96.9 0.9 fusion.5
  97.8 0.3 copy.11
  98.1 32.4 %all_to_all.25 = bf16[64,64,128]{2,0,1:T(8,128)(2,1)S(1)} all-to-all(bf16[64,64,128]{2,0,1:T(8,128)(2,1)S(1)} %bitcast.25), channel_id=1, replica_groups=mesh['tm'=64,'series'=4] {'tm'}, dimensions={1} | all-to-all | bytes 2097152 | tf_op jit(solution)/shard_map/all_to_all | solution.py:260
  130.5 1.0 copy.19
  (2 shorter events, 0.0 us)
Async XLA Ops:
  0.6 11.8 %copy-start = (bf16[8192,128]{1,0:T(8,128)(2,1)S(1)}, bf16[8192,128]{1,0:T(8,128)(2,1)}, u32[]{:S(2)}) copy-start(bf16[8192,128]{1,0:T(8,128)(2,1)} %param.7) | copy-start | bytes 6291460
  1.5 12.9 %collective-permute-start.1 = (f32[40,128]{1,0:T(8,128)S(1)}, f32[40,128]{1,0:T(8,128)S(1)}, u32[]{:S(2)}, u32[]{:S(2)}) collective-permute-start(f32[40,128]{1,0:T(8,128)S(1)} %slice_select_fusion.1), channel_id=1, source_target_pairs={{0,12},{4,16},{8,20},{12,24},{16,28},{20,32},{24,36},{28,40},{32,4... | collective-permute-start | bytes 61448 | tf_op jit(solution)/shard_map/ppermute | solution.py:183
  8.6 5.9 %collective-permute-start = (f32[48,128]{1,0:T(8,128)S(1)}, f32[48,128]{1,0:T(8,128)S(1)}, u32[]{:S(2)}, u32[]{:S(2)}) collective-permute-start(f32[48,128]{1,0:T(8,128)S(1)} %slice_select_fusion), channel_id=1, source_target_pairs={{0,4},{4,8},{8,12},{12,16},{16,20},{20,24},{24,28},{28,32},{32,36}... | collective-permute-start | bytes 73736 | tf_op jit(solution)/shard_map/ppermute | solution.py:183
  10.5 2.0 %copy-start.3 = (bf16[64,8192]{1,0:T(8,128)(2,1)S(1)}, bf16[64,8192]{1,0:T(8,128)(2,1)}, u32[]{:S(2)}) copy-start(bf16[64,8192]{1,0:T(8,128)(2,1)} %param.5) | copy-start | bytes 3145732
  12.5 0.8 copy-start.1
  13.3 1.2 copy-start.2
  15.3 2.8 %collective-permute-start.4 = (f32[64,128]{1,0:T(8,128)S(1)}, f32[64,128]{1,0:T(8,128)S(1)}, u32[]{:S(2)}, u32[]{:S(2)}) collective-permute-start(f32[64,128]{1,0:T(8,128)S(1)} %shard_map.68.own_ref), channel_id=1, source_target_pairs={{0,3},{1,0},{2,1},{3,2},{4,7},{5,4},{6,5},{7,6},{8,11},{9,8},{10,9... | collective-permute-start | bytes 98312 | tf_op jit(solution)/shard_map/ppermute | solution.py:198
  15.4 4.4 %collective-permute-start.3 = (f32[64,128]{1,0:T(8,128)S(1)}, f32[64,128]{1,0:T(8,128)S(1)}, u32[]{:S(2)}, u32[]{:S(2)}) collective-permute-start(f32[64,128]{1,0:T(8,128)S(1)} %shard_map.68.own_ref), channel_id=1, source_target_pairs={{0,2},{1,3},{2,0},{3,1},{4,6},{5,7},{6,4},{7,5},{8,10},{9,11},{10,... | collective-permute-start | bytes 98312 | tf_op jit(solution)/shard_map/ppermute | solution.py:198
  15.5 5.5 %collective-permute-start.2 = (f32[64,128]{1,0:T(8,128)S(1)}, f32[64,128]{1,0:T(8,128)S(1)}, u32[]{:S(2)}, u32[]{:S(2)}) collective-permute-start(f32[64,128]{1,0:T(8,128)S(1)} %shard_map.68.own_ref), channel_id=1, source_target_pairs={{0,1},{1,2},{2,3},{3,0},{4,5},{5,6},{6,7},{7,4},{8,9},{9,10},{10,1... | collective-permute-start | bytes 98312 | tf_op jit(solution)/shard_map/ppermute | solution.py:198
  21.5 8.7 %collective-permute-start.6 = (f32[40,128]{1,0:T(8,128)S(1)}, f32[40,128]{1,0:T(8,128)S(1)}, u32[]{:S(2)}, u32[]{:S(2)}) collective-permute-start(f32[40,128]{1,0:T(8,128)S(1)} %get-tuple-element.18), channel_id=1, source_target_pairs={{0,12},{4,16},{8,20},{12,24},{16,28},{20,32},{24,36},{28,40},{32,4... | collective-permute-start | bytes 61448 | tf_op jit(solution)/shard_map/ppermute | solution.py:183
  27.1 3.1 %collective-permute-start.5 = (f32[48,128]{1,0:T(8,128)S(1)}, f32[48,128]{1,0:T(8,128)S(1)}, u32[]{:S(2)}, u32[]{:S(2)}) collective-permute-start(f32[48,128]{1,0:T(8,128)S(1)} %get-tuple-element.17), channel_id=1, source_target_pairs={{0,4},{4,8},{8,12},{12,16},{16,20},{20,24},{24,28},{28,32},{32,36}... | collective-permute-start | bytes 73736 | tf_op jit(solution)/shard_map/ppermute | solution.py:183
  31.0 2.8 %collective-permute-start.9 = (f32[64,128]{1,0:T(8,128)S(1)}, f32[64,128]{1,0:T(8,128)S(1)}, u32[]{:S(2)}, u32[]{:S(2)}) collective-permute-start(f32[64,128]{1,0:T(8,128)S(1)} %shard_map.70.own_ref), channel_id=1, source_target_pairs={{0,3},{1,0},{2,1},{3,2},{4,7},{5,4},{6,5},{7,6},{8,11},{9,8},{10,9... | collective-permute-start | bytes 98312 | tf_op jit(solution)/shard_map/ppermute | solution.py:198
  31.1 4.4 %collective-permute-start.8 = (f32[64,128]{1,0:T(8,128)S(1)}, f32[64,128]{1,0:T(8,128)S(1)}, u32[]{:S(2)}, u32[]{:S(2)}) collective-permute-start(f32[64,128]{1,0:T(8,128)S(1)} %shard_map.70.own_ref), channel_id=1, source_target_pairs={{0,2},{1,3},{2,0},{3,1},{4,6},{5,7},{6,4},{7,5},{8,10},{9,11},{10,... | collective-permute-start | bytes 98312 | tf_op jit(solution)/shard_map/ppermute | solution.py:198
  31.2 5.0 %collective-permute-start.7 = (f32[64,128]{1,0:T(8,128)S(1)}, f32[64,128]{1,0:T(8,128)S(1)}, u32[]{:S(2)}, u32[]{:S(2)}) collective-permute-start(f32[64,128]{1,0:T(8,128)S(1)} %shard_map.70.own_ref), channel_id=1, source_target_pairs={{0,1},{1,2},{2,3},{3,0},{4,5},{5,6},{6,7},{7,4},{8,9},{9,10},{10,1... | collective-permute-start | bytes 98312 | tf_op jit(solution)/shard_map/ppermute | solution.py:198
  36.8 10.6 %collective-permute-start.11 = (f32[40,128]{1,0:T(8,128)S(1)}, f32[40,128]{1,0:T(8,128)S(1)}, u32[]{:S(2)}, u32[]{:S(2)}) collective-permute-start(f32[40,128]{1,0:T(8,128)S(1)} %get-tuple-element.22), channel_id=1, source_target_pairs={{0,12},{4,16},{8,20},{12,24},{16,28},{20,32},{24,36},{28,40},{32,4... | collective-permute-start | bytes 61448 | tf_op jit(solution)/shard_map/ppermute | solution.py:183
  44.3 3.1 %collective-permute-start.10 = (f32[48,128]{1,0:T(8,128)S(1)}, f32[48,128]{1,0:T(8,128)S(1)}, u32[]{:S(2)}, u32[]{:S(2)}) collective-permute-start(f32[48,128]{1,0:T(8,128)S(1)} %get-tuple-element.21), channel_id=1, source_target_pairs={{0,4},{4,8},{8,12},{12,16},{16,20},{20,24},{24,28},{28,32},{32,36}... | collective-permute-start | bytes 73736 | tf_op jit(solution)/shard_map/ppermute | solution.py:183
  47.4 49.5 %copy-start.4 = (bf16[64,8192]{1,0:T(8,128)(2,1)S(1)}, bf16[64,8192]{1,0:T(8,128)(2,1)}, u32[]{:S(2)}) copy-start(bf16[64,8192]{1,0:T(8,128)(2,1)} %param.5) | copy-start | bytes 3145732
  48.2 2.8 %collective-permute-start.14 = (f32[64,128]{1,0:T(8,128)S(1)}, f32[64,128]{1,0:T(8,128)S(1)}, u32[]{:S(2)}, u32[]{:S(2)}) collective-permute-start(f32[64,128]{1,0:T(8,128)S(1)} %shard_map.72.own_ref), channel_id=1, source_target_pairs={{0,3},{1,0},{2,1},{3,2},{4,7},{5,4},{6,5},{7,6},{8,11},{9,8},{10,9... | collective-permute-start | bytes 98312 | tf_op jit(solution)/shard_map/ppermute | solution.py:198
  48.3 4.4 %collective-permute-start.13 = (f32[64,128]{1,0:T(8,128)S(1)}, f32[64,128]{1,0:T(8,128)S(1)}, u32[]{:S(2)}, u32[]{:S(2)}) collective-permute-start(f32[64,128]{1,0:T(8,128)S(1)} %shard_map.72.own_ref), channel_id=1, source_target_pairs={{0,2},{1,3},{2,0},{3,1},{4,6},{5,7},{6,4},{7,5},{8,10},{9,11},{10,... | collective-permute-start | bytes 98312 | tf_op jit(solution)/shard_map/ppermute | solution.py:198
  49.0 4.9 %collective-permute-start.12 = (f32[64,128]{1,0:T(8,128)S(1)}, f32[64,128]{1,0:T(8,128)S(1)}, u32[]{:S(2)}, u32[]{:S(2)}) collective-permute-start(f32[64,128]{1,0:T(8,128)S(1)} %shard_map.72.own_ref), channel_id=1, source_target_pairs={{0,1},{1,2},{2,3},{3,0},{4,5},{5,6},{6,7},{7,4},{8,9},{9,10},{10,1... | collective-permute-start | bytes 98312 | tf_op jit(solution)/shard_map/ppermute | solution.py:198
  54.5 11.2 %collective-permute-start.16 = (f32[40,128]{1,0:T(8,128)S(1)}, f32[40,128]{1,0:T(8,128)S(1)}, u32[]{:S(2)}, u32[]{:S(2)}) collective-permute-start(f32[40,128]{1,0:T(8,128)S(1)} %get-tuple-element.27), channel_id=1, source_target_pairs={{0,12},{4,16},{8,20},{12,24},{16,28},{20,32},{24,36},{28,40},{32,4... | collective-permute-start | bytes 61448 | tf_op jit(solution)/shard_map/ppermute | solution.py:183
  62.2 3.4 %collective-permute-start.15 = (f32[48,128]{1,0:T(8,128)S(1)}, f32[48,128]{1,0:T(8,128)S(1)}, u32[]{:S(2)}, u32[]{:S(2)}) collective-permute-start(f32[48,128]{1,0:T(8,128)S(1)} %get-tuple-element.26), channel_id=1, source_target_pairs={{0,4},{4,8},{8,12},{12,16},{16,20},{20,24},{24,28},{28,32},{32,36}... | collective-permute-start | bytes 73736 | tf_op jit(solution)/shard_map/ppermute | solution.py:183

commit v3 on v2

v3 whole, which is shorter than its diff:
```python
import functools

import jax
import jax.numpy as jnp
from jax import lax
from jax.experimental import pallas as pl
from jax.experimental.pallas import tpu as pltpu
from jax.sharding import PartitionSpec as P

SHORT = 24
SEASON = 168
LAGS = list(range(1, SHORT + 1)) + [SEASON]
MANY = 48
FEW = 24
EDGE = SEASON + 8
data_weight = 2.0
penalty_weight = 0.5
ridge_weight = 0.2

VMEM = pl.BlockSpec(memory_space=pltpu.VMEM)
SMEM = pl.BlockSpec(memory_space=pltpu.SMEM)
SMALL = pltpu.CompilerParams(vmem_limit_bytes=2 << 20)


def against(left_rows, factors):
    return lax.dot_general(
        left_rows, factors, (((1,), (1,)), ((), ())), preferred_element_type=jnp.float32
    )


def lag_product(place_ref, blocks, weights_ref, window, short, last_time):
    rank = weights_ref.shape[1]
    rows = window.shape[0] - 2 * EDGE
    first_time = place_ref[1]
    window[...] = jnp.zeros_like(window)
    for start, block in blocks:
        if not isinstance(start, int):
            start = pl.multiple_of(start, 8)
        window[pl.ds(start, block.shape[0]), :] = block

    def weight(number):
        return weights_ref[number : number + 1, :]

    def lagged(start, count):
        base = EDGE + start
        result = window[base : base + count, :]
        for number, lag in enumerate(LAGS):
            result = result - weight(number) * window[base - lag : base - lag + count, :]
        stamp = first_time + start + lax.broadcasted_iota(jnp.int32, (count, rank), 0)
        return jnp.where(stamp < last_time, result, 0.0)

    short[...] = lagged(0, rows + SHORT)
    result = short[0:rows, :] - weight(SHORT) * lagged(SEASON, rows)
    for number in range(SHORT):
        lag = LAGS[number]
        result = result - weight(number) * short[lag : lag + rows, :]
    return result


def penalty_kernel(
    scale, last_time, place_ref, field_ref, many_ref, few_ref, weights_ref, local_ref,
    part_ref, window, short,
):
    here = place_ref[0]
    many_at = jnp.where(
        here == 0, 0, jnp.where(here == 1, 368, jnp.where(here == 2, 48, 320))
    )
    blocks = [
        (EDGE, jnp.where(here == 0, field_ref[...], 0.0)),
        (many_at, many_ref[...]),
        (jnp.where(here == 3, 240, 152), few_ref[...]),
    ]
    product = lag_product(place_ref, blocks, weights_ref, window, short, last_time)
    part_ref[...] = data_weight * local_ref[...] + scale * product


def halo(here, field, many_ref, few_ref):
    rows = field.shape[0]
    late = jnp.logical_or(here == 0, here == 3)
    many_ref[...] = jnp.where(late, field[rows - MANY :], field[:MANY])
    few_ref[...] = jnp.where(here == 2, field[rows - FEW :], field[:FEW])


def start_kernel(place_ref, field_ref, low_ref, many_ref, few_ref):
    field = field_ref[...]
    low_ref[...] = field.astype(jnp.bfloat16)
    halo(place_ref[0], field, many_ref, few_ref)


def sum_kernel(
    scale, place_ref, own_ref, first_ref, second_ref, third_ref, field_ref,
    total_ref, low_ref, many_ref, few_ref,
):
    here = place_ref[0]
    total = (own_ref[...] + second_ref[...]) + (first_ref[...] + third_ref[...])
    total = total + scale * field_ref[...]
    total_ref[...] = total
    low_ref[...] = total.astype(jnp.bfloat16)
    halo(here, total, many_ref, few_ref)


def moments_kernel(
    share, last_time, place_ref, squares_ref, zero_ref, one_ref, two_ref, many_ref,
    weights_ref, spread_ref, window, short,
):
    zero, one, two = zero_ref[...], one_ref[...], two_ref[...]
    here = place_ref[0]
    many_at = jnp.where(here == 0, 0, jnp.where(here == 2, 48, 128))
    blocks = [
        (EDGE, jnp.where(here == 1, two, 0.0)),
        (many_at, jnp.where(here == 1, 0.0, 2.0 * many_ref[...])),
    ]
    product = lag_product(place_ref, blocks, weights_ref, window, short, last_time)

    def inner(left, right):
        return jnp.sum(jnp.sum(left * right, axis=0, keepdims=True), axis=1, keepdims=True)

    sums = [
        share * inner(zero, zero),
        share * inner(zero, one),
        share * inner(zero, two),
        share * inner(one, one),
        share * inner(one, two),
        share * inner(two, two),
        data_weight * squares_ref[0, 0] + penalty_weight * inner(two, product),
    ]
    lane = lax.broadcasted_iota(jnp.int32, (1, zero.shape[1]), 1)
    packed = jnp.zeros((1, zero.shape[1]), jnp.float32)
    for number, value in enumerate(sums):
        packed = jnp.where(lane == number, value, packed)
    spread_ref[...] = jnp.broadcast_to(packed[None], spread_ref.shape)


def update_kernel(
    gathered_ref, start_ref, zero_ref, one_ref, two_ref, values_ref, factors_ref,
    final_ref, misfit_ref,
):
    total = jnp.sum(gathered_ref[...], axis=0)
    lane = lax.broadcasted_iota(jnp.int32, total.shape, 1)

    def pick(number):
        return jnp.sum(jnp.where(lane == number, total, 0.0), axis=1, keepdims=True)

    m00, m01, m02, m11, m12, m22, m23 = [pick(number) for number in range(7)]
    m23 = m23 + ridge_weight * m22
    alpha0 = m00 / m01
    norm1 = m00 - 2.0 * alpha0 * m01 + alpha0 * alpha0 * m11
    g0 = 1.0 + norm1 / m00
    curvature1 = g0 * g0 * m01 - g0 * alpha0 * (m02 + m11) + alpha0 * alpha0 * m12
    alpha1 = norm1 / curvature1
    a = -(alpha0 + alpha1 * g0)
    b = alpha0 * alpha1
    norm2 = m00 + a * a * m11 + b * b * m22 + 2.0 * (a * m01 + b * m02 + a * b * m12)
    beta1 = norm2 / norm1
    c = 1.0 + beta1 * g0
    d = a - beta1 * alpha0
    curvature2 = (
        c * c * m01
        + c * d * (m02 + m11)
        + 2.0 * c * b * m12
        + d * d * m12
        + 2.0 * d * b * m22
        + b * b * m23
    )
    alpha2 = norm2 / curvature2
    k0 = alpha0 + alpha1 * g0 + alpha2 * c
    k1 = alpha2 * d - alpha1 * alpha0
    k2 = alpha2 * b
    final = start_ref[...] + (k0 * zero_ref[...] + k1 * one_ref[...] + k2 * two_ref[...])
    final_ref[...] = final
    low = final.astype(jnp.bfloat16)
    lanes = misfit_ref.shape[2]
    for first in range(0, values_ref.shape[1], 2 * lanes):
        columns = slice(first, first + 2 * lanes)
        fitted = against(low, factors_ref[columns, :])
        block = (values_ref[:, columns].astype(jnp.float32) - fitted).astype(jnp.bfloat16)
        misfit_ref[first // lanes] = block[:, :lanes]
        misfit_ref[first // lanes + 1] = block[:, lanes:]


def on_device(series_values, observed, series_factors, time_factors, lag_weights):
    rows, rank = time_factors.shape
    n_tm = lax.axis_size("tm")
    n_series = lax.axis_size("series")
    everyone = n_tm * n_series
    last_time = n_tm * rows
    here = lax.axis_index("series")
    place = jnp.stack([here, lax.axis_index("tm") * rows]).astype(jnp.int32)
    field_shape = jax.ShapeDtypeStruct((rows, rank), jnp.float32)
    many_shape = jax.ShapeDtypeStruct((MANY, rank), jnp.float32)
    few_shape = jax.ShapeDtypeStruct((FEW, rank), jnp.float32)
    low_shape = jax.ShapeDtypeStruct((rows, rank), jnp.bfloat16)
    lag_scratch = [
        pltpu.VMEM((2 * EDGE + rows, rank), jnp.float32),
        pltpu.VMEM((rows + SHORT, rank), jnp.float32),
    ]

    def route(steps):
        pairs = []
        for column, step in enumerate(steps):
            if step is None:
                continue
            for source in range(n_tm):
                target = source + step
                if 0 <= target < n_tm:
                    pairs.append((source * n_series + column, target * n_series + column))
        return pairs

    many_route = route([3, -3, 2, -2])
    few_route = route([None, None, 1, -1])
    last_route = route([3, None, 2, 1])
    both = ("tm", "series")

    def fetch(many, few):
        few = lax.ppermute(few, both, few_route)
        return lax.ppermute(many, both, many_route), few

    def penalty(scale, field, many, few, local):
        return pl.pallas_call(
            functools.partial(penalty_kernel, scale, last_time),
            out_shape=field_shape,
            in_specs=[SMEM] + [VMEM] * 5,
            out_specs=VMEM,
            scratch_shapes=lag_scratch,
            compiler_params=SMALL,
        )(place, field, many, few, lag_weights, local)

    def series_sum(scale, part, field):
        def moved(distance):
            pairs = [(i, (i + distance) % n_series) for i in range(n_series)]
            return lax.ppermute(part, "series", pairs)

        first, third = moved(1), moved(3)
        second = moved(2)
        return pl.pallas_call(
            functools.partial(sum_kernel, scale),
            out_shape=(
                field_shape,
                low_shape,
                many_shape,
                few_shape,
            ),
            in_specs=[SMEM] + [VMEM] * 5,
            out_specs=(VMEM,) * 4,
            compiler_params=SMALL,
        )(place, part, first, second, third, field)

    seen = observed == 1

    def fit(low):
        return jnp.where(seen, against(low, series_factors), 0.0)

    def back(rows_here):
        return jnp.dot(rows_here, series_factors, preferred_element_type=jnp.float32)

    low, many, few = pl.pallas_call(
        start_kernel,
        out_shape=(low_shape, many_shape, few_shape),
        in_specs=[SMEM, VMEM],
        out_specs=(VMEM,) * 3,
        compiler_params=SMALL,
    )(place, time_factors)
    many, few = fetch(many, few)
    kept = jnp.where(seen, series_values, jnp.zeros((), jnp.bfloat16))
    local = back(kept) - back(fit(low).astype(jnp.bfloat16))
    part = penalty(-penalty_weight, time_factors, many, few, local)
    power0, low, many, few = series_sum(-ridge_weight, part, time_factors)

    def image(field, low, many, few):
        many, few = fetch(many, few)
        local = back(fit(low).astype(jnp.bfloat16))
        part = penalty(penalty_weight, field, many, few, local)
        return series_sum(ridge_weight, part, field)

    power1, low, many, few = image(power0, low, many, few)
    power2, low, many, few = image(power1, low, many, few)
    many = lax.ppermute(many, both, last_route)
    fitted = fit(low)
    squares = jnp.sum(fitted * fitted).reshape(1, 1)
    spread = pl.pallas_call(
        functools.partial(moments_kernel, 1.0 / n_series, last_time),
        out_shape=jax.ShapeDtypeStruct((everyone, 1, rank), jnp.float32),
        in_specs=[SMEM, SMEM] + [VMEM] * 5,
        out_specs=VMEM,
        scratch_shapes=lag_scratch,
        compiler_params=SMALL,
    )(place, squares, power0, power1, power2, many, lag_weights)
    gathered = lax.all_to_all(spread, both, split_axis=0, concat_axis=0, tiled=True)
    final, misfit = pl.pallas_call(
        update_kernel,
        out_shape=(field_shape, jax.ShapeDtypeStruct((n_tm, rows, rank), jnp.bfloat16)),
        in_specs=[VMEM] * 7,
        out_specs=(VMEM, VMEM),
        compiler_params=SMALL,
    )(gathered, time_factors, power0, power1, power2, series_values, series_factors)
    misfit = lax.all_to_all(misfit, "tm", split_axis=0, concat_axis=0, tiled=True)
    return final, misfit.reshape(n_tm * rows, rank)


def solution(mesh):
    placed = (P("tm", "series"), P("tm", "series"), P("series", None), P("tm", None), P())
    return jax.shard_map(
        on_device,
        mesh=mesh,
        in_specs=placed,
        out_specs=(P("tm", None), P(None, ("series", "tm"))),
        check_vma=False,
    )
```

time: 132 us -> 131 us (level)
  starting transfers between devices: 39.4 us -> 36.6 us
  other arithmetic: 3.75 us -> 1.94 us
  blocking collectives: 61.1 us -> 62.9 us
  Pallas kernels: 6.51 us -> 7.91 us
    ppermute x8 -> x7, starting transfers between devices: 34.7 us -> 25.9 us  [the longest x3 17 us: fetch(): return (lax.ppermute(many, both, many_route), few)]
    ppermute x9, starting transfers between devices: 4.61 us -> 10.7 us  [moved(): return lax.ppermute(part, 'series', pairs)]
    all_to_all x2, blocking collectives: 61.1 us -> 62.9 us  [the longest x1 32.4 us: on_device(): lax.all_to_all(misfit, 'tm', split_axis=0, concat_axis=0, tiled=True)]
    select_n x2 -> x0, other arithmetic: 1.72 us -> none  [the longest x1 0.9 us: on_device(): far = jnp.where(here == 0, time_factors[rows - FAR:], time_factors[:FAR])]
  transfers between devices with their start and end apart: 17 -> 16, of which waited for: 9 -> 7; matrix products, arithmetic and copies ran while one was open for 6% -> 7% of each run, Pallas kernels for 0% -> 0%
where the time goes in v3:
time: 131 us; the launch traced here: 130 us
  blocking collectives  62.9 us (48%)
  starting transfers between devices  36.6 us (28%)
  waiting for transfers between devices  11.3 us (9%)
  Pallas kernels  7.91 us (6%)
  matrix products  6.77 us (5%)
  other arithmetic  1.94 us (1%)
  local copies, waits for them, and re-layouts  1.88 us (1%)
    all_to_all x1, blocking collectives, on_device(): lax.all_to_all(misfit, 'tm', split_axis=0, concat_axis=0, tiled=True)  32.4 us
    all_to_all x1, blocking collectives, on_device(): lax.all_to_all(spread, both, split_axis=0, concat_axis=0, tiled=True)  30.5 us
    ppermute x3, starting transfers between devices, fetch(): return (lax.ppermute(many, both, many_route), few)  17 us
    ppermute x9, waiting for transfers between devices, moved(): return lax.ppermute(part, 'series', pairs)  11.3 us
    ppermute x9, starting transfers between devices, moved(): return lax.ppermute(part, 'series', pairs)  10.7 us
    ppermute x1, starting transfers between devices, on_device(): many = lax.ppermute(many, both, last_route)  6.9 us
    dot_general x4, matrix products, back(): jnp.dot(rows_here, series_factors, preferred_element_type=jnp.float32)  5.3 us
  transfers between devices with their start and end apart: 16, of which 7 were waited for; matrix products, arithmetic and copies ran while one was open for 7% of the time, Pallas kernels for 0%

profile of v3, /device:TPU:1, one launch (start us, length us, event | category | flops | bytes accessed | tf_op | source)
XLA Modules:
  0.0 130.2 jit_solution(5819515092159945152)
XLA Ops:
  0.6 0.0 copy-start
  0.6 0.1 pad_add_fusion.place_ref
  0.7 0.0 copy-start.2
  0.7 0.9 copy-done.2
  1.6 0.5 shard_map.68
  2.2 0.7 collective-permute-start.1
  2.8 6.2 %collective-permute-start = (f32[48,128]{1,0:T(8,128)S(1)}, f32[48,128]{1,0:T(8,128)S(1)}, u32[]{:S(2)}, u32[]{:S(2)}) collective-permute-start(f32[48,128]{1,0:T(8,128)S(1)} %get-tuple-element.18), channel_id=1, source_target_pairs={{0,12},{4,16},{8,20},{12,24},{16,28},{20,32},{24,36},{28,40},{32,4... | collective-permute-start | bytes 73736 | tf_op jit(solution)/shard_map/ppermute | solution.py:216
  9.1 1.9 %broadcast_compare_fusion = pred[64,8192]{1,0:T(32,128)(4,1)S(1)} fusion(s32[64,8192]{1,0:T(8,128)} %param.6), kind=kLoop, calls=%fused_computation.17 | loop fusion | flops 524288 | bytes 2621440 | tf_op jit(solution)/shard_map/eq | solution.py:248
  10.9 0.0 copy-done
  10.9 1.8 %fusion.11 = f32[64,128]{1,0:T(8,128)S(1)} fusion(bf16[8192,128]{1,0:T(8,128)(2,1)S(1)} %copy-done, pred[64,8192]{1,0:T(32,128)(4,1)S(1)} %broadcast_compare_fusion, bf16[64,8192]{1,0:T(8,128)(2,1)} %values_ref.1), kind=kOutput, calls=%fused_computation.15 | convolution fusion | flops 134742016 | bytes 3702784 | tf_op jit(solution)/shard_map/dot_general | solution.py:254
  12.7 0.0 copy-start.3
  12.8 0.0 copy-start.4
  12.8 1.2 fusion.7.local_ref
  13.9 0.0 collective-permute-done.1.few_ref
  13.9 0.0 collective-permute-done.many_ref
  14.0 0.0 copy-done.3
  14.0 0.0 copy-done.4
  14.0 0.8 shard_map.69.own_ref
  14.7 0.4 collective-permute-start.4
  15.1 3.4 %collective-permute-start.3 = (f32[64,128]{1,0:T(8,128)S(1)}, f32[64,128]{1,0:T(8,128)S(1)}, u32[]{:S(2)}, u32[]{:S(2)}) collective-permute-start(f32[64,128]{1,0:T(8,128)S(1)} %shard_map.69.own_ref), channel_id=1, source_target_pairs={{0,2},{1,3},{2,0},{3,1},{4,6},{5,7},{6,4},{7,5},{8,10},{9,11},{10,... | collective-permute-start | bytes 98312 | tf_op jit(solution)/shard_map/ppermute | solution.py:231
  18.6 0.8 collective-permute-start.2
  19.4 0.0 collective-permute-done.4.third_ref
  19.4 0.5 collective-permute-done.3.second_ref
  19.9 3.0 %collective-permute-done.2.first_ref = f32[64,128]{1,0:T(8,128)S(1)} collective-permute-done((f32[64,128]{1,0:T(8,128)S(1)}, f32[64,128]{1,0:T(8,128)S(1)}, u32[]{:S(2)}, u32[]{:S(2)}) %collective-permute-start.2) | collective-permute-done | bytes 32800 | tf_op jit(solution)/shard_map/ppermute | solution.py:231
  22.9 0.6 shard_map.70
  23.5 0.7 collective-permute-start.6
  24.2 4.8 %collective-permute-start.5 = (f32[48,128]{1,0:T(8,128)S(1)}, f32[48,128]{1,0:T(8,128)S(1)}, u32[]{:S(2)}, u32[]{:S(2)}) collective-permute-start(f32[48,128]{1,0:T(8,128)S(1)} %get-tuple-element.22), channel_id=1, source_target_pairs={{0,12},{4,16},{8,20},{12,24},{16,28},{20,32},{24,36},{28,40},{32,4... | collective-permute-start | bytes 73736 | tf_op jit(solution)/shard_map/ppermute | solution.py:216
  29.0 1.2 fusion.5.local_ref
  30.1 0.0 collective-permute-done.6.few_ref
  30.1 0.0 collective-permute-done.5.many_ref
  30.2 0.8 shard_map.71.own_ref
  30.9 1.1 collective-permute-start.9
  32.1 1.1 collective-permute-start.8
  33.1 0.5 collective-permute-start.7
  33.7 0.1 collective-permute-done.9.third_ref
  33.8 2.6 %collective-permute-done.8.second_ref = f32[64,128]{1,0:T(8,128)S(1)} collective-permute-done((f32[64,128]{1,0:T(8,128)S(1)}, f32[64,128]{1,0:T(8,128)S(1)}, u32[]{:S(2)}, u32[]{:S(2)}) %collective-permute-start.8) | collective-permute-done | bytes 32800 | tf_op jit(solution)/shard_map/ppermute | solution.py:231
  36.3 1.2 collective-permute-done.7.first_ref
  37.5 0.6 shard_map.72
  38.1 0.7 collective-permute-start.11
  38.7 6.0 %collective-permute-start.10 = (f32[48,128]{1,0:T(8,128)S(1)}, f32[48,128]{1,0:T(8,128)S(1)}, u32[]{:S(2)}, u32[]{:S(2)}) collective-permute-start(f32[48,128]{1,0:T(8,128)S(1)} %get-tuple-element.26), channel_id=1, source_target_pairs={{0,12},{4,16},{8,20},{12,24},{16,28},{20,32},{24,36},{28,40},{32,4... | collective-permute-start | bytes 73736 | tf_op jit(solution)/shard_map/ppermute | solution.py:216
  44.7 1.2 fusion.4.local_ref
  45.9 0.0 copy-start.1
  45.9 0.0 collective-permute-done.11.few_ref
  45.9 0.0 collective-permute-done.10.many_ref
  46.0 0.8 shard_map.73.own_ref
  46.7 0.7 collective-permute-start.14
  47.4 1.9 %collective-permute-start.13 = (f32[64,128]{1,0:T(8,128)S(1)}, f32[64,128]{1,0:T(8,128)S(1)}, u32[]{:S(2)}, u32[]{:S(2)}) collective-permute-start(f32[64,128]{1,0:T(8,128)S(1)} %shard_map.73.own_ref), channel_id=1, source_target_pairs={{0,2},{1,3},{2,0},{3,1},{4,6},{5,7},{6,4},{7,5},{8,10},{9,11},{10,... | collective-permute-start | bytes 98312 | tf_op jit(solution)/shard_map/ppermute | solution.py:231
  49.3 0.8 collective-permute-start.12
  50.1 0.0 collective-permute-done.14.third_ref
  50.1 1.6 %collective-permute-done.13.second_ref = f32[64,128]{1,0:T(8,128)S(1)} collective-permute-done((f32[64,128]{1,0:T(8,128)S(1)}, f32[64,128]{1,0:T(8,128)S(1)}, u32[]{:S(2)}, u32[]{:S(2)}) %collective-permute-start.13) | collective-permute-done | bytes 32800 | tf_op jit(solution)/shard_map/ppermute | solution.py:231
  51.7 2.3 %collective-permute-done.12.first_ref = f32[64,128]{1,0:T(8,128)S(1)} collective-permute-done((f32[64,128]{1,0:T(8,128)S(1)}, f32[64,128]{1,0:T(8,128)S(1)}, u32[]{:S(2)}, u32[]{:S(2)}) %collective-permute-start.12) | collective-permute-done | bytes 32800 | tf_op jit(solution)/shard_map/ppermute | solution.py:231
  54.0 1.1 shard_map.74
  55.1 6.9 %collective-permute-start.15 = (f32[48,128]{1,0:T(8,128)S(1)}, f32[48,128]{1,0:T(8,128)S(1)}, u32[]{:S(2)}, u32[]{:S(2)}) collective-permute-start(f32[48,128]{1,0:T(8,128)S(1)} %get-tuple-element.31), channel_id=1, source_target_pairs={{0,12},{4,16},{8,20},{12,24},{16,28},{20,32},{24,36},{28,40},{32,4... | collective-permute-start | bytes 73736 | tf_op jit(solution)/shard_map/ppermute | solution.py:277
  62.0 1.5 %fusion.13 = f32[]{:T(128)} fusion(pred[64,8192]{1,0:T(32,128)(4,1)S(1)} %broadcast_compare_fusion, bf16[64,128]{1,0:T(8,128)(2,1)S(1)} %get-tuple-element.29, bf16[8192,128]{1,0:T(8,128)(2,1)S(1)} %copy-done), kind=kOutput, calls=%fused_computation.18 | convolution fusion | flops 135790592 | bytes 2637828 | tf_op jit(solution)/shard_map/dot_general | solution.py:26
  63.5 0.0 collective-permute-done.15.many_ref
  63.5 1.6 %shard_map.75 = f32[256,1,128]{2,1,0:T(1,128)S(1)} custom-call(s32[2]{0:T(128)S(1)} %pad_add_fusion.place_ref, f32[1,1]{1,0:T(1,128)} %bitcast.2.squares_ref, f32[64,128]{1,0:T(8,128)S(1)} %get-tuple-element.21.field_ref.zero_ref, f32[64,128]{1,0:T(8,128)S(1)} %get-tuple-element.25.field_ref.one_ref, f32[64,128]{1,0:T(8,128)S(1)} %get-tuple-element.30.two_ref, ...), custom_call_target="tpu_custom_call" | custom-call | tf_op jit(solution)/shard_map/pallas_call | solution.py:280
  65.1 30.5 %all_to_all.10.gathered_ref = f32[256,1,128]{2,1,0:T(1,128)S(1)} all-to-all(f32[256,1,128]{2,1,0:T(1,128)S(1)} %shard_map.75), channel_id=1, replica_groups=mesh['tm'=64,'series'=4] {'tm','series'}, dimensions={0} | all-to-all | bytes 262144 | tf_op jit(solution)/shard_map/all_to_all | solution.py:288
  95.6 0.0 copy-done.1
  95.6 1.2 shard_map.76
  96.8 32.4 %all_to_all.11 = bf16[64,64,128]{2,1,0:T(8,128)(2,1)S(1)} all-to-all(bf16[64,64,128]{2,1,0:T(8,128)(2,1)S(1)} %get-tuple-element.33), channel_id=1, replica_groups=mesh['tm'=64,'series'=4] {'tm'}, dimensions={0} | all-to-all | bytes 2097152 | tf_op jit(solution)/shard_map/all_to_all | solution.py:296
  129.2 1.0 copy.14
Async XLA Ops:
  0.6 10.3 %copy-start = (bf16[8192,128]{1,0:T(8,128)(2,1)S(1)}, bf16[8192,128]{1,0:T(8,128)(2,1)}, u32[]{:S(2)}) copy-start(bf16[8192,128]{1,0:T(8,128)(2,1)} %factors_ref.1) | copy-start | bytes 6291460
  0.7 0.9 copy-start.2
  2.2 11.8 %collective-permute-start.1 = (f32[24,128]{1,0:T(8,128)S(1)}, f32[24,128]{1,0:T(8,128)S(1)}, u32[]{:S(2)}, u32[]{:S(2)}) collective-permute-start(f32[24,128]{1,0:T(8,128)S(1)} %get-tuple-element.19), channel_id=1, source_target_pairs={{2,6},{6,10},{10,14},{14,18},{18,22},{22,26},{26,30},{30,34},{34,3... | collective-permute-start | bytes 36872 | tf_op jit(solution)/shard_map/ppermute | solution.py:215
  2.8 11.1 %collective-permute-start = (f32[48,128]{1,0:T(8,128)S(1)}, f32[48,128]{1,0:T(8,128)S(1)}, u32[]{:S(2)}, u32[]{:S(2)}) collective-permute-start(f32[48,128]{1,0:T(8,128)S(1)} %get-tuple-element.18), channel_id=1, source_target_pairs={{0,12},{4,16},{8,20},{12,24},{16,28},{20,32},{24,36},{28,40},{32,4... | collective-permute-start | bytes 73736 | tf_op jit(solution)/shard_map/ppermute | solution.py:216
  12.7 1.2 copy-start.3
  12.8 1.2 copy-start.4
  14.7 4.6 %collective-permute-start.4 = (f32[64,128]{1,0:T(8,128)S(1)}, f32[64,128]{1,0:T(8,128)S(1)}, u32[]{:S(2)}, u32[]{:S(2)}) collective-permute-start(f32[64,128]{1,0:T(8,128)S(1)} %shard_map.69.own_ref), channel_id=1, source_target_pairs={{0,3},{1,0},{2,1},{3,2},{4,7},{5,4},{6,5},{7,6},{8,11},{9,8},{10,9... | collective-permute-start | bytes 98312 | tf_op jit(solution)/shard_map/ppermute | solution.py:231
  15.1 4.8 %collective-permute-start.3 = (f32[64,128]{1,0:T(8,128)S(1)}, f32[64,128]{1,0:T(8,128)S(1)}, u32[]{:S(2)}, u32[]{:S(2)}) collective-permute-start(f32[64,128]{1,0:T(8,128)S(1)} %shard_map.69.own_ref), channel_id=1, source_target_pairs={{0,2},{1,3},{2,0},{3,1},{4,6},{5,7},{6,4},{7,5},{8,10},{9,11},{10,... | collective-permute-start | bytes 98312 | tf_op jit(solution)/shard_map/ppermute | solution.py:231
  18.6 4.3 %collective-permute-start.2 = (f32[64,128]{1,0:T(8,128)S(1)}, f32[64,128]{1,0:T(8,128)S(1)}, u32[]{:S(2)}, u32[]{:S(2)}) collective-permute-start(f32[64,128]{1,0:T(8,128)S(1)} %shard_map.69.own_ref), channel_id=1, source_target_pairs={{0,1},{1,2},{2,3},{3,0},{4,5},{5,6},{6,7},{7,4},{8,9},{9,10},{10,1... | collective-permute-start | bytes 98312 | tf_op jit(solution)/shard_map/ppermute | solution.py:231
  23.5 6.7 %collective-permute-start.6 = (f32[24,128]{1,0:T(8,128)S(1)}, f32[24,128]{1,0:T(8,128)S(1)}, u32[]{:S(2)}, u32[]{:S(2)}) collective-permute-start(f32[24,128]{1,0:T(8,128)S(1)} %get-tuple-element.23), channel_id=1, source_target_pairs={{2,6},{6,10},{10,14},{14,18},{18,22},{22,26},{26,30},{30,34},{34,3... | collective-permute-start | bytes 36872 | tf_op jit(solution)/shard_map/ppermute | solution.py:215
  24.2 6.0 %collective-permute-start.5 = (f32[48,128]{1,0:T(8,128)S(1)}, f32[48,128]{1,0:T(8,128)S(1)}, u32[]{:S(2)}, u32[]{:S(2)}) collective-permute-start(f32[48,128]{1,0:T(8,128)S(1)} %get-tuple-element.22), channel_id=1, source_target_pairs={{0,12},{4,16},{8,20},{12,24},{16,28},{20,32},{24,36},{28,40},{32,4... | collective-permute-start | bytes 73736 | tf_op jit(solution)/shard_map/ppermute | solution.py:216
  30.9 2.8 %collective-permute-start.9 = (f32[64,128]{1,0:T(8,128)S(1)}, f32[64,128]{1,0:T(8,128)S(1)}, u32[]{:S(2)}, u32[]{:S(2)}) collective-permute-start(f32[64,128]{1,0:T(8,128)S(1)} %shard_map.71.own_ref), channel_id=1, source_target_pairs={{0,3},{1,0},{2,1},{3,2},{4,7},{5,4},{6,5},{7,6},{8,11},{9,8},{10,9... | collective-permute-start | bytes 98312 | tf_op jit(solution)/shard_map/ppermute | solution.py:231
  32.1 4.3 %collective-permute-start.8 = (f32[64,128]{1,0:T(8,128)S(1)}, f32[64,128]{1,0:T(8,128)S(1)}, u32[]{:S(2)}, u32[]{:S(2)}) collective-permute-start(f32[64,128]{1,0:T(8,128)S(1)} %shard_map.71.own_ref), channel_id=1, source_target_pairs={{0,2},{1,3},{2,0},{3,1},{4,6},{5,7},{6,4},{7,5},{8,10},{9,11},{10,... | collective-permute-start | bytes 98312 | tf_op jit(solution)/shard_map/ppermute | solution.py:231
  33.1 4.4 %collective-permute-start.7 = (f32[64,128]{1,0:T(8,128)S(1)}, f32[64,128]{1,0:T(8,128)S(1)}, u32[]{:S(2)}, u32[]{:S(2)}) collective-permute-start(f32[64,128]{1,0:T(8,128)S(1)} %shard_map.71.own_ref), channel_id=1, source_target_pairs={{0,1},{1,2},{2,3},{3,0},{4,5},{5,6},{6,7},{7,4},{8,9},{9,10},{10,1... | collective-permute-start | bytes 98312 | tf_op jit(solution)/shard_map/ppermute | solution.py:231
  38.1 7.9 %collective-permute-start.11 = (f32[24,128]{1,0:T(8,128)S(1)}, f32[24,128]{1,0:T(8,128)S(1)}, u32[]{:S(2)}, u32[]{:S(2)}) collective-permute-start(f32[24,128]{1,0:T(8,128)S(1)} %get-tuple-element.27), channel_id=1, source_target_pairs={{2,6},{6,10},{10,14},{14,18},{18,22},{22,26},{26,30},{30,34},{34,3... | collective-permute-start | bytes 36872 | tf_op jit(solution)/shard_map/ppermute | solution.py:215
  38.7 7.2 %collective-permute-start.10 = (f32[48,128]{1,0:T(8,128)S(1)}, f32[48,128]{1,0:T(8,128)S(1)}, u32[]{:S(2)}, u32[]{:S(2)}) collective-permute-start(f32[48,128]{1,0:T(8,128)S(1)} %get-tuple-element.26), channel_id=1, source_target_pairs={{0,12},{4,16},{8,20},{12,24},{16,28},{20,32},{24,36},{28,40},{32,4... | collective-permute-start | bytes 73736 | tf_op jit(solution)/shard_map/ppermute | solution.py:216
  45.9 49.6 %copy-start.1 = (bf16[64,8192]{1,0:T(8,128)(2,1)S(1)}, bf16[64,8192]{1,0:T(8,128)(2,1)}, u32[]{:S(2)}) copy-start(bf16[64,8192]{1,0:T(8,128)(2,1)} %values_ref.1) | copy-start | bytes 3145732
  46.7 3.4 %collective-permute-start.14 = (f32[64,128]{1,0:T(8,128)S(1)}, f32[64,128]{1,0:T(8,128)S(1)}, u32[]{:S(2)}, u32[]{:S(2)}) collective-permute-start(f32[64,128]{1,0:T(8,128)S(1)} %shard_map.73.own_ref), channel_id=1, source_target_pairs={{0,3},{1,0},{2,1},{3,2},{4,7},{5,4},{6,5},{7,6},{8,11},{9,8},{10,9... | collective-permute-start | bytes 98312 | tf_op jit(solution)/shard_map/ppermute | solution.py:231
  47.4 4.3 %collective-permute-start.13 = (f32[64,128]{1,0:T(8,128)S(1)}, f32[64,128]{1,0:T(8,128)S(1)}, u32[]{:S(2)}, u32[]{:S(2)}) collective-permute-start(f32[64,128]{1,0:T(8,128)S(1)} %shard_map.73.own_ref), channel_id=1, source_target_pairs={{0,2},{1,3},{2,0},{3,1},{4,6},{5,7},{6,4},{7,5},{8,10},{9,11},{10,... | collective-permute-start | bytes 98312 | tf_op jit(solution)/shard_map/ppermute | solution.py:231
  49.3 4.6 %collective-permute-start.12 = (f32[64,128]{1,0:T(8,128)S(1)}, f32[64,128]{1,0:T(8,128)S(1)}, u32[]{:S(2)}, u32[]{:S(2)}) collective-permute-start(f32[64,128]{1,0:T(8,128)S(1)} %shard_map.73.own_ref), channel_id=1, source_target_pairs={{0,1},{1,2},{2,3},{3,0},{4,5},{5,6},{6,7},{7,4},{8,9},{9,10},{10,1... | collective-permute-start | bytes 98312 | tf_op jit(solution)/shard_map/ppermute | solution.py:231
  55.1 8.4 %collective-permute-start.15 = (f32[48,128]{1,0:T(8,128)S(1)}, f32[48,128]{1,0:T(8,128)S(1)}, u32[]{:S(2)}, u32[]{:S(2)}) collective-permute-start(f32[48,128]{1,0:T(8,128)S(1)} %get-tuple-element.31), channel_id=1, source_target_pairs={{0,12},{4,16},{8,20},{12,24},{16,28},{20,32},{24,36},{28,40},{32,4... | collective-permute-start | bytes 73736 | tf_op jit(solution)/shard_map/ppermute | solution.py:277

commit v4 on v3

--- a/solution.py
+++ b/solution.py
@@ -11,7 +11,7 @@
 SEASON = 168
 LAGS = list(range(1, SHORT + 1)) + [SEASON]
 MANY = 48
-FEW = 24
+REACH = (24, 48, 40)
 EDGE = SEASON + 8
 data_weight = 2.0
 penalty_weight = 0.5
@@ -58,45 +58,44 @@
 
 
 def penalty_kernel(
-    scale, last_time, place_ref, field_ref, many_ref, few_ref, weights_ref, local_ref,
-    part_ref, window, short,
+    scale, last_time, place_ref, field_ref, one_ref, two_ref, three_ref, weights_ref, local_ref,
+    other_ref, part_ref, window, short,
 ):
-    here = place_ref[0]
-    many_at = jnp.where(
-        here == 0, 0, jnp.where(here == 1, 368, jnp.where(here == 2, 48, 320))
-    )
+    behind = place_ref[0] < 2
     blocks = [
-        (EDGE, jnp.where(here == 0, field_ref[...], 0.0)),
-        (many_at, many_ref[...]),
-        (jnp.where(here == 3, 240, 152), few_ref[...]),
+        (EDGE, jnp.where(behind, field_ref[...], 0.0)),
+        (jnp.where(behind, 152, 240), one_ref[...]),
+        (jnp.where(behind, 48, 320), two_ref[...]),
+        (jnp.where(behind, 8, 368), three_ref[...]),
     ]
     product = lag_product(place_ref, blocks, weights_ref, window, short, last_time)
-    part_ref[...] = data_weight * local_ref[...] + scale * product
-
-
-def halo(here, field, many_ref, few_ref):
+    part_ref[...] = data_weight * (local_ref[...] + other_ref[...]) + scale * product
+
+
+def halo(here, field, one_ref, two_ref, three_ref):
     rows = field.shape[0]
-    late = jnp.logical_or(here == 0, here == 3)
-    many_ref[...] = jnp.where(late, field[rows - MANY :], field[:MANY])
-    few_ref[...] = jnp.where(here == 2, field[rows - FEW :], field[:FEW])
-
-
-def start_kernel(place_ref, field_ref, low_ref, many_ref, few_ref):
+    behind = here < 2
+    one_ref[...] = jnp.where(behind, field[rows - REACH[0] :], field[: REACH[0]])
+    two_ref[...] = jnp.where(behind, field[: REACH[1]], field[rows - REACH[1] :])
+    three_ref[...] = jnp.where(behind, field[rows - REACH[2] :], field[: REACH[2]])
+
+
+def start_kernel(place_ref, field_ref, low_ref, one_ref, two_ref, three_ref):
     field = field_ref[...]
     low_ref[...] = field.astype(jnp.bfloat16)
-    halo(place_ref[0], field, many_ref, few_ref)
-
-
-def sum_kernel(
-    scale, place_ref, own_ref, first_ref, second_ref, third_ref, field_ref,
-    total_ref, low_ref, many_ref, few_ref,
-):
+    halo(place_ref[0], field, one_ref, two_ref, three_ref)
+
+
+def sum_kernel(scale, place_ref, own_ref, other_ref, field_ref, total_ref, low_ref, *halo_refs):
     here = place_ref[0]
-    total = (own_ref[...] + second_ref[...]) + (first_ref[...] + third_ref[...])
-    total = total + scale * field_ref[...]
+    total = (own_ref[...] + other_ref[...]) + scale * field_ref[...]
     total_ref[...] = total
     low_ref[...] = total.astype(jnp.bfloat16)
-    halo(here, total, many_ref, few_ref)
+    if len(halo_refs) == 1:
+        rows = total.shape[0]
+        halo_refs[0][...] = jnp.where(here == 2, total[:MANY], total[rows - MANY :])
+    else:
+        halo(here, total, *halo_refs)
 
 
 def moments_kernel(
@@ -187,8 +186,8 @@
     here = lax.axis_index("series")
     place = jnp.stack([here, lax.axis_index("tm") * rows]).astype(jnp.int32)
     field_shape = jax.ShapeDtypeStruct((rows, rank), jnp.float32)
-    many_shape = jax.ShapeDtypeStruct((MANY, rank), jnp.float32)
-    few_shape = jax.ShapeDtypeStruct((FEW, rank), jnp.float32)
+    halo_shapes = tuple(jax.ShapeDtypeStruct((count, rank), jnp.float32) for count in REACH)
+    last_shape = (jax.ShapeDtypeStruct((MANY, rank), jnp.float32),)
     low_shape = jax.ShapeDtypeStruct((rows, rank), jnp.bfloat16)
     lag_scratch = [
         pltpu.VMEM((2 * EDGE + rows, rank), jnp.float32),
@@ -206,44 +205,33 @@
                     pairs.append((source * n_series + column, target * n_series + column))
         return pairs
 
-    many_route = route([3, -3, 2, -2])
-    few_route = route([None, None, 1, -1])
+    routes = [route([step, step, -step, -step]) for step in (1, 2, 3)]
     last_route = route([3, None, 2, 1])
     both = ("tm", "series")
 
-    def fetch(many, few):
-        few = lax.ppermute(few, both, few_route)
-        return lax.ppermute(many, both, many_route), few
-
-    def penalty(scale, field, many, few, local):
-        return pl.pallas_call(
+    def with_pair(field, partner):
+        return lax.ppermute(field, "series", [(i, partner(i)) for i in range(n_series)])
+
+    def finish(scale, field, halos, local, ridge, out_halos):
+        fetched = [lax.ppermute(rows_out, both, pairs) for rows_out, pairs in zip(halos, routes)]
+        other = with_pair(local, lambda i: i ^ 1)
+        part = pl.pallas_call(
             functools.partial(penalty_kernel, scale, last_time),
             out_shape=field_shape,
-            in_specs=[SMEM] + [VMEM] * 5,
+            in_specs=[SMEM] + [VMEM] * 7,
             out_specs=VMEM,
             scratch_shapes=lag_scratch,
             compiler_params=SMALL,
-        )(place, field, many, few, lag_weights, local)
-
-    def series_sum(scale, part, field):
-        def moved(distance):
-            pairs = [(i, (i + distance) % n_series) for i in range(n_series)]
-            return lax.ppermute(part, "series", pairs)
-
-        first, third = moved(1), moved(3)
-        second = moved(2)
-        return pl.pallas_call(
-            functools.partial(sum_kernel, scale),
-            out_shape=(
-                field_shape,
-                low_shape,
-                many_shape,
-                few_shape,
-            ),
-            in_specs=[SMEM] + [VMEM] * 5,
-            out_specs=(VMEM,) * 4,
+        )(place, field, *fetched, lag_weights, local, other)
+        second = with_pair(part, lambda i: n_series - 1 - i)
+        total, low, *halos = pl.pallas_call(
+            functools.partial(sum_kernel, ridge),
+            out_shape=(field_shape, low_shape) + out_halos,
+            in_specs=[SMEM] + [VMEM] * 3,
+            out_specs=(VMEM,) * (2 + len(out_halos)),
             compiler_params=SMALL,
-        )(place, part, first, second, third, field)
+        )(place, part, second, field)
+        return total, low, halos
 
     seen = observed == 1
 
@@ -253,27 +241,25 @@
     def back(rows_here):
         return jnp.dot(rows_here, series_factors, preferred_element_type=jnp.float32)
 
-    low, many, few = pl.pallas_call(
+    low, *halos = pl.pallas_call(
         start_kernel,
-        out_shape=(low_shape, many_shape, few_shape),
+        out_shape=(low_shape,) + halo_shapes,
         in_specs=[SMEM, VMEM],
-        out_specs=(VMEM,) * 3,
+        out_specs=(VMEM,) * 4,
         compiler_params=SMALL,
     )(place, time_factors)
-    many, few = fetch(many, few)
     kept = jnp.where(seen, series_values, jnp.zeros((), jnp.bfloat16))
     local = back(kept) - back(fit(low).astype(jnp.bfloat16))
-    part = penalty(-penalty_weight, time_factors, many, few, local)
-    power0, low, many, few = series_sum(-ridge_weight, part, time_factors)
-
-    def image(field, low, many, few):
-        many, few = fetch(many, few)
+    power0, low, halos = finish(
+        -penalty_weight, time_factors, halos, local, -ridge_weight, halo_shapes
+    )
+
+    def image(field, low, halos, out_halos):
         local = back(fit(low).astype(jnp.bfloat16))
-        part = penalty(penalty_weight, field, many, few, local)
-        return series_sum(ridge_weight, part, field)
-
-    power1, low, many, few = image(power0, low, many, few)
-    power2, low, many, few = image(power1, low, many, few)
+        return finish(penalty_weight, field, halos, local, ridge_weight, out_halos)
+
+    power1, low, halos = image(power0, low, halos, halo_shapes)
+    power2, low, (many,) = image(power1, low, halos, last_shape)
     many = lax.ppermute(many, both, last_route)
     fitted = fit(low)
     squares = jnp.sum(fitted * fitted).reshape(1, 1)

time: 131 us -> 139 us (1.061)
  starting transfers between devices: 36.6 us -> 44.8 us
  waiting for transfers between devices: 11.3 us -> 15.3 us
  blocking collectives: 62.9 us -> 59.9 us
    ppermute x15, starting transfers between devices: 29.7 us -> 38.1 us  [the longest x9 35 us: finish(): lax.ppermute(rows_out, both, pairs)]
    ppermute x15, waiting for transfers between devices: 11.3 us -> 15.3 us  [the longest x6 11.9 us: with_pair(): lax.ppermute(field, 'series', [(i, partner(i)) for i in range(n_series)])]
    all_to_all x1, blocking collectives: 30.5 us -> 27.5 us  [on_device(): lax.all_to_all(spread, both, split_axis=0, concat_axis=0, tiled=True)]
  transfers between devices with their start and end apart: 16 -> 16, of which waited for: 7 -> 6; matrix products, arithmetic and copies ran while one was open for 7% -> 1% of each run, Pallas kernels for 0% -> 0%
where the time goes in v4:
time: 139 us; the launch traced here: 138 us
  blocking collectives  59.9 us (43%)
  starting transfers between devices  44.8 us (32%)
  waiting for transfers between devices  15.3 us (11%)
  Pallas kernels  7.33 us (5%)
  matrix products  6.7 us (5%)
  other arithmetic  2.09 us (2%)
    ppermute x9, starting transfers between devices, finish(): lax.ppermute(rows_out, both, pairs)  35 us
    all_to_all x1, blocking collectives, on_device(): lax.all_to_all(misfit, 'tm', split_axis=0, concat_axis=0, tiled=True)  32.4 us
    all_to_all x1, blocking collectives, on_device(): lax.all_to_all(spread, both, split_axis=0, concat_axis=0, tiled=True)  27.5 us
    ppermute x6, waiting for transfers between devices, with_pair(): lax.ppermute(field, 'series', [(i, partner(i)) for i in range(n_series)])  11.9 us
    ppermute x1, starting transfers between devices, on_device(): many = lax.ppermute(many, both, last_route)  6.74 us
    dot_general x4, matrix products, back(): jnp.dot(rows_here, series_factors, preferred_element_type=jnp.float32)  5.23 us
    ppermute x9, waiting for transfers between devices, finish(): lax.ppermute(rows_out, both, pairs)  3.45 us
    ppermute x6, starting transfers between devices, with_pair(): lax.ppermute(field, 'series', [(i, partner(i)) for i in range(n_series)])  3.1 us
  transfers between devices with their start and end apart: 16, of which 6 were waited for; matrix products, arithmetic and copies ran while one was open for 1% of the time, Pallas kernels for 0%

profile of v4, /device:TPU:1, one launch (start us, length us, event | category | flops | bytes accessed | tf_op | source)
XLA Modules:
  0.0 138.1 jit_solution(1373665505633228249)
XLA Ops:
  0.6 0.0 copy-start.2
  0.6 0.0 copy-start
  0.7 2.0 %broadcast_compare_fusion = pred[64,8192]{1,0:T(32,128)(4,1)S(1)} fusion(s32[64,8192]{1,0:T(8,128)} %param.6), kind=kLoop, calls=%fused_computation.17 | loop fusion | flops 524288 | bytes 2621440 | tf_op jit(solution)/shard_map/eq | solution.py:236
  2.7 0.1 pad_add_fusion.place_ref
  2.8 0.0 copy-done.2
  2.8 0.6 shard_map.68
  3.3 0.0 copy-done
  3.3 1.8 %fusion.11 = f32[64,128]{1,0:T(8,128)S(1)} fusion(bf16[8192,128]{1,0:T(8,128)(2,1)S(1)} %copy-done, pred[64,8192]{1,0:T(32,128)(4,1)S(1)} %broadcast_compare_fusion, bf16[64,8192]{1,0:T(8,128)(2,1)} %values_ref.1), kind=kOutput, calls=%fused_computation.15 | convolution fusion | flops 134742016 | bytes 3702784 | tf_op jit(solution)/shard_map/dot_general | solution.py:242
  5.1 0.0 copy-start.3
  5.1 1.2 fusion.7.local_ref
  6.3 2.1 %collective-permute-start.3 = (f32[64,128]{1,0:T(8,128)S(1)}, f32[64,128]{1,0:T(8,128)S(1)}, u32[]{:S(2)}, u32[]{:S(2)}) collective-permute-start(f32[64,128]{1,0:T(8,128)S(1)} %fusion.7.local_ref), channel_id=1, source_target_pairs={{0,1},{1,0},{2,3},{3,2},{4,5},{5,4},{6,7},{7,6},{8,9},{9,8},{10,11... | collective-permute-start | bytes 98312 | tf_op jit(solution)/shard_map/ppermute | solution.py:213
  8.4 3.2 %collective-permute-start.1 = (f32[48,128]{1,0:T(8,128)S(1)}, f32[48,128]{1,0:T(8,128)S(1)}, u32[]{:S(2)}, u32[]{:S(2)}) collective-permute-start(f32[48,128]{1,0:T(8,128)S(1)} %get-tuple-element.22), channel_id=1, source_target_pairs={{0,8},{4,12},{8,16},{12,20},{16,24},{20,28},{24,32},{28,36},{32,40... | collective-permute-start | bytes 73736 | tf_op jit(solution)/shard_map/ppermute | solution.py:216
  11.6 5.6 %collective-permute-start.2 = (f32[40,128]{1,0:T(8,128)S(1)}, f32[40,128]{1,0:T(8,128)S(1)}, u32[]{:S(2)}, u32[]{:S(2)}) collective-permute-start(f32[40,128]{1,0:T(8,128)S(1)} %get-tuple-element.23), channel_id=1, source_target_pairs={{0,12},{4,16},{8,20},{12,24},{16,28},{20,32},{24,36},{28,40},{32,4... | collective-permute-start | bytes 61448 | tf_op jit(solution)/shard_map/ppermute | solution.py:216
  17.3 1.9 %collective-permute-start = (f32[24,128]{1,0:T(8,128)S(1)}, f32[24,128]{1,0:T(8,128)S(1)}, u32[]{:S(2)}, u32[]{:S(2)}) collective-permute-start(f32[24,128]{1,0:T(8,128)S(1)} %get-tuple-element.21), channel_id=1, source_target_pairs={{0,4},{4,8},{8,12},{12,16},{16,20},{20,24},{24,28},{28,32},{32,36}... | collective-permute-start | bytes 36872 | tf_op jit(solution)/shard_map/ppermute | solution.py:216
  19.2 1.1 collective-permute-done.one_ref
  20.3 0.0 collective-permute-done.2.three_ref
  20.3 0.0 collective-permute-done.1.two_ref
  20.4 0.0 collective-permute-done.3.other_ref
  20.4 0.0 copy-done.3
  20.4 0.8 shard_map.69.own_ref
  21.1 0.1 collective-permute-start.4
  21.2 4.0 %collective-permute-done.4.other_ref = f32[64,128]{1,0:T(8,128)S(1)} collective-permute-done((f32[64,128]{1,0:T(8,128)S(1)}, f32[64,128]{1,0:T(8,128)S(1)}, u32[]{:S(2)}, u32[]{:S(2)}) %collective-permute-start.4) | collective-permute-done | bytes 32800 | tf_op jit(solution)/shard_map/ppermute | solution.py:213
  25.2 0.6 shard_map.70
  25.8 1.1 fusion.5.local_ref
  26.9 0.1 collective-permute-start.8
  27.0 2.6 %collective-permute-start.6 = (f32[48,128]{1,0:T(8,128)S(1)}, f32[48,128]{1,0:T(8,128)S(1)}, u32[]{:S(2)}, u32[]{:S(2)}) collective-permute-start(f32[48,128]{1,0:T(8,128)S(1)} %get-tuple-element.27), channel_id=1, source_target_pairs={{0,8},{4,12},{8,16},{12,20},{16,24},{20,28},{24,32},{28,36},{32,40... | collective-permute-start | bytes 73736 | tf_op jit(solution)/shard_map/ppermute | solution.py:216
  29.6 6.3 %collective-permute-start.7 = (f32[40,128]{1,0:T(8,128)S(1)}, f32[40,128]{1,0:T(8,128)S(1)}, u32[]{:S(2)}, u32[]{:S(2)}) collective-permute-start(f32[40,128]{1,0:T(8,128)S(1)} %get-tuple-element.28), channel_id=1, source_target_pairs={{0,12},{4,16},{8,20},{12,24},{16,28},{20,32},{24,36},{28,40},{32,4... | collective-permute-start | bytes 61448 | tf_op jit(solution)/shard_map/ppermute | solution.py:216
  36.0 1.9 %collective-permute-start.5 = (f32[24,128]{1,0:T(8,128)S(1)}, f32[24,128]{1,0:T(8,128)S(1)}, u32[]{:S(2)}, u32[]{:S(2)}) collective-permute-start(f32[24,128]{1,0:T(8,128)S(1)} %get-tuple-element.26), channel_id=1, source_target_pairs={{0,4},{4,8},{8,12},{12,16},{16,20},{20,24},{24,28},{28,32},{32,36}... | collective-permute-start | bytes 36872 | tf_op jit(solution)/shard_map/ppermute | solution.py:216
  37.9 1.1 collective-permute-done.5.one_ref
  39.0 0.0 collective-permute-done.7.three_ref
  39.1 0.0 collective-permute-done.6.two_ref
  39.1 0.0 collective-permute-done.8.other_ref
  39.1 0.8 shard_map.71.own_ref
  39.8 0.1 collective-permute-start.9
  39.9 4.0 %collective-permute-done.9.other_ref = f32[64,128]{1,0:T(8,128)S(1)} collective-permute-done((f32[64,128]{1,0:T(8,128)S(1)}, f32[64,128]{1,0:T(8,128)S(1)}, u32[]{:S(2)}, u32[]{:S(2)}) %collective-permute-start.9) | collective-permute-done | bytes 32800 | tf_op jit(solution)/shard_map/ppermute | solution.py:213
  43.9 0.6 shard_map.72
  44.5 1.1 fusion.4.local_ref
  45.6 0.0 copy-start.1
  45.6 0.6 collective-permute-start.13
  46.2 5.3 %collective-permute-start.11 = (f32[48,128]{1,0:T(8,128)S(1)}, f32[48,128]{1,0:T(8,128)S(1)}, u32[]{:S(2)}, u32[]{:S(2)}) collective-permute-start(f32[48,128]{1,0:T(8,128)S(1)} %get-tuple-element.32), channel_id=1, source_target_pairs={{0,8},{4,12},{8,16},{12,20},{16,24},{20,28},{24,32},{28,36},{32,40... | collective-permute-start | bytes 73736 | tf_op jit(solution)/shard_map/ppermute | solution.py:216
  51.5 6.2 %collective-permute-start.12 = (f32[40,128]{1,0:T(8,128)S(1)}, f32[40,128]{1,0:T(8,128)S(1)}, u32[]{:S(2)}, u32[]{:S(2)}) collective-permute-start(f32[40,128]{1,0:T(8,128)S(1)} %get-tuple-element.33), channel_id=1, source_target_pairs={{0,12},{4,16},{8,20},{12,24},{16,28},{20,32},{24,36},{28,40},{32,4... | collective-permute-start | bytes 61448 | tf_op jit(solution)/shard_map/ppermute | solution.py:216
  57.7 1.9 %collective-permute-start.10 = (f32[24,128]{1,0:T(8,128)S(1)}, f32[24,128]{1,0:T(8,128)S(1)}, u32[]{:S(2)}, u32[]{:S(2)}) collective-permute-start(f32[24,128]{1,0:T(8,128)S(1)} %get-tuple-element.31), channel_id=1, source_target_pairs={{0,4},{4,8},{8,12},{12,16},{16,20},{20,24},{24,28},{28,32},{32,36}... | collective-permute-start | bytes 36872 | tf_op jit(solution)/shard_map/ppermute | solution.py:216
  59.6 1.1 collective-permute-done.10.one_ref
  60.8 0.0 collective-permute-done.12.three_ref
  60.8 0.0 collective-permute-done.11.two_ref
  60.8 0.0 collective-permute-done.13.other_ref
  60.8 0.8 shard_map.73.own_ref
  61.6 0.1 collective-permute-start.14
  61.7 4.0 %collective-permute-done.14.other_ref = f32[64,128]{1,0:T(8,128)S(1)} collective-permute-done((f32[64,128]{1,0:T(8,128)S(1)}, f32[64,128]{1,0:T(8,128)S(1)}, u32[]{:S(2)}, u32[]{:S(2)}) %collective-permute-start.14) | collective-permute-done | bytes 32800 | tf_op jit(solution)/shard_map/ppermute | solution.py:213
  65.6 0.6 shard_map.74
  66.2 6.7 %collective-permute-start.15 = (f32[48,128]{1,0:T(8,128)S(1)}, f32[48,128]{1,0:T(8,128)S(1)}, u32[]{:S(2)}, u32[]{:S(2)}) collective-permute-start(f32[48,128]{1,0:T(8,128)S(1)} %get-tuple-element.37), channel_id=1, source_target_pairs={{0,12},{4,16},{8,20},{12,24},{16,28},{20,32},{24,36},{28,40},{32,4... | collective-permute-start | bytes 73736 | tf_op jit(solution)/shard_map/ppermute | solution.py:263
  72.9 1.5 %fusion.13 = f32[]{:T(128)} fusion(pred[64,8192]{1,0:T(32,128)(4,1)S(1)} %broadcast_compare_fusion, bf16[64,128]{1,0:T(8,128)(2,1)S(1)} %get-tuple-element.35, bf16[8192,128]{1,0:T(8,128)(2,1)S(1)} %copy-done), kind=kOutput, calls=%fused_computation.18 | convolution fusion | flops 135790592 | bytes 2637828 | tf_op jit(solution)/shard_map/dot_general | solution.py:26
  74.4 0.0 collective-permute-done.15.many_ref
  74.4 1.6 %shard_map.75 = f32[256,1,128]{2,1,0:T(1,128)S(1)} custom-call(s32[2]{0:T(128)S(1)} %pad_add_fusion.place_ref, f32[1,1]{1,0:T(1,128)} %bitcast.2.squares_ref, f32[64,128]{1,0:T(8,128)S(1)} %get-tuple-element.25.field_ref.zero_ref, f32[64,128]{1,0:T(8,128)S(1)} %get-tuple-element.30.field_ref.one_ref, f32[64,128]{1,0:T(8,128)S(1)} %get-tuple-element.36.two_ref, ...), custom_call_target="tpu_custom_call" | custom-call | tf_op jit(solution)/shard_map/pallas_call | solution.py:266
  76.0 27.5 %all_to_all.10.gathered_ref = f32[256,1,128]{2,1,0:T(1,128)S(1)} all-to-all(f32[256,1,128]{2,1,0:T(1,128)S(1)} %shard_map.75), channel_id=1, replica_groups=mesh['tm'=64,'series'=4] {'tm','series'}, dimensions={0} | all-to-all | bytes 262144 | tf_op jit(solution)/shard_map/all_to_all | solution.py:274
  103.5 0.0 copy-done.1
  103.5 1.2 shard_map.76
  104.7 32.4 %all_to_all.11 = bf16[64,64,128]{2,1,0:T(8,128)(2,1)S(1)} all-to-all(bf16[64,64,128]{2,1,0:T(8,128)(2,1)S(1)} %get-tuple-element.39), channel_id=1, replica_groups=mesh['tm'=64,'series'=4] {'tm'}, dimensions={0} | all-to-all | bytes 2097152 | tf_op jit(solution)/shard_map/all_to_all | solution.py:282
  137.1 1.0 copy.14
Async XLA Ops:
  0.6 2.1 %copy-start.2 = (f32[64,128]{1,0:T(8,128)S(1)}, f32[64,128]{1,0:T(8,128)}, u32[]{:S(2)}) copy-start(f32[64,128]{1,0:T(8,128)} %start_ref.1) | copy-start | bytes 98308
  0.6 2.7 %copy-start = (bf16[8192,128]{1,0:T(8,128)(2,1)S(1)}, bf16[8192,128]{1,0:T(8,128)(2,1)}, u32[]{:S(2)}) copy-start(bf16[8192,128]{1,0:T(8,128)(2,1)} %factors_ref.1) | copy-start | bytes 6291460
  5.1 15.2 %copy-start.3 = (f32[25,128]{1,0:T(8,128)S(1)}, f32[25,128]{1,0:T(8,128)}, u32[]{:S(2)}) copy-start(f32[25,128]{1,0:T(8,128)} %weights_ref.7) | copy-start | bytes 38404
  6.3 14.1 %collective-permute-start.3 = (f32[64,128]{1,0:T(8,128)S(1)}, f32[64,128]{1,0:T(8,128)S(1)}, u32[]{:S(2)}, u32[]{:S(2)}) collective-permute-start(f32[64,128]{1,0:T(8,128)S(1)} %fusion.7.local_ref), channel_id=1, source_target_pairs={{0,1},{1,0},{2,3},{3,2},{4,5},{5,4},{6,7},{7,6},{8,9},{9,8},{10,11... | collective-permute-start | bytes 98312 | tf_op jit(solution)/shard_map/ppermute | solution.py:213
  8.4 11.9 %collective-permute-start.1 = (f32[48,128]{1,0:T(8,128)S(1)}, f32[48,128]{1,0:T(8,128)S(1)}, u32[]{:S(2)}, u32[]{:S(2)}) collective-permute-start(f32[48,128]{1,0:T(8,128)S(1)} %get-tuple-element.22), channel_id=1, source_target_pairs={{0,8},{4,12},{8,16},{12,20},{16,24},{20,28},{24,32},{28,36},{32,40... | collective-permute-start | bytes 73736 | tf_op jit(solution)/shard_map/ppermute | solution.py:216
  11.6 8.7 %collective-permute-start.2 = (f32[40,128]{1,0:T(8,128)S(1)}, f32[40,128]{1,0:T(8,128)S(1)}, u32[]{:S(2)}, u32[]{:S(2)}) collective-permute-start(f32[40,128]{1,0:T(8,128)S(1)} %get-tuple-element.23), channel_id=1, source_target_pairs={{0,12},{4,16},{8,20},{12,24},{16,28},{20,32},{24,36},{28,40},{32,4... | collective-permute-start | bytes 61448 | tf_op jit(solution)/shard_map/ppermute | solution.py:216
  17.3 3.1 %collective-permute-start = (f32[24,128]{1,0:T(8,128)S(1)}, f32[24,128]{1,0:T(8,128)S(1)}, u32[]{:S(2)}, u32[]{:S(2)}) collective-permute-start(f32[24,128]{1,0:T(8,128)S(1)} %get-tuple-element.21), channel_id=1, source_target_pairs={{0,4},{4,8},{8,12},{12,16},{16,20},{20,24},{24,28},{28,32},{32,36}... | collective-permute-start | bytes 36872 | tf_op jit(solution)/shard_map/ppermute | solution.py:216
  21.1 4.1 %collective-permute-start.4 = (f32[64,128]{1,0:T(8,128)S(1)}, f32[64,128]{1,0:T(8,128)S(1)}, u32[]{:S(2)}, u32[]{:S(2)}) collective-permute-start(f32[64,128]{1,0:T(8,128)S(1)} %shard_map.69.own_ref), channel_id=1, source_target_pairs={{0,3},{1,2},{2,1},{3,0},{4,7},{5,6},{6,5},{7,4},{8,11},{9,10},{10,... | collective-permute-start | bytes 98312 | tf_op jit(solution)/shard_map/ppermute | solution.py:213
  26.9 12.1 %collective-permute-start.8 = (f32[64,128]{1,0:T(8,128)S(1)}, f32[64,128]{1,0:T(8,128)S(1)}, u32[]{:S(2)}, u32[]{:S(2)}) collective-permute-start(f32[64,128]{1,0:T(8,128)S(1)} %fusion.5.local_ref), channel_id=1, source_target_pairs={{0,1},{1,0},{2,3},{3,2},{4,5},{5,4},{6,7},{7,6},{8,9},{9,8},{10,11... | collective-permute-start | bytes 98312 | tf_op jit(solution)/shard_map/ppermute | solution.py:213
  27.0 12.0 %collective-permute-start.6 = (f32[48,128]{1,0:T(8,128)S(1)}, f32[48,128]{1,0:T(8,128)S(1)}, u32[]{:S(2)}, u32[]{:S(2)}) collective-permute-start(f32[48,128]{1,0:T(8,128)S(1)} %get-tuple-element.27), channel_id=1, source_target_pairs={{0,8},{4,12},{8,16},{12,20},{16,24},{20,28},{24,32},{28,36},{32,40... | collective-permute-start | bytes 73736 | tf_op jit(solution)/shard_map/ppermute | solution.py:216
  29.6 9.4 %collective-permute-start.7 = (f32[40,128]{1,0:T(8,128)S(1)}, f32[40,128]{1,0:T(8,128)S(1)}, u32[]{:S(2)}, u32[]{:S(2)}) collective-permute-start(f32[40,128]{1,0:T(8,128)S(1)} %get-tuple-element.28), channel_id=1, source_target_pairs={{0,12},{4,16},{8,20},{12,24},{16,28},{20,32},{24,36},{28,40},{32,4... | collective-permute-start | bytes 61448 | tf_op jit(solution)/shard_map/ppermute | solution.py:216
  36.0 3.1 %collective-permute-start.5 = (f32[24,128]{1,0:T(8,128)S(1)}, f32[24,128]{1,0:T(8,128)S(1)}, u32[]{:S(2)}, u32[]{:S(2)}) collective-permute-start(f32[24,128]{1,0:T(8,128)S(1)} %get-tuple-element.26), channel_id=1, source_target_pairs={{0,4},{4,8},{8,12},{12,16},{16,20},{20,24},{24,28},{28,32},{32,36}... | collective-permute-start | bytes 36872 | tf_op jit(solution)/shard_map/ppermute | solution.py:216
  39.8 4.1 %collective-permute-start.9 = (f32[64,128]{1,0:T(8,128)S(1)}, f32[64,128]{1,0:T(8,128)S(1)}, u32[]{:S(2)}, u32[]{:S(2)}) collective-permute-start(f32[64,128]{1,0:T(8,128)S(1)} %shard_map.71.own_ref), channel_id=1, source_target_pairs={{0,3},{1,2},{2,1},{3,0},{4,7},{5,6},{6,5},{7,4},{8,11},{9,10},{10,... | collective-permute-start | bytes 98312 | tf_op jit(solution)/shard_map/ppermute | solution.py:213
  45.6 57.9 %copy-start.1 = (bf16[64,8192]{1,0:T(8,128)(2,1)S(1)}, bf16[64,8192]{1,0:T(8,128)(2,1)}, u32[]{:S(2)}) copy-start(bf16[64,8192]{1,0:T(8,128)(2,1)} %values_ref.1) | copy-start | bytes 3145732
  45.6 15.1 %collective-permute-start.13 = (f32[64,128]{1,0:T(8,128)S(1)}, f32[64,128]{1,0:T(8,128)S(1)}, u32[]{:S(2)}, u32[]{:S(2)}) collective-permute-start(f32[64,128]{1,0:T(8,128)S(1)} %fusion.4.local_ref), channel_id=1, source_target_pairs={{0,1},{1,0},{2,3},{3,2},{4,5},{5,4},{6,7},{7,6},{8,9},{9,8},{10,11... | collective-permute-start | bytes 98312 | tf_op jit(solution)/shard_map/ppermute | solution.py:213
  46.2 14.5 %collective-permute-start.11 = (f32[48,128]{1,0:T(8,128)S(1)}, f32[48,128]{1,0:T(8,128)S(1)}, u32[]{:S(2)}, u32[]{:S(2)}) collective-permute-start(f32[48,128]{1,0:T(8,128)S(1)} %get-tuple-element.32), channel_id=1, source_target_pairs={{0,8},{4,12},{8,16},{12,20},{16,24},{20,28},{24,32},{28,36},{32,40... | collective-permute-start | bytes 73736 | tf_op jit(solution)/shard_map/ppermute | solution.py:216
  51.5 9.3 %collective-permute-start.12 = (f32[40,128]{1,0:T(8,128)S(1)}, f32[40,128]{1,0:T(8,128)S(1)}, u32[]{:S(2)}, u32[]{:S(2)}) collective-permute-start(f32[40,128]{1,0:T(8,128)S(1)} %get-tuple-element.33), channel_id=1, source_target_pairs={{0,12},{4,16},{8,20},{12,24},{16,28},{20,32},{24,36},{28,40},{32,4... | collective-permute-start | bytes 61448 | tf_op jit(solution)/shard_map/ppermute | solution.py:216
  57.7 3.1 %collective-permute-start.10 = (f32[24,128]{1,0:T(8,128)S(1)}, f32[24,128]{1,0:T(8,128)S(1)}, u32[]{:S(2)}, u32[]{:S(2)}) collective-permute-start(f32[24,128]{1,0:T(8,128)S(1)} %get-tuple-element.31), channel_id=1, source_target_pairs={{0,4},{4,8},{8,12},{12,16},{16,20},{20,24},{24,28},{28,32},{32,36}... | collective-permute-start | bytes 36872 | tf_op jit(solution)/shard_map/ppermute | solution.py:216
  61.6 4.1 %collective-permute-start.14 = (f32[64,128]{1,0:T(8,128)S(1)}, f32[64,128]{1,0:T(8,128)S(1)}, u32[]{:S(2)}, u32[]{:S(2)}) collective-permute-start(f32[64,128]{1,0:T(8,128)S(1)} %shard_map.73.own_ref), channel_id=1, source_target_pairs={{0,3},{1,2},{2,1},{3,0},{4,7},{5,6},{6,5},{7,4},{8,11},{9,10},{10,... | collective-permute-start | bytes 98312 | tf_op jit(solution)/shard_map/ppermute | solution.py:213
  66.2 8.2 %collective-permute-start.15 = (f32[48,128]{1,0:T(8,128)S(1)}, f32[48,128]{1,0:T(8,128)S(1)}, u32[]{:S(2)}, u32[]{:S(2)}) collective-permute-start(f32[48,128]{1,0:T(8,128)S(1)} %get-tuple-element.37), channel_id=1, source_target_pairs={{0,12},{4,16},{8,20},{12,24},{16,28},{20,32},{24,36},{28,40},{32,4... | collective-permute-start | bytes 73736 | tf_op jit(solution)/shard_map/ppermute | solution.py:263

commit v5 on v3

--- a/solution.py
+++ b/solution.py
@@ -12,6 +12,7 @@
 LAGS = list(range(1, SHORT + 1)) + [SEASON]
 MANY = 48
 FEW = 24
+FOLD = 16
 EDGE = SEASON + 8
 data_weight = 2.0
 penalty_weight = 0.5
@@ -113,21 +114,28 @@
     product = lag_product(place_ref, blocks, weights_ref, window, short, last_time)
 
     def inner(left, right):
-        return jnp.sum(jnp.sum(left * right, axis=0, keepdims=True), axis=1, keepdims=True)
-
-    sums = [
-        share * inner(zero, zero),
-        share * inner(zero, one),
-        share * inner(zero, two),
-        share * inner(one, one),
-        share * inner(one, two),
-        share * inner(two, two),
-        data_weight * squares_ref[0, 0] + penalty_weight * inner(two, product),
-    ]
-    lane = lax.broadcasted_iota(jnp.int32, (1, zero.shape[1]), 1)
-    packed = jnp.zeros((1, zero.shape[1]), jnp.float32)
-    for number, value in enumerate(sums):
-        packed = jnp.where(lane == number, value, packed)
+        return jnp.sum(left * right, axis=0, keepdims=True)
+
+    tile = jnp.concatenate(
+        [
+            share * inner(zero, zero),
+            share * inner(zero, one),
+            share * inner(zero, two),
+            share * inner(one, one),
+            share * inner(one, two),
+            share * inner(two, two),
+            penalty_weight * inner(two, product),
+            jnp.zeros_like(zero[:1]),
+        ],
+        axis=0,
+    )
+    for shift in (64, 32, 16):
+        tile = tile + pltpu.roll(tile, shift, 1)
+    group = lax.broadcasted_iota(jnp.int32, tile.shape, 1) // FOLD
+    number = lax.broadcasted_iota(jnp.int32, tile.shape, 0)
+    packed = jnp.sum(jnp.where(group == number, tile, 0.0), axis=0, keepdims=True)
+    lane = lax.broadcasted_iota(jnp.int32, packed.shape, 1)
+    packed = packed + jnp.where(lane == 6 * FOLD, data_weight * squares_ref[0, 0], 0.0)
     spread_ref[...] = jnp.broadcast_to(packed[None], spread_ref.shape)
 
 
@@ -139,7 +147,7 @@
     lane = lax.broadcasted_iota(jnp.int32, total.shape, 1)
 
     def pick(number):
-        return jnp.sum(jnp.where(lane == number, total, 0.0), axis=1, keepdims=True)
+        return jnp.sum(jnp.where(lane // FOLD == number, total, 0.0), axis=1, keepdims=True)
 
     m00, m01, m02, m11, m12, m22, m23 = [pick(number) for number in range(7)]
     m23 = m23 + ridge_weight * m22
@@ -211,9 +219,10 @@
     last_route = route([3, None, 2, 1])
     both = ("tm", "series")
 
-    def fetch(many, few):
+    def fetch(many, few, local):
+        few, local = lax.optimization_barrier((few, local))
         few = lax.ppermute(few, both, few_route)
-        return lax.ppermute(many, both, many_route), few
+        return lax.ppermute(many, both, many_route), few, local
 
     def penalty(scale, field, many, few, local):
         return pl.pallas_call(
@@ -260,15 +269,15 @@
         out_specs=(VMEM,) * 3,
         compiler_params=SMALL,
     )(place, time_factors)
-    many, few = fetch(many, few)
     kept = jnp.where(seen, series_values, jnp.zeros((), jnp.bfloat16))
     local = back(kept) - back(fit(low).astype(jnp.bfloat16))
+    many, few, local = fetch(many, few, local)
     part = penalty(-penalty_weight, time_factors, many, few, local)
     power0, low, many, few = series_sum(-ridge_weight, part, time_factors)
 
     def image(field, low, many, few):
-        many, few = fetch(many, few)
         local = back(fit(low).astype(jnp.bfloat16))
+        many, few, local = fetch(many, few, local)
         part = penalty(penalty_weight, field, many, few, local)
         return series_sum(ridge_weight, part, field)
 

time: 131 us -> 135 us (1.031)
  starting transfers between devices: 36.6 us -> 43.8 us
  waiting for transfers between devices: 11.3 us -> 9.75 us
    ppermute x3, starting transfers between devices: 17 us -> 20.6 us  [fetch(): return (lax.ppermute(many, both, many_route), few, local)]
    ppermute x1, starting transfers between devices: 6.9 us -> 8.7 us  [on_device(): many = lax.ppermute(many, both, last_route)]
    ppermute x9, starting transfers between devices: 10.7 us -> 12.3 us  [moved(): return lax.ppermute(part, 'series', pairs)]
    ppermute x9, waiting for transfers between devices: 11.3 us -> 9.73 us  [moved(): return lax.ppermute(part, 'series', pairs)]
  transfers between devices with their start and end apart: 16 -> 16, of which waited for: 7 -> 6; matrix products, arithmetic and copies ran while one was open for 7% -> 6% of each run, Pallas kernels for 0% -> 0%
where the time goes in v5:
time: 135 us
  blocking collectives  61.9 us (46%)
  starting transfers between devices  43.8 us (32%)
  waiting for transfers between devices  9.75 us (7%)
  Pallas kernels  8.03 us (6%)
  matrix products  6.78 us (5%)
  other arithmetic  1.94 us (1%)
  local copies, waits for them, and re-layouts  1.88 us (1%)
    all_to_all x1, blocking collectives, on_device(): lax.all_to_all(misfit, 'tm', split_axis=0, concat_axis=0, tiled=True)  32.4 us
    all_to_all x1, blocking collectives, on_device(): lax.all_to_all(spread, both, split_axis=0, concat_axis=0, tiled=True)  29.5 us
    ppermute x3, starting transfers between devices, fetch(): return (lax.ppermute(many, both, many_route), few, local)  20.6 us
    ppermute x9, starting transfers between devices, moved(): return lax.ppermute(part, 'series', pairs)  12.3 us
    ppermute x9, waiting for transfers between devices, moved(): return lax.ppermute(part, 'series', pairs)  9.73 us
    ppermute x1, starting transfers between devices, on_device(): many = lax.ppermute(many, both, last_route)  8.7 us
    dot_general x4, matrix products, back(): jnp.dot(rows_here, series_factors, preferred_element_type=jnp.float32)  5.3 us
  transfers between devices with their start and end apart: 16, of which 6 were waited for; matrix products, arithmetic and copies ran while one was open for 6% of the time, Pallas kernels for 0%

profile of v5, /device:TPU:1, one launch (start us, length us, event | category | flops | bytes accessed | tf_op | source)
XLA Modules:
  0.0 134.9 jit_solution(8552082331091730213)
XLA Ops:
  0.6 0.0 copy-start
  0.6 0.1 pad_add_fusion.place_ref
  0.7 0.0 copy-start.2
  0.7 0.9 copy-done.2
  1.6 0.5 shard_map.68
  2.2 6.2 %collective-permute-start = (f32[48,128]{1,0:T(8,128)S(1)}, f32[48,128]{1,0:T(8,128)S(1)}, u32[]{:S(2)}, u32[]{:S(2)}) collective-permute-start(f32[48,128]{1,0:T(8,128)S(1)} %get-tuple-element.24), channel_id=1, source_target_pairs={{0,12},{4,16},{8,20},{12,24},{16,28},{20,32},{24,36},{28,40},{32,4... | collective-permute-start | bytes 73736 | tf_op jit(solution)/shard_map/ppermute | solution.py:225
  8.4 1.9 %broadcast_compare_fusion = pred[64,8192]{1,0:T(32,128)(4,1)S(1)} fusion(s32[64,8192]{1,0:T(8,128)} %param.6), kind=kLoop, calls=%fused_computation.17 | loop fusion | flops 524288 | bytes 2621440 | tf_op jit(solution)/shard_map/eq | solution.py:257
  10.3 0.0 copy-done
  10.3 1.8 %fusion.11 = f32[64,128]{1,0:T(8,128)S(1)} fusion(bf16[8192,128]{1,0:T(8,128)(2,1)S(1)} %copy-done, pred[64,8192]{1,0:T(32,128)(4,1)S(1)} %broadcast_compare_fusion, bf16[64,8192]{1,0:T(8,128)(2,1)} %values_ref.1), kind=kOutput, calls=%fused_computation.15 | convolution fusion | flops 134742016 | bytes 3702784 | tf_op jit(solution)/shard_map/dot_general | solution.py:263
  12.1 0.0 copy-start.3
  12.1 0.0 copy-start.4
  12.1 1.2 fusion.7.local_ref
  13.3 0.7 collective-permute-start.1
  13.9 0.0 collective-permute-done.1.few_ref
  13.9 0.0 collective-permute-done.many_ref
  14.0 0.0 copy-done.3
  14.0 0.0 copy-done.4
  14.0 0.8 shard_map.69.own_ref
  14.7 4.0 %collective-permute-start.4 = (f32[64,128]{1,0:T(8,128)S(1)}, f32[64,128]{1,0:T(8,128)S(1)}, u32[]{:S(2)}, u32[]{:S(2)}) collective-permute-start(f32[64,128]{1,0:T(8,128)S(1)} %shard_map.69.own_ref), channel_id=1, source_target_pairs={{0,3},{1,0},{2,1},{3,2},{4,7},{5,4},{6,5},{7,6},{8,11},{9,8},{10,9... | collective-permute-start | bytes 98312 | tf_op jit(solution)/shard_map/ppermute | solution.py:240
  18.7 0.9 collective-permute-start.3
  19.7 0.8 collective-permute-start.2
  20.4 0.0 collective-permute-done.4.third_ref
  20.4 2.7 %collective-permute-done.3.second_ref = f32[64,128]{1,0:T(8,128)S(1)} collective-permute-done((f32[64,128]{1,0:T(8,128)S(1)}, f32[64,128]{1,0:T(8,128)S(1)}, u32[]{:S(2)}, u32[]{:S(2)}) %collective-permute-start.3) | collective-permute-done | bytes 32800 | tf_op jit(solution)/shard_map/ppermute | solution.py:240
  23.1 0.5 collective-permute-done.2.first_ref
  23.6 0.6 shard_map.70
  24.2 7.0 %collective-permute-start.5 = (f32[48,128]{1,0:T(8,128)S(1)}, f32[48,128]{1,0:T(8,128)S(1)}, u32[]{:S(2)}, u32[]{:S(2)}) collective-permute-start(f32[48,128]{1,0:T(8,128)S(1)} %get-tuple-element.30), channel_id=1, source_target_pairs={{0,12},{4,16},{8,20},{12,24},{16,28},{20,32},{24,36},{28,40},{32,4... | collective-permute-start | bytes 73736 | tf_op jit(solution)/shard_map/ppermute | solution.py:225
  31.2 1.2 fusion.5.local_ref
  32.3 0.7 collective-permute-start.6
  33.0 0.0 collective-permute-done.6.few_ref
  33.0 0.0 collective-permute-done.5.many_ref
  33.0 0.8 shard_map.71.own_ref
  33.8 1.8 %collective-permute-start.9 = (f32[64,128]{1,0:T(8,128)S(1)}, f32[64,128]{1,0:T(8,128)S(1)}, u32[]{:S(2)}, u32[]{:S(2)}) collective-permute-start(f32[64,128]{1,0:T(8,128)S(1)} %shard_map.71.own_ref), channel_id=1, source_target_pairs={{0,3},{1,0},{2,1},{3,2},{4,7},{5,4},{6,5},{7,6},{8,11},{9,8},{10,9... | collective-permute-start | bytes 98312 | tf_op jit(solution)/shard_map/ppermute | solution.py:240
  35.6 0.6 collective-permute-start.8
  36.2 0.8 collective-permute-start.7
  36.9 0.0 collective-permute-done.9.third_ref
  37.0 3.0 %collective-permute-done.8.second_ref = f32[64,128]{1,0:T(8,128)S(1)} collective-permute-done((f32[64,128]{1,0:T(8,128)S(1)}, f32[64,128]{1,0:T(8,128)S(1)}, u32[]{:S(2)}, u32[]{:S(2)}) %collective-permute-start.8) | collective-permute-done | bytes 32800 | tf_op jit(solution)/shard_map/ppermute | solution.py:240
  39.9 0.3 collective-permute-done.7.first_ref
  40.3 0.6 shard_map.72
  40.8 7.4 %collective-permute-start.10 = (f32[48,128]{1,0:T(8,128)S(1)}, f32[48,128]{1,0:T(8,128)S(1)}, u32[]{:S(2)}, u32[]{:S(2)}) collective-permute-start(f32[48,128]{1,0:T(8,128)S(1)} %get-tuple-element.36), channel_id=1, source_target_pairs={{0,12},{4,16},{8,20},{12,24},{16,28},{20,32},{24,36},{28,40},{32,4... | collective-permute-start | bytes 73736 | tf_op jit(solution)/shard_map/ppermute | solution.py:225
  48.3 1.2 fusion.4.local_ref
  49.4 0.0 copy-start.1
  49.4 0.8 collective-permute-start.11
  50.2 0.0 collective-permute-done.11.few_ref
  50.3 0.0 collective-permute-done.10.many_ref
  50.3 0.8 shard_map.73.own_ref
  51.0 1.3 collective-permute-start.14
  52.3 1.5 %collective-permute-start.13 = (f32[64,128]{1,0:T(8,128)S(1)}, f32[64,128]{1,0:T(8,128)S(1)}, u32[]{:S(2)}, u32[]{:S(2)}) collective-permute-start(f32[64,128]{1,0:T(8,128)S(1)} %shard_map.73.own_ref), channel_id=1, source_target_pairs={{0,2},{1,3},{2,0},{3,1},{4,6},{5,7},{6,4},{7,5},{8,10},{9,11},{10,... | collective-permute-start | bytes 98312 | tf_op jit(solution)/shard_map/ppermute | solution.py:240
  53.8 0.8 collective-permute-start.12
  54.6 0.0 collective-permute-done.14.third_ref
  54.6 2.0 %collective-permute-done.13.second_ref = f32[64,128]{1,0:T(8,128)S(1)} collective-permute-done((f32[64,128]{1,0:T(8,128)S(1)}, f32[64,128]{1,0:T(8,128)S(1)}, u32[]{:S(2)}, u32[]{:S(2)}) %collective-permute-start.13) | collective-permute-done | bytes 32800 | tf_op jit(solution)/shard_map/ppermute | solution.py:240
  56.6 1.2 collective-permute-done.12.first_ref
  57.8 1.1 shard_map.74
  58.9 8.7 %collective-permute-start.15 = (f32[48,128]{1,0:T(8,128)S(1)}, f32[48,128]{1,0:T(8,128)S(1)}, u32[]{:S(2)}, u32[]{:S(2)}) collective-permute-start(f32[48,128]{1,0:T(8,128)S(1)} %get-tuple-element.43), channel_id=1, source_target_pairs={{0,12},{4,16},{8,20},{12,24},{16,28},{20,32},{24,36},{28,40},{32,4... | collective-permute-start | bytes 73736 | tf_op jit(solution)/shard_map/ppermute | solution.py:286
  67.6 1.5 %fusion.13 = f32[]{:T(128)} fusion(pred[64,8192]{1,0:T(32,128)(4,1)S(1)} %broadcast_compare_fusion, bf16[64,128]{1,0:T(8,128)(2,1)S(1)} %get-tuple-element.41, bf16[8192,128]{1,0:T(8,128)(2,1)S(1)} %copy-done), kind=kOutput, calls=%fused_computation.18 | convolution fusion | flops 135790592 | bytes 2637828 | tf_op jit(solution)/shard_map/dot_general | solution.py:27
  69.1 0.0 collective-permute-done.15.many_ref
  69.1 1.7 %shard_map.75 = f32[256,1,128]{2,1,0:T(1,128)S(1)} custom-call(s32[2]{0:T(128)S(1)} %pad_add_fusion.place_ref, f32[1,1]{1,0:T(1,128)} %bitcast.2.squares_ref, f32[64,128]{1,0:T(8,128)S(1)} %get-tuple-element.29.field_ref.zero_ref, f32[64,128]{1,0:T(8,128)S(1)} %get-tuple-element.35.field_ref.one_ref, f32[64,128]{1,0:T(8,128)S(1)} %get-tuple-element.42.two_ref, ...), custom_call_target="tpu_custom_call" | custom-call | tf_op jit(solution)/shard_map/pallas_call | solution.py:289
  70.8 29.5 %all_to_all.10.gathered_ref = f32[256,1,128]{2,1,0:T(1,128)S(1)} all-to-all(f32[256,1,128]{2,1,0:T(1,128)S(1)} %shard_map.75), channel_id=1, replica_groups=mesh['tm'=64,'series'=4] {'tm','series'}, dimensions={0} | all-to-all | bytes 262144 | tf_op jit(solution)/shard_map/all_to_all | solution.py:297
  100.3 0.0 copy-done.1
  100.3 1.2 shard_map.76
  101.5 32.4 %all_to_all.11 = bf16[64,64,128]{2,1,0:T(8,128)(2,1)S(1)} all-to-all(bf16[64,64,128]{2,1,0:T(8,128)(2,1)S(1)} %get-tuple-element.45), channel_id=1, replica_groups=mesh['tm'=64,'series'=4] {'tm'}, dimensions={0} | all-to-all | bytes 2097152 | tf_op jit(solution)/shard_map/all_to_all | solution.py:305
  133.9 1.0 copy.14
Async XLA Ops:
  0.6 9.6 %copy-start = (bf16[8192,128]{1,0:T(8,128)(2,1)S(1)}, bf16[8192,128]{1,0:T(8,128)(2,1)}, u32[]{:S(2)}) copy-start(bf16[8192,128]{1,0:T(8,128)(2,1)} %factors_ref.1) | copy-start | bytes 6291460
  0.7 0.9 copy-start.2
  2.2 11.8 %collective-permute-start = (f32[48,128]{1,0:T(8,128)S(1)}, f32[48,128]{1,0:T(8,128)S(1)}, u32[]{:S(2)}, u32[]{:S(2)}) collective-permute-start(f32[48,128]{1,0:T(8,128)S(1)} %get-tuple-element.24), channel_id=1, source_target_pairs={{0,12},{4,16},{8,20},{12,24},{16,28},{20,32},{24,36},{28,40},{32,4... | collective-permute-start | bytes 73736 | tf_op jit(solution)/shard_map/ppermute | solution.py:225
  12.1 1.9 %copy-start.3 = (f32[64,128]{1,0:T(8,128)S(1)}, f32[64,128]{1,0:T(8,128)}, u32[]{:S(2)}) copy-start(f32[64,128]{1,0:T(8,128)} %start_ref.1) | copy-start | bytes 98308
  12.1 1.9 %copy-start.4 = (f32[25,128]{1,0:T(8,128)S(1)}, f32[25,128]{1,0:T(8,128)}, u32[]{:S(2)}) copy-start(f32[25,128]{1,0:T(8,128)} %weights_ref.7) | copy-start | bytes 38404
  13.3 0.7 collective-permute-start.1
  14.7 5.7 %collective-permute-start.4 = (f32[64,128]{1,0:T(8,128)S(1)}, f32[64,128]{1,0:T(8,128)S(1)}, u32[]{:S(2)}, u32[]{:S(2)}) collective-permute-start(f32[64,128]{1,0:T(8,128)S(1)} %shard_map.69.own_ref), channel_id=1, source_target_pairs={{0,3},{1,0},{2,1},{3,2},{4,7},{5,4},{6,5},{7,6},{8,11},{9,8},{10,9... | collective-permute-start | bytes 98312 | tf_op jit(solution)/shard_map/ppermute | solution.py:240
  18.7 4.4 %collective-permute-start.3 = (f32[64,128]{1,0:T(8,128)S(1)}, f32[64,128]{1,0:T(8,128)S(1)}, u32[]{:S(2)}, u32[]{:S(2)}) collective-permute-start(f32[64,128]{1,0:T(8,128)S(1)} %shard_map.69.own_ref), channel_id=1, source_target_pairs={{0,2},{1,3},{2,0},{3,1},{4,6},{5,7},{6,4},{7,5},{8,10},{9,11},{10,... | collective-permute-start | bytes 98312 | tf_op jit(solution)/shard_map/ppermute | solution.py:240
  19.7 4.0 %collective-permute-start.2 = (f32[64,128]{1,0:T(8,128)S(1)}, f32[64,128]{1,0:T(8,128)S(1)}, u32[]{:S(2)}, u32[]{:S(2)}) collective-permute-start(f32[64,128]{1,0:T(8,128)S(1)} %shard_map.69.own_ref), channel_id=1, source_target_pairs={{0,1},{1,2},{2,3},{3,0},{4,5},{5,6},{6,7},{7,4},{8,9},{9,10},{10,1... | collective-permute-start | bytes 98312 | tf_op jit(solution)/shard_map/ppermute | solution.py:240
  24.2 8.8 %collective-permute-start.5 = (f32[48,128]{1,0:T(8,128)S(1)}, f32[48,128]{1,0:T(8,128)S(1)}, u32[]{:S(2)}, u32[]{:S(2)}) collective-permute-start(f32[48,128]{1,0:T(8,128)S(1)} %get-tuple-element.30), channel_id=1, source_target_pairs={{0,12},{4,16},{8,20},{12,24},{16,28},{20,32},{24,36},{28,40},{32,4... | collective-permute-start | bytes 73736 | tf_op jit(solution)/shard_map/ppermute | solution.py:225
  32.3 0.7 collective-permute-start.6
  33.8 3.2 %collective-permute-start.9 = (f32[64,128]{1,0:T(8,128)S(1)}, f32[64,128]{1,0:T(8,128)S(1)}, u32[]{:S(2)}, u32[]{:S(2)}) collective-permute-start(f32[64,128]{1,0:T(8,128)S(1)} %shard_map.71.own_ref), channel_id=1, source_target_pairs={{0,3},{1,0},{2,1},{3,2},{4,7},{5,4},{6,5},{7,6},{8,11},{9,8},{10,9... | collective-permute-start | bytes 98312 | tf_op jit(solution)/shard_map/ppermute | solution.py:240
  35.6 4.3 %collective-permute-start.8 = (f32[64,128]{1,0:T(8,128)S(1)}, f32[64,128]{1,0:T(8,128)S(1)}, u32[]{:S(2)}, u32[]{:S(2)}) collective-permute-start(f32[64,128]{1,0:T(8,128)S(1)} %shard_map.71.own_ref), channel_id=1, source_target_pairs={{0,2},{1,3},{2,0},{3,1},{4,6},{5,7},{6,4},{7,5},{8,10},{9,11},{10,... | collective-permute-start | bytes 98312 | tf_op jit(solution)/shard_map/ppermute | solution.py:240
  36.2 4.1 %collective-permute-start.7 = (f32[64,128]{1,0:T(8,128)S(1)}, f32[64,128]{1,0:T(8,128)S(1)}, u32[]{:S(2)}, u32[]{:S(2)}) collective-permute-start(f32[64,128]{1,0:T(8,128)S(1)} %shard_map.71.own_ref), channel_id=1, source_target_pairs={{0,1},{1,2},{2,3},{3,0},{4,5},{5,6},{6,7},{7,4},{8,9},{9,10},{10,1... | collective-permute-start | bytes 98312 | tf_op jit(solution)/shard_map/ppermute | solution.py:240
  40.8 9.4 %collective-permute-start.10 = (f32[48,128]{1,0:T(8,128)S(1)}, f32[48,128]{1,0:T(8,128)S(1)}, u32[]{:S(2)}, u32[]{:S(2)}) collective-permute-start(f32[48,128]{1,0:T(8,128)S(1)} %get-tuple-element.36), channel_id=1, source_target_pairs={{0,12},{4,16},{8,20},{12,24},{16,28},{20,32},{24,36},{28,40},{32,4... | collective-permute-start | bytes 73736 | tf_op jit(solution)/shard_map/ppermute | solution.py:225
  49.4 50.9 %copy-start.1 = (bf16[64,8192]{1,0:T(8,128)(2,1)S(1)}, bf16[64,8192]{1,0:T(8,128)(2,1)}, u32[]{:S(2)}) copy-start(bf16[64,8192]{1,0:T(8,128)(2,1)} %values_ref.1) | copy-start | bytes 3145732
  49.4 0.8 collective-permute-start.11
  51.0 3.5 %collective-permute-start.14 = (f32[64,128]{1,0:T(8,128)S(1)}, f32[64,128]{1,0:T(8,128)S(1)}, u32[]{:S(2)}, u32[]{:S(2)}) collective-permute-start(f32[64,128]{1,0:T(8,128)S(1)} %shard_map.73.own_ref), channel_id=1, source_target_pairs={{0,3},{1,0},{2,1},{3,2},{4,7},{5,4},{6,5},{7,6},{8,11},{9,8},{10,9... | collective-permute-start | bytes 98312 | tf_op jit(solution)/shard_map/ppermute | solution.py:240
  52.3 4.3 %collective-permute-start.13 = (f32[64,128]{1,0:T(8,128)S(1)}, f32[64,128]{1,0:T(8,128)S(1)}, u32[]{:S(2)}, u32[]{:S(2)}) collective-permute-start(f32[64,128]{1,0:T(8,128)S(1)} %shard_map.73.own_ref), channel_id=1, source_target_pairs={{0,2},{1,3},{2,0},{3,1},{4,6},{5,7},{6,4},{7,5},{8,10},{9,11},{10,... | collective-permute-start | bytes 98312 | tf_op jit(solution)/shard_map/ppermute | solution.py:240
  53.8 4.0 %collective-permute-start.12 = (f32[64,128]{1,0:T(8,128)S(1)}, f32[64,128]{1,0:T(8,128)S(1)}, u32[]{:S(2)}, u32[]{:S(2)}) collective-permute-start(f32[64,128]{1,0:T(8,128)S(1)} %shard_map.73.own_ref), channel_id=1, source_target_pairs={{0,1},{1,2},{2,3},{3,0},{4,5},{5,6},{6,7},{7,4},{8,9},{9,10},{10,1... | collective-permute-start | bytes 98312 | tf_op jit(solution)/shard_map/ppermute | solution.py:240
  58.9 10.2 %collective-permute-start.15 = (f32[48,128]{1,0:T(8,128)S(1)}, f32[48,128]{1,0:T(8,128)S(1)}, u32[]{:S(2)}, u32[]{:S(2)}) collective-permute-start(f32[48,128]{1,0:T(8,128)S(1)} %get-tuple-element.43), channel_id=1, source_target_pairs={{0,12},{4,16},{8,20},{12,24},{16,28},{20,32},{24,36},{28,40},{32,4... | collective-permute-start | bytes 73736 | tf_op jit(solution)/shard_map/ppermute | solution.py:286

commit v6 on v3

--- a/solution.py
+++ b/solution.py
@@ -67,18 +67,21 @@
     )
     blocks = [
         (EDGE, jnp.where(here == 0, field_ref[...], 0.0)),
-        (many_at, many_ref[...]),
-        (jnp.where(here == 3, 240, 152), few_ref[...]),
+        (many_at, many_ref[...].astype(jnp.float32)),
+        (jnp.where(here == 3, 240, 152), few_ref[...].astype(jnp.float32)),
     ]
     product = lag_product(place_ref, blocks, weights_ref, window, short, last_time)
     part_ref[...] = data_weight * local_ref[...] + scale * product
 
 
-def halo(here, field, many_ref, few_ref):
+def halo(here, field, many_ref, few_ref=None):
     rows = field.shape[0]
     late = jnp.logical_or(here == 0, here == 3)
-    many_ref[...] = jnp.where(late, field[rows - MANY :], field[:MANY])
-    few_ref[...] = jnp.where(here == 2, field[rows - FEW :], field[:FEW])
+    many = jnp.where(late, field[rows - MANY :], field[:MANY])
+    many_ref[...] = many.astype(many_ref.dtype)
+    if few_ref is not None:
+        few = jnp.where(here == 2, field[rows - FEW :], field[:FEW])
+        few_ref[...] = few.astype(few_ref.dtype)
 
 
 def start_kernel(place_ref, field_ref, low_ref, many_ref, few_ref):
@@ -89,45 +92,56 @@
 
 def sum_kernel(
     scale, place_ref, own_ref, first_ref, second_ref, third_ref, field_ref,
-    total_ref, low_ref, many_ref, few_ref,
+    total_ref, low_ref, *halo_refs,
 ):
     here = place_ref[0]
     total = (own_ref[...] + second_ref[...]) + (first_ref[...] + third_ref[...])
     total = total + scale * field_ref[...]
     total_ref[...] = total
     low_ref[...] = total.astype(jnp.bfloat16)
-    halo(here, total, many_ref, few_ref)
+    halo(here, total, *halo_refs)
+
+
+def place_sums(sums, first, rank):
+    lane = lax.broadcasted_iota(jnp.int32, (1, rank), 1)
+    packed = jnp.zeros((1, rank), jnp.float32)
+    for number, value in enumerate(sums):
+        packed = jnp.where(lane == first + number, value, packed)
+    return packed
+
+
+def inner(left, right):
+    return jnp.sum(jnp.sum(left * right, axis=0, keepdims=True), axis=1, keepdims=True)
+
+
+def products_kernel(share, zero_ref, one_ref, two_ref, packed_ref):
+    zero, one, two = zero_ref[...], one_ref[...], two_ref[...]
+    sums = [
+        inner(zero, zero),
+        inner(zero, one),
+        inner(zero, two),
+        inner(one, one),
+        inner(one, two),
+        inner(two, two),
+    ]
+    packed = share * place_sums(sums, 0, zero.shape[1])
+    packed_ref[...] = jnp.broadcast_to(packed, packed_ref.shape)
 
 
 def moments_kernel(
-    share, last_time, place_ref, squares_ref, zero_ref, one_ref, two_ref, many_ref,
+    last_time, place_ref, squares_ref, packed_ref, two_ref, many_ref,
     weights_ref, spread_ref, window, short,
 ):
-    zero, one, two = zero_ref[...], one_ref[...], two_ref[...]
+    two = two_ref[...]
     here = place_ref[0]
     many_at = jnp.where(here == 0, 0, jnp.where(here == 2, 48, 128))
     blocks = [
         (EDGE, jnp.where(here == 1, two, 0.0)),
-        (many_at, jnp.where(here == 1, 0.0, 2.0 * many_ref[...])),
+        (many_at, jnp.where(here == 1, 0.0, 2.0 * many_ref[...].astype(jnp.float32))),
     ]
     product = lag_product(place_ref, blocks, weights_ref, window, short, last_time)
-
-    def inner(left, right):
-        return jnp.sum(jnp.sum(left * right, axis=0, keepdims=True), axis=1, keepdims=True)
-
-    sums = [
-        share * inner(zero, zero),
-        share * inner(zero, one),
-        share * inner(zero, two),
-        share * inner(one, one),
-        share * inner(one, two),
-        share * inner(two, two),
-        data_weight * squares_ref[0, 0] + penalty_weight * inner(two, product),
-    ]
-    lane = lax.broadcasted_iota(jnp.int32, (1, zero.shape[1]), 1)
-    packed = jnp.zeros((1, zero.shape[1]), jnp.float32)
-    for number, value in enumerate(sums):
-        packed = jnp.where(lane == number, value, packed)
+    quadratic = data_weight * squares_ref[0, 0] + penalty_weight * inner(two, product)
+    packed = packed_ref[0:1, :] + place_sums([quadratic], 6, two.shape[1])
     spread_ref[...] = jnp.broadcast_to(packed[None], spread_ref.shape)
 
 
@@ -187,8 +201,9 @@
     here = lax.axis_index("series")
     place = jnp.stack([here, lax.axis_index("tm") * rows]).astype(jnp.int32)
     field_shape = jax.ShapeDtypeStruct((rows, rank), jnp.float32)
-    many_shape = jax.ShapeDtypeStruct((MANY, rank), jnp.float32)
-    few_shape = jax.ShapeDtypeStruct((FEW, rank), jnp.float32)
+    many_shape = jax.ShapeDtypeStruct((MANY, rank), jnp.bfloat16)
+    few_shape = jax.ShapeDtypeStruct((FEW, rank), jnp.bfloat16)
+    halo_shapes = (many_shape, few_shape)
     low_shape = jax.ShapeDtypeStruct((rows, rank), jnp.bfloat16)
     lag_scratch = [
         pltpu.VMEM((2 * EDGE + rows, rank), jnp.float32),
@@ -225,7 +240,7 @@
             compiler_params=SMALL,
         )(place, field, many, few, lag_weights, local)
 
-    def series_sum(scale, part, field):
+    def series_sum(scale, part, field, out_halos):
         def moved(distance):
             pairs = [(i, (i + distance) % n_series) for i in range(n_series)]
             return lax.ppermute(part, "series", pairs)
@@ -234,14 +249,9 @@
         second = moved(2)
         return pl.pallas_call(
             functools.partial(sum_kernel, scale),
-            out_shape=(
-                field_shape,
-                low_shape,
-                many_shape,
-                few_shape,
-            ),
+            out_shape=(field_shape, low_shape) + out_halos,
             in_specs=[SMEM] + [VMEM] * 5,
-            out_specs=(VMEM,) * 4,
+            out_specs=(VMEM,) * (2 + len(out_halos)),
             compiler_params=SMALL,
         )(place, part, first, second, third, field)
 
@@ -264,27 +274,34 @@
     kept = jnp.where(seen, series_values, jnp.zeros((), jnp.bfloat16))
     local = back(kept) - back(fit(low).astype(jnp.bfloat16))
     part = penalty(-penalty_weight, time_factors, many, few, local)
-    power0, low, many, few = series_sum(-ridge_weight, part, time_factors)
-
-    def image(field, low, many, few):
+    power0, low, many, few = series_sum(-ridge_weight, part, time_factors, halo_shapes)
+
+    def image(field, low, many, few, out_halos):
         many, few = fetch(many, few)
         local = back(fit(low).astype(jnp.bfloat16))
         part = penalty(penalty_weight, field, many, few, local)
-        return series_sum(ridge_weight, part, field)
-
-    power1, low, many, few = image(power0, low, many, few)
-    power2, low, many, few = image(power1, low, many, few)
+        return series_sum(ridge_weight, part, field, out_halos)
+
+    power1, low, many, few = image(power0, low, many, few, halo_shapes)
+    power2, low, many = image(power1, low, many, few, (many_shape,))
     many = lax.ppermute(many, both, last_route)
     fitted = fit(low)
     squares = jnp.sum(fitted * fitted).reshape(1, 1)
+    packed = pl.pallas_call(
+        functools.partial(products_kernel, 1.0 / n_series),
+        out_shape=jax.ShapeDtypeStruct((8, rank), jnp.float32),
+        in_specs=[VMEM] * 3,
+        out_specs=VMEM,
+        compiler_params=SMALL,
+    )(power0, power1, power2)
     spread = pl.pallas_call(
-        functools.partial(moments_kernel, 1.0 / n_series, last_time),
+        functools.partial(moments_kernel, last_time),
         out_shape=jax.ShapeDtypeStruct((everyone, 1, rank), jnp.float32),
-        in_specs=[SMEM, SMEM] + [VMEM] * 5,
+        in_specs=[SMEM, SMEM] + [VMEM] * 4,
         out_specs=VMEM,
         scratch_shapes=lag_scratch,
         compiler_params=SMALL,
-    )(place, squares, power0, power1, power2, many, lag_weights)
+    )(place, squares, packed, power2, many, lag_weights)
     gathered = lax.all_to_all(spread, both, split_axis=0, concat_axis=0, tiled=True)
     final, misfit = pl.pallas_call(
         update_kernel,

time: 131 us -> 130 us (level)
  no operation moved by 1% of the time
where the time goes in v6:
time: 130 us; the launch traced here: 129 us
  blocking collectives  62.7 us (48%)
  starting transfers between devices  36.4 us (28%)
  waiting for transfers between devices  11.2 us (9%)
  Pallas kernels  7.41 us (6%)
  matrix products  6.78 us (5%)
  other arithmetic  1.94 us (1%)
  local copies, waits for them, and re-layouts  1.88 us (1%)
    all_to_all x1, blocking collectives, on_device(): lax.all_to_all(misfit, 'tm', split_axis=0, concat_axis=0, tiled=True)  32.4 us
    all_to_all x1, blocking collectives, on_device(): lax.all_to_all(spread, both, split_axis=0, concat_axis=0, tiled=True)  30.3 us
    ppermute x3, starting transfers between devices, fetch(): return (lax.ppermute(many, both, many_route), few)  16.9 us
    ppermute x9, waiting for transfers between devices, moved(): return lax.ppermute(part, 'series', pairs)  11.1 us
    ppermute x9, starting transfers between devices, moved(): return lax.ppermute(part, 'series', pairs)  10.8 us
    ppermute x1, starting transfers between devices, on_device(): many = lax.ppermute(many, both, last_route)  6.79 us
    dot_general x4, matrix products, back(): jnp.dot(rows_here, series_factors, preferred_element_type=jnp.float32)  5.3 us
  transfers between devices with their start and end apart: 16, of which 7 were waited for; matrix products, arithmetic and copies ran while one was open for 7% of the time, Pallas kernels for 0%

profile of v6, /device:TPU:1, one launch (start us, length us, event | category | flops | bytes accessed | tf_op | source)
XLA Modules:
  0.0 129.2 jit_solution(8941868892093275629)
XLA Ops:
  0.6 0.0 copy-start
  0.6 0.1 pad_add_fusion.place_ref
  0.7 0.0 copy-start.2
  0.7 0.9 copy-done.2
  1.6 0.6 shard_map.68
  2.2 0.7 collective-permute-start.1
  2.8 6.2 %collective-permute-start = (bf16[48,128]{1,0:T(8,128)(2,1)S(1)}, bf16[48,128]{1,0:T(8,128)(2,1)S(1)}, u32[]{:S(2)}, u32[]{:S(2)}) collective-permute-start(bf16[48,128]{1,0:T(8,128)(2,1)S(1)} %get-tuple-element.18), channel_id=1, source_target_pairs={{0,12},{4,16},{8,20},{12,24},{16,28},{20,32},{24,36},{28,40},{32,4... | collective-permute-start | bytes 36872 | tf_op jit(solution)/shard_map/ppermute | solution.py:231
  9.1 1.9 %broadcast_compare_fusion = pred[64,8192]{1,0:T(32,128)(4,1)S(1)} fusion(s32[64,8192]{1,0:T(8,128)} %param.6), kind=kLoop, calls=%fused_computation.17 | loop fusion | flops 524288 | bytes 2621440 | tf_op jit(solution)/shard_map/eq | solution.py:258
  10.9 0.0 copy-done
  10.9 1.8 %fusion.11 = f32[64,128]{1,0:T(8,128)S(1)} fusion(bf16[8192,128]{1,0:T(8,128)(2,1)S(1)} %copy-done, pred[64,8192]{1,0:T(32,128)(4,1)S(1)} %broadcast_compare_fusion, bf16[64,8192]{1,0:T(8,128)(2,1)} %values_ref.1), kind=kOutput, calls=%fused_computation.15 | convolution fusion | flops 134742016 | bytes 3702784 | tf_op jit(solution)/shard_map/dot_general | solution.py:264
  12.7 0.0 copy-start.3
  12.8 0.0 copy-start.4
  12.8 1.2 fusion.7.local_ref
  13.9 0.0 collective-permute-done.1.few_ref
  13.9 0.0 collective-permute-done.many_ref
  14.0 0.0 copy-done.3
  14.0 0.0 copy-done.4
  14.0 0.8 shard_map.69.own_ref
  14.7 0.4 collective-permute-start.4
  15.1 3.4 %collective-permute-start.3 = (f32[64,128]{1,0:T(8,128)S(1)}, f32[64,128]{1,0:T(8,128)S(1)}, u32[]{:S(2)}, u32[]{:S(2)}) collective-permute-start(f32[64,128]{1,0:T(8,128)S(1)} %shard_map.69.own_ref), channel_id=1, source_target_pairs={{0,2},{1,3},{2,0},{3,1},{4,6},{5,7},{6,4},{7,5},{8,10},{9,11},{10,... | collective-permute-start | bytes 98312 | tf_op jit(solution)/shard_map/ppermute | solution.py:246
  18.6 0.8 collective-permute-start.2
  19.4 0.0 collective-permute-done.4.third_ref
  19.4 0.5 collective-permute-done.3.second_ref
  19.9 3.0 %collective-permute-done.2.first_ref = f32[64,128]{1,0:T(8,128)S(1)} collective-permute-done((f32[64,128]{1,0:T(8,128)S(1)}, f32[64,128]{1,0:T(8,128)S(1)}, u32[]{:S(2)}, u32[]{:S(2)}) %collective-permute-start.2) | collective-permute-done | bytes 32800 | tf_op jit(solution)/shard_map/ppermute | solution.py:246
  22.9 0.6 shard_map.70
  23.5 0.7 collective-permute-start.6
  24.1 4.8 %collective-permute-start.5 = (bf16[48,128]{1,0:T(8,128)(2,1)S(1)}, bf16[48,128]{1,0:T(8,128)(2,1)S(1)}, u32[]{:S(2)}, u32[]{:S(2)}) collective-permute-start(bf16[48,128]{1,0:T(8,128)(2,1)S(1)} %get-tuple-element.22), channel_id=1, source_target_pairs={{0,12},{4,16},{8,20},{12,24},{16,28},{20,32},{24,36},{28,40},{32,4... | collective-permute-start | bytes 36872 | tf_op jit(solution)/shard_map/ppermute | solution.py:231
  29.0 1.2 fusion.5.local_ref
  30.1 0.0 collective-permute-done.6.few_ref
  30.1 0.0 collective-permute-done.5.many_ref
  30.2 0.8 shard_map.71.own_ref
  30.9 0.6 collective-permute-start.9
  31.6 1.4 %collective-permute-start.8 = (f32[64,128]{1,0:T(8,128)S(1)}, f32[64,128]{1,0:T(8,128)S(1)}, u32[]{:S(2)}, u32[]{:S(2)}) collective-permute-start(f32[64,128]{1,0:T(8,128)S(1)} %shard_map.71.own_ref), channel_id=1, source_target_pairs={{0,2},{1,3},{2,0},{3,1},{4,6},{5,7},{6,4},{7,5},{8,10},{9,11},{10,... | collective-permute-start | bytes 98312 | tf_op jit(solution)/shard_map/ppermute | solution.py:246
  33.0 0.7 collective-permute-start.7
  33.7 0.1 collective-permute-done.9.third_ref
  33.8 2.1 %collective-permute-done.8.second_ref = f32[64,128]{1,0:T(8,128)S(1)} collective-permute-done((f32[64,128]{1,0:T(8,128)S(1)}, f32[64,128]{1,0:T(8,128)S(1)}, u32[]{:S(2)}, u32[]{:S(2)}) %collective-permute-start.8) | collective-permute-done | bytes 32800 | tf_op jit(solution)/shard_map/ppermute | solution.py:246
  35.8 1.7 %collective-permute-done.7.first_ref = f32[64,128]{1,0:T(8,128)S(1)} collective-permute-done((f32[64,128]{1,0:T(8,128)S(1)}, f32[64,128]{1,0:T(8,128)S(1)}, u32[]{:S(2)}, u32[]{:S(2)}) %collective-permute-start.7) | collective-permute-done | bytes 32800 | tf_op jit(solution)/shard_map/ppermute | solution.py:246
  37.5 0.6 shard_map.72
  38.1 0.7 collective-permute-start.11
  38.7 5.9 %collective-permute-start.10 = (bf16[48,128]{1,0:T(8,128)(2,1)S(1)}, bf16[48,128]{1,0:T(8,128)(2,1)S(1)}, u32[]{:S(2)}, u32[]{:S(2)}) collective-permute-start(bf16[48,128]{1,0:T(8,128)(2,1)S(1)} %get-tuple-element.26), channel_id=1, source_target_pairs={{0,12},{4,16},{8,20},{12,24},{16,28},{20,32},{24,36},{28,40},{32,4... | collective-permute-start | bytes 36872 | tf_op jit(solution)/shard_map/ppermute | solution.py:231
  44.6 1.2 fusion.4.local_ref
  45.8 0.0 copy-start.1
  45.8 0.0 collective-permute-done.11.few_ref
  45.8 0.0 collective-permute-done.10.many_ref
  45.8 0.8 shard_map.73.own_ref
  46.6 0.2 collective-permute-start.14
  46.8 2.4 %collective-permute-start.13 = (f32[64,128]{1,0:T(8,128)S(1)}, f32[64,128]{1,0:T(8,128)S(1)}, u32[]{:S(2)}, u32[]{:S(2)}) collective-permute-start(f32[64,128]{1,0:T(8,128)S(1)} %shard_map.73.own_ref), channel_id=1, source_target_pairs={{0,2},{1,3},{2,0},{3,1},{4,6},{5,7},{6,4},{7,5},{8,10},{9,11},{10,... | collective-permute-start | bytes 98312 | tf_op jit(solution)/shard_map/ppermute | solution.py:246
  49.3 0.8 collective-permute-start.12
  50.0 0.0 collective-permute-done.14.third_ref
  50.0 1.1 collective-permute-done.13.second_ref
  51.1 2.7 %collective-permute-done.12.first_ref = f32[64,128]{1,0:T(8,128)S(1)} collective-permute-done((f32[64,128]{1,0:T(8,128)S(1)}, f32[64,128]{1,0:T(8,128)S(1)}, u32[]{:S(2)}, u32[]{:S(2)}) %collective-permute-start.12) | collective-permute-done | bytes 32800 | tf_op jit(solution)/shard_map/ppermute | solution.py:246
  53.8 0.6 shard_map.74
  54.3 6.8 %collective-permute-start.15 = (bf16[48,128]{1,0:T(8,128)(2,1)S(1)}, bf16[48,128]{1,0:T(8,128)(2,1)S(1)}, u32[]{:S(2)}, u32[]{:S(2)}) collective-permute-start(bf16[48,128]{1,0:T(8,128)(2,1)S(1)} %get-tuple-element.31), channel_id=1, source_target_pairs={{0,12},{4,16},{8,20},{12,24},{16,28},{20,32},{24,36},{28,40},{32,4... | collective-permute-start | bytes 36872 | tf_op jit(solution)/shard_map/ppermute | solution.py:287
  61.1 1.5 %fusion.13 = f32[]{:T(128)} fusion(pred[64,8192]{1,0:T(32,128)(4,1)S(1)} %broadcast_compare_fusion, bf16[64,128]{1,0:T(8,128)(2,1)S(1)} %get-tuple-element.29, bf16[8192,128]{1,0:T(8,128)(2,1)S(1)} %copy-done), kind=kOutput, calls=%fused_computation.18 | convolution fusion | flops 135790592 | bytes 2637828 | tf_op jit(solution)/shard_map/dot_general | solution.py:26
  62.6 0.1 shard_map.75.packed_ref
  62.7 0.0 collective-permute-done.15.many_ref
  62.7 1.6 %shard_map.76 = f32[256,1,128]{2,1,0:T(1,128)S(1)} custom-call(s32[2]{0:T(128)S(1)} %pad_add_fusion.place_ref, f32[1,1]{1,0:T(1,128)} %bitcast.2.squares_ref, f32[8,128]{1,0:T(8,128)S(1)} %shard_map.75.packed_ref, f32[64,128]{1,0:T(8,128)S(1)} %get-tuple-element.30.two_ref, bf16[48,128]{1,0:T(8,128)(2,1)S(1)} %collective-permute-done.15.many_ref, ...), custom_call_target="tpu_custom_call" | custom-call | tf_op jit(solution)/shard_map/pallas_call | solution.py:297
  64.3 30.3 %all_to_all.10.gathered_ref = f32[256,1,128]{2,1,0:T(1,128)S(1)} all-to-all(f32[256,1,128]{2,1,0:T(1,128)S(1)} %shard_map.76), channel_id=1, replica_groups=mesh['tm'=64,'series'=4] {'tm','series'}, dimensions={0} | all-to-all | bytes 262144 | tf_op jit(solution)/shard_map/all_to_all | solution.py:305
  94.6 0.0 copy-done.1
  94.6 1.2 shard_map.77
  95.8 32.4 %all_to_all.11 = bf16[64,64,128]{2,1,0:T(8,128)(2,1)S(1)} all-to-all(bf16[64,64,128]{2,1,0:T(8,128)(2,1)S(1)} %get-tuple-element.33), channel_id=1, replica_groups=mesh['tm'=64,'series'=4] {'tm'}, dimensions={0} | all-to-all | bytes 2097152 | tf_op jit(solution)/shard_map/all_to_all | solution.py:313
  128.2 1.0 copy.14
Async XLA Ops:
  0.6 10.3 %copy-start = (bf16[8192,128]{1,0:T(8,128)(2,1)S(1)}, bf16[8192,128]{1,0:T(8,128)(2,1)}, u32[]{:S(2)}) copy-start(bf16[8192,128]{1,0:T(8,128)(2,1)} %factors_ref.1) | copy-start | bytes 6291460
  0.7 0.9 copy-start.2
  2.2 11.8 %collective-permute-start.1 = (bf16[24,128]{1,0:T(8,128)(2,1)S(1)}, bf16[24,128]{1,0:T(8,128)(2,1)S(1)}, u32[]{:S(2)}, u32[]{:S(2)}) collective-permute-start(bf16[24,128]{1,0:T(8,128)(2,1)S(1)} %get-tuple-element.19), channel_id=1, source_target_pairs={{2,6},{6,10},{10,14},{14,18},{18,22},{22,26},{26,30},{30,34},{34,3... | collective-permute-start | bytes 18440 | tf_op jit(solution)/shard_map/ppermute | solution.py:230
  2.8 11.1 %collective-permute-start = (bf16[48,128]{1,0:T(8,128)(2,1)S(1)}, bf16[48,128]{1,0:T(8,128)(2,1)S(1)}, u32[]{:S(2)}, u32[]{:S(2)}) collective-permute-start(bf16[48,128]{1,0:T(8,128)(2,1)S(1)} %get-tuple-element.18), channel_id=1, source_target_pairs={{0,12},{4,16},{8,20},{12,24},{16,28},{20,32},{24,36},{28,40},{32,4... | collective-permute-start | bytes 36872 | tf_op jit(solution)/shard_map/ppermute | solution.py:231
  12.7 1.2 copy-start.3
  12.8 1.2 copy-start.4
  14.7 4.6 %collective-permute-start.4 = (f32[64,128]{1,0:T(8,128)S(1)}, f32[64,128]{1,0:T(8,128)S(1)}, u32[]{:S(2)}, u32[]{:S(2)}) collective-permute-start(f32[64,128]{1,0:T(8,128)S(1)} %shard_map.69.own_ref), channel_id=1, source_target_pairs={{0,3},{1,0},{2,1},{3,2},{4,7},{5,4},{6,5},{7,6},{8,11},{9,8},{10,9... | collective-permute-start | bytes 98312 | tf_op jit(solution)/shard_map/ppermute | solution.py:246
  15.1 4.8 %collective-permute-start.3 = (f32[64,128]{1,0:T(8,128)S(1)}, f32[64,128]{1,0:T(8,128)S(1)}, u32[]{:S(2)}, u32[]{:S(2)}) collective-permute-start(f32[64,128]{1,0:T(8,128)S(1)} %shard_map.69.own_ref), channel_id=1, source_target_pairs={{0,2},{1,3},{2,0},{3,1},{4,6},{5,7},{6,4},{7,5},{8,10},{9,11},{10,... | collective-permute-start | bytes 98312 | tf_op jit(solution)/shard_map/ppermute | solution.py:246
  18.6 4.3 %collective-permute-start.2 = (f32[64,128]{1,0:T(8,128)S(1)}, f32[64,128]{1,0:T(8,128)S(1)}, u32[]{:S(2)}, u32[]{:S(2)}) collective-permute-start(f32[64,128]{1,0:T(8,128)S(1)} %shard_map.69.own_ref), channel_id=1, source_target_pairs={{0,1},{1,2},{2,3},{3,0},{4,5},{5,6},{6,7},{7,4},{8,9},{9,10},{10,1... | collective-permute-start | bytes 98312 | tf_op jit(solution)/shard_map/ppermute | solution.py:246
  23.5 6.7 %collective-permute-start.6 = (bf16[24,128]{1,0:T(8,128)(2,1)S(1)}, bf16[24,128]{1,0:T(8,128)(2,1)S(1)}, u32[]{:S(2)}, u32[]{:S(2)}) collective-permute-start(bf16[24,128]{1,0:T(8,128)(2,1)S(1)} %get-tuple-element.23), channel_id=1, source_target_pairs={{2,6},{6,10},{10,14},{14,18},{18,22},{22,26},{26,30},{30,34},{34,3... | collective-permute-start | bytes 18440 | tf_op jit(solution)/shard_map/ppermute | solution.py:230
  24.1 6.0 %collective-permute-start.5 = (bf16[48,128]{1,0:T(8,128)(2,1)S(1)}, bf16[48,128]{1,0:T(8,128)(2,1)S(1)}, u32[]{:S(2)}, u32[]{:S(2)}) collective-permute-start(bf16[48,128]{1,0:T(8,128)(2,1)S(1)} %get-tuple-element.22), channel_id=1, source_target_pairs={{0,12},{4,16},{8,20},{12,24},{16,28},{20,32},{24,36},{28,40},{32,4... | collective-permute-start | bytes 36872 | tf_op jit(solution)/shard_map/ppermute | solution.py:231
  30.9 2.8 %collective-permute-start.9 = (f32[64,128]{1,0:T(8,128)S(1)}, f32[64,128]{1,0:T(8,128)S(1)}, u32[]{:S(2)}, u32[]{:S(2)}) collective-permute-start(f32[64,128]{1,0:T(8,128)S(1)} %shard_map.71.own_ref), channel_id=1, source_target_pairs={{0,3},{1,0},{2,1},{3,2},{4,7},{5,4},{6,5},{7,6},{8,11},{9,8},{10,9... | collective-permute-start | bytes 98312 | tf_op jit(solution)/shard_map/ppermute | solution.py:246
  31.6 4.3 %collective-permute-start.8 = (f32[64,128]{1,0:T(8,128)S(1)}, f32[64,128]{1,0:T(8,128)S(1)}, u32[]{:S(2)}, u32[]{:S(2)}) collective-permute-start(f32[64,128]{1,0:T(8,128)S(1)} %shard_map.71.own_ref), channel_id=1, source_target_pairs={{0,2},{1,3},{2,0},{3,1},{4,6},{5,7},{6,4},{7,5},{8,10},{9,11},{10,... | collective-permute-start | bytes 98312 | tf_op jit(solution)/shard_map/ppermute | solution.py:246
  33.0 4.5 %collective-permute-start.7 = (f32[64,128]{1,0:T(8,128)S(1)}, f32[64,128]{1,0:T(8,128)S(1)}, u32[]{:S(2)}, u32[]{:S(2)}) collective-permute-start(f32[64,128]{1,0:T(8,128)S(1)} %shard_map.71.own_ref), channel_id=1, source_target_pairs={{0,1},{1,2},{2,3},{3,0},{4,5},{5,6},{6,7},{7,4},{8,9},{9,10},{10,1... | collective-permute-start | bytes 98312 | tf_op jit(solution)/shard_map/ppermute | solution.py:246
  38.1 7.7 %collective-permute-start.11 = (bf16[24,128]{1,0:T(8,128)(2,1)S(1)}, bf16[24,128]{1,0:T(8,128)(2,1)S(1)}, u32[]{:S(2)}, u32[]{:S(2)}) collective-permute-start(bf16[24,128]{1,0:T(8,128)(2,1)S(1)} %get-tuple-element.27), channel_id=1, source_target_pairs={{2,6},{6,10},{10,14},{14,18},{18,22},{22,26},{26,30},{30,34},{34,3... | collective-permute-start | bytes 18440 | tf_op jit(solution)/shard_map/ppermute | solution.py:230
  38.7 7.1 %collective-permute-start.10 = (bf16[48,128]{1,0:T(8,128)(2,1)S(1)}, bf16[48,128]{1,0:T(8,128)(2,1)S(1)}, u32[]{:S(2)}, u32[]{:S(2)}) collective-permute-start(bf16[48,128]{1,0:T(8,128)(2,1)S(1)} %get-tuple-element.26), channel_id=1, source_target_pairs={{0,12},{4,16},{8,20},{12,24},{16,28},{20,32},{24,36},{28,40},{32,4... | collective-permute-start | bytes 36872 | tf_op jit(solution)/shard_map/ppermute | solution.py:231
  45.8 48.8 %copy-start.1 = (bf16[64,8192]{1,0:T(8,128)(2,1)S(1)}, bf16[64,8192]{1,0:T(8,128)(2,1)}, u32[]{:S(2)}) copy-start(bf16[64,8192]{1,0:T(8,128)(2,1)} %values_ref.1) | copy-start | bytes 3145732
  46.6 3.4 %collective-permute-start.14 = (f32[64,128]{1,0:T(8,128)S(1)}, f32[64,128]{1,0:T(8,128)S(1)}, u32[]{:S(2)}, u32[]{:S(2)}) collective-permute-start(f32[64,128]{1,0:T(8,128)S(1)} %shard_map.73.own_ref), channel_id=1, source_target_pairs={{0,3},{1,0},{2,1},{3,2},{4,7},{5,4},{6,5},{7,6},{8,11},{9,8},{10,9... | collective-permute-start | bytes 98312 | tf_op jit(solution)/shard_map/ppermute | solution.py:246
  46.8 4.3 %collective-permute-start.13 = (f32[64,128]{1,0:T(8,128)S(1)}, f32[64,128]{1,0:T(8,128)S(1)}, u32[]{:S(2)}, u32[]{:S(2)}) collective-permute-start(f32[64,128]{1,0:T(8,128)S(1)} %shard_map.73.own_ref), channel_id=1, source_target_pairs={{0,2},{1,3},{2,0},{3,1},{4,6},{5,7},{6,4},{7,5},{8,10},{9,11},{10,... | collective-permute-start | bytes 98312 | tf_op jit(solution)/shard_map/ppermute | solution.py:246
  49.3 4.5 %collective-permute-start.12 = (f32[64,128]{1,0:T(8,128)S(1)}, f32[64,128]{1,0:T(8,128)S(1)}, u32[]{:S(2)}, u32[]{:S(2)}) collective-permute-start(f32[64,128]{1,0:T(8,128)S(1)} %shard_map.73.own_ref), channel_id=1, source_target_pairs={{0,1},{1,2},{2,3},{3,0},{4,5},{5,6},{6,7},{7,4},{8,9},{9,10},{10,1... | collective-permute-start | bytes 98312 | tf_op jit(solution)/shard_map/ppermute | solution.py:246
  54.3 8.4 %collective-permute-start.15 = (bf16[48,128]{1,0:T(8,128)(2,1)S(1)}, bf16[48,128]{1,0:T(8,128)(2,1)S(1)}, u32[]{:S(2)}, u32[]{:S(2)}) collective-permute-start(bf16[48,128]{1,0:T(8,128)(2,1)S(1)} %get-tuple-element.31), channel_id=1, source_target_pairs={{0,12},{4,16},{8,20},{12,24},{16,28},{20,32},{24,36},{28,40},{32,4... | collective-permute-start | bytes 36872 | tf_op jit(solution)/shard_map/ppermute | solution.py:287

commit v7 on v6

--- a/solution.py
+++ b/solution.py
@@ -18,7 +18,6 @@
 ridge_weight = 0.2
 
 VMEM = pl.BlockSpec(memory_space=pltpu.VMEM)
-SMEM = pl.BlockSpec(memory_space=pltpu.SMEM)
 SMALL = pltpu.CompilerParams(vmem_limit_bytes=2 << 20)
 
 
@@ -28,10 +27,10 @@
     )
 
 
-def lag_product(place_ref, blocks, weights_ref, window, short, last_time):
+def lag_product(blocks, weights_ref, window, short, last_time):
     rank = weights_ref.shape[1]
     rows = window.shape[0] - 2 * EDGE
-    first_time = place_ref[1]
+    first_time = lax.axis_index("tm") * rows
     window[...] = jnp.zeros_like(window)
     for start, block in blocks:
         if not isinstance(start, int):
@@ -58,10 +57,10 @@
 
 
 def penalty_kernel(
-    scale, last_time, place_ref, field_ref, many_ref, few_ref, weights_ref, local_ref,
+    scale, last_time, field_ref, many_ref, few_ref, weights_ref, local_ref,
     part_ref, window, short,
 ):
-    here = place_ref[0]
+    here = lax.axis_index("series")
     many_at = jnp.where(
         here == 0, 0, jnp.where(here == 1, 368, jnp.where(here == 2, 48, 320))
     )
@@ -70,7 +69,7 @@
         (many_at, many_ref[...].astype(jnp.float32)),
         (jnp.where(here == 3, 240, 152), few_ref[...].astype(jnp.float32)),
     ]
-    product = lag_product(place_ref, blocks, weights_ref, window, short, last_time)
+    product = lag_product(blocks, weights_ref, window, short, last_time)
     part_ref[...] = data_weight * local_ref[...] + scale * product
 
 
@@ -84,17 +83,17 @@
         few_ref[...] = few.astype(few_ref.dtype)
 
 
-def start_kernel(place_ref, field_ref, low_ref, many_ref, few_ref):
+def start_kernel(field_ref, low_ref, many_ref, few_ref):
     field = field_ref[...]
     low_ref[...] = field.astype(jnp.bfloat16)
-    halo(place_ref[0], field, many_ref, few_ref)
+    halo(lax.axis_index("series"), field, many_ref, few_ref)
 
 
 def sum_kernel(
-    scale, place_ref, own_ref, first_ref, second_ref, third_ref, field_ref,
+    scale, own_ref, first_ref, second_ref, third_ref, field_ref,
     total_ref, low_ref, *halo_refs,
 ):
-    here = place_ref[0]
+    here = lax.axis_index("series")
     total = (own_ref[...] + second_ref[...]) + (first_ref[...] + third_ref[...])
     total = total + scale * field_ref[...]
     total_ref[...] = total
@@ -114,7 +113,7 @@
     return jnp.sum(jnp.sum(left * right, axis=0, keepdims=True), axis=1, keepdims=True)
 
 
-def products_kernel(share, zero_ref, one_ref, two_ref, packed_ref):
+def products_kernel(share, squares_ref, zero_ref, one_ref, two_ref, packed_ref):
     zero, one, two = zero_ref[...], one_ref[...], two_ref[...]
     sums = [
         inner(zero, zero),
@@ -124,23 +123,25 @@
         inner(one, two),
         inner(two, two),
     ]
+    squares = jnp.sum(squares_ref[...], axis=1, keepdims=True)
     packed = share * place_sums(sums, 0, zero.shape[1])
+    packed = packed + place_sums([data_weight * squares], len(sums), zero.shape[1])
     packed_ref[...] = jnp.broadcast_to(packed, packed_ref.shape)
 
 
 def moments_kernel(
-    last_time, place_ref, squares_ref, packed_ref, two_ref, many_ref,
+    last_time, packed_ref, two_ref, many_ref,
     weights_ref, spread_ref, window, short,
 ):
     two = two_ref[...]
-    here = place_ref[0]
+    here = lax.axis_index("series")
     many_at = jnp.where(here == 0, 0, jnp.where(here == 2, 48, 128))
     blocks = [
         (EDGE, jnp.where(here == 1, two, 0.0)),
         (many_at, jnp.where(here == 1, 0.0, 2.0 * many_ref[...].astype(jnp.float32))),
     ]
-    product = lag_product(place_ref, blocks, weights_ref, window, short, last_time)
-    quadratic = data_weight * squares_ref[0, 0] + penalty_weight * inner(two, product)
+    product = lag_product(blocks, weights_ref, window, short, last_time)
+    quadratic = penalty_weight * inner(two, product)
     packed = packed_ref[0:1, :] + place_sums([quadratic], 6, two.shape[1])
     spread_ref[...] = jnp.broadcast_to(packed[None], spread_ref.shape)
 
@@ -198,8 +199,6 @@
     n_series = lax.axis_size("series")
     everyone = n_tm * n_series
     last_time = n_tm * rows
-    here = lax.axis_index("series")
-    place = jnp.stack([here, lax.axis_index("tm") * rows]).astype(jnp.int32)
     field_shape = jax.ShapeDtypeStruct((rows, rank), jnp.float32)
     many_shape = jax.ShapeDtypeStruct((MANY, rank), jnp.bfloat16)
     few_shape = jax.ShapeDtypeStruct((FEW, rank), jnp.bfloat16)
@@ -234,11 +233,11 @@
         return pl.pallas_call(
             functools.partial(penalty_kernel, scale, last_time),
             out_shape=field_shape,
-            in_specs=[SMEM] + [VMEM] * 5,
+            in_specs=[VMEM] * 5,
             out_specs=VMEM,
             scratch_shapes=lag_scratch,
             compiler_params=SMALL,
-        )(place, field, many, few, lag_weights, local)
+        )(field, many, few, lag_weights, local)
 
     def series_sum(scale, part, field, out_halos):
         def moved(distance):
@@ -250,10 +249,10 @@
         return pl.pallas_call(
             functools.partial(sum_kernel, scale),
             out_shape=(field_shape, low_shape) + out_halos,
-            in_specs=[SMEM] + [VMEM] * 5,
+            in_specs=[VMEM] * 5,
             out_specs=(VMEM,) * (2 + len(out_halos)),
             compiler_params=SMALL,
-        )(place, part, first, second, third, field)
+        )(part, first, second, third, field)
 
     seen = observed == 1
 
@@ -266,10 +265,10 @@
     low, many, few = pl.pallas_call(
         start_kernel,
         out_shape=(low_shape, many_shape, few_shape),
-        in_specs=[SMEM, VMEM],
+        in_specs=[VMEM],
         out_specs=(VMEM,) * 3,
         compiler_params=SMALL,
-    )(place, time_factors)
+    )(time_factors)
     many, few = fetch(many, few)
     kept = jnp.where(seen, series_values, jnp.zeros((), jnp.bfloat16))
     local = back(kept) - back(fit(low).astype(jnp.bfloat16))
@@ -286,22 +285,22 @@
     power2, low, many = image(power1, low, many, few, (many_shape,))
     many = lax.ppermute(many, both, last_route)
     fitted = fit(low)
-    squares = jnp.sum(fitted * fitted).reshape(1, 1)
+    squares = jnp.sum(fitted * fitted, axis=0, keepdims=True)
     packed = pl.pallas_call(
         functools.partial(products_kernel, 1.0 / n_series),
         out_shape=jax.ShapeDtypeStruct((8, rank), jnp.float32),
-        in_specs=[VMEM] * 3,
+        in_specs=[VMEM] * 4,
         out_specs=VMEM,
         compiler_params=SMALL,
-    )(power0, power1, power2)
+    )(squares, power0, power1, power2)
     spread = pl.pallas_call(
         functools.partial(moments_kernel, last_time),
         out_shape=jax.ShapeDtypeStruct((everyone, 1, rank), jnp.float32),
-        in_specs=[SMEM, SMEM] + [VMEM] * 4,
+        in_specs=[VMEM] * 4,
         out_specs=VMEM,
         scratch_shapes=lag_scratch,
         compiler_params=SMALL,
-    )(place, squares, packed, power2, many, lag_weights)
+    )(packed, power2, many, lag_weights)
     gathered = lax.all_to_all(spread, both, split_axis=0, concat_axis=0, tiled=True)
     final, misfit = pl.pallas_call(
         update_kernel,

time: 130 us -> 125 us (0.962)
  Pallas kernels: 7.41 us -> 2.47 us
    pallas_call x3, Pallas kernels: 2.3 us -> 0.66 us  [penalty(): pl.pallas_call(functools.partial(penalty_kernel, scale, last_time), out_s...]
    pallas_call x3, Pallas kernels: 1.66 us -> 0.05 us  [series_sum(): pl.pallas_call(functools.partial(sum_kernel, scale), out_shape=(field_sha...]
  transfers between devices with their start and end apart: 16 -> 16, of which waited for: 7 -> 7; matrix products, arithmetic and copies ran while one was open for 7% -> 6% of each run, Pallas kernels for 0% -> 0%
where the time goes in v7:
time: 125 us; the launch traced here: 124 us
  blocking collectives  63.3 us (51%)
  starting transfers between devices  36.4 us (29%)
  waiting for transfers between devices  11.2 us (9%)
  matrix products  6.18 us (5%)
  Pallas kernels  2.47 us (2%)
  local copies, waits for them, and re-layouts  1.89 us (2%)
  other arithmetic  1.87 us (1%)
    all_to_all x1, blocking collectives, on_device(): lax.all_to_all(misfit, 'tm', split_axis=0, concat_axis=0, tiled=True)  32.4 us
    all_to_all x1, blocking collectives, on_device(): lax.all_to_all(spread, both, split_axis=0, concat_axis=0, tiled=True)  30.8 us
    ppermute x3, starting transfers between devices, fetch(): return (lax.ppermute(many, both, many_route), few)  16.9 us
    ppermute x9, waiting for transfers between devices, moved(): return lax.ppermute(part, 'series', pairs)  11.2 us
    ppermute x9, starting transfers between devices, moved(): return lax.ppermute(part, 'series', pairs)  10.8 us
    ppermute x1, starting transfers between devices, on_device(): many = lax.ppermute(many, both, last_route)  6.76 us
    dot_general x4, matrix products, back(): jnp.dot(rows_here, series_factors, preferred_element_type=jnp.float32)  5.32 us
  transfers between devices with their start and end apart: 16, of which 7 were waited for; matrix products, arithmetic and copies ran while one was open for 6% of the time, Pallas kernels for 0%

profile of v7, /device:TPU:1, one launch (start us, length us, event | category | flops | bytes accessed | tf_op | source)
XLA Modules:
  0.0 124.1 jit_solution(5816040201840675268)
XLA Ops:
  0.6 0.0 copy-start
  0.6 0.0 copy-start.2
  0.7 0.9 copy-done.2
  1.6 0.7 collective-permute-start.1
  2.2 6.2 %collective-permute-start = (bf16[48,128]{1,0:T(8,128)(2,1)S(1)}, bf16[48,128]{1,0:T(8,128)(2,1)S(1)}, u32[]{:S(2)}, u32[]{:S(2)}) collective-permute-start(bf16[48,128]{1,0:T(8,128)(2,1)S(1)} %get-tuple-element.18), channel_id=1, source_target_pairs={{0,12},{4,16},{8,20},{12,24},{16,28},{20,32},{24,36},{28,40},{32,4... | collective-permute-start | bytes 36872 | tf_op jit(solution)/shard_map/ppermute | solution.py:230
  8.4 1.9 %broadcast_compare_fusion = pred[64,8192]{1,0:T(32,128)(4,1)S(1)} fusion(s32[64,8192]{1,0:T(8,128)} %param.6), kind=kLoop, calls=%fused_computation.18 | loop fusion | flops 524288 | bytes 2621440 | tf_op jit(solution)/shard_map/eq | solution.py:257
  10.3 0.0 copy-done
  10.3 1.8 %fusion.12 = f32[64,128]{1,0:T(8,128)S(1)} fusion(bf16[8192,128]{1,0:T(8,128)(2,1)S(1)} %copy-done, pred[64,8192]{1,0:T(32,128)(4,1)S(1)} %broadcast_compare_fusion, bf16[64,8192]{1,0:T(8,128)(2,1)} %values_ref.1), kind=kOutput, calls=%fused_computation.16 | convolution fusion | flops 134742016 | bytes 3702784 | tf_op jit(solution)/shard_map/dot_general | solution.py:263
  12.1 0.0 copy-start.3
  12.1 0.0 copy-start.4
  12.2 1.2 fusion.8.local_ref
  13.3 0.0 collective-permute-done.1.few_ref
  13.3 0.0 collective-permute-done.many_ref
  13.4 0.0 copy-done.3
  13.4 0.0 copy-done.4
  13.4 0.2 shard_map.69.own_ref
  13.6 0.4 collective-permute-start.4
  14.0 3.5 %collective-permute-start.3 = (f32[64,128]{1,0:T(8,128)S(1)}, f32[64,128]{1,0:T(8,128)S(1)}, u32[]{:S(2)}, u32[]{:S(2)}) collective-permute-start(f32[64,128]{1,0:T(8,128)S(1)} %shard_map.69.own_ref), channel_id=1, source_target_pairs={{0,2},{1,3},{2,0},{3,1},{4,6},{5,7},{6,4},{7,5},{8,10},{9,11},{10,... | collective-permute-start | bytes 98312 | tf_op jit(solution)/shard_map/ppermute | solution.py:245
  17.4 0.8 collective-permute-start.2
  18.2 0.0 collective-permute-done.4.third_ref
  18.2 0.5 collective-permute-done.3.second_ref
  18.7 3.0 %collective-permute-done.2.first_ref = f32[64,128]{1,0:T(8,128)S(1)} collective-permute-done((f32[64,128]{1,0:T(8,128)S(1)}, f32[64,128]{1,0:T(8,128)S(1)}, u32[]{:S(2)}, u32[]{:S(2)}) %collective-permute-start.2) | collective-permute-done | bytes 32800 | tf_op jit(solution)/shard_map/ppermute | solution.py:245
  21.8 0.7 collective-permute-start.6
  22.5 4.8 %collective-permute-start.5 = (bf16[48,128]{1,0:T(8,128)(2,1)S(1)}, bf16[48,128]{1,0:T(8,128)(2,1)S(1)}, u32[]{:S(2)}, u32[]{:S(2)}) collective-permute-start(bf16[48,128]{1,0:T(8,128)(2,1)S(1)} %get-tuple-element.22), channel_id=1, source_target_pairs={{0,12},{4,16},{8,20},{12,24},{16,28},{20,32},{24,36},{28,40},{32,4... | collective-permute-start | bytes 36872 | tf_op jit(solution)/shard_map/ppermute | solution.py:230
  27.3 1.2 fusion.6.local_ref
  28.4 0.0 collective-permute-done.6.few_ref
  28.5 0.0 collective-permute-done.5.many_ref
  28.5 0.2 shard_map.71.own_ref
  28.7 0.6 collective-permute-start.9
  29.3 1.5 %collective-permute-start.8 = (f32[64,128]{1,0:T(8,128)S(1)}, f32[64,128]{1,0:T(8,128)S(1)}, u32[]{:S(2)}, u32[]{:S(2)}) collective-permute-start(f32[64,128]{1,0:T(8,128)S(1)} %shard_map.71.own_ref), channel_id=1, source_target_pairs={{0,2},{1,3},{2,0},{3,1},{4,6},{5,7},{6,4},{7,5},{8,10},{9,11},{10,... | collective-permute-start | bytes 98312 | tf_op jit(solution)/shard_map/ppermute | solution.py:245
  30.8 0.7 collective-permute-start.7
  31.4 0.1 collective-permute-done.9.third_ref
  31.5 2.1 %collective-permute-done.8.second_ref = f32[64,128]{1,0:T(8,128)S(1)} collective-permute-done((f32[64,128]{1,0:T(8,128)S(1)}, f32[64,128]{1,0:T(8,128)S(1)}, u32[]{:S(2)}, u32[]{:S(2)}) %collective-permute-start.8) | collective-permute-done | bytes 32800 | tf_op jit(solution)/shard_map/ppermute | solution.py:245
  33.6 1.7 %collective-permute-done.7.first_ref = f32[64,128]{1,0:T(8,128)S(1)} collective-permute-done((f32[64,128]{1,0:T(8,128)S(1)}, f32[64,128]{1,0:T(8,128)S(1)}, u32[]{:S(2)}, u32[]{:S(2)}) %collective-permute-start.7) | collective-permute-done | bytes 32800 | tf_op jit(solution)/shard_map/ppermute | solution.py:245
  35.3 0.7 collective-permute-start.11
  36.0 5.9 %collective-permute-start.10 = (bf16[48,128]{1,0:T(8,128)(2,1)S(1)}, bf16[48,128]{1,0:T(8,128)(2,1)S(1)}, u32[]{:S(2)}, u32[]{:S(2)}) collective-permute-start(bf16[48,128]{1,0:T(8,128)(2,1)S(1)} %get-tuple-element.26), channel_id=1, source_target_pairs={{0,12},{4,16},{8,20},{12,24},{16,28},{20,32},{24,36},{28,40},{32,4... | collective-permute-start | bytes 36872 | tf_op jit(solution)/shard_map/ppermute | solution.py:230
  41.8 1.2 fusion.5.local_ref
  43.0 0.0 copy-start.1
  43.0 0.0 collective-permute-done.11.few_ref
  43.0 0.0 collective-permute-done.10.many_ref
  43.0 0.2 shard_map.73.own_ref
  43.3 0.2 collective-permute-start.14
  43.5 2.5 %collective-permute-start.13 = (f32[64,128]{1,0:T(8,128)S(1)}, f32[64,128]{1,0:T(8,128)S(1)}, u32[]{:S(2)}, u32[]{:S(2)}) collective-permute-start(f32[64,128]{1,0:T(8,128)S(1)} %shard_map.73.own_ref), channel_id=1, source_target_pairs={{0,2},{1,3},{2,0},{3,1},{4,6},{5,7},{6,4},{7,5},{8,10},{9,11},{10,... | collective-permute-start | bytes 98312 | tf_op jit(solution)/shard_map/ppermute | solution.py:245
  45.9 0.8 collective-permute-start.12
  46.7 0.0 collective-permute-done.14.third_ref
  46.7 1.0 collective-permute-done.13.second_ref
  47.8 2.7 %collective-permute-done.12.first_ref = f32[64,128]{1,0:T(8,128)S(1)} collective-permute-done((f32[64,128]{1,0:T(8,128)S(1)}, f32[64,128]{1,0:T(8,128)S(1)}, u32[]{:S(2)}, u32[]{:S(2)}) %collective-permute-start.12) | collective-permute-done | bytes 32800 | tf_op jit(solution)/shard_map/ppermute | solution.py:245
  50.5 6.8 %collective-permute-start.15 = (bf16[48,128]{1,0:T(8,128)(2,1)S(1)}, bf16[48,128]{1,0:T(8,128)(2,1)S(1)}, u32[]{:S(2)}, u32[]{:S(2)}) collective-permute-start(bf16[48,128]{1,0:T(8,128)(2,1)S(1)} %get-tuple-element.31), channel_id=1, source_target_pairs={{0,12},{4,16},{8,20},{12,24},{16,28},{20,32},{24,36},{28,40},{32,4... | collective-permute-start | bytes 36872 | tf_op jit(solution)/shard_map/ppermute | solution.py:286
  57.3 0.9 fusion.4
  58.1 0.2 shard_map.75.packed_ref
  58.3 0.0 collective-permute-done.15.many_ref
  58.3 0.4 shard_map.76
  58.7 30.8 %all_to_all.10.gathered_ref = f32[256,1,128]{2,1,0:T(1,128)S(1)} all-to-all(f32[256,1,128]{2,1,0:T(1,128)S(1)} %shard_map.76), channel_id=1, replica_groups=mesh['tm'=64,'series'=4] {'tm','series'}, dimensions={0} | all-to-all | bytes 262144 | tf_op jit(solution)/shard_map/all_to_all | solution.py:304
  89.5 0.0 copy-done.1
  89.5 1.2 shard_map.77
  90.7 32.4 %all_to_all.11 = bf16[64,64,128]{2,1,0:T(8,128)(2,1)S(1)} all-to-all(bf16[64,64,128]{2,1,0:T(8,128)(2,1)S(1)} %get-tuple-element.33), channel_id=1, replica_groups=mesh['tm'=64,'series'=4] {'tm'}, dimensions={0} | all-to-all | bytes 2097152 | tf_op jit(solution)/shard_map/all_to_all | solution.py:312
  123.2 1.0 copy.14
  (4 shorter events, 0.1 us)
Async XLA Ops:
  0.6 9.7 %copy-start = (bf16[8192,128]{1,0:T(8,128)(2,1)S(1)}, bf16[8192,128]{1,0:T(8,128)(2,1)}, u32[]{:S(2)}) copy-start(bf16[8192,128]{1,0:T(8,128)(2,1)} %factors_ref.1) | copy-start | bytes 6291460
  0.6 0.9 copy-start.2
  1.6 11.8 %collective-permute-start.1 = (bf16[24,128]{1,0:T(8,128)(2,1)S(1)}, bf16[24,128]{1,0:T(8,128)(2,1)S(1)}, u32[]{:S(2)}, u32[]{:S(2)}) collective-permute-start(bf16[24,128]{1,0:T(8,128)(2,1)S(1)} %get-tuple-element.19), channel_id=1, source_target_pairs={{2,6},{6,10},{10,14},{14,18},{18,22},{22,26},{26,30},{30,34},{34,3... | collective-permute-start | bytes 18440 | tf_op jit(solution)/shard_map/ppermute | solution.py:229
  2.2 11.1 %collective-permute-start = (bf16[48,128]{1,0:T(8,128)(2,1)S(1)}, bf16[48,128]{1,0:T(8,128)(2,1)S(1)}, u32[]{:S(2)}, u32[]{:S(2)}) collective-permute-start(bf16[48,128]{1,0:T(8,128)(2,1)S(1)} %get-tuple-element.18), channel_id=1, source_target_pairs={{0,12},{4,16},{8,20},{12,24},{16,28},{20,32},{24,36},{28,40},{32,4... | collective-permute-start | bytes 36872 | tf_op jit(solution)/shard_map/ppermute | solution.py:230
  12.1 1.2 copy-start.3
  12.1 1.2 copy-start.4
  13.6 4.6 %collective-permute-start.4 = (f32[64,128]{1,0:T(8,128)S(1)}, f32[64,128]{1,0:T(8,128)S(1)}, u32[]{:S(2)}, u32[]{:S(2)}) collective-permute-start(f32[64,128]{1,0:T(8,128)S(1)} %shard_map.69.own_ref), channel_id=1, source_target_pairs={{0,3},{1,0},{2,1},{3,2},{4,7},{5,4},{6,5},{7,6},{8,11},{9,8},{10,9... | collective-permute-start | bytes 98312 | tf_op jit(solution)/shard_map/ppermute | solution.py:245
  14.0 4.8 %collective-permute-start.3 = (f32[64,128]{1,0:T(8,128)S(1)}, f32[64,128]{1,0:T(8,128)S(1)}, u32[]{:S(2)}, u32[]{:S(2)}) collective-permute-start(f32[64,128]{1,0:T(8,128)S(1)} %shard_map.69.own_ref), channel_id=1, source_target_pairs={{0,2},{1,3},{2,0},{3,1},{4,6},{5,7},{6,4},{7,5},{8,10},{9,11},{10,... | collective-permute-start | bytes 98312 | tf_op jit(solution)/shard_map/ppermute | solution.py:245
  17.4 4.3 %collective-permute-start.2 = (f32[64,128]{1,0:T(8,128)S(1)}, f32[64,128]{1,0:T(8,128)S(1)}, u32[]{:S(2)}, u32[]{:S(2)}) collective-permute-start(f32[64,128]{1,0:T(8,128)S(1)} %shard_map.69.own_ref), channel_id=1, source_target_pairs={{0,1},{1,2},{2,3},{3,0},{4,5},{5,6},{6,7},{7,4},{8,9},{9,10},{10,1... | collective-permute-start | bytes 98312 | tf_op jit(solution)/shard_map/ppermute | solution.py:245
  21.8 6.7 %collective-permute-start.6 = (bf16[24,128]{1,0:T(8,128)(2,1)S(1)}, bf16[24,128]{1,0:T(8,128)(2,1)S(1)}, u32[]{:S(2)}, u32[]{:S(2)}) collective-permute-start(bf16[24,128]{1,0:T(8,128)(2,1)S(1)} %get-tuple-element.23), channel_id=1, source_target_pairs={{2,6},{6,10},{10,14},{14,18},{18,22},{22,26},{26,30},{30,34},{34,3... | collective-permute-start | bytes 18440 | tf_op jit(solution)/shard_map/ppermute | solution.py:229
  22.5 6.0 %collective-permute-start.5 = (bf16[48,128]{1,0:T(8,128)(2,1)S(1)}, bf16[48,128]{1,0:T(8,128)(2,1)S(1)}, u32[]{:S(2)}, u32[]{:S(2)}) collective-permute-start(bf16[48,128]{1,0:T(8,128)(2,1)S(1)} %get-tuple-element.22), channel_id=1, source_target_pairs={{0,12},{4,16},{8,20},{12,24},{16,28},{20,32},{24,36},{28,40},{32,4... | collective-permute-start | bytes 36872 | tf_op jit(solution)/shard_map/ppermute | solution.py:230
  28.7 2.8 %collective-permute-start.9 = (f32[64,128]{1,0:T(8,128)S(1)}, f32[64,128]{1,0:T(8,128)S(1)}, u32[]{:S(2)}, u32[]{:S(2)}) collective-permute-start(f32[64,128]{1,0:T(8,128)S(1)} %shard_map.71.own_ref), channel_id=1, source_target_pairs={{0,3},{1,0},{2,1},{3,2},{4,7},{5,4},{6,5},{7,6},{8,11},{9,8},{10,9... | collective-permute-start | bytes 98312 | tf_op jit(solution)/shard_map/ppermute | solution.py:245
  29.3 4.3 %collective-permute-start.8 = (f32[64,128]{1,0:T(8,128)S(1)}, f32[64,128]{1,0:T(8,128)S(1)}, u32[]{:S(2)}, u32[]{:S(2)}) collective-permute-start(f32[64,128]{1,0:T(8,128)S(1)} %shard_map.71.own_ref), channel_id=1, source_target_pairs={{0,2},{1,3},{2,0},{3,1},{4,6},{5,7},{6,4},{7,5},{8,10},{9,11},{10,... | collective-permute-start | bytes 98312 | tf_op jit(solution)/shard_map/ppermute | solution.py:245
  30.8 4.5 %collective-permute-start.7 = (f32[64,128]{1,0:T(8,128)S(1)}, f32[64,128]{1,0:T(8,128)S(1)}, u32[]{:S(2)}, u32[]{:S(2)}) collective-permute-start(f32[64,128]{1,0:T(8,128)S(1)} %shard_map.71.own_ref), channel_id=1, source_target_pairs={{0,1},{1,2},{2,3},{3,0},{4,5},{5,6},{6,7},{7,4},{8,9},{9,10},{10,1... | collective-permute-start | bytes 98312 | tf_op jit(solution)/shard_map/ppermute | solution.py:245
  35.3 7.7 %collective-permute-start.11 = (bf16[24,128]{1,0:T(8,128)(2,1)S(1)}, bf16[24,128]{1,0:T(8,128)(2,1)S(1)}, u32[]{:S(2)}, u32[]{:S(2)}) collective-permute-start(bf16[24,128]{1,0:T(8,128)(2,1)S(1)} %get-tuple-element.27), channel_id=1, source_target_pairs={{2,6},{6,10},{10,14},{14,18},{18,22},{22,26},{26,30},{30,34},{34,3... | collective-permute-start | bytes 18440 | tf_op jit(solution)/shard_map/ppermute | solution.py:229
  36.0 7.1 %collective-permute-start.10 = (bf16[48,128]{1,0:T(8,128)(2,1)S(1)}, bf16[48,128]{1,0:T(8,128)(2,1)S(1)}, u32[]{:S(2)}, u32[]{:S(2)}) collective-permute-start(bf16[48,128]{1,0:T(8,128)(2,1)S(1)} %get-tuple-element.26), channel_id=1, source_target_pairs={{0,12},{4,16},{8,20},{12,24},{16,28},{20,32},{24,36},{28,40},{32,4... | collective-permute-start | bytes 36872 | tf_op jit(solution)/shard_map/ppermute | solution.py:230
  43.0 46.5 %copy-start.1 = (bf16[64,8192]{1,0:T(8,128)(2,1)S(1)}, bf16[64,8192]{1,0:T(8,128)(2,1)}, u32[]{:S(2)}) copy-start(bf16[64,8192]{1,0:T(8,128)(2,1)} %values_ref.1) | copy-start | bytes 3145732
  43.3 3.4 %collective-permute-start.14 = (f32[64,128]{1,0:T(8,128)S(1)}, f32[64,128]{1,0:T(8,128)S(1)}, u32[]{:S(2)}, u32[]{:S(2)}) collective-permute-start(f32[64,128]{1,0:T(8,128)S(1)} %shard_map.73.own_ref), channel_id=1, source_target_pairs={{0,3},{1,0},{2,1},{3,2},{4,7},{5,4},{6,5},{7,6},{8,11},{9,8},{10,9... | collective-permute-start | bytes 98312 | tf_op jit(solution)/shard_map/ppermute | solution.py:245
  43.5 4.3 %collective-permute-start.13 = (f32[64,128]{1,0:T(8,128)S(1)}, f32[64,128]{1,0:T(8,128)S(1)}, u32[]{:S(2)}, u32[]{:S(2)}) collective-permute-start(f32[64,128]{1,0:T(8,128)S(1)} %shard_map.73.own_ref), channel_id=1, source_target_pairs={{0,2},{1,3},{2,0},{3,1},{4,6},{5,7},{6,4},{7,5},{8,10},{9,11},{10,... | collective-permute-start | bytes 98312 | tf_op jit(solution)/shard_map/ppermute | solution.py:245
  45.9 4.5 %collective-permute-start.12 = (f32[64,128]{1,0:T(8,128)S(1)}, f32[64,128]{1,0:T(8,128)S(1)}, u32[]{:S(2)}, u32[]{:S(2)}) collective-permute-start(f32[64,128]{1,0:T(8,128)S(1)} %shard_map.73.own_ref), channel_id=1, source_target_pairs={{0,1},{1,2},{2,3},{3,0},{4,5},{5,6},{6,7},{7,4},{8,9},{9,10},{10,1... | collective-permute-start | bytes 98312 | tf_op jit(solution)/shard_map/ppermute | solution.py:245
  50.5 7.8 %collective-permute-start.15 = (bf16[48,128]{1,0:T(8,128)(2,1)S(1)}, bf16[48,128]{1,0:T(8,128)(2,1)S(1)}, u32[]{:S(2)}, u32[]{:S(2)}) collective-permute-start(bf16[48,128]{1,0:T(8,128)(2,1)S(1)} %get-tuple-element.31), channel_id=1, source_target_pairs={{0,12},{4,16},{8,20},{12,24},{16,28},{20,32},{24,36},{28,40},{32,4... | collective-permute-start | bytes 36872 | tf_op jit(solution)/shard_map/ppermute | solution.py:286

commit v8 on v7

--- a/solution.py
+++ b/solution.py
@@ -11,7 +11,7 @@
 SEASON = 168
 LAGS = list(range(1, SHORT + 1)) + [SEASON]
 MANY = 48
-FEW = 24
+FEW = 48
 EDGE = SEASON + 8
 data_weight = 2.0
 penalty_weight = 0.5
@@ -67,7 +67,7 @@
     blocks = [
         (EDGE, jnp.where(here == 0, field_ref[...], 0.0)),
         (many_at, many_ref[...].astype(jnp.float32)),
-        (jnp.where(here == 3, 240, 152), few_ref[...].astype(jnp.float32)),
+        (jnp.where(here == 3, 240, 128), few_ref[...].astype(jnp.float32)),
     ]
     product = lag_product(blocks, weights_ref, window, short, last_time)
     part_ref[...] = data_weight * local_ref[...] + scale * product
@@ -90,7 +90,7 @@
 
 
 def sum_kernel(
-    scale, own_ref, first_ref, second_ref, third_ref, field_ref,
+    scale, own_ref, first_ref, third_ref, second_ref, field_ref,
     total_ref, low_ref, *halo_refs,
 ):
     here = lax.axis_index("series")
@@ -252,7 +252,7 @@
             in_specs=[VMEM] * 5,
             out_specs=(VMEM,) * (2 + len(out_halos)),
             compiler_params=SMALL,
-        )(part, first, second, third, field)
+        )(part, first, third, second, field)
 
     seen = observed == 1
 

time: 125 us -> 124 us (level)
  starting transfers between devices: 36.4 us -> 39.8 us
  waiting for transfers between devices: 11.2 us -> 8.21 us
    ppermute x9, waiting for transfers between devices: 11.2 us -> 8.19 us  [moved(): return lax.ppermute(part, 'series', pairs)]
    ppermute x9, starting transfers between devices: 10.8 us -> 12.8 us  [moved(): return lax.ppermute(part, 'series', pairs)]
  transfers between devices with their start and end apart: 16 -> 16, of which waited for: 7 -> 8; matrix products, arithmetic and copies ran while one was open for 6% -> 6% of each run, Pallas kernels for 0% -> 0%
where the time goes in v8:
time: 124 us
  blocking collectives  62.4 us (50%)
  starting transfers between devices  39.8 us (32%)
  waiting for transfers between devices  8.21 us (7%)
  matrix products  6.09 us (5%)
  Pallas kernels  2.47 us (2%)
  local copies, waits for them, and re-layouts  1.89 us (2%)
  other arithmetic  1.87 us (2%)
    all_to_all x1, blocking collectives, on_device(): lax.all_to_all(misfit, 'tm', split_axis=0, concat_axis=0, tiled=True)  32.4 us
    all_to_all x1, blocking collectives, on_device(): lax.all_to_all(spread, both, split_axis=0, concat_axis=0, tiled=True)  30 us
    ppermute x3, starting transfers between devices, fetch(): return (lax.ppermute(many, both, many_route), few)  17.5 us
    ppermute x9, starting transfers between devices, moved(): return lax.ppermute(part, 'series', pairs)  12.8 us
    ppermute x9, waiting for transfers between devices, moved(): return lax.ppermute(part, 'series', pairs)  8.19 us
    ppermute x1, starting transfers between devices, on_device(): many = lax.ppermute(many, both, last_route)  7.46 us
    dot_general x4, matrix products, back(): jnp.dot(rows_here, series_factors, preferred_element_type=jnp.float32)  5.23 us
  transfers between devices with their start and end apart: 16, of which 8 were waited for; matrix products, arithmetic and copies ran while one was open for 6% of the time, Pallas kernels for 0%

profile of v8, /device:TPU:1, one launch (start us, length us, event | category | flops | bytes accessed | tf_op | source)
XLA Modules:
  0.0 123.6 jit_solution(12137661418181086128)
XLA Ops:
  0.6 0.0 copy-start
  0.6 0.0 copy-start.2
  0.7 0.9 copy-done.2
  1.6 6.2 %collective-permute-start = (bf16[48,128]{1,0:T(8,128)(2,1)S(1)}, bf16[48,128]{1,0:T(8,128)(2,1)S(1)}, u32[]{:S(2)}, u32[]{:S(2)}) collective-permute-start(bf16[48,128]{1,0:T(8,128)(2,1)S(1)} %get-tuple-element.18), channel_id=1, source_target_pairs={{0,12},{4,16},{8,20},{12,24},{16,28},{20,32},{24,36},{28,40},{32,4... | collective-permute-start | bytes 36872 | tf_op jit(solution)/shard_map/ppermute | solution.py:230
  7.8 0.7 collective-permute-start.1
  8.4 1.9 %broadcast_compare_fusion = pred[64,8192]{1,0:T(32,128)(4,1)S(1)} fusion(s32[64,8192]{1,0:T(8,128)} %param.6), kind=kLoop, calls=%fused_computation.18 | loop fusion | flops 524288 | bytes 2621440 | tf_op jit(solution)/shard_map/eq | solution.py:257
  10.3 0.0 copy-done
  10.3 1.8 %fusion.12 = f32[64,128]{1,0:T(8,128)S(1)} fusion(bf16[8192,128]{1,0:T(8,128)(2,1)S(1)} %copy-done, pred[64,8192]{1,0:T(32,128)(4,1)S(1)} %broadcast_compare_fusion, bf16[64,8192]{1,0:T(8,128)(2,1)} %values_ref.1), kind=kOutput, calls=%fused_computation.16 | convolution fusion | flops 134742016 | bytes 3702784 | tf_op jit(solution)/shard_map/dot_general | solution.py:263
  12.1 0.0 copy-start.3
  12.1 0.0 copy-start.4
  12.1 1.1 fusion.8.local_ref
  13.3 0.0 collective-permute-done.many_ref
  13.3 0.0 collective-permute-done.1.few_ref
  13.3 0.0 copy-done.3
  13.3 0.0 copy-done.4
  13.3 0.2 shard_map.69.own_ref
  13.6 4.0 %collective-permute-start.4 = (f32[64,128]{1,0:T(8,128)S(1)}, f32[64,128]{1,0:T(8,128)S(1)}, u32[]{:S(2)}, u32[]{:S(2)}) collective-permute-start(f32[64,128]{1,0:T(8,128)S(1)} %shard_map.69.own_ref), channel_id=1, source_target_pairs={{0,2},{1,3},{2,0},{3,1},{4,6},{5,7},{6,4},{7,5},{8,10},{9,11},{10,... | collective-permute-start | bytes 98312 | tf_op jit(solution)/shard_map/ppermute | solution.py:245
  17.6 0.0 collective-permute-start.3
  17.6 1.5 %collective-permute-start.2 = (f32[64,128]{1,0:T(8,128)S(1)}, f32[64,128]{1,0:T(8,128)S(1)}, u32[]{:S(2)}, u32[]{:S(2)}) collective-permute-start(f32[64,128]{1,0:T(8,128)S(1)} %shard_map.69.own_ref), channel_id=1, source_target_pairs={{0,1},{1,2},{2,3},{3,0},{4,5},{5,6},{6,7},{7,4},{8,9},{9,10},{10,1... | collective-permute-start | bytes 98312 | tf_op jit(solution)/shard_map/ppermute | solution.py:245
  19.1 0.0 collective-permute-done.4.second_ref
  19.1 1.6 %collective-permute-done.3.third_ref = f32[64,128]{1,0:T(8,128)S(1)} collective-permute-done((f32[64,128]{1,0:T(8,128)S(1)}, f32[64,128]{1,0:T(8,128)S(1)}, u32[]{:S(2)}, u32[]{:S(2)}) %collective-permute-start.3) | collective-permute-done | bytes 32800 | tf_op jit(solution)/shard_map/ppermute | solution.py:245
  20.7 0.9 collective-permute-done.2.first_ref
  21.6 4.7 %collective-permute-start.5 = (bf16[48,128]{1,0:T(8,128)(2,1)S(1)}, bf16[48,128]{1,0:T(8,128)(2,1)S(1)}, u32[]{:S(2)}, u32[]{:S(2)}) collective-permute-start(bf16[48,128]{1,0:T(8,128)(2,1)S(1)} %get-tuple-element.22), channel_id=1, source_target_pairs={{0,12},{4,16},{8,20},{12,24},{16,28},{20,32},{24,36},{28,40},{32,4... | collective-permute-start | bytes 36872 | tf_op jit(solution)/shard_map/ppermute | solution.py:230
  26.3 0.7 collective-permute-start.6
  27.0 1.1 fusion.6.local_ref
  28.1 0.0 collective-permute-done.5.many_ref
  28.1 0.0 collective-permute-done.6.few_ref
  28.1 0.2 shard_map.71.own_ref
  28.3 2.3 %collective-permute-start.9 = (f32[64,128]{1,0:T(8,128)S(1)}, f32[64,128]{1,0:T(8,128)S(1)}, u32[]{:S(2)}, u32[]{:S(2)}) collective-permute-start(f32[64,128]{1,0:T(8,128)S(1)} %shard_map.71.own_ref), channel_id=1, source_target_pairs={{0,2},{1,3},{2,0},{3,1},{4,6},{5,7},{6,4},{7,5},{8,10},{9,11},{10,... | collective-permute-start | bytes 98312 | tf_op jit(solution)/shard_map/ppermute | solution.py:245
  30.7 0.4 collective-permute-start.8
  31.1 1.1 collective-permute-start.7
  32.1 0.6 collective-permute-done.9.second_ref
  32.7 0.9 collective-permute-done.8.third_ref
  33.6 1.5 %collective-permute-done.7.first_ref = f32[64,128]{1,0:T(8,128)S(1)} collective-permute-done((f32[64,128]{1,0:T(8,128)S(1)}, f32[64,128]{1,0:T(8,128)S(1)}, u32[]{:S(2)}, u32[]{:S(2)}) %collective-permute-start.7) | collective-permute-done | bytes 32800 | tf_op jit(solution)/shard_map/ppermute | solution.py:245
  35.1 6.7 %collective-permute-start.10 = (bf16[48,128]{1,0:T(8,128)(2,1)S(1)}, bf16[48,128]{1,0:T(8,128)(2,1)S(1)}, u32[]{:S(2)}, u32[]{:S(2)}) collective-permute-start(bf16[48,128]{1,0:T(8,128)(2,1)S(1)} %get-tuple-element.26), channel_id=1, source_target_pairs={{0,12},{4,16},{8,20},{12,24},{16,28},{20,32},{24,36},{28,40},{32,4... | collective-permute-start | bytes 36872 | tf_op jit(solution)/shard_map/ppermute | solution.py:230
  41.8 0.7 collective-permute-start.11
  42.4 1.1 fusion.5.local_ref
  43.6 0.0 copy-start.1
  43.6 0.0 collective-permute-done.10.many_ref
  43.6 0.0 collective-permute-done.11.few_ref
  43.6 0.2 shard_map.73.own_ref
  43.9 2.1 %collective-permute-start.14 = (f32[64,128]{1,0:T(8,128)S(1)}, f32[64,128]{1,0:T(8,128)S(1)}, u32[]{:S(2)}, u32[]{:S(2)}) collective-permute-start(f32[64,128]{1,0:T(8,128)S(1)} %shard_map.73.own_ref), channel_id=1, source_target_pairs={{0,2},{1,3},{2,0},{3,1},{4,6},{5,7},{6,4},{7,5},{8,10},{9,11},{10,... | collective-permute-start | bytes 98312 | tf_op jit(solution)/shard_map/ppermute | solution.py:245
  45.9 0.2 collective-permute-start.13
  46.2 1.2 %collective-permute-start.12 = (f32[64,128]{1,0:T(8,128)S(1)}, f32[64,128]{1,0:T(8,128)S(1)}, u32[]{:S(2)}, u32[]{:S(2)}) collective-permute-start(f32[64,128]{1,0:T(8,128)S(1)} %shard_map.73.own_ref), channel_id=1, source_target_pairs={{0,1},{1,2},{2,3},{3,0},{4,5},{5,6},{6,7},{7,4},{8,9},{9,10},{10,1... | collective-permute-start | bytes 98312 | tf_op jit(solution)/shard_map/ppermute | solution.py:245
  47.4 0.8 collective-permute-done.14.second_ref
  48.2 0.8 collective-permute-done.13.third_ref
  49.0 1.1 collective-permute-done.12.first_ref
  50.2 7.5 %collective-permute-start.15 = (bf16[48,128]{1,0:T(8,128)(2,1)S(1)}, bf16[48,128]{1,0:T(8,128)(2,1)S(1)}, u32[]{:S(2)}, u32[]{:S(2)}) collective-permute-start(bf16[48,128]{1,0:T(8,128)(2,1)S(1)} %get-tuple-element.31), channel_id=1, source_target_pairs={{0,12},{4,16},{8,20},{12,24},{16,28},{20,32},{24,36},{28,40},{32,4... | collective-permute-start | bytes 36872 | tf_op jit(solution)/shard_map/ppermute | solution.py:286
  57.6 0.9 fusion.4
  58.5 0.2 shard_map.75.packed_ref
  58.6 0.0 collective-permute-done.15.many_ref
  58.6 0.4 shard_map.76
  59.0 30.0 %all_to_all.10.gathered_ref = f32[256,1,128]{2,1,0:T(1,128)S(1)} all-to-all(f32[256,1,128]{2,1,0:T(1,128)S(1)} %shard_map.76), channel_id=1, replica_groups=mesh['tm'=64,'series'=4] {'tm','series'}, dimensions={0} | all-to-all | bytes 262144 | tf_op jit(solution)/shard_map/all_to_all | solution.py:304
  89.0 0.0 copy-done.1
  89.0 1.2 shard_map.77
  90.2 32.4 %all_to_all.11 = bf16[64,64,128]{2,1,0:T(8,128)(2,1)S(1)} all-to-all(bf16[64,64,128]{2,1,0:T(8,128)(2,1)S(1)} %get-tuple-element.33), channel_id=1, replica_groups=mesh['tm'=64,'series'=4] {'tm'}, dimensions={0} | all-to-all | bytes 2097152 | tf_op jit(solution)/shard_map/all_to_all | solution.py:312
  122.6 1.0 copy.14
  (4 shorter events, 0.1 us)
Async XLA Ops:
  0.6 9.7 %copy-start = (bf16[8192,128]{1,0:T(8,128)(2,1)S(1)}, bf16[8192,128]{1,0:T(8,128)(2,1)}, u32[]{:S(2)}) copy-start(bf16[8192,128]{1,0:T(8,128)(2,1)} %factors_ref.1) | copy-start | bytes 6291460
  0.6 0.9 copy-start.2
  1.6 11.7 %collective-permute-start = (bf16[48,128]{1,0:T(8,128)(2,1)S(1)}, bf16[48,128]{1,0:T(8,128)(2,1)S(1)}, u32[]{:S(2)}, u32[]{:S(2)}) collective-permute-start(bf16[48,128]{1,0:T(8,128)(2,1)S(1)} %get-tuple-element.18), channel_id=1, source_target_pairs={{0,12},{4,16},{8,20},{12,24},{16,28},{20,32},{24,36},{28,40},{32,4... | collective-permute-start | bytes 36872 | tf_op jit(solution)/shard_map/ppermute | solution.py:230
  7.8 5.5 %collective-permute-start.1 = (bf16[48,128]{1,0:T(8,128)(2,1)S(1)}, bf16[48,128]{1,0:T(8,128)(2,1)S(1)}, u32[]{:S(2)}, u32[]{:S(2)}) collective-permute-start(bf16[48,128]{1,0:T(8,128)(2,1)S(1)} %get-tuple-element.19), channel_id=1, source_target_pairs={{2,6},{6,10},{10,14},{14,18},{18,22},{22,26},{26,30},{30,34},{34,3... | collective-permute-start | bytes 36872 | tf_op jit(solution)/shard_map/ppermute | solution.py:229
  12.1 1.2 copy-start.3
  12.1 1.2 copy-start.4
  13.6 5.5 %collective-permute-start.4 = (f32[64,128]{1,0:T(8,128)S(1)}, f32[64,128]{1,0:T(8,128)S(1)}, u32[]{:S(2)}, u32[]{:S(2)}) collective-permute-start(f32[64,128]{1,0:T(8,128)S(1)} %shard_map.69.own_ref), channel_id=1, source_target_pairs={{0,2},{1,3},{2,0},{3,1},{4,6},{5,7},{6,4},{7,5},{8,10},{9,11},{10,... | collective-permute-start | bytes 98312 | tf_op jit(solution)/shard_map/ppermute | solution.py:245
  17.6 3.1 %collective-permute-start.3 = (f32[64,128]{1,0:T(8,128)S(1)}, f32[64,128]{1,0:T(8,128)S(1)}, u32[]{:S(2)}, u32[]{:S(2)}) collective-permute-start(f32[64,128]{1,0:T(8,128)S(1)} %shard_map.69.own_ref), channel_id=1, source_target_pairs={{0,3},{1,0},{2,1},{3,2},{4,7},{5,4},{6,5},{7,6},{8,11},{9,8},{10,9... | collective-permute-start | bytes 98312 | tf_op jit(solution)/shard_map/ppermute | solution.py:245
  17.6 4.0 %collective-permute-start.2 = (f32[64,128]{1,0:T(8,128)S(1)}, f32[64,128]{1,0:T(8,128)S(1)}, u32[]{:S(2)}, u32[]{:S(2)}) collective-permute-start(f32[64,128]{1,0:T(8,128)S(1)} %shard_map.69.own_ref), channel_id=1, source_target_pairs={{0,1},{1,2},{2,3},{3,0},{4,5},{5,6},{6,7},{7,4},{8,9},{9,10},{10,1... | collective-permute-start | bytes 98312 | tf_op jit(solution)/shard_map/ppermute | solution.py:245
  21.6 6.5 %collective-permute-start.5 = (bf16[48,128]{1,0:T(8,128)(2,1)S(1)}, bf16[48,128]{1,0:T(8,128)(2,1)S(1)}, u32[]{:S(2)}, u32[]{:S(2)}) collective-permute-start(bf16[48,128]{1,0:T(8,128)(2,1)S(1)} %get-tuple-element.22), channel_id=1, source_target_pairs={{0,12},{4,16},{8,20},{12,24},{16,28},{20,32},{24,36},{28,40},{32,4... | collective-permute-start | bytes 36872 | tf_op jit(solution)/shard_map/ppermute | solution.py:230
  26.3 1.8 %collective-permute-start.6 = (bf16[48,128]{1,0:T(8,128)(2,1)S(1)}, bf16[48,128]{1,0:T(8,128)(2,1)S(1)}, u32[]{:S(2)}, u32[]{:S(2)}) collective-permute-start(bf16[48,128]{1,0:T(8,128)(2,1)S(1)} %get-tuple-element.23), channel_id=1, source_target_pairs={{2,6},{6,10},{10,14},{14,18},{18,22},{22,26},{26,30},{30,34},{34,3... | collective-permute-start | bytes 36872 | tf_op jit(solution)/shard_map/ppermute | solution.py:229
  28.3 4.4 %collective-permute-start.9 = (f32[64,128]{1,0:T(8,128)S(1)}, f32[64,128]{1,0:T(8,128)S(1)}, u32[]{:S(2)}, u32[]{:S(2)}) collective-permute-start(f32[64,128]{1,0:T(8,128)S(1)} %shard_map.71.own_ref), channel_id=1, source_target_pairs={{0,2},{1,3},{2,0},{3,1},{4,6},{5,7},{6,4},{7,5},{8,10},{9,11},{10,... | collective-permute-start | bytes 98312 | tf_op jit(solution)/shard_map/ppermute | solution.py:245
  30.7 2.9 %collective-permute-start.8 = (f32[64,128]{1,0:T(8,128)S(1)}, f32[64,128]{1,0:T(8,128)S(1)}, u32[]{:S(2)}, u32[]{:S(2)}) collective-permute-start(f32[64,128]{1,0:T(8,128)S(1)} %shard_map.71.own_ref), channel_id=1, source_target_pairs={{0,3},{1,0},{2,1},{3,2},{4,7},{5,4},{6,5},{7,6},{8,11},{9,8},{10,9... | collective-permute-start | bytes 98312 | tf_op jit(solution)/shard_map/ppermute | solution.py:245
  31.1 4.0 %collective-permute-start.7 = (f32[64,128]{1,0:T(8,128)S(1)}, f32[64,128]{1,0:T(8,128)S(1)}, u32[]{:S(2)}, u32[]{:S(2)}) collective-permute-start(f32[64,128]{1,0:T(8,128)S(1)} %shard_map.71.own_ref), channel_id=1, source_target_pairs={{0,1},{1,2},{2,3},{3,0},{4,5},{5,6},{6,7},{7,4},{8,9},{9,10},{10,1... | collective-permute-start | bytes 98312 | tf_op jit(solution)/shard_map/ppermute | solution.py:245
  35.1 8.5 %collective-permute-start.10 = (bf16[48,128]{1,0:T(8,128)(2,1)S(1)}, bf16[48,128]{1,0:T(8,128)(2,1)S(1)}, u32[]{:S(2)}, u32[]{:S(2)}) collective-permute-start(bf16[48,128]{1,0:T(8,128)(2,1)S(1)} %get-tuple-element.26), channel_id=1, source_target_pairs={{0,12},{4,16},{8,20},{12,24},{16,28},{20,32},{24,36},{28,40},{32,4... | collective-permute-start | bytes 36872 | tf_op jit(solution)/shard_map/ppermute | solution.py:230
  41.8 1.8 %collective-permute-start.11 = (bf16[48,128]{1,0:T(8,128)(2,1)S(1)}, bf16[48,128]{1,0:T(8,128)(2,1)S(1)}, u32[]{:S(2)}, u32[]{:S(2)}) collective-permute-start(bf16[48,128]{1,0:T(8,128)(2,1)S(1)} %get-tuple-element.27), channel_id=1, source_target_pairs={{2,6},{6,10},{10,14},{14,18},{18,22},{22,26},{26,30},{30,34},{34,3... | collective-permute-start | bytes 36872 | tf_op jit(solution)/shard_map/ppermute | solution.py:229
  43.6 45.4 %copy-start.1 = (bf16[64,8192]{1,0:T(8,128)(2,1)S(1)}, bf16[64,8192]{1,0:T(8,128)(2,1)}, u32[]{:S(2)}) copy-start(bf16[64,8192]{1,0:T(8,128)(2,1)} %values_ref.1) | copy-start | bytes 3145732
  43.9 4.4 %collective-permute-start.14 = (f32[64,128]{1,0:T(8,128)S(1)}, f32[64,128]{1,0:T(8,128)S(1)}, u32[]{:S(2)}, u32[]{:S(2)}) collective-permute-start(f32[64,128]{1,0:T(8,128)S(1)} %shard_map.73.own_ref), channel_id=1, source_target_pairs={{0,2},{1,3},{2,0},{3,1},{4,6},{5,7},{6,4},{7,5},{8,10},{9,11},{10,... | collective-permute-start | bytes 98312 | tf_op jit(solution)/shard_map/ppermute | solution.py:245
  45.9 3.1 %collective-permute-start.13 = (f32[64,128]{1,0:T(8,128)S(1)}, f32[64,128]{1,0:T(8,128)S(1)}, u32[]{:S(2)}, u32[]{:S(2)}) collective-permute-start(f32[64,128]{1,0:T(8,128)S(1)} %shard_map.73.own_ref), channel_id=1, source_target_pairs={{0,3},{1,0},{2,1},{3,2},{4,7},{5,4},{6,5},{7,6},{8,11},{9,8},{10,9... | collective-permute-start | bytes 98312 | tf_op jit(solution)/shard_map/ppermute | solution.py:245
  46.2 4.0 %collective-permute-start.12 = (f32[64,128]{1,0:T(8,128)S(1)}, f32[64,128]{1,0:T(8,128)S(1)}, u32[]{:S(2)}, u32[]{:S(2)}) collective-permute-start(f32[64,128]{1,0:T(8,128)S(1)} %shard_map.73.own_ref), channel_id=1, source_target_pairs={{0,1},{1,2},{2,3},{3,0},{4,5},{5,6},{6,7},{7,4},{8,9},{9,10},{10,1... | collective-permute-start | bytes 98312 | tf_op jit(solution)/shard_map/ppermute | solution.py:245
  50.2 8.5 %collective-permute-start.15 = (bf16[48,128]{1,0:T(8,128)(2,1)S(1)}, bf16[48,128]{1,0:T(8,128)(2,1)S(1)}, u32[]{:S(2)}, u32[]{:S(2)}) collective-permute-start(bf16[48,128]{1,0:T(8,128)(2,1)S(1)} %get-tuple-element.31), channel_id=1, source_target_pairs={{0,12},{4,16},{8,20},{12,24},{16,28},{20,32},{24,36},{28,40},{32,4... | collective-permute-start | bytes 36872 | tf_op jit(solution)/shard_map/ppermute | solution.py:286

commit v9 on v8

--- a/solution.py
+++ b/solution.py
@@ -11,7 +11,6 @@
 SEASON = 168
 LAGS = list(range(1, SHORT + 1)) + [SEASON]
 MANY = 48
-FEW = 48
 EDGE = SEASON + 8
 data_weight = 2.0
 penalty_weight = 0.5
@@ -67,38 +66,34 @@
     blocks = [
         (EDGE, jnp.where(here == 0, field_ref[...], 0.0)),
         (many_at, many_ref[...].astype(jnp.float32)),
-        (jnp.where(here == 3, 240, 128), few_ref[...].astype(jnp.float32)),
+        (jnp.where(here == 2, 240, 128), few_ref[...].astype(jnp.float32)),
     ]
     product = lag_product(blocks, weights_ref, window, short, last_time)
     part_ref[...] = data_weight * local_ref[...] + scale * product
 
 
-def halo(here, field, many_ref, few_ref=None):
+def halo_rows(field):
+    here = lax.axis_index("series")
+    late = jnp.logical_or(here == 0, here == 3)
     rows = field.shape[0]
-    late = jnp.logical_or(here == 0, here == 3)
-    many = jnp.where(late, field[rows - MANY :], field[:MANY])
-    many_ref[...] = many.astype(many_ref.dtype)
-    if few_ref is not None:
-        few = jnp.where(here == 2, field[rows - FEW :], field[:FEW])
-        few_ref[...] = few.astype(few_ref.dtype)
-
-
-def start_kernel(field_ref, low_ref, many_ref, few_ref):
+    return jnp.where(late, field[rows - MANY :], field[:MANY]).astype(jnp.bfloat16)
+
+
+def start_kernel(field_ref, low_ref, halo_ref):
     field = field_ref[...]
     low_ref[...] = field.astype(jnp.bfloat16)
-    halo(lax.axis_index("series"), field, many_ref, few_ref)
+    halo_ref[...] = halo_rows(field)
 
 
 def sum_kernel(
     scale, own_ref, first_ref, third_ref, second_ref, field_ref,
-    total_ref, low_ref, *halo_refs,
+    total_ref, low_ref, halo_ref,
 ):
-    here = lax.axis_index("series")
     total = (own_ref[...] + second_ref[...]) + (first_ref[...] + third_ref[...])
     total = total + scale * field_ref[...]
     total_ref[...] = total
     low_ref[...] = total.astype(jnp.bfloat16)
-    halo(here, total, *halo_refs)
+    halo_ref[...] = halo_rows(total)
 
 
 def place_sums(sums, first, rank):
@@ -200,9 +195,7 @@
     everyone = n_tm * n_series
     last_time = n_tm * rows
     field_shape = jax.ShapeDtypeStruct((rows, rank), jnp.float32)
-    many_shape = jax.ShapeDtypeStruct((MANY, rank), jnp.bfloat16)
-    few_shape = jax.ShapeDtypeStruct((FEW, rank), jnp.bfloat16)
-    halo_shapes = (many_shape, few_shape)
+    halo_shape = jax.ShapeDtypeStruct((MANY, rank), jnp.bfloat16)
     low_shape = jax.ShapeDtypeStruct((rows, rank), jnp.bfloat16)
     lag_scratch = [
         pltpu.VMEM((2 * EDGE + rows, rank), jnp.float32),
@@ -221,13 +214,12 @@
         return pairs
 
     many_route = route([3, -3, 2, -2])
-    few_route = route([None, None, 1, -1])
+    few_route = route([None, None, -1, 1])
     last_route = route([3, None, 2, 1])
     both = ("tm", "series")
 
-    def fetch(many, few):
-        few = lax.ppermute(few, both, few_route)
-        return lax.ppermute(many, both, many_route), few
+    def fetch(halo):
+        return lax.ppermute(halo, both, many_route), lax.ppermute(halo, both, few_route)
 
     def penalty(scale, field, many, few, local):
         return pl.pallas_call(
@@ -239,7 +231,7 @@
             compiler_params=SMALL,
         )(field, many, few, lag_weights, local)
 
-    def series_sum(scale, part, field, out_halos):
+    def series_sum(scale, part, field):
         def moved(distance):
             pairs = [(i, (i + distance) % n_series) for i in range(n_series)]
             return lax.ppermute(part, "series", pairs)
@@ -248,9 +240,9 @@
         second = moved(2)
         return pl.pallas_call(
             functools.partial(sum_kernel, scale),
-            out_shape=(field_shape, low_shape) + out_halos,
+            out_shape=(field_shape, low_shape, halo_shape),
             in_specs=[VMEM] * 5,
-            out_specs=(VMEM,) * (2 + len(out_halos)),
+            out_specs=(VMEM,) * 3,
             compiler_params=SMALL,
         )(part, first, third, second, field)
 
@@ -262,28 +254,28 @@
     def back(rows_here):
         return jnp.dot(rows_here, series_factors, preferred_element_type=jnp.float32)
 
-    low, many, few = pl.pallas_call(
+    low, halo = pl.pallas_call(
         start_kernel,
-        out_shape=(low_shape, many_shape, few_shape),
+        out_shape=(low_shape, halo_shape),
         in_specs=[VMEM],
-        out_specs=(VMEM,) * 3,
+        out_specs=(VMEM,) * 2,
         compiler_params=SMALL,
     )(time_factors)
-    many, few = fetch(many, few)
+    many, few = fetch(halo)
     kept = jnp.where(seen, series_values, jnp.zeros((), jnp.bfloat16))
     local = back(kept) - back(fit(low).astype(jnp.bfloat16))
     part = penalty(-penalty_weight, time_factors, many, few, local)
-    power0, low, many, few = series_sum(-ridge_weight, part, time_factors, halo_shapes)
-
-    def image(field, low, many, few, out_halos):
-        many, few = fetch(many, few)
+    power0, low, halo = series_sum(-ridge_weight, part, time_factors)
+
+    def image(field, low, halo):
+        many, few = fetch(halo)
         local = back(fit(low).astype(jnp.bfloat16))
         part = penalty(penalty_weight, field, many, few, local)
-        return series_sum(ridge_weight, part, field, out_halos)
-
-    power1, low, many, few = image(power0, low, many, few, halo_shapes)
-    power2, low, many = image(power1, low, many, few, (many_shape,))
-    many = lax.ppermute(many, both, last_route)
+        return series_sum(ridge_weight, part, field)
+
+    power1, low, halo = image(power0, low, halo)
+    power2, low, halo = image(power1, low, halo)
+    many = lax.ppermute(halo, both, last_route)
     fitted = fit(low)
     squares = jnp.sum(fitted * fitted, axis=0, keepdims=True)
     packed = pl.pallas_call(

time: 124 us -> 128 us (1.032)
  blocking collectives: 62.4 us -> 66.2 us
  waiting for transfers between devices: 8.21 us -> 11 us
  starting transfers between devices: 39.8 us -> 37.1 us
    all_to_all x1, blocking collectives: 30 us -> 33.8 us  [on_device(): lax.all_to_all(spread, both, split_axis=0, concat_axis=0, tiled=True)]
    ppermute x9, waiting for transfers between devices: 8.19 us -> 11 us  [moved(): return lax.ppermute(part, 'series', pairs)]
    ppermute x9, starting transfers between devices: 12.8 us -> 10.4 us  [moved(): return lax.ppermute(part, 'series', pairs)]
  transfers between devices with their start and end apart: 16 -> 16, of which waited for: 8 -> 7; matrix products, arithmetic and copies ran while one was open for 6% -> 6% of each run, Pallas kernels for 0% -> 0%
where the time goes in v9:
time: 128 us
  blocking collectives  66.2 us (52%)
  starting transfers between devices  37.1 us (29%)
  waiting for transfers between devices  11 us (9%)
  matrix products  6.16 us (5%)
  Pallas kernels  2.48 us (2%)
  local copies, waits for them, and re-layouts  1.89 us (1%)
  other arithmetic  1.87 us (1%)
    all_to_all x1, blocking collectives, on_device(): lax.all_to_all(spread, both, split_axis=0, concat_axis=0, tiled=True)  33.8 us
    all_to_all x1, blocking collectives, on_device(): lax.all_to_all(misfit, 'tm', split_axis=0, concat_axis=0, tiled=True)  32.4 us
    ppermute x3, starting transfers between devices, fetch(): lax.ppermute(halo, both, many_route)  17.6 us
    ppermute x9, waiting for transfers between devices, moved(): return lax.ppermute(part, 'series', pairs)  11 us
    ppermute x9, starting transfers between devices, moved(): return lax.ppermute(part, 'series', pairs)  10.4 us
    ppermute x1, starting transfers between devices, on_device(): many = lax.ppermute(halo, both, last_route)  7.17 us
    dot_general x4, matrix products, back(): jnp.dot(rows_here, series_factors, preferred_element_type=jnp.float32)  5.3 us
  transfers between devices with their start and end apart: 16, of which 7 were waited for; matrix products, arithmetic and copies ran while one was open for 6% of the time, Pallas kernels for 0%

profile of v9, /device:TPU:1, one launch (start us, length us, event | category | flops | bytes accessed | tf_op | source)
XLA Modules:
  0.0 127.7 jit_solution(2137072250693853582)
XLA Ops:
  0.6 0.0 copy-start
  0.6 0.0 copy-start.2
  0.7 0.9 copy-done.2
  1.6 0.7 collective-permute-start.1
  2.2 6.2 %collective-permute-start = (bf16[48,128]{1,0:T(8,128)(2,1)S(1)}, bf16[48,128]{1,0:T(8,128)(2,1)S(1)}, u32[]{:S(2)}, u32[]{:S(2)}) collective-permute-start(bf16[48,128]{1,0:T(8,128)(2,1)S(1)} %get-tuple-element.15), channel_id=1, source_target_pairs={{0,12},{4,16},{8,20},{12,24},{16,28},{20,32},{24,36},{28,40},{32,4... | collective-permute-start | bytes 36872 | tf_op jit(solution)/shard_map/ppermute | solution.py:222
  8.4 1.9 %broadcast_compare_fusion = pred[64,8192]{1,0:T(32,128)(4,1)S(1)} fusion(s32[64,8192]{1,0:T(8,128)} %param.6), kind=kLoop, calls=%fused_computation.18 | loop fusion | flops 524288 | bytes 2621440 | tf_op jit(solution)/shard_map/eq | solution.py:249
  10.3 0.0 copy-done
  10.3 1.8 %fusion.12 = f32[64,128]{1,0:T(8,128)S(1)} fusion(bf16[8192,128]{1,0:T(8,128)(2,1)S(1)} %copy-done, pred[64,8192]{1,0:T(32,128)(4,1)S(1)} %broadcast_compare_fusion, bf16[64,8192]{1,0:T(8,128)(2,1)} %values_ref.1), kind=kOutput, calls=%fused_computation.16 | convolution fusion | flops 134742016 | bytes 3702784 | tf_op jit(solution)/shard_map/dot_general | solution.py:255
  12.1 0.0 copy-start.3
  12.1 0.0 copy-start.4
  12.1 1.2 fusion.8.local_ref
  13.3 0.0 collective-permute-done.1.few_ref
  13.3 0.0 collective-permute-done.many_ref
  13.3 0.0 copy-done.3
  13.3 0.0 copy-done.4
  13.4 0.2 shard_map.69.own_ref
  13.6 2.6 %collective-permute-start.4 = (f32[64,128]{1,0:T(8,128)S(1)}, f32[64,128]{1,0:T(8,128)S(1)}, u32[]{:S(2)}, u32[]{:S(2)}) collective-permute-start(f32[64,128]{1,0:T(8,128)S(1)} %shard_map.69.own_ref), channel_id=1, source_target_pairs={{0,2},{1,3},{2,0},{3,1},{4,6},{5,7},{6,4},{7,5},{8,10},{9,11},{10,... | collective-permute-start | bytes 98312 | tf_op jit(solution)/shard_map/ppermute | solution.py:237
  16.2 0.0 collective-permute-start.3
  16.2 1.5 %collective-permute-start.2 = (f32[64,128]{1,0:T(8,128)S(1)}, f32[64,128]{1,0:T(8,128)S(1)}, u32[]{:S(2)}, u32[]{:S(2)}) collective-permute-start(f32[64,128]{1,0:T(8,128)S(1)} %shard_map.69.own_ref), channel_id=1, source_target_pairs={{0,1},{1,2},{2,3},{3,0},{4,5},{5,6},{6,7},{7,4},{8,9},{9,10},{10,1... | collective-permute-start | bytes 98312 | tf_op jit(solution)/shard_map/ppermute | solution.py:237
  17.6 0.9 collective-permute-done.4.second_ref
  18.6 0.4 collective-permute-done.3.third_ref
  18.9 1.2 collective-permute-done.2.first_ref
  20.2 0.7 collective-permute-start.6
  20.8 6.3 %collective-permute-start.5 = (bf16[48,128]{1,0:T(8,128)(2,1)S(1)}, bf16[48,128]{1,0:T(8,128)(2,1)S(1)}, u32[]{:S(2)}, u32[]{:S(2)}) collective-permute-start(bf16[48,128]{1,0:T(8,128)(2,1)S(1)} %get-tuple-element.18), channel_id=1, source_target_pairs={{0,12},{4,16},{8,20},{12,24},{16,28},{20,32},{24,36},{28,40},{32,4... | collective-permute-start | bytes 36872 | tf_op jit(solution)/shard_map/ppermute | solution.py:222
  27.1 1.2 fusion.6.local_ref
  28.3 0.0 collective-permute-done.6.few_ref
  28.3 0.0 collective-permute-done.5.many_ref
  28.3 0.2 shard_map.71.own_ref
  28.6 0.6 collective-permute-start.9
  29.1 2.6 %collective-permute-start.8 = (f32[64,128]{1,0:T(8,128)S(1)}, f32[64,128]{1,0:T(8,128)S(1)}, u32[]{:S(2)}, u32[]{:S(2)}) collective-permute-start(f32[64,128]{1,0:T(8,128)S(1)} %shard_map.71.own_ref), channel_id=1, source_target_pairs={{0,3},{1,0},{2,1},{3,2},{4,7},{5,4},{6,5},{7,6},{8,11},{9,8},{10,9... | collective-permute-start | bytes 98312 | tf_op jit(solution)/shard_map/ppermute | solution.py:237
  31.7 0.0 collective-permute-start.7
  31.7 1.2 collective-permute-done.9.second_ref
  32.9 0.0 collective-permute-done.8.third_ref
  32.9 3.4 %collective-permute-done.7.first_ref = f32[64,128]{1,0:T(8,128)S(1)} collective-permute-done((f32[64,128]{1,0:T(8,128)S(1)}, f32[64,128]{1,0:T(8,128)S(1)}, u32[]{:S(2)}, u32[]{:S(2)}) %collective-permute-start.7) | collective-permute-done | bytes 32800 | tf_op jit(solution)/shard_map/ppermute | solution.py:237
  36.3 0.7 collective-permute-start.11
  37.0 5.1 %collective-permute-start.10 = (bf16[48,128]{1,0:T(8,128)(2,1)S(1)}, bf16[48,128]{1,0:T(8,128)(2,1)S(1)}, u32[]{:S(2)}, u32[]{:S(2)}) collective-permute-start(bf16[48,128]{1,0:T(8,128)(2,1)S(1)} %get-tuple-element.21), channel_id=1, source_target_pairs={{0,12},{4,16},{8,20},{12,24},{16,28},{20,32},{24,36},{28,40},{32,4... | collective-permute-start | bytes 36872 | tf_op jit(solution)/shard_map/ppermute | solution.py:222
  42.1 1.2 fusion.5.local_ref
  43.2 0.0 copy-start.1
  43.3 0.0 collective-permute-done.11.few_ref
  43.3 0.0 collective-permute-done.10.many_ref
  43.3 0.2 shard_map.73.own_ref
  43.5 0.1 collective-permute-start.14
  43.6 3.1 %collective-permute-start.13 = (f32[64,128]{1,0:T(8,128)S(1)}, f32[64,128]{1,0:T(8,128)S(1)}, u32[]{:S(2)}, u32[]{:S(2)}) collective-permute-start(f32[64,128]{1,0:T(8,128)S(1)} %shard_map.73.own_ref), channel_id=1, source_target_pairs={{0,3},{1,0},{2,1},{3,2},{4,7},{5,4},{6,5},{7,6},{8,11},{9,8},{10,9... | collective-permute-start | bytes 98312 | tf_op jit(solution)/shard_map/ppermute | solution.py:237
  46.7 0.0 collective-permute-start.12
  46.7 1.4 %collective-permute-done.14.second_ref = f32[64,128]{1,0:T(8,128)S(1)} collective-permute-done((f32[64,128]{1,0:T(8,128)S(1)}, f32[64,128]{1,0:T(8,128)S(1)}, u32[]{:S(2)}, u32[]{:S(2)}) %collective-permute-start.14) | collective-permute-done | bytes 32800 | tf_op jit(solution)/shard_map/ppermute | solution.py:237
  48.1 0.0 collective-permute-done.13.third_ref
  48.1 2.6 %collective-permute-done.12.first_ref = f32[64,128]{1,0:T(8,128)S(1)} collective-permute-done((f32[64,128]{1,0:T(8,128)S(1)}, f32[64,128]{1,0:T(8,128)S(1)}, u32[]{:S(2)}, u32[]{:S(2)}) %collective-permute-start.12) | collective-permute-done | bytes 32800 | tf_op jit(solution)/shard_map/ppermute | solution.py:237
  50.7 7.2 %collective-permute-start.15 = (bf16[48,128]{1,0:T(8,128)(2,1)S(1)}, bf16[48,128]{1,0:T(8,128)(2,1)S(1)}, u32[]{:S(2)}, u32[]{:S(2)}) collective-permute-start(bf16[48,128]{1,0:T(8,128)(2,1)S(1)} %get-tuple-element.25), channel_id=1, source_target_pairs={{0,12},{4,16},{8,20},{12,24},{16,28},{20,32},{24,36},{28,40},{32,4... | collective-permute-start | bytes 36872 | tf_op jit(solution)/shard_map/ppermute | solution.py:278
  57.8 0.9 fusion.4
  58.7 0.2 shard_map.75.packed_ref
  58.9 0.0 collective-permute-done.15.many_ref
  58.9 0.4 shard_map.76
  59.2 33.8 %all_to_all.10.gathered_ref = f32[256,1,128]{2,1,0:T(1,128)S(1)} all-to-all(f32[256,1,128]{2,1,0:T(1,128)S(1)} %shard_map.76), channel_id=1, replica_groups=mesh['tm'=64,'series'=4] {'tm','series'}, dimensions={0} | all-to-all | bytes 262144 | tf_op jit(solution)/shard_map/all_to_all | solution.py:296
  93.0 0.0 copy-done.1
  93.0 1.2 shard_map.77
  94.3 32.4 %all_to_all.11 = bf16[64,64,128]{2,1,0:T(8,128)(2,1)S(1)} all-to-all(bf16[64,64,128]{2,1,0:T(8,128)(2,1)S(1)} %get-tuple-element.27), channel_id=1, replica_groups=mesh['tm'=64,'series'=4] {'tm'}, dimensions={0} | all-to-all | bytes 2097152 | tf_op jit(solution)/shard_map/all_to_all | solution.py:304
  126.7 1.0 copy.14
  (4 shorter events, 0.1 us)
Async XLA Ops:
  0.6 9.7 %copy-start = (bf16[8192,128]{1,0:T(8,128)(2,1)S(1)}, bf16[8192,128]{1,0:T(8,128)(2,1)}, u32[]{:S(2)}) copy-start(bf16[8192,128]{1,0:T(8,128)(2,1)} %factors_ref.1) | copy-start | bytes 6291460
  0.6 0.9 copy-start.2
  1.6 11.8 %collective-permute-start.1 = (bf16[48,128]{1,0:T(8,128)(2,1)S(1)}, bf16[48,128]{1,0:T(8,128)(2,1)S(1)}, u32[]{:S(2)}, u32[]{:S(2)}) collective-permute-start(bf16[48,128]{1,0:T(8,128)(2,1)S(1)} %get-tuple-element.15), channel_id=1, source_target_pairs={{6,2},{10,6},{14,10},{18,14},{22,18},{26,22},{30,26},{34,30},{38,3... | collective-permute-start | bytes 36872 | tf_op jit(solution)/shard_map/ppermute | solution.py:222
  2.2 11.1 %collective-permute-start = (bf16[48,128]{1,0:T(8,128)(2,1)S(1)}, bf16[48,128]{1,0:T(8,128)(2,1)S(1)}, u32[]{:S(2)}, u32[]{:S(2)}) collective-permute-start(bf16[48,128]{1,0:T(8,128)(2,1)S(1)} %get-tuple-element.15), channel_id=1, source_target_pairs={{0,12},{4,16},{8,20},{12,24},{16,28},{20,32},{24,36},{28,40},{32,4... | collective-permute-start | bytes 36872 | tf_op jit(solution)/shard_map/ppermute | solution.py:222
  12.1 1.2 copy-start.3
  12.1 1.2 copy-start.4
  13.6 5.0 %collective-permute-start.4 = (f32[64,128]{1,0:T(8,128)S(1)}, f32[64,128]{1,0:T(8,128)S(1)}, u32[]{:S(2)}, u32[]{:S(2)}) collective-permute-start(f32[64,128]{1,0:T(8,128)S(1)} %shard_map.69.own_ref), channel_id=1, source_target_pairs={{0,2},{1,3},{2,0},{3,1},{4,6},{5,7},{6,4},{7,5},{8,10},{9,11},{10,... | collective-permute-start | bytes 98312 | tf_op jit(solution)/shard_map/ppermute | solution.py:237
  16.2 2.8 %collective-permute-start.3 = (f32[64,128]{1,0:T(8,128)S(1)}, f32[64,128]{1,0:T(8,128)S(1)}, u32[]{:S(2)}, u32[]{:S(2)}) collective-permute-start(f32[64,128]{1,0:T(8,128)S(1)} %shard_map.69.own_ref), channel_id=1, source_target_pairs={{0,3},{1,0},{2,1},{3,2},{4,7},{5,4},{6,5},{7,6},{8,11},{9,8},{10,9... | collective-permute-start | bytes 98312 | tf_op jit(solution)/shard_map/ppermute | solution.py:237
  16.2 4.0 %collective-permute-start.2 = (f32[64,128]{1,0:T(8,128)S(1)}, f32[64,128]{1,0:T(8,128)S(1)}, u32[]{:S(2)}, u32[]{:S(2)}) collective-permute-start(f32[64,128]{1,0:T(8,128)S(1)} %shard_map.69.own_ref), channel_id=1, source_target_pairs={{0,1},{1,2},{2,3},{3,0},{4,5},{5,6},{6,7},{7,4},{8,9},{9,10},{10,1... | collective-permute-start | bytes 98312 | tf_op jit(solution)/shard_map/ppermute | solution.py:237
  20.2 8.2 %collective-permute-start.6 = (bf16[48,128]{1,0:T(8,128)(2,1)S(1)}, bf16[48,128]{1,0:T(8,128)(2,1)S(1)}, u32[]{:S(2)}, u32[]{:S(2)}) collective-permute-start(bf16[48,128]{1,0:T(8,128)(2,1)S(1)} %get-tuple-element.18), channel_id=1, source_target_pairs={{6,2},{10,6},{14,10},{18,14},{22,18},{26,22},{30,26},{34,30},{38,3... | collective-permute-start | bytes 36872 | tf_op jit(solution)/shard_map/ppermute | solution.py:222
  20.8 7.5 %collective-permute-start.5 = (bf16[48,128]{1,0:T(8,128)(2,1)S(1)}, bf16[48,128]{1,0:T(8,128)(2,1)S(1)}, u32[]{:S(2)}, u32[]{:S(2)}) collective-permute-start(bf16[48,128]{1,0:T(8,128)(2,1)S(1)} %get-tuple-element.18), channel_id=1, source_target_pairs={{0,12},{4,16},{8,20},{12,24},{16,28},{20,32},{24,36},{28,40},{32,4... | collective-permute-start | bytes 36872 | tf_op jit(solution)/shard_map/ppermute | solution.py:222
  28.6 4.4 %collective-permute-start.9 = (f32[64,128]{1,0:T(8,128)S(1)}, f32[64,128]{1,0:T(8,128)S(1)}, u32[]{:S(2)}, u32[]{:S(2)}) collective-permute-start(f32[64,128]{1,0:T(8,128)S(1)} %shard_map.71.own_ref), channel_id=1, source_target_pairs={{0,2},{1,3},{2,0},{3,1},{4,6},{5,7},{6,4},{7,5},{8,10},{9,11},{10,... | collective-permute-start | bytes 98312 | tf_op jit(solution)/shard_map/ppermute | solution.py:237
  29.1 3.8 %collective-permute-start.8 = (f32[64,128]{1,0:T(8,128)S(1)}, f32[64,128]{1,0:T(8,128)S(1)}, u32[]{:S(2)}, u32[]{:S(2)}) collective-permute-start(f32[64,128]{1,0:T(8,128)S(1)} %shard_map.71.own_ref), channel_id=1, source_target_pairs={{0,3},{1,0},{2,1},{3,2},{4,7},{5,4},{6,5},{7,6},{8,11},{9,8},{10,9... | collective-permute-start | bytes 98312 | tf_op jit(solution)/shard_map/ppermute | solution.py:237
  31.7 4.5 %collective-permute-start.7 = (f32[64,128]{1,0:T(8,128)S(1)}, f32[64,128]{1,0:T(8,128)S(1)}, u32[]{:S(2)}, u32[]{:S(2)}) collective-permute-start(f32[64,128]{1,0:T(8,128)S(1)} %shard_map.71.own_ref), channel_id=1, source_target_pairs={{0,1},{1,2},{2,3},{3,0},{4,5},{5,6},{6,7},{7,4},{8,9},{9,10},{10,1... | collective-permute-start | bytes 98312 | tf_op jit(solution)/shard_map/ppermute | solution.py:237
  36.3 6.9 %collective-permute-start.11 = (bf16[48,128]{1,0:T(8,128)(2,1)S(1)}, bf16[48,128]{1,0:T(8,128)(2,1)S(1)}, u32[]{:S(2)}, u32[]{:S(2)}) collective-permute-start(bf16[48,128]{1,0:T(8,128)(2,1)S(1)} %get-tuple-element.21), channel_id=1, source_target_pairs={{6,2},{10,6},{14,10},{18,14},{22,18},{26,22},{30,26},{34,30},{38,3... | collective-permute-start | bytes 36872 | tf_op jit(solution)/shard_map/ppermute | solution.py:222
  37.0 6.3 %collective-permute-start.10 = (bf16[48,128]{1,0:T(8,128)(2,1)S(1)}, bf16[48,128]{1,0:T(8,128)(2,1)S(1)}, u32[]{:S(2)}, u32[]{:S(2)}) collective-permute-start(bf16[48,128]{1,0:T(8,128)(2,1)S(1)} %get-tuple-element.21), channel_id=1, source_target_pairs={{0,12},{4,16},{8,20},{12,24},{16,28},{20,32},{24,36},{28,40},{32,4... | collective-permute-start | bytes 36872 | tf_op jit(solution)/shard_map/ppermute | solution.py:222
  43.2 49.8 %copy-start.1 = (bf16[64,8192]{1,0:T(8,128)(2,1)S(1)}, bf16[64,8192]{1,0:T(8,128)(2,1)}, u32[]{:S(2)}) copy-start(bf16[64,8192]{1,0:T(8,128)(2,1)} %values_ref.1) | copy-start | bytes 3145732
  43.5 4.6 %collective-permute-start.14 = (f32[64,128]{1,0:T(8,128)S(1)}, f32[64,128]{1,0:T(8,128)S(1)}, u32[]{:S(2)}, u32[]{:S(2)}) collective-permute-start(f32[64,128]{1,0:T(8,128)S(1)} %shard_map.73.own_ref), channel_id=1, source_target_pairs={{0,2},{1,3},{2,0},{3,1},{4,6},{5,7},{6,4},{7,5},{8,10},{9,11},{10,... | collective-permute-start | bytes 98312 | tf_op jit(solution)/shard_map/ppermute | solution.py:237
  43.6 4.5 %collective-permute-start.13 = (f32[64,128]{1,0:T(8,128)S(1)}, f32[64,128]{1,0:T(8,128)S(1)}, u32[]{:S(2)}, u32[]{:S(2)}) collective-permute-start(f32[64,128]{1,0:T(8,128)S(1)} %shard_map.73.own_ref), channel_id=1, source_target_pairs={{0,3},{1,0},{2,1},{3,2},{4,7},{5,4},{6,5},{7,6},{8,11},{9,8},{10,9... | collective-permute-start | bytes 98312 | tf_op jit(solution)/shard_map/ppermute | solution.py:237
  46.7 4.0 %collective-permute-start.12 = (f32[64,128]{1,0:T(8,128)S(1)}, f32[64,128]{1,0:T(8,128)S(1)}, u32[]{:S(2)}, u32[]{:S(2)}) collective-permute-start(f32[64,128]{1,0:T(8,128)S(1)} %shard_map.73.own_ref), channel_id=1, source_target_pairs={{0,1},{1,2},{2,3},{3,0},{4,5},{5,6},{6,7},{7,4},{8,9},{9,10},{10,1... | collective-permute-start | bytes 98312 | tf_op jit(solution)/shard_map/ppermute | solution.py:237
  50.7 8.2 %collective-permute-start.15 = (bf16[48,128]{1,0:T(8,128)(2,1)S(1)}, bf16[48,128]{1,0:T(8,128)(2,1)S(1)}, u32[]{:S(2)}, u32[]{:S(2)}) collective-permute-start(bf16[48,128]{1,0:T(8,128)(2,1)S(1)} %get-tuple-element.25), channel_id=1, source_target_pairs={{0,12},{4,16},{8,20},{12,24},{16,28},{20,32},{24,36},{28,40},{32,4... | collective-permute-start | bytes 36872 | tf_op jit(solution)/shard_map/ppermute | solution.py:278

commit v10 on v9

--- a/solution.py
+++ b/solution.py
@@ -56,7 +56,7 @@
 
 
 def penalty_kernel(
-    scale, last_time, field_ref, many_ref, few_ref, weights_ref, local_ref,
+    scale, last_time, field_ref, few_ref, many_ref, weights_ref, local_ref,
     part_ref, window, short,
 ):
     here = lax.axis_index("series")
@@ -65,8 +65,8 @@
     )
     blocks = [
         (EDGE, jnp.where(here == 0, field_ref[...], 0.0)),
-        (many_at, many_ref[...].astype(jnp.float32)),
-        (jnp.where(here == 2, 240, 128), few_ref[...].astype(jnp.float32)),
+        (many_at, halo_rows(many_ref[...].astype(jnp.float32))),
+        (jnp.where(here == 2, 240, 128), halo_rows(few_ref[...].astype(jnp.float32))),
     ]
     product = lag_product(blocks, weights_ref, window, short, last_time)
     part_ref[...] = data_weight * local_ref[...] + scale * product
@@ -76,13 +76,9 @@
     here = lax.axis_index("series")
     late = jnp.logical_or(here == 0, here == 3)
     rows = field.shape[0]
-    return jnp.where(late, field[rows - MANY :], field[:MANY]).astype(jnp.bfloat16)
-
-
-def start_kernel(field_ref, low_ref, halo_ref):
-    field = field_ref[...]
-    low_ref[...] = field.astype(jnp.bfloat16)
-    halo_ref[...] = halo_rows(field)
+    if rows == MANY:
+        return field
+    return jnp.where(late, field[rows - MANY :], field[:MANY])
 
 
 def sum_kernel(
@@ -93,7 +89,7 @@
     total = total + scale * field_ref[...]
     total_ref[...] = total
     low_ref[...] = total.astype(jnp.bfloat16)
-    halo_ref[...] = halo_rows(total)
+    halo_ref[...] = halo_rows(total).astype(jnp.bfloat16)
 
 
 def place_sums(sums, first, rank):
@@ -145,7 +141,11 @@
     gathered_ref, start_ref, zero_ref, one_ref, two_ref, values_ref, factors_ref,
     final_ref, misfit_ref,
 ):
-    total = jnp.sum(gathered_ref[...], axis=0)
+    total = gathered_ref[...]
+    while total.shape[0] > 1:
+        half = total.shape[0] // 2
+        total = total[:half] + total[half:]
+    total = total[0]
     lane = lax.broadcasted_iota(jnp.int32, total.shape, 1)
 
     def pick(number):
@@ -229,7 +229,7 @@
             out_specs=VMEM,
             scratch_shapes=lag_scratch,
             compiler_params=SMALL,
-        )(field, many, few, lag_weights, local)
+        )(field, few, many, lag_weights, local)
 
     def series_sum(scale, part, field):
         def moved(distance):
@@ -254,14 +254,8 @@
     def back(rows_here):
         return jnp.dot(rows_here, series_factors, preferred_element_type=jnp.float32)
 
-    low, halo = pl.pallas_call(
-        start_kernel,
-        out_shape=(low_shape, halo_shape),
-        in_specs=[VMEM],
-        out_specs=(VMEM,) * 2,
-        compiler_params=SMALL,
-    )(time_factors)
-    many, few = fetch(halo)
+    low = time_factors.astype(jnp.bfloat16)
+    many, few = fetch(time_factors)
     kept = jnp.where(seen, series_values, jnp.zeros((), jnp.bfloat16))
     local = back(kept) - back(fit(low).astype(jnp.bfloat16))
     part = penalty(-penalty_weight, time_factors, many, few, local)

time: 128 us -> 125 us (0.977)
  waiting for transfers between devices: 11 us -> 8.31 us
    ppermute x9, waiting for transfers between devices: 11 us -> 8.29 us  [moved(): return lax.ppermute(part, 'series', pairs)]
    ppermute x9, starting transfers between devices: 10.4 us -> 11.8 us  [moved(): return lax.ppermute(part, 'series', pairs)]
  transfers between devices with their start and end apart: 16 -> 16, of which waited for: 7 -> 8; matrix products, arithmetic and copies ran while one was open for 6% -> 6% of each run, Pallas kernels for 0% -> 0%
where the time goes in v10:
time: 125 us
  blocking collectives  66.6 us (53%)
  starting transfers between devices  37.7 us (30%)
  waiting for transfers between devices  8.31 us (7%)
  matrix products  6.15 us (5%)
  Pallas kernels  2.26 us (2%)
  other arithmetic  1.86 us (1%)
    all_to_all x1, blocking collectives, on_device(): lax.all_to_all(spread, both, split_axis=0, concat_axis=0, tiled=True)  34.1 us
    all_to_all x1, blocking collectives, on_device(): lax.all_to_all(misfit, 'tm', split_axis=0, concat_axis=0, tiled=True)  32.4 us
    ppermute x3, starting transfers between devices, fetch(): lax.ppermute(halo, both, many_route)  17 us
    ppermute x9, starting transfers between devices, moved(): return lax.ppermute(part, 'series', pairs)  11.8 us
    ppermute x9, waiting for transfers between devices, moved(): return lax.ppermute(part, 'series', pairs)  8.29 us
    ppermute x1, starting transfers between devices, on_device(): many = lax.ppermute(halo, both, last_route)  6.87 us
    dot_general x4, matrix products, back(): jnp.dot(rows_here, series_factors, preferred_element_type=jnp.float32)  5.29 us
  transfers between devices with their start and end apart: 16, of which 8 were waited for; matrix products, arithmetic and copies ran while one was open for 6% of the time, Pallas kernels for 0%

profile of v10, /device:TPU:1, one launch (start us, length us, event | category | flops | bytes accessed | tf_op | source)
XLA Modules:
  0.0 124.7 jit_solution(16279240341218000761)
XLA Ops:
  0.6 0.0 copy-start
  0.6 6.3 %collective-permute-start.1 = (f32[64,128]{1,0:T(8,128)}, f32[64,128]{1,0:T(8,128)S(1)}, u32[]{:S(2)}, u32[]{:S(2)}) collective-permute-start(f32[64,128]{1,0:T(8,128)} %start_ref.1), channel_id=1, source_target_pairs={{0,12},{4,16},{8,20},{12,24},{16,28},{20,32},{24,36},{28,40},{32,4... | collective-permute-start | bytes 98312 | tf_op jit(solution)/shard_map/ppermute | solution.py:222
  7.0 0.7 collective-permute-start
  7.7 1.9 %broadcast_compare_fusion = pred[64,8192]{1,0:T(32,128)(4,1)S(1)} fusion(s32[64,8192]{1,0:T(8,128)} %param.6), kind=kLoop, calls=%fused_computation.18 | loop fusion | flops 524288 | bytes 2621440 | tf_op jit(solution)/shard_map/eq | solution.py:249
  9.5 0.0 copy-done
  9.5 0.0 copy-start.2
  9.6 1.8 %fusion.12 = f32[64,128]{1,0:T(8,128)S(1)} fusion(bf16[8192,128]{1,0:T(8,128)(2,1)S(1)} %copy-done, pred[64,8192]{1,0:T(32,128)(4,1)S(1)} %broadcast_compare_fusion, bf16[64,8192]{1,0:T(8,128)(2,1)} %values_ref.1), kind=kOutput, calls=%fused_computation.16 | convolution fusion | flops 134742016 | bytes 3702784 | tf_op jit(solution)/shard_map/dot_general | solution.py:255
  11.4 0.0 copy-done.2
  11.4 0.0 copy-start.3
  11.4 1.2 fusion.8.local_ref
  12.6 0.0 collective-permute-done.1.many_ref
  12.6 0.0 collective-permute-done.few_ref
  12.6 0.0 copy-done.3
  12.6 0.2 shard_map.68.own_ref
  12.8 2.9 %collective-permute-start.4 = (f32[64,128]{1,0:T(8,128)S(1)}, f32[64,128]{1,0:T(8,128)S(1)}, u32[]{:S(2)}, u32[]{:S(2)}) collective-permute-start(f32[64,128]{1,0:T(8,128)S(1)} %shard_map.68.own_ref), channel_id=1, source_target_pairs={{0,2},{1,3},{2,0},{3,1},{4,6},{5,7},{6,4},{7,5},{8,10},{9,11},{10,... | collective-permute-start | bytes 98312 | tf_op jit(solution)/shard_map/ppermute | solution.py:237
  15.7 0.0 collective-permute-start.3
  15.7 1.5 %collective-permute-start.2 = (f32[64,128]{1,0:T(8,128)S(1)}, f32[64,128]{1,0:T(8,128)S(1)}, u32[]{:S(2)}, u32[]{:S(2)}) collective-permute-start(f32[64,128]{1,0:T(8,128)S(1)} %shard_map.68.own_ref), channel_id=1, source_target_pairs={{0,1},{1,2},{2,3},{3,0},{4,5},{5,6},{6,7},{7,4},{8,9},{9,10},{10,1... | collective-permute-start | bytes 98312 | tf_op jit(solution)/shard_map/ppermute | solution.py:237
  17.1 0.0 collective-permute-done.4.second_ref
  17.2 1.8 %collective-permute-done.3.third_ref = f32[64,128]{1,0:T(8,128)S(1)} collective-permute-done((f32[64,128]{1,0:T(8,128)S(1)}, f32[64,128]{1,0:T(8,128)S(1)}, u32[]{:S(2)}, u32[]{:S(2)}) %collective-permute-start.3) | collective-permute-done | bytes 32800 | tf_op jit(solution)/shard_map/ppermute | solution.py:237
  19.0 1.2 collective-permute-done.2.first_ref
  20.2 5.3 %collective-permute-start.6 = (bf16[48,128]{1,0:T(8,128)(2,1)S(1)}, bf16[48,128]{1,0:T(8,128)(2,1)S(1)}, u32[]{:S(2)}, u32[]{:S(2)}) collective-permute-start(bf16[48,128]{1,0:T(8,128)(2,1)S(1)} %get-tuple-element.14), channel_id=1, source_target_pairs={{0,12},{4,16},{8,20},{12,24},{16,28},{20,32},{24,36},{28,40},{32,4... | collective-permute-start | bytes 36872 | tf_op jit(solution)/shard_map/ppermute | solution.py:222
  25.5 0.7 collective-permute-start.5
  26.2 1.2 fusion.6.local_ref
  27.4 0.0 collective-permute-done.6.many_ref
  27.4 0.0 collective-permute-done.5.few_ref
  27.4 0.2 shard_map.70.own_ref
  27.6 2.3 %collective-permute-start.9 = (f32[64,128]{1,0:T(8,128)S(1)}, f32[64,128]{1,0:T(8,128)S(1)}, u32[]{:S(2)}, u32[]{:S(2)}) collective-permute-start(f32[64,128]{1,0:T(8,128)S(1)} %shard_map.70.own_ref), channel_id=1, source_target_pairs={{0,2},{1,3},{2,0},{3,1},{4,6},{5,7},{6,4},{7,5},{8,10},{9,11},{10,... | collective-permute-start | bytes 98312 | tf_op jit(solution)/shard_map/ppermute | solution.py:237
  29.9 0.2 collective-permute-start.8
  30.1 1.2 collective-permute-start.7
  31.4 0.7 collective-permute-done.9.second_ref
  32.0 0.6 collective-permute-done.8.third_ref
  32.7 1.4 %collective-permute-done.7.first_ref = f32[64,128]{1,0:T(8,128)S(1)} collective-permute-done((f32[64,128]{1,0:T(8,128)S(1)}, f32[64,128]{1,0:T(8,128)S(1)}, u32[]{:S(2)}, u32[]{:S(2)}) %collective-permute-start.7) | collective-permute-done | bytes 32800 | tf_op jit(solution)/shard_map/ppermute | solution.py:237
  34.1 5.3 %collective-permute-start.11 = (bf16[48,128]{1,0:T(8,128)(2,1)S(1)}, bf16[48,128]{1,0:T(8,128)(2,1)S(1)}, u32[]{:S(2)}, u32[]{:S(2)}) collective-permute-start(bf16[48,128]{1,0:T(8,128)(2,1)S(1)} %get-tuple-element.17), channel_id=1, source_target_pairs={{0,12},{4,16},{8,20},{12,24},{16,28},{20,32},{24,36},{28,40},{32,4... | collective-permute-start | bytes 36872 | tf_op jit(solution)/shard_map/ppermute | solution.py:222
  39.5 0.7 collective-permute-start.10
  40.1 1.2 fusion.5.local_ref
  41.3 0.0 copy-start.1
  41.3 0.0 collective-permute-done.11.many_ref
  41.3 0.0 collective-permute-done.10.few_ref
  41.4 0.2 shard_map.72.own_ref
  41.6 2.3 %collective-permute-start.14 = (f32[64,128]{1,0:T(8,128)S(1)}, f32[64,128]{1,0:T(8,128)S(1)}, u32[]{:S(2)}, u32[]{:S(2)}) collective-permute-start(f32[64,128]{1,0:T(8,128)S(1)} %shard_map.72.own_ref), channel_id=1, source_target_pairs={{0,2},{1,3},{2,0},{3,1},{4,6},{5,7},{6,4},{7,5},{8,10},{9,11},{10,... | collective-permute-start | bytes 98312 | tf_op jit(solution)/shard_map/ppermute | solution.py:237
  43.9 0.0 collective-permute-start.13
  43.9 1.5 %collective-permute-start.12 = (f32[64,128]{1,0:T(8,128)S(1)}, f32[64,128]{1,0:T(8,128)S(1)}, u32[]{:S(2)}, u32[]{:S(2)}) collective-permute-start(f32[64,128]{1,0:T(8,128)S(1)} %shard_map.72.own_ref), channel_id=1, source_target_pairs={{0,1},{1,2},{2,3},{3,0},{4,5},{5,6},{6,7},{7,4},{8,9},{9,10},{10,1... | collective-permute-start | bytes 98312 | tf_op jit(solution)/shard_map/ppermute | solution.py:237
  45.3 0.6 collective-permute-done.14.second_ref
  45.9 0.7 collective-permute-done.13.third_ref
  46.6 1.2 collective-permute-done.12.first_ref
  47.9 6.9 %collective-permute-start.15 = (bf16[48,128]{1,0:T(8,128)(2,1)S(1)}, bf16[48,128]{1,0:T(8,128)(2,1)S(1)}, u32[]{:S(2)}, u32[]{:S(2)}) collective-permute-start(bf16[48,128]{1,0:T(8,128)(2,1)S(1)} %get-tuple-element.21), channel_id=1, source_target_pairs={{0,12},{4,16},{8,20},{12,24},{16,28},{20,32},{24,36},{28,40},{32,4... | collective-permute-start | bytes 36872 | tf_op jit(solution)/shard_map/ppermute | solution.py:272
  54.8 0.9 fusion.4
  55.6 0.2 shard_map.74.packed_ref
  55.8 0.0 collective-permute-done.15.many_ref
  55.8 0.4 shard_map.75
  56.2 34.1 %all_to_all.10.gathered_ref = f32[256,1,128]{2,1,0:T(1,128)S(1)} all-to-all(f32[256,1,128]{2,1,0:T(1,128)S(1)} %shard_map.75), channel_id=1, replica_groups=mesh['tm'=64,'series'=4] {'tm','series'}, dimensions={0} | all-to-all | bytes 262144 | tf_op jit(solution)/shard_map/all_to_all | solution.py:290
  90.3 0.0 copy-done.1
  90.3 1.0 shard_map.76
  91.3 32.4 %all_to_all.11 = bf16[64,64,128]{2,1,0:T(8,128)(2,1)S(1)} all-to-all(bf16[64,64,128]{2,1,0:T(8,128)(2,1)S(1)} %get-tuple-element.23), channel_id=1, replica_groups=mesh['tm'=64,'series'=4] {'tm'}, dimensions={0} | all-to-all | bytes 2097152 | tf_op jit(solution)/shard_map/all_to_all | solution.py:298
  123.8 1.0 copy.14
  (3 shorter events, 0.0 us)
Async XLA Ops:
  0.6 8.9 %copy-start = (bf16[8192,128]{1,0:T(8,128)(2,1)S(1)}, bf16[8192,128]{1,0:T(8,128)(2,1)}, u32[]{:S(2)}) copy-start(bf16[8192,128]{1,0:T(8,128)(2,1)} %factors_ref.1) | copy-start | bytes 6291460
  0.6 11.9 %collective-permute-start.1 = (f32[64,128]{1,0:T(8,128)}, f32[64,128]{1,0:T(8,128)S(1)}, u32[]{:S(2)}, u32[]{:S(2)}) collective-permute-start(f32[64,128]{1,0:T(8,128)} %start_ref.1), channel_id=1, source_target_pairs={{0,12},{4,16},{8,20},{12,24},{16,28},{20,32},{24,36},{28,40},{32,4... | collective-permute-start | bytes 98312 | tf_op jit(solution)/shard_map/ppermute | solution.py:222
  7.0 5.6 %collective-permute-start = (f32[64,128]{1,0:T(8,128)}, f32[64,128]{1,0:T(8,128)S(1)}, u32[]{:S(2)}, u32[]{:S(2)}) collective-permute-start(f32[64,128]{1,0:T(8,128)} %start_ref.1), channel_id=1, source_target_pairs={{6,2},{10,6},{14,10},{18,14},{22,18},{26,22},{30,26},{34,30},{38,3... | collective-permute-start | bytes 98312 | tf_op jit(solution)/shard_map/ppermute | solution.py:222
  9.5 1.8 %copy-start.2 = (f32[64,128]{1,0:T(8,128)S(1)}, f32[64,128]{1,0:T(8,128)}, u32[]{:S(2)}) copy-start(f32[64,128]{1,0:T(8,128)} %start_ref.1) | copy-start | bytes 98308
  11.4 1.2 copy-start.3
  12.8 4.4 %collective-permute-start.4 = (f32[64,128]{1,0:T(8,128)S(1)}, f32[64,128]{1,0:T(8,128)S(1)}, u32[]{:S(2)}, u32[]{:S(2)}) collective-permute-start(f32[64,128]{1,0:T(8,128)S(1)} %shard_map.68.own_ref), channel_id=1, source_target_pairs={{0,2},{1,3},{2,0},{3,1},{4,6},{5,7},{6,4},{7,5},{8,10},{9,11},{10,... | collective-permute-start | bytes 98312 | tf_op jit(solution)/shard_map/ppermute | solution.py:237
  15.7 3.3 %collective-permute-start.3 = (f32[64,128]{1,0:T(8,128)S(1)}, f32[64,128]{1,0:T(8,128)S(1)}, u32[]{:S(2)}, u32[]{:S(2)}) collective-permute-start(f32[64,128]{1,0:T(8,128)S(1)} %shard_map.68.own_ref), channel_id=1, source_target_pairs={{0,3},{1,0},{2,1},{3,2},{4,7},{5,4},{6,5},{7,6},{8,11},{9,8},{10,9... | collective-permute-start | bytes 98312 | tf_op jit(solution)/shard_map/ppermute | solution.py:237
  15.7 4.5 %collective-permute-start.2 = (f32[64,128]{1,0:T(8,128)S(1)}, f32[64,128]{1,0:T(8,128)S(1)}, u32[]{:S(2)}, u32[]{:S(2)}) collective-permute-start(f32[64,128]{1,0:T(8,128)S(1)} %shard_map.68.own_ref), channel_id=1, source_target_pairs={{0,1},{1,2},{2,3},{3,0},{4,5},{5,6},{6,7},{7,4},{8,9},{9,10},{10,1... | collective-permute-start | bytes 98312 | tf_op jit(solution)/shard_map/ppermute | solution.py:237
  20.2 7.2 %collective-permute-start.6 = (bf16[48,128]{1,0:T(8,128)(2,1)S(1)}, bf16[48,128]{1,0:T(8,128)(2,1)S(1)}, u32[]{:S(2)}, u32[]{:S(2)}) collective-permute-start(bf16[48,128]{1,0:T(8,128)(2,1)S(1)} %get-tuple-element.14), channel_id=1, source_target_pairs={{0,12},{4,16},{8,20},{12,24},{16,28},{20,32},{24,36},{28,40},{32,4... | collective-permute-start | bytes 36872 | tf_op jit(solution)/shard_map/ppermute | solution.py:222
  25.5 1.9 %collective-permute-start.5 = (bf16[48,128]{1,0:T(8,128)(2,1)S(1)}, bf16[48,128]{1,0:T(8,128)(2,1)S(1)}, u32[]{:S(2)}, u32[]{:S(2)}) collective-permute-start(bf16[48,128]{1,0:T(8,128)(2,1)S(1)} %get-tuple-element.14), channel_id=1, source_target_pairs={{6,2},{10,6},{14,10},{18,14},{22,18},{26,22},{30,26},{34,30},{38,3... | collective-permute-start | bytes 36872 | tf_op jit(solution)/shard_map/ppermute | solution.py:222
  27.6 4.4 %collective-permute-start.9 = (f32[64,128]{1,0:T(8,128)S(1)}, f32[64,128]{1,0:T(8,128)S(1)}, u32[]{:S(2)}, u32[]{:S(2)}) collective-permute-start(f32[64,128]{1,0:T(8,128)S(1)} %shard_map.70.own_ref), channel_id=1, source_target_pairs={{0,2},{1,3},{2,0},{3,1},{4,6},{5,7},{6,4},{7,5},{8,10},{9,11},{10,... | collective-permute-start | bytes 98312 | tf_op jit(solution)/shard_map/ppermute | solution.py:237
  29.9 2.8 %collective-permute-start.8 = (f32[64,128]{1,0:T(8,128)S(1)}, f32[64,128]{1,0:T(8,128)S(1)}, u32[]{:S(2)}, u32[]{:S(2)}) collective-permute-start(f32[64,128]{1,0:T(8,128)S(1)} %shard_map.70.own_ref), channel_id=1, source_target_pairs={{0,3},{1,0},{2,1},{3,2},{4,7},{5,4},{6,5},{7,6},{8,11},{9,8},{10,9... | collective-permute-start | bytes 98312 | tf_op jit(solution)/shard_map/ppermute | solution.py:237
  30.1 4.0 %collective-permute-start.7 = (f32[64,128]{1,0:T(8,128)S(1)}, f32[64,128]{1,0:T(8,128)S(1)}, u32[]{:S(2)}, u32[]{:S(2)}) collective-permute-start(f32[64,128]{1,0:T(8,128)S(1)} %shard_map.70.own_ref), channel_id=1, source_target_pairs={{0,1},{1,2},{2,3},{3,0},{4,5},{5,6},{6,7},{7,4},{8,9},{9,10},{10,1... | collective-permute-start | bytes 98312 | tf_op jit(solution)/shard_map/ppermute | solution.py:237
  34.1 7.2 %collective-permute-start.11 = (bf16[48,128]{1,0:T(8,128)(2,1)S(1)}, bf16[48,128]{1,0:T(8,128)(2,1)S(1)}, u32[]{:S(2)}, u32[]{:S(2)}) collective-permute-start(bf16[48,128]{1,0:T(8,128)(2,1)S(1)} %get-tuple-element.17), channel_id=1, source_target_pairs={{0,12},{4,16},{8,20},{12,24},{16,28},{20,32},{24,36},{28,40},{32,4... | collective-permute-start | bytes 36872 | tf_op jit(solution)/shard_map/ppermute | solution.py:222
  39.5 1.9 %collective-permute-start.10 = (bf16[48,128]{1,0:T(8,128)(2,1)S(1)}, bf16[48,128]{1,0:T(8,128)(2,1)S(1)}, u32[]{:S(2)}, u32[]{:S(2)}) collective-permute-start(bf16[48,128]{1,0:T(8,128)(2,1)S(1)} %get-tuple-element.17), channel_id=1, source_target_pairs={{6,2},{10,6},{14,10},{18,14},{22,18},{26,22},{30,26},{34,30},{38,3... | collective-permute-start | bytes 36872 | tf_op jit(solution)/shard_map/ppermute | solution.py:222
  41.3 49.0 %copy-start.1 = (bf16[64,8192]{1,0:T(8,128)(2,1)S(1)}, bf16[64,8192]{1,0:T(8,128)(2,1)}, u32[]{:S(2)}) copy-start(bf16[64,8192]{1,0:T(8,128)(2,1)} %values_ref.1) | copy-start | bytes 3145732
  41.6 4.4 %collective-permute-start.14 = (f32[64,128]{1,0:T(8,128)S(1)}, f32[64,128]{1,0:T(8,128)S(1)}, u32[]{:S(2)}, u32[]{:S(2)}) collective-permute-start(f32[64,128]{1,0:T(8,128)S(1)} %shard_map.72.own_ref), channel_id=1, source_target_pairs={{0,2},{1,3},{2,0},{3,1},{4,6},{5,7},{6,4},{7,5},{8,10},{9,11},{10,... | collective-permute-start | bytes 98312 | tf_op jit(solution)/shard_map/ppermute | solution.py:237
  43.9 2.8 %collective-permute-start.13 = (f32[64,128]{1,0:T(8,128)S(1)}, f32[64,128]{1,0:T(8,128)S(1)}, u32[]{:S(2)}, u32[]{:S(2)}) collective-permute-start(f32[64,128]{1,0:T(8,128)S(1)} %shard_map.72.own_ref), channel_id=1, source_target_pairs={{0,3},{1,0},{2,1},{3,2},{4,7},{5,4},{6,5},{7,6},{8,11},{9,8},{10,9... | collective-permute-start | bytes 98312 | tf_op jit(solution)/shard_map/ppermute | solution.py:237
  43.9 4.0 %collective-permute-start.12 = (f32[64,128]{1,0:T(8,128)S(1)}, f32[64,128]{1,0:T(8,128)S(1)}, u32[]{:S(2)}, u32[]{:S(2)}) collective-permute-start(f32[64,128]{1,0:T(8,128)S(1)} %shard_map.72.own_ref), channel_id=1, source_target_pairs={{0,1},{1,2},{2,3},{3,0},{4,5},{5,6},{6,7},{7,4},{8,9},{9,10},{10,1... | collective-permute-start | bytes 98312 | tf_op jit(solution)/shard_map/ppermute | solution.py:237
  47.9 7.9 %collective-permute-start.15 = (bf16[48,128]{1,0:T(8,128)(2,1)S(1)}, bf16[48,128]{1,0:T(8,128)(2,1)S(1)}, u32[]{:S(2)}, u32[]{:S(2)}) collective-permute-start(bf16[48,128]{1,0:T(8,128)(2,1)S(1)} %get-tuple-element.21), channel_id=1, source_target_pairs={{0,12},{4,16},{8,20},{12,24},{16,28},{20,32},{24,36},{28,40},{32,4... | collective-permute-start | bytes 36872 | tf_op jit(solution)/shard_map/ppermute | solution.py:272

commit v11 on v8

--- a/solution.py
+++ b/solution.py
@@ -11,7 +11,6 @@
 SEASON = 168
 LAGS = list(range(1, SHORT + 1)) + [SEASON]
 MANY = 48
-FEW = 48
 EDGE = SEASON + 8
 data_weight = 2.0
 penalty_weight = 0.5
@@ -66,27 +65,26 @@
     )
     blocks = [
         (EDGE, jnp.where(here == 0, field_ref[...], 0.0)),
-        (many_at, many_ref[...].astype(jnp.float32)),
-        (jnp.where(here == 3, 240, 128), few_ref[...].astype(jnp.float32)),
+        (many_at, long_rows(here, many_ref[...].astype(jnp.float32))),
+        (jnp.where(here == 3, 240, 128), short_rows(here, few_ref[...].astype(jnp.float32))),
     ]
     product = lag_product(blocks, weights_ref, window, short, last_time)
     part_ref[...] = data_weight * local_ref[...] + scale * product
 
 
-def halo(here, field, many_ref, few_ref=None):
+def rows_for(late, field):
     rows = field.shape[0]
-    late = jnp.logical_or(here == 0, here == 3)
-    many = jnp.where(late, field[rows - MANY :], field[:MANY])
-    many_ref[...] = many.astype(many_ref.dtype)
-    if few_ref is not None:
-        few = jnp.where(here == 2, field[rows - FEW :], field[:FEW])
-        few_ref[...] = few.astype(few_ref.dtype)
-
-
-def start_kernel(field_ref, low_ref, many_ref, few_ref):
-    field = field_ref[...]
-    low_ref[...] = field.astype(jnp.bfloat16)
-    halo(lax.axis_index("series"), field, many_ref, few_ref)
+    if rows == MANY:
+        return field
+    return jnp.where(late, field[rows - MANY :], field[:MANY])
+
+
+def long_rows(here, field):
+    return rows_for(jnp.logical_or(here == 0, here == 3), field)
+
+
+def short_rows(here, field):
+    return rows_for(here == 2, field)
 
 
 def sum_kernel(
@@ -98,7 +96,9 @@
     total = total + scale * field_ref[...]
     total_ref[...] = total
     low_ref[...] = total.astype(jnp.bfloat16)
-    halo(here, total, *halo_refs)
+    halo_refs[0][...] = long_rows(here, total).astype(jnp.bfloat16)
+    if len(halo_refs) > 1:
+        halo_refs[1][...] = short_rows(here, total).astype(jnp.bfloat16)
 
 
 def place_sums(sums, first, rank):
@@ -150,7 +150,11 @@
     gathered_ref, start_ref, zero_ref, one_ref, two_ref, values_ref, factors_ref,
     final_ref, misfit_ref,
 ):
-    total = jnp.sum(gathered_ref[...], axis=0)
+    total = gathered_ref[...]
+    while total.shape[0] > 1:
+        half = total.shape[0] // 2
+        total = total[:half] + total[half:]
+    total = total[0]
     lane = lax.broadcasted_iota(jnp.int32, total.shape, 1)
 
     def pick(number):
@@ -201,7 +205,7 @@
     last_time = n_tm * rows
     field_shape = jax.ShapeDtypeStruct((rows, rank), jnp.float32)
     many_shape = jax.ShapeDtypeStruct((MANY, rank), jnp.bfloat16)
-    few_shape = jax.ShapeDtypeStruct((FEW, rank), jnp.bfloat16)
+    few_shape = jax.ShapeDtypeStruct((MANY, rank), jnp.bfloat16)
     halo_shapes = (many_shape, few_shape)
     low_shape = jax.ShapeDtypeStruct((rows, rank), jnp.bfloat16)
     lag_scratch = [
@@ -262,14 +266,8 @@
     def back(rows_here):
         return jnp.dot(rows_here, series_factors, preferred_element_type=jnp.float32)
 
-    low, many, few = pl.pallas_call(
-        start_kernel,
-        out_shape=(low_shape, many_shape, few_shape),
-        in_specs=[VMEM],
-        out_specs=(VMEM,) * 3,
-        compiler_params=SMALL,
-    )(time_factors)
-    many, few = fetch(many, few)
+    low = time_factors.astype(jnp.bfloat16)
+    many, few = fetch(time_factors, time_factors)
     kept = jnp.where(seen, series_values, jnp.zeros((), jnp.bfloat16))
     local = back(kept) - back(fit(low).astype(jnp.bfloat16))
     part = penalty(-penalty_weight, time_factors, many, few, local)

time: 124 us -> 123 us (level)
  no operation moved by 1% of the time
where the time goes in v11:
time: 123 us
  blocking collectives  62.5 us (51%)
  starting transfers between devices  39.1 us (32%)
  waiting for transfers between devices  9.2 us (7%)
  matrix products  6.1 us (5%)
  Pallas kernels  2.27 us (2%)
  other arithmetic  1.86 us (2%)
    all_to_all x1, blocking collectives, on_device(): lax.all_to_all(misfit, 'tm', split_axis=0, concat_axis=0, tiled=True)  32.4 us
    all_to_all x1, blocking collectives, on_device(): lax.all_to_all(spread, both, split_axis=0, concat_axis=0, tiled=True)  30.1 us
    ppermute x3, starting transfers between devices, fetch(): return (lax.ppermute(many, both, many_route), few)  16.9 us
    ppermute x9, starting transfers between devices, moved(): return lax.ppermute(part, 'series', pairs)  12.6 us
    ppermute x9, waiting for transfers between devices, moved(): return lax.ppermute(part, 'series', pairs)  9.18 us
    ppermute x1, starting transfers between devices, on_device(): many = lax.ppermute(many, both, last_route)  7.52 us
    dot_general x4, matrix products, back(): jnp.dot(rows_here, series_factors, preferred_element_type=jnp.float32)  5.24 us
  transfers between devices with their start and end apart: 16, of which 8 were waited for; matrix products, arithmetic and copies ran while one was open for 6% of the time, Pallas kernels for 0%

profile of v11, /device:TPU:1, one launch (start us, length us, event | category | flops | bytes accessed | tf_op | source)
XLA Modules:
  0.0 122.9 jit_solution(17030188434796715521)
XLA Ops:
  0.6 0.0 copy-start
  0.6 0.8 collective-permute-start.1
  1.4 6.2 %collective-permute-start = (f32[64,128]{1,0:T(8,128)}, f32[64,128]{1,0:T(8,128)S(1)}, u32[]{:S(2)}, u32[]{:S(2)}) collective-permute-start(f32[64,128]{1,0:T(8,128)} %start_ref.1), channel_id=1, source_target_pairs={{0,12},{4,16},{8,20},{12,24},{16,28},{20,32},{24,36},{28,40},{32,4... | collective-permute-start | bytes 98312 | tf_op jit(solution)/shard_map/ppermute | solution.py:234
  7.7 1.9 %broadcast_compare_fusion = pred[64,8192]{1,0:T(32,128)(4,1)S(1)} fusion(s32[64,8192]{1,0:T(8,128)} %param.6), kind=kLoop, calls=%fused_computation.18 | loop fusion | flops 524288 | bytes 2621440 | tf_op jit(solution)/shard_map/eq | solution.py:261
  9.5 0.0 copy-done
  9.5 0.0 copy-start.2
  9.6 1.8 %fusion.12 = f32[64,128]{1,0:T(8,128)S(1)} fusion(bf16[8192,128]{1,0:T(8,128)(2,1)S(1)} %copy-done, pred[64,8192]{1,0:T(32,128)(4,1)S(1)} %broadcast_compare_fusion, bf16[64,8192]{1,0:T(8,128)(2,1)} %values_ref.1), kind=kOutput, calls=%fused_computation.16 | convolution fusion | flops 134742016 | bytes 3702784 | tf_op jit(solution)/shard_map/dot_general | solution.py:267
  11.4 0.0 copy-done.2
  11.4 0.0 copy-start.3
  11.4 1.2 fusion.8.local_ref
  12.5 0.0 collective-permute-done.1.few_ref
  12.5 0.0 collective-permute-done.many_ref
  12.6 0.0 copy-done.3
  12.6 0.2 shard_map.68.own_ref
  12.8 3.8 %collective-permute-start.4 = (f32[64,128]{1,0:T(8,128)S(1)}, f32[64,128]{1,0:T(8,128)S(1)}, u32[]{:S(2)}, u32[]{:S(2)}) collective-permute-start(f32[64,128]{1,0:T(8,128)S(1)} %shard_map.68.own_ref), channel_id=1, source_target_pairs={{0,2},{1,3},{2,0},{3,1},{4,6},{5,7},{6,4},{7,5},{8,10},{9,11},{10,... | collective-permute-start | bytes 98312 | tf_op jit(solution)/shard_map/ppermute | solution.py:249
  16.5 0.0 collective-permute-start.3
  16.6 1.5 %collective-permute-start.2 = (f32[64,128]{1,0:T(8,128)S(1)}, f32[64,128]{1,0:T(8,128)S(1)}, u32[]{:S(2)}, u32[]{:S(2)}) collective-permute-start(f32[64,128]{1,0:T(8,128)S(1)} %shard_map.68.own_ref), channel_id=1, source_target_pairs={{0,1},{1,2},{2,3},{3,0},{4,5},{5,6},{6,7},{7,4},{8,9},{9,10},{10,1... | collective-permute-start | bytes 98312 | tf_op jit(solution)/shard_map/ppermute | solution.py:249
  18.0 0.0 collective-permute-done.4.second_ref
  18.0 1.6 %collective-permute-done.3.third_ref = f32[64,128]{1,0:T(8,128)S(1)} collective-permute-done((f32[64,128]{1,0:T(8,128)S(1)}, f32[64,128]{1,0:T(8,128)S(1)}, u32[]{:S(2)}, u32[]{:S(2)}) %collective-permute-start.3) | collective-permute-done | bytes 32800 | tf_op jit(solution)/shard_map/ppermute | solution.py:249
  19.7 1.2 collective-permute-done.2.first_ref
  20.9 4.8 %collective-permute-start.5 = (bf16[48,128]{1,0:T(8,128)(2,1)S(1)}, bf16[48,128]{1,0:T(8,128)(2,1)S(1)}, u32[]{:S(2)}, u32[]{:S(2)}) collective-permute-start(bf16[48,128]{1,0:T(8,128)(2,1)S(1)} %get-tuple-element.16), channel_id=1, source_target_pairs={{0,12},{4,16},{8,20},{12,24},{16,28},{20,32},{24,36},{28,40},{32,4... | collective-permute-start | bytes 36872 | tf_op jit(solution)/shard_map/ppermute | solution.py:234
  25.7 0.7 collective-permute-start.6
  26.4 1.1 fusion.6.local_ref
  27.5 0.0 collective-permute-done.5.many_ref
  27.6 0.0 collective-permute-done.6.few_ref
  27.6 0.2 shard_map.70.own_ref
  27.8 2.2 %collective-permute-start.9 = (f32[64,128]{1,0:T(8,128)S(1)}, f32[64,128]{1,0:T(8,128)S(1)}, u32[]{:S(2)}, u32[]{:S(2)}) collective-permute-start(f32[64,128]{1,0:T(8,128)S(1)} %shard_map.70.own_ref), channel_id=1, source_target_pairs={{0,2},{1,3},{2,0},{3,1},{4,6},{5,7},{6,4},{7,5},{8,10},{9,11},{10,... | collective-permute-start | bytes 98312 | tf_op jit(solution)/shard_map/ppermute | solution.py:249
  30.0 0.5 collective-permute-start.8
  30.5 0.9 collective-permute-start.7
  31.5 0.7 collective-permute-done.9.second_ref
  32.1 0.6 collective-permute-done.8.third_ref
  32.8 2.3 %collective-permute-done.7.first_ref = f32[64,128]{1,0:T(8,128)S(1)} collective-permute-done((f32[64,128]{1,0:T(8,128)S(1)}, f32[64,128]{1,0:T(8,128)S(1)}, u32[]{:S(2)}, u32[]{:S(2)}) %collective-permute-start.7) | collective-permute-done | bytes 32800 | tf_op jit(solution)/shard_map/ppermute | solution.py:249
  35.1 5.8 %collective-permute-start.10 = (bf16[48,128]{1,0:T(8,128)(2,1)S(1)}, bf16[48,128]{1,0:T(8,128)(2,1)S(1)}, u32[]{:S(2)}, u32[]{:S(2)}) collective-permute-start(bf16[48,128]{1,0:T(8,128)(2,1)S(1)} %get-tuple-element.20), channel_id=1, source_target_pairs={{0,12},{4,16},{8,20},{12,24},{16,28},{20,32},{24,36},{28,40},{32,4... | collective-permute-start | bytes 36872 | tf_op jit(solution)/shard_map/ppermute | solution.py:234
  41.0 0.7 collective-permute-start.11
  41.6 1.1 fusion.5.local_ref
  42.8 0.0 copy-start.1
  42.8 0.0 collective-permute-done.10.many_ref
  42.8 0.0 collective-permute-done.11.few_ref
  42.8 0.2 shard_map.72.own_ref
  43.1 2.3 %collective-permute-start.14 = (f32[64,128]{1,0:T(8,128)S(1)}, f32[64,128]{1,0:T(8,128)S(1)}, u32[]{:S(2)}, u32[]{:S(2)}) collective-permute-start(f32[64,128]{1,0:T(8,128)S(1)} %shard_map.72.own_ref), channel_id=1, source_target_pairs={{0,2},{1,3},{2,0},{3,1},{4,6},{5,7},{6,4},{7,5},{8,10},{9,11},{10,... | collective-permute-start | bytes 98312 | tf_op jit(solution)/shard_map/ppermute | solution.py:249
  45.3 0.2 collective-permute-start.13
  45.5 1.3 %collective-permute-start.12 = (f32[64,128]{1,0:T(8,128)S(1)}, f32[64,128]{1,0:T(8,128)S(1)}, u32[]{:S(2)}, u32[]{:S(2)}) collective-permute-start(f32[64,128]{1,0:T(8,128)S(1)} %shard_map.72.own_ref), channel_id=1, source_target_pairs={{0,1},{1,2},{2,3},{3,0},{4,5},{5,6},{6,7},{7,4},{8,9},{9,10},{10,1... | collective-permute-start | bytes 98312 | tf_op jit(solution)/shard_map/ppermute | solution.py:249
  46.8 0.6 collective-permute-done.14.second_ref
  47.4 0.7 collective-permute-done.13.third_ref
  48.1 1.4 %collective-permute-done.12.first_ref = f32[64,128]{1,0:T(8,128)S(1)} collective-permute-done((f32[64,128]{1,0:T(8,128)S(1)}, f32[64,128]{1,0:T(8,128)S(1)}, u32[]{:S(2)}, u32[]{:S(2)}) %collective-permute-start.12) | collective-permute-done | bytes 32800 | tf_op jit(solution)/shard_map/ppermute | solution.py:249
  49.5 7.5 %collective-permute-start.15 = (bf16[48,128]{1,0:T(8,128)(2,1)S(1)}, bf16[48,128]{1,0:T(8,128)(2,1)S(1)}, u32[]{:S(2)}, u32[]{:S(2)}) collective-permute-start(bf16[48,128]{1,0:T(8,128)(2,1)S(1)} %get-tuple-element.25), channel_id=1, source_target_pairs={{0,12},{4,16},{8,20},{12,24},{16,28},{20,32},{24,36},{28,40},{32,4... | collective-permute-start | bytes 36872 | tf_op jit(solution)/shard_map/ppermute | solution.py:284
  57.0 0.9 fusion.4
  57.9 0.2 shard_map.74.packed_ref
  58.0 0.0 collective-permute-done.15.many_ref
  58.0 0.4 shard_map.75
  58.4 30.1 %all_to_all.10.gathered_ref = f32[256,1,128]{2,1,0:T(1,128)S(1)} all-to-all(f32[256,1,128]{2,1,0:T(1,128)S(1)} %shard_map.75), channel_id=1, replica_groups=mesh['tm'=64,'series'=4] {'tm','series'}, dimensions={0} | all-to-all | bytes 262144 | tf_op jit(solution)/shard_map/all_to_all | solution.py:302
  88.5 0.0 copy-done.1
  88.5 1.0 shard_map.76
  89.5 32.4 %all_to_all.11 = bf16[64,64,128]{2,1,0:T(8,128)(2,1)S(1)} all-to-all(bf16[64,64,128]{2,1,0:T(8,128)(2,1)S(1)} %get-tuple-element.27), channel_id=1, replica_groups=mesh['tm'=64,'series'=4] {'tm'}, dimensions={0} | all-to-all | bytes 2097152 | tf_op jit(solution)/shard_map/all_to_all | solution.py:310
  121.9 1.0 copy.14
  (3 shorter events, 0.0 us)
Async XLA Ops:
  0.6 8.9 %copy-start = (bf16[8192,128]{1,0:T(8,128)(2,1)S(1)}, bf16[8192,128]{1,0:T(8,128)(2,1)}, u32[]{:S(2)}) copy-start(bf16[8192,128]{1,0:T(8,128)(2,1)} %factors_ref.1) | copy-start | bytes 6291460
  0.6 11.9 %collective-permute-start.1 = (f32[64,128]{1,0:T(8,128)}, f32[64,128]{1,0:T(8,128)S(1)}, u32[]{:S(2)}, u32[]{:S(2)}) collective-permute-start(f32[64,128]{1,0:T(8,128)} %start_ref.1), channel_id=1, source_target_pairs={{2,6},{6,10},{10,14},{14,18},{18,22},{22,26},{26,30},{30,34},{34,3... | collective-permute-start | bytes 98312 | tf_op jit(solution)/shard_map/ppermute | solution.py:233
  1.4 11.1 %collective-permute-start = (f32[64,128]{1,0:T(8,128)}, f32[64,128]{1,0:T(8,128)S(1)}, u32[]{:S(2)}, u32[]{:S(2)}) collective-permute-start(f32[64,128]{1,0:T(8,128)} %start_ref.1), channel_id=1, source_target_pairs={{0,12},{4,16},{8,20},{12,24},{16,28},{20,32},{24,36},{28,40},{32,4... | collective-permute-start | bytes 98312 | tf_op jit(solution)/shard_map/ppermute | solution.py:234
  9.5 1.8 %copy-start.2 = (f32[64,128]{1,0:T(8,128)S(1)}, f32[64,128]{1,0:T(8,128)}, u32[]{:S(2)}) copy-start(f32[64,128]{1,0:T(8,128)} %start_ref.1) | copy-start | bytes 98308
  11.4 1.2 copy-start.3
  12.8 5.2 %collective-permute-start.4 = (f32[64,128]{1,0:T(8,128)S(1)}, f32[64,128]{1,0:T(8,128)S(1)}, u32[]{:S(2)}, u32[]{:S(2)}) collective-permute-start(f32[64,128]{1,0:T(8,128)S(1)} %shard_map.68.own_ref), channel_id=1, source_target_pairs={{0,2},{1,3},{2,0},{3,1},{4,6},{5,7},{6,4},{7,5},{8,10},{9,11},{10,... | collective-permute-start | bytes 98312 | tf_op jit(solution)/shard_map/ppermute | solution.py:249
  16.5 3.1 %collective-permute-start.3 = (f32[64,128]{1,0:T(8,128)S(1)}, f32[64,128]{1,0:T(8,128)S(1)}, u32[]{:S(2)}, u32[]{:S(2)}) collective-permute-start(f32[64,128]{1,0:T(8,128)S(1)} %shard_map.68.own_ref), channel_id=1, source_target_pairs={{0,3},{1,0},{2,1},{3,2},{4,7},{5,4},{6,5},{7,6},{8,11},{9,8},{10,9... | collective-permute-start | bytes 98312 | tf_op jit(solution)/shard_map/ppermute | solution.py:249
  16.6 4.3 %collective-permute-start.2 = (f32[64,128]{1,0:T(8,128)S(1)}, f32[64,128]{1,0:T(8,128)S(1)}, u32[]{:S(2)}, u32[]{:S(2)}) collective-permute-start(f32[64,128]{1,0:T(8,128)S(1)} %shard_map.68.own_ref), channel_id=1, source_target_pairs={{0,1},{1,2},{2,3},{3,0},{4,5},{5,6},{6,7},{7,4},{8,9},{9,10},{10,1... | collective-permute-start | bytes 98312 | tf_op jit(solution)/shard_map/ppermute | solution.py:249
  20.9 6.6 %collective-permute-start.5 = (bf16[48,128]{1,0:T(8,128)(2,1)S(1)}, bf16[48,128]{1,0:T(8,128)(2,1)S(1)}, u32[]{:S(2)}, u32[]{:S(2)}) collective-permute-start(bf16[48,128]{1,0:T(8,128)(2,1)S(1)} %get-tuple-element.16), channel_id=1, source_target_pairs={{0,12},{4,16},{8,20},{12,24},{16,28},{20,32},{24,36},{28,40},{32,4... | collective-permute-start | bytes 36872 | tf_op jit(solution)/shard_map/ppermute | solution.py:234
  25.7 1.8 %collective-permute-start.6 = (bf16[48,128]{1,0:T(8,128)(2,1)S(1)}, bf16[48,128]{1,0:T(8,128)(2,1)S(1)}, u32[]{:S(2)}, u32[]{:S(2)}) collective-permute-start(bf16[48,128]{1,0:T(8,128)(2,1)S(1)} %get-tuple-element.17), channel_id=1, source_target_pairs={{2,6},{6,10},{10,14},{14,18},{18,22},{22,26},{26,30},{30,34},{34,3... | collective-permute-start | bytes 36872 | tf_op jit(solution)/shard_map/ppermute | solution.py:233
  27.8 4.4 %collective-permute-start.9 = (f32[64,128]{1,0:T(8,128)S(1)}, f32[64,128]{1,0:T(8,128)S(1)}, u32[]{:S(2)}, u32[]{:S(2)}) collective-permute-start(f32[64,128]{1,0:T(8,128)S(1)} %shard_map.70.own_ref), channel_id=1, source_target_pairs={{0,2},{1,3},{2,0},{3,1},{4,6},{5,7},{6,4},{7,5},{8,10},{9,11},{10,... | collective-permute-start | bytes 98312 | tf_op jit(solution)/shard_map/ppermute | solution.py:249
  30.0 2.8 %collective-permute-start.8 = (f32[64,128]{1,0:T(8,128)S(1)}, f32[64,128]{1,0:T(8,128)S(1)}, u32[]{:S(2)}, u32[]{:S(2)}) collective-permute-start(f32[64,128]{1,0:T(8,128)S(1)} %shard_map.70.own_ref), channel_id=1, source_target_pairs={{0,3},{1,0},{2,1},{3,2},{4,7},{5,4},{6,5},{7,6},{8,11},{9,8},{10,9... | collective-permute-start | bytes 98312 | tf_op jit(solution)/shard_map/ppermute | solution.py:249
  30.5 4.6 %collective-permute-start.7 = (f32[64,128]{1,0:T(8,128)S(1)}, f32[64,128]{1,0:T(8,128)S(1)}, u32[]{:S(2)}, u32[]{:S(2)}) collective-permute-start(f32[64,128]{1,0:T(8,128)S(1)} %shard_map.70.own_ref), channel_id=1, source_target_pairs={{0,1},{1,2},{2,3},{3,0},{4,5},{5,6},{6,7},{7,4},{8,9},{9,10},{10,1... | collective-permute-start | bytes 98312 | tf_op jit(solution)/shard_map/ppermute | solution.py:249
  35.1 7.7 %collective-permute-start.10 = (bf16[48,128]{1,0:T(8,128)(2,1)S(1)}, bf16[48,128]{1,0:T(8,128)(2,1)S(1)}, u32[]{:S(2)}, u32[]{:S(2)}) collective-permute-start(bf16[48,128]{1,0:T(8,128)(2,1)S(1)} %get-tuple-element.20), channel_id=1, source_target_pairs={{0,12},{4,16},{8,20},{12,24},{16,28},{20,32},{24,36},{28,40},{32,4... | collective-permute-start | bytes 36872 | tf_op jit(solution)/shard_map/ppermute | solution.py:234
  41.0 1.8 %collective-permute-start.11 = (bf16[48,128]{1,0:T(8,128)(2,1)S(1)}, bf16[48,128]{1,0:T(8,128)(2,1)S(1)}, u32[]{:S(2)}, u32[]{:S(2)}) collective-permute-start(bf16[48,128]{1,0:T(8,128)(2,1)S(1)} %get-tuple-element.21), channel_id=1, source_target_pairs={{2,6},{6,10},{10,14},{14,18},{18,22},{22,26},{26,30},{30,34},{34,3... | collective-permute-start | bytes 36872 | tf_op jit(solution)/shard_map/ppermute | solution.py:233
  42.8 45.7 %copy-start.1 = (bf16[64,8192]{1,0:T(8,128)(2,1)S(1)}, bf16[64,8192]{1,0:T(8,128)(2,1)}, u32[]{:S(2)}) copy-start(bf16[64,8192]{1,0:T(8,128)(2,1)} %values_ref.1) | copy-start | bytes 3145732
  43.1 4.4 %collective-permute-start.14 = (f32[64,128]{1,0:T(8,128)S(1)}, f32[64,128]{1,0:T(8,128)S(1)}, u32[]{:S(2)}, u32[]{:S(2)}) collective-permute-start(f32[64,128]{1,0:T(8,128)S(1)} %shard_map.72.own_ref), channel_id=1, source_target_pairs={{0,2},{1,3},{2,0},{3,1},{4,6},{5,7},{6,4},{7,5},{8,10},{9,11},{10,... | collective-permute-start | bytes 98312 | tf_op jit(solution)/shard_map/ppermute | solution.py:249
  45.3 2.8 %collective-permute-start.13 = (f32[64,128]{1,0:T(8,128)S(1)}, f32[64,128]{1,0:T(8,128)S(1)}, u32[]{:S(2)}, u32[]{:S(2)}) collective-permute-start(f32[64,128]{1,0:T(8,128)S(1)} %shard_map.72.own_ref), channel_id=1, source_target_pairs={{0,3},{1,0},{2,1},{3,2},{4,7},{5,4},{6,5},{7,6},{8,11},{9,8},{10,9... | collective-permute-start | bytes 98312 | tf_op jit(solution)/shard_map/ppermute | solution.py:249
  45.5 4.0 %collective-permute-start.12 = (f32[64,128]{1,0:T(8,128)S(1)}, f32[64,128]{1,0:T(8,128)S(1)}, u32[]{:S(2)}, u32[]{:S(2)}) collective-permute-start(f32[64,128]{1,0:T(8,128)S(1)} %shard_map.72.own_ref), channel_id=1, source_target_pairs={{0,1},{1,2},{2,3},{3,0},{4,5},{5,6},{6,7},{7,4},{8,9},{9,10},{10,1... | collective-permute-start | bytes 98312 | tf_op jit(solution)/shard_map/ppermute | solution.py:249
  49.5 8.6 %collective-permute-start.15 = (bf16[48,128]{1,0:T(8,128)(2,1)S(1)}, bf16[48,128]{1,0:T(8,128)(2,1)S(1)}, u32[]{:S(2)}, u32[]{:S(2)}) collective-permute-start(bf16[48,128]{1,0:T(8,128)(2,1)S(1)} %get-tuple-element.25), channel_id=1, source_target_pairs={{0,12},{4,16},{8,20},{12,24},{16,28},{20,32},{24,36},{28,40},{32,4... | collective-permute-start | bytes 36872 | tf_op jit(solution)/shard_map/ppermute | solution.py:284

commit v12 on v11

--- a/solution.py
+++ b/solution.py
@@ -135,10 +135,10 @@
 ):
     two = two_ref[...]
     here = lax.axis_index("series")
-    many_at = jnp.where(here == 0, 0, jnp.where(here == 2, 48, 128))
+    many_at = jnp.where(here == 1, 368, jnp.where(here == 2, 240, 320))
     blocks = [
-        (EDGE, jnp.where(here == 1, two, 0.0)),
-        (many_at, jnp.where(here == 1, 0.0, 2.0 * many_ref[...].astype(jnp.float32))),
+        (EDGE, jnp.where(here == 0, two, 0.0)),
+        (many_at, jnp.where(here == 0, 0.0, 2.0 * many_ref[...].astype(jnp.float32))),
     ]
     product = lag_product(blocks, weights_ref, window, short, last_time)
     quadratic = penalty_weight * inner(two, product)
@@ -226,7 +226,7 @@
 
     many_route = route([3, -3, 2, -2])
     few_route = route([None, None, 1, -1])
-    last_route = route([3, None, 2, 1])
+    last_route = route([None, -3, -1, -2])
     both = ("tm", "series")
 
     def fetch(many, few):

time: 123 us -> 122 us (level)
  starting transfers between devices: 39.1 us -> 32.3 us
  blocking collectives: 62.5 us -> 68.1 us
    ppermute x1, starting transfers between devices: 7.52 us -> 0.66 us  [on_device(): many = lax.ppermute(many, both, last_route)]
    all_to_all x1, blocking collectives: 30.1 us -> 35.6 us  [on_device(): lax.all_to_all(spread, both, split_axis=0, concat_axis=0, tiled=True)]
  transfers between devices with their start and end apart: 16 -> 16, of which waited for: 8 -> 8; matrix products, arithmetic and copies ran while one was open for 6% -> 7% of each run, Pallas kernels for 0% -> 0%
where the time goes in v12:
time: 122 us
  blocking collectives  68.1 us (56%)
  starting transfers between devices  32.3 us (26%)
  waiting for transfers between devices  9.2 us (8%)
  matrix products  6.1 us (5%)
  Pallas kernels  2.26 us (2%)
  other arithmetic  1.86 us (2%)
    all_to_all x1, blocking collectives, on_device(): lax.all_to_all(spread, both, split_axis=0, concat_axis=0, tiled=True)  35.6 us
    all_to_all x1, blocking collectives, on_device(): lax.all_to_all(misfit, 'tm', split_axis=0, concat_axis=0, tiled=True)  32.4 us
    ppermute x3, starting transfers between devices, fetch(): return (lax.ppermute(many, both, many_route), few)  16.9 us
    ppermute x9, starting transfers between devices, moved(): return lax.ppermute(part, 'series', pairs)  12.6 us
    ppermute x9, waiting for transfers between devices, moved(): return lax.ppermute(part, 'series', pairs)  9.18 us
    dot_general x4, matrix products, back(): jnp.dot(rows_here, series_factors, preferred_element_type=jnp.float32)  5.24 us
  transfers between devices with their start and end apart: 16, of which 8 were waited for; matrix products, arithmetic and copies ran while one was open for 7% of the time, Pallas kernels for 0%

profile of v12, /device:TPU:1, one launch (start us, length us, event | category | flops | bytes accessed | tf_op | source)
XLA Modules:
  0.0 121.6 jit_solution(11463062388018158846)
XLA Ops:
  0.6 0.0 copy-start
  0.6 0.8 collective-permute-start.1
  1.4 6.2 %collective-permute-start = (f32[64,128]{1,0:T(8,128)}, f32[64,128]{1,0:T(8,128)S(1)}, u32[]{:S(2)}, u32[]{:S(2)}) collective-permute-start(f32[64,128]{1,0:T(8,128)} %start_ref.1), channel_id=1, source_target_pairs={{0,12},{4,16},{8,20},{12,24},{16,28},{20,32},{24,36},{28,40},{32,4... | collective-permute-start | bytes 98312 | tf_op jit(solution)/shard_map/ppermute | solution.py:234
  7.7 1.9 %broadcast_compare_fusion = pred[64,8192]{1,0:T(32,128)(4,1)S(1)} fusion(s32[64,8192]{1,0:T(8,128)} %param.6), kind=kLoop, calls=%fused_computation.18 | loop fusion | flops 524288 | bytes 2621440 | tf_op jit(solution)/shard_map/eq | solution.py:261
  9.5 0.0 copy-done
  9.5 0.0 copy-start.2
  9.6 1.8 %fusion.12 = f32[64,128]{1,0:T(8,128)S(1)} fusion(bf16[8192,128]{1,0:T(8,128)(2,1)S(1)} %copy-done, pred[64,8192]{1,0:T(32,128)(4,1)S(1)} %broadcast_compare_fusion, bf16[64,8192]{1,0:T(8,128)(2,1)} %values_ref.1), kind=kOutput, calls=%fused_computation.16 | convolution fusion | flops 134742016 | bytes 3702784 | tf_op jit(solution)/shard_map/dot_general | solution.py:267
  11.4 0.0 copy-done.2
  11.4 0.0 copy-start.3
  11.4 1.2 fusion.8.local_ref
  12.5 0.0 collective-permute-done.1.few_ref
  12.5 0.0 collective-permute-done.many_ref
  12.6 0.0 copy-done.3
  12.6 0.2 shard_map.68.own_ref
  12.8 3.8 %collective-permute-start.4 = (f32[64,128]{1,0:T(8,128)S(1)}, f32[64,128]{1,0:T(8,128)S(1)}, u32[]{:S(2)}, u32[]{:S(2)}) collective-permute-start(f32[64,128]{1,0:T(8,128)S(1)} %shard_map.68.own_ref), channel_id=1, source_target_pairs={{0,2},{1,3},{2,0},{3,1},{4,6},{5,7},{6,4},{7,5},{8,10},{9,11},{10,... | collective-permute-start | bytes 98312 | tf_op jit(solution)/shard_map/ppermute | solution.py:249
  16.5 0.0 collective-permute-start.3
  16.6 1.5 %collective-permute-start.2 = (f32[64,128]{1,0:T(8,128)S(1)}, f32[64,128]{1,0:T(8,128)S(1)}, u32[]{:S(2)}, u32[]{:S(2)}) collective-permute-start(f32[64,128]{1,0:T(8,128)S(1)} %shard_map.68.own_ref), channel_id=1, source_target_pairs={{0,1},{1,2},{2,3},{3,0},{4,5},{5,6},{6,7},{7,4},{8,9},{9,10},{10,1... | collective-permute-start | bytes 98312 | tf_op jit(solution)/shard_map/ppermute | solution.py:249
  18.0 0.0 collective-permute-done.4.second_ref
  18.0 1.6 %collective-permute-done.3.third_ref = f32[64,128]{1,0:T(8,128)S(1)} collective-permute-done((f32[64,128]{1,0:T(8,128)S(1)}, f32[64,128]{1,0:T(8,128)S(1)}, u32[]{:S(2)}, u32[]{:S(2)}) %collective-permute-start.3) | collective-permute-done | bytes 32800 | tf_op jit(solution)/shard_map/ppermute | solution.py:249
  19.7 1.2 collective-permute-done.2.first_ref
  20.9 4.8 %collective-permute-start.5 = (bf16[48,128]{1,0:T(8,128)(2,1)S(1)}, bf16[48,128]{1,0:T(8,128)(2,1)S(1)}, u32[]{:S(2)}, u32[]{:S(2)}) collective-permute-start(bf16[48,128]{1,0:T(8,128)(2,1)S(1)} %get-tuple-element.16), channel_id=1, source_target_pairs={{0,12},{4,16},{8,20},{12,24},{16,28},{20,32},{24,36},{28,40},{32,4... | collective-permute-start | bytes 36872 | tf_op jit(solution)/shard_map/ppermute | solution.py:234
  25.7 0.7 collective-permute-start.6
  26.4 1.1 fusion.6.local_ref
  27.5 0.0 collective-permute-done.5.many_ref
  27.6 0.0 collective-permute-done.6.few_ref
  27.6 0.2 shard_map.70.own_ref
  27.8 2.2 %collective-permute-start.9 = (f32[64,128]{1,0:T(8,128)S(1)}, f32[64,128]{1,0:T(8,128)S(1)}, u32[]{:S(2)}, u32[]{:S(2)}) collective-permute-start(f32[64,128]{1,0:T(8,128)S(1)} %shard_map.70.own_ref), channel_id=1, source_target_pairs={{0,2},{1,3},{2,0},{3,1},{4,6},{5,7},{6,4},{7,5},{8,10},{9,11},{10,... | collective-permute-start | bytes 98312 | tf_op jit(solution)/shard_map/ppermute | solution.py:249
  30.0 0.5 collective-permute-start.8
  30.5 0.9 collective-permute-start.7
  31.5 0.7 collective-permute-done.9.second_ref
  32.1 0.6 collective-permute-done.8.third_ref
  32.8 2.3 %collective-permute-done.7.first_ref = f32[64,128]{1,0:T(8,128)S(1)} collective-permute-done((f32[64,128]{1,0:T(8,128)S(1)}, f32[64,128]{1,0:T(8,128)S(1)}, u32[]{:S(2)}, u32[]{:S(2)}) %collective-permute-start.7) | collective-permute-done | bytes 32800 | tf_op jit(solution)/shard_map/ppermute | solution.py:249
  35.1 5.8 %collective-permute-start.10 = (bf16[48,128]{1,0:T(8,128)(2,1)S(1)}, bf16[48,128]{1,0:T(8,128)(2,1)S(1)}, u32[]{:S(2)}, u32[]{:S(2)}) collective-permute-start(bf16[48,128]{1,0:T(8,128)(2,1)S(1)} %get-tuple-element.20), channel_id=1, source_target_pairs={{0,12},{4,16},{8,20},{12,24},{16,28},{20,32},{24,36},{28,40},{32,4... | collective-permute-start | bytes 36872 | tf_op jit(solution)/shard_map/ppermute | solution.py:234
  41.0 0.7 collective-permute-start.11
  41.6 1.1 fusion.5.local_ref
  42.8 0.0 copy-start.1
  42.8 0.0 collective-permute-done.10.many_ref
  42.8 0.0 collective-permute-done.11.few_ref
  42.8 0.2 shard_map.72.own_ref
  43.1 2.3 %collective-permute-start.14 = (f32[64,128]{1,0:T(8,128)S(1)}, f32[64,128]{1,0:T(8,128)S(1)}, u32[]{:S(2)}, u32[]{:S(2)}) collective-permute-start(f32[64,128]{1,0:T(8,128)S(1)} %shard_map.72.own_ref), channel_id=1, source_target_pairs={{0,2},{1,3},{2,0},{3,1},{4,6},{5,7},{6,4},{7,5},{8,10},{9,11},{10,... | collective-permute-start | bytes 98312 | tf_op jit(solution)/shard_map/ppermute | solution.py:249
  45.3 0.2 collective-permute-start.13
  45.5 1.3 %collective-permute-start.12 = (f32[64,128]{1,0:T(8,128)S(1)}, f32[64,128]{1,0:T(8,128)S(1)}, u32[]{:S(2)}, u32[]{:S(2)}) collective-permute-start(f32[64,128]{1,0:T(8,128)S(1)} %shard_map.72.own_ref), channel_id=1, source_target_pairs={{0,1},{1,2},{2,3},{3,0},{4,5},{5,6},{6,7},{7,4},{8,9},{9,10},{10,1... | collective-permute-start | bytes 98312 | tf_op jit(solution)/shard_map/ppermute | solution.py:249
  46.8 0.6 collective-permute-done.14.second_ref
  47.4 0.7 collective-permute-done.13.third_ref
  48.1 1.4 %collective-permute-done.12.first_ref = f32[64,128]{1,0:T(8,128)S(1)} collective-permute-done((f32[64,128]{1,0:T(8,128)S(1)}, f32[64,128]{1,0:T(8,128)S(1)}, u32[]{:S(2)}, u32[]{:S(2)}) %collective-permute-start.12) | collective-permute-done | bytes 32800 | tf_op jit(solution)/shard_map/ppermute | solution.py:249
  49.5 0.7 collective-permute-start.15
  50.2 0.9 fusion.4
  51.0 0.2 shard_map.74.packed_ref
  51.2 0.0 collective-permute-done.15.many_ref
  51.2 0.4 shard_map.75
  51.6 35.6 %all_to_all.10.gathered_ref = f32[256,1,128]{2,1,0:T(1,128)S(1)} all-to-all(f32[256,1,128]{2,1,0:T(1,128)S(1)} %shard_map.75), channel_id=1, replica_groups=mesh['tm'=64,'series'=4] {'tm','series'}, dimensions={0} | all-to-all | bytes 262144 | tf_op jit(solution)/shard_map/all_to_all | solution.py:302
  87.2 0.0 copy-done.1
  87.2 1.0 shard_map.76
  88.2 32.4 %all_to_all.11 = bf16[64,64,128]{2,1,0:T(8,128)(2,1)S(1)} all-to-all(bf16[64,64,128]{2,1,0:T(8,128)(2,1)S(1)} %get-tuple-element.27), channel_id=1, replica_groups=mesh['tm'=64,'series'=4] {'tm'}, dimensions={0} | all-to-all | bytes 2097152 | tf_op jit(solution)/shard_map/all_to_all | solution.py:310
  120.7 1.0 copy.14
  (3 shorter events, 0.0 us)
Async XLA Ops:
  0.6 8.9 %copy-start = (bf16[8192,128]{1,0:T(8,128)(2,1)S(1)}, bf16[8192,128]{1,0:T(8,128)(2,1)}, u32[]{:S(2)}) copy-start(bf16[8192,128]{1,0:T(8,128)(2,1)} %factors_ref.1) | copy-start | bytes 6291460
  0.6 11.9 %collective-permute-start.1 = (f32[64,128]{1,0:T(8,128)}, f32[64,128]{1,0:T(8,128)S(1)}, u32[]{:S(2)}, u32[]{:S(2)}) collective-permute-start(f32[64,128]{1,0:T(8,128)} %start_ref.1), channel_id=1, source_target_pairs={{2,6},{6,10},{10,14},{14,18},{18,22},{22,26},{26,30},{30,34},{34,3... | collective-permute-start | bytes 98312 | tf_op jit(solution)/shard_map/ppermute | solution.py:233
  1.4 11.1 %collective-permute-start = (f32[64,128]{1,0:T(8,128)}, f32[64,128]{1,0:T(8,128)S(1)}, u32[]{:S(2)}, u32[]{:S(2)}) collective-permute-start(f32[64,128]{1,0:T(8,128)} %start_ref.1), channel_id=1, source_target_pairs={{0,12},{4,16},{8,20},{12,24},{16,28},{20,32},{24,36},{28,40},{32,4... | collective-permute-start | bytes 98312 | tf_op jit(solution)/shard_map/ppermute | solution.py:234
  9.5 1.8 %copy-start.2 = (f32[64,128]{1,0:T(8,128)S(1)}, f32[64,128]{1,0:T(8,128)}, u32[]{:S(2)}) copy-start(f32[64,128]{1,0:T(8,128)} %start_ref.1) | copy-start | bytes 98308
  11.4 1.2 copy-start.3
  12.8 5.2 %collective-permute-start.4 = (f32[64,128]{1,0:T(8,128)S(1)}, f32[64,128]{1,0:T(8,128)S(1)}, u32[]{:S(2)}, u32[]{:S(2)}) collective-permute-start(f32[64,128]{1,0:T(8,128)S(1)} %shard_map.68.own_ref), channel_id=1, source_target_pairs={{0,2},{1,3},{2,0},{3,1},{4,6},{5,7},{6,4},{7,5},{8,10},{9,11},{10,... | collective-permute-start | bytes 98312 | tf_op jit(solution)/shard_map/ppermute | solution.py:249
  16.5 3.1 %collective-permute-start.3 = (f32[64,128]{1,0:T(8,128)S(1)}, f32[64,128]{1,0:T(8,128)S(1)}, u32[]{:S(2)}, u32[]{:S(2)}) collective-permute-start(f32[64,128]{1,0:T(8,128)S(1)} %shard_map.68.own_ref), channel_id=1, source_target_pairs={{0,3},{1,0},{2,1},{3,2},{4,7},{5,4},{6,5},{7,6},{8,11},{9,8},{10,9... | collective-permute-start | bytes 98312 | tf_op jit(solution)/shard_map/ppermute | solution.py:249
  16.6 4.3 %collective-permute-start.2 = (f32[64,128]{1,0:T(8,128)S(1)}, f32[64,128]{1,0:T(8,128)S(1)}, u32[]{:S(2)}, u32[]{:S(2)}) collective-permute-start(f32[64,128]{1,0:T(8,128)S(1)} %shard_map.68.own_ref), channel_id=1, source_target_pairs={{0,1},{1,2},{2,3},{3,0},{4,5},{5,6},{6,7},{7,4},{8,9},{9,10},{10,1... | collective-permute-start | bytes 98312 | tf_op jit(solution)/shard_map/ppermute | solution.py:249
  20.9 6.6 %collective-permute-start.5 = (bf16[48,128]{1,0:T(8,128)(2,1)S(1)}, bf16[48,128]{1,0:T(8,128)(2,1)S(1)}, u32[]{:S(2)}, u32[]{:S(2)}) collective-permute-start(bf16[48,128]{1,0:T(8,128)(2,1)S(1)} %get-tuple-element.16), channel_id=1, source_target_pairs={{0,12},{4,16},{8,20},{12,24},{16,28},{20,32},{24,36},{28,40},{32,4... | collective-permute-start | bytes 36872 | tf_op jit(solution)/shard_map/ppermute | solution.py:234
  25.7 1.8 %collective-permute-start.6 = (bf16[48,128]{1,0:T(8,128)(2,1)S(1)}, bf16[48,128]{1,0:T(8,128)(2,1)S(1)}, u32[]{:S(2)}, u32[]{:S(2)}) collective-permute-start(bf16[48,128]{1,0:T(8,128)(2,1)S(1)} %get-tuple-element.17), channel_id=1, source_target_pairs={{2,6},{6,10},{10,14},{14,18},{18,22},{22,26},{26,30},{30,34},{34,3... | collective-permute-start | bytes 36872 | tf_op jit(solution)/shard_map/ppermute | solution.py:233
  27.8 4.4 %collective-permute-start.9 = (f32[64,128]{1,0:T(8,128)S(1)}, f32[64,128]{1,0:T(8,128)S(1)}, u32[]{:S(2)}, u32[]{:S(2)}) collective-permute-start(f32[64,128]{1,0:T(8,128)S(1)} %shard_map.70.own_ref), channel_id=1, source_target_pairs={{0,2},{1,3},{2,0},{3,1},{4,6},{5,7},{6,4},{7,5},{8,10},{9,11},{10,... | collective-permute-start | bytes 98312 | tf_op jit(solution)/shard_map/ppermute | solution.py:249
  30.0 2.8 %collective-permute-start.8 = (f32[64,128]{1,0:T(8,128)S(1)}, f32[64,128]{1,0:T(8,128)S(1)}, u32[]{:S(2)}, u32[]{:S(2)}) collective-permute-start(f32[64,128]{1,0:T(8,128)S(1)} %shard_map.70.own_ref), channel_id=1, source_target_pairs={{0,3},{1,0},{2,1},{3,2},{4,7},{5,4},{6,5},{7,6},{8,11},{9,8},{10,9... | collective-permute-start | bytes 98312 | tf_op jit(solution)/shard_map/ppermute | solution.py:249
  30.5 4.6 %collective-permute-start.7 = (f32[64,128]{1,0:T(8,128)S(1)}, f32[64,128]{1,0:T(8,128)S(1)}, u32[]{:S(2)}, u32[]{:S(2)}) collective-permute-start(f32[64,128]{1,0:T(8,128)S(1)} %shard_map.70.own_ref), channel_id=1, source_target_pairs={{0,1},{1,2},{2,3},{3,0},{4,5},{5,6},{6,7},{7,4},{8,9},{9,10},{10,1... | collective-permute-start | bytes 98312 | tf_op jit(solution)/shard_map/ppermute | solution.py:249
  35.1 7.7 %collective-permute-start.10 = (bf16[48,128]{1,0:T(8,128)(2,1)S(1)}, bf16[48,128]{1,0:T(8,128)(2,1)S(1)}, u32[]{:S(2)}, u32[]{:S(2)}) collective-permute-start(bf16[48,128]{1,0:T(8,128)(2,1)S(1)} %get-tuple-element.20), channel_id=1, source_target_pairs={{0,12},{4,16},{8,20},{12,24},{16,28},{20,32},{24,36},{28,40},{32,4... | collective-permute-start | bytes 36872 | tf_op jit(solution)/shard_map/ppermute | solution.py:234
  41.0 1.8 %collective-permute-start.11 = (bf16[48,128]{1,0:T(8,128)(2,1)S(1)}, bf16[48,128]{1,0:T(8,128)(2,1)S(1)}, u32[]{:S(2)}, u32[]{:S(2)}) collective-permute-start(bf16[48,128]{1,0:T(8,128)(2,1)S(1)} %get-tuple-element.21), channel_id=1, source_target_pairs={{2,6},{6,10},{10,14},{14,18},{18,22},{22,26},{26,30},{30,34},{34,3... | collective-permute-start | bytes 36872 | tf_op jit(solution)/shard_map/ppermute | solution.py:233
  42.8 44.4 %copy-start.1 = (bf16[64,8192]{1,0:T(8,128)(2,1)S(1)}, bf16[64,8192]{1,0:T(8,128)(2,1)}, u32[]{:S(2)}) copy-start(bf16[64,8192]{1,0:T(8,128)(2,1)} %values_ref.1) | copy-start | bytes 3145732
  43.1 4.4 %collective-permute-start.14 = (f32[64,128]{1,0:T(8,128)S(1)}, f32[64,128]{1,0:T(8,128)S(1)}, u32[]{:S(2)}, u32[]{:S(2)}) collective-permute-start(f32[64,128]{1,0:T(8,128)S(1)} %shard_map.72.own_ref), channel_id=1, source_target_pairs={{0,2},{1,3},{2,0},{3,1},{4,6},{5,7},{6,4},{7,5},{8,10},{9,11},{10,... | collective-permute-start | bytes 98312 | tf_op jit(solution)/shard_map/ppermute | solution.py:249
  45.3 2.8 %collective-permute-start.13 = (f32[64,128]{1,0:T(8,128)S(1)}, f32[64,128]{1,0:T(8,128)S(1)}, u32[]{:S(2)}, u32[]{:S(2)}) collective-permute-start(f32[64,128]{1,0:T(8,128)S(1)} %shard_map.72.own_ref), channel_id=1, source_target_pairs={{0,3},{1,0},{2,1},{3,2},{4,7},{5,4},{6,5},{7,6},{8,11},{9,8},{10,9... | collective-permute-start | bytes 98312 | tf_op jit(solution)/shard_map/ppermute | solution.py:249
  45.5 4.0 %collective-permute-start.12 = (f32[64,128]{1,0:T(8,128)S(1)}, f32[64,128]{1,0:T(8,128)S(1)}, u32[]{:S(2)}, u32[]{:S(2)}) collective-permute-start(f32[64,128]{1,0:T(8,128)S(1)} %shard_map.72.own_ref), channel_id=1, source_target_pairs={{0,1},{1,2},{2,3},{3,0},{4,5},{5,6},{6,7},{7,4},{8,9},{9,10},{10,1... | collective-permute-start | bytes 98312 | tf_op jit(solution)/shard_map/ppermute | solution.py:249
  49.5 1.7 %collective-permute-start.15 = (bf16[48,128]{1,0:T(8,128)(2,1)S(1)}, bf16[48,128]{1,0:T(8,128)(2,1)S(1)}, u32[]{:S(2)}, u32[]{:S(2)}) collective-permute-start(bf16[48,128]{1,0:T(8,128)(2,1)S(1)} %get-tuple-element.25), channel_id=1, source_target_pairs={{13,1},{17,5},{21,9},{25,13},{29,17},{33,21},{37,25},{41,29},{45,3... | collective-permute-start | bytes 36872 | tf_op jit(solution)/shard_map/ppermute | solution.py:284

commit v13 on v12

--- a/solution.py
+++ b/solution.py
@@ -148,7 +148,7 @@
 
 def update_kernel(
     gathered_ref, start_ref, zero_ref, one_ref, two_ref, values_ref, factors_ref,
-    final_ref, misfit_ref,
+    steps_ref, misfit_ref,
 ):
     total = gathered_ref[...]
     while total.shape[0] > 1:
@@ -186,7 +186,8 @@
     k1 = alpha2 * d - alpha1 * alpha0
     k2 = alpha2 * b
     final = start_ref[...] + (k0 * zero_ref[...] + k1 * one_ref[...] + k2 * two_ref[...])
-    final_ref[...] = final
+    number = lax.broadcasted_iota(jnp.int32, steps_ref.shape, 0)
+    steps_ref[...] = jnp.where(number == 0, k0, jnp.where(number == 1, k1, k2))
     low = final.astype(jnp.bfloat16)
     lanes = misfit_ref.shape[2]
     for first in range(0, values_ref.shape[1], 2 * lanes):
@@ -195,6 +196,13 @@
         block = (values_ref[:, columns].astype(jnp.float32) - fitted).astype(jnp.bfloat16)
         misfit_ref[first // lanes] = block[:, :lanes]
         misfit_ref[first // lanes + 1] = block[:, lanes:]
+
+
+def final_kernel(steps_ref, start_ref, zero_ref, one_ref, two_ref, final_ref):
+    k0, k1, k2 = [steps_ref[number : number + 1, :] for number in range(3)]
+    final_ref[...] = start_ref[...] + (
+        k0 * zero_ref[...] + k1 * one_ref[...] + k2 * two_ref[...]
+    )
 
 
 def on_device(series_values, observed, series_factors, time_factors, lag_weights):
@@ -300,13 +308,20 @@
         compiler_params=SMALL,
     )(packed, power2, many, lag_weights)
     gathered = lax.all_to_all(spread, both, split_axis=0, concat_axis=0, tiled=True)
-    final, misfit = pl.pallas_call(
+    steps, misfit = pl.pallas_call(
         update_kernel,
-        out_shape=(field_shape, jax.ShapeDtypeStruct((n_tm, rows, rank), jnp.bfloat16)),
+        out_shape=(jax.ShapeDtypeStruct((8, rank), jnp.float32), jax.ShapeDtypeStruct((n_tm, rows, rank), jnp.bfloat16)),
         in_specs=[VMEM] * 7,
         out_specs=(VMEM, VMEM),
         compiler_params=SMALL,
     )(gathered, time_factors, power0, power1, power2, series_values, series_factors)
+    final = pl.pallas_call(
+        final_kernel,
+        out_shape=field_shape,
+        in_specs=[VMEM] * 5,
+        out_specs=VMEM,
+        compiler_params=SMALL,
+    )(steps, time_factors, power0, power1, power2)
     misfit = lax.all_to_all(misfit, "tm", split_axis=0, concat_axis=0, tiled=True)
     return final, misfit.reshape(n_tm * rows, rank)
 

time: 122 us -> 123 us (level)
  blocking collectives: 68.1 us -> 35.6 us
  waiting for transfers between devices: 9.2 us -> 36.7 us
  starting transfers between devices: 32.3 us -> 37 us
  Pallas kernels: 2.26 us -> 3.87 us
    all_to_all x1 -> x0, blocking collectives: 32.4 us -> none  [on_device(): lax.all_to_all(misfit, 'tm', split_axis=0, concat_axis=0, tiled=True)]
    all_to_all x0 -> x1, waiting for transfers between devices: none -> 27.5 us  [on_device(): lax.all_to_all(misfit, 'tm', split_axis=0, concat_axis=0, tiled=True)]
    all_to_all x0 -> x1, starting transfers between devices: none -> 4.7 us  [on_device(): lax.all_to_all(misfit, 'tm', split_axis=0, concat_axis=0, tiled=True)]
    pallas_call x1 -> x2, Pallas kernels: 1.03 us -> 2.64 us  [the longest x1 2.01 us: on_device(): pl.pallas_call(update_kernel, out_shape=(jax.ShapeDtypeStruct((8, rank),...]
  transfers between devices with their start and end apart: 16 -> 17, of which waited for: 8 -> 9; matrix products, arithmetic and copies ran while one was open for 7% -> 6% of each run, Pallas kernels for 0% -> 1%
where the time goes in v13:
time: 123 us
  starting transfers between devices  37 us (30%)
  waiting for transfers between devices  36.7 us (30%)
  blocking collectives  35.6 us (29%)
  matrix products  6.1 us (5%)
  Pallas kernels  3.87 us (3%)
  other arithmetic  1.86 us (2%)
    all_to_all x1, blocking collectives, on_device(): lax.all_to_all(spread, both, split_axis=0, concat_axis=0, tiled=True)  35.6 us
    all_to_all x1, waiting for transfers between devices, on_device(): lax.all_to_all(misfit, 'tm', split_axis=0, concat_axis=0, tiled=True)  27.5 us
    ppermute x3, starting transfers between devices, fetch(): return (lax.ppermute(many, both, many_route), few)  16.9 us
    ppermute x9, starting transfers between devices, moved(): return lax.ppermute(part, 'series', pairs)  12.6 us
    ppermute x9, waiting for transfers between devices, moved(): return lax.ppermute(part, 'series', pairs)  9.18 us
    dot_general x4, matrix products, back(): jnp.dot(rows_here, series_factors, preferred_element_type=jnp.float32)  5.24 us
    all_to_all x1, starting transfers between devices, on_device(): lax.all_to_all(misfit, 'tm', split_axis=0, concat_axis=0, tiled=True)  4.7 us
  transfers between devices with their start and end apart: 17, of which 9 were waited for; matrix products, arithmetic and copies ran while one was open for 6% of the time, Pallas kernels for 1%

profile of v13, /device:TPU:1, one launch (start us, length us, event | category | flops | bytes accessed | tf_op | source)
XLA Modules:
  0.0 123.1 jit_solution(13765836300681609912)
XLA Ops:
  0.6 0.0 copy-start
  0.6 0.8 collective-permute-start.1
  1.4 6.2 %collective-permute-start = (f32[64,128]{1,0:T(8,128)}, f32[64,128]{1,0:T(8,128)S(1)}, u32[]{:S(2)}, u32[]{:S(2)}) collective-permute-start(f32[64,128]{1,0:T(8,128)} %start_ref.3), channel_id=1, source_target_pairs={{0,12},{4,16},{8,20},{12,24},{16,28},{20,32},{24,36},{28,40},{32,4... | collective-permute-start | bytes 98312 | tf_op jit(solution)/shard_map/ppermute | solution.py:242
  7.7 1.9 %broadcast_compare_fusion = pred[64,8192]{1,0:T(32,128)(4,1)S(1)} fusion(s32[64,8192]{1,0:T(8,128)} %param.6), kind=kLoop, calls=%fused_computation.18 | loop fusion | flops 524288 | bytes 2621440 | tf_op jit(solution)/shard_map/eq | solution.py:269
  9.5 0.0 copy-done
  9.5 0.0 copy-start.2
  9.6 1.8 %fusion.12 = f32[64,128]{1,0:T(8,128)S(1)} fusion(bf16[8192,128]{1,0:T(8,128)(2,1)S(1)} %copy-done, pred[64,8192]{1,0:T(32,128)(4,1)S(1)} %broadcast_compare_fusion, bf16[64,8192]{1,0:T(8,128)(2,1)} %values_ref.1), kind=kOutput, calls=%fused_computation.16 | convolution fusion | flops 134742016 | bytes 3702784 | tf_op jit(solution)/shard_map/dot_general | solution.py:275
  11.4 0.0 copy-done.2
  11.4 0.0 copy-start.3
  11.4 1.2 fusion.8.local_ref
  12.5 0.0 collective-permute-done.1.few_ref
  12.5 0.0 collective-permute-done.many_ref
  12.6 0.0 copy-done.3
  12.6 0.2 shard_map.68.own_ref
  12.8 3.8 %collective-permute-start.4 = (f32[64,128]{1,0:T(8,128)S(1)}, f32[64,128]{1,0:T(8,128)S(1)}, u32[]{:S(2)}, u32[]{:S(2)}) collective-permute-start(f32[64,128]{1,0:T(8,128)S(1)} %shard_map.68.own_ref), channel_id=1, source_target_pairs={{0,2},{1,3},{2,0},{3,1},{4,6},{5,7},{6,4},{7,5},{8,10},{9,11},{10,... | collective-permute-start | bytes 98312 | tf_op jit(solution)/shard_map/ppermute | solution.py:257
  16.5 0.0 collective-permute-start.3
  16.6 1.5 %collective-permute-start.2 = (f32[64,128]{1,0:T(8,128)S(1)}, f32[64,128]{1,0:T(8,128)S(1)}, u32[]{:S(2)}, u32[]{:S(2)}) collective-permute-start(f32[64,128]{1,0:T(8,128)S(1)} %shard_map.68.own_ref), channel_id=1, source_target_pairs={{0,1},{1,2},{2,3},{3,0},{4,5},{5,6},{6,7},{7,4},{8,9},{9,10},{10,1... | collective-permute-start | bytes 98312 | tf_op jit(solution)/shard_map/ppermute | solution.py:257
  18.0 0.0 collective-permute-done.4.second_ref
  18.0 1.6 %collective-permute-done.3.third_ref = f32[64,128]{1,0:T(8,128)S(1)} collective-permute-done((f32[64,128]{1,0:T(8,128)S(1)}, f32[64,128]{1,0:T(8,128)S(1)}, u32[]{:S(2)}, u32[]{:S(2)}) %collective-permute-start.3) | collective-permute-done | bytes 32800 | tf_op jit(solution)/shard_map/ppermute | solution.py:257
  19.7 1.2 collective-permute-done.2.first_ref
  20.9 4.8 %collective-permute-start.5 = (bf16[48,128]{1,0:T(8,128)(2,1)S(1)}, bf16[48,128]{1,0:T(8,128)(2,1)S(1)}, u32[]{:S(2)}, u32[]{:S(2)}) collective-permute-start(bf16[48,128]{1,0:T(8,128)(2,1)S(1)} %get-tuple-element.16), channel_id=1, source_target_pairs={{0,12},{4,16},{8,20},{12,24},{16,28},{20,32},{24,36},{28,40},{32,4... | collective-permute-start | bytes 36872 | tf_op jit(solution)/shard_map/ppermute | solution.py:242
  25.7 0.7 collective-permute-start.6
  26.4 1.1 fusion.6.local_ref
  27.5 0.0 collective-permute-done.5.many_ref
  27.6 0.0 collective-permute-done.6.few_ref
  27.6 0.2 shard_map.70.own_ref
  27.8 2.2 %collective-permute-start.9 = (f32[64,128]{1,0:T(8,128)S(1)}, f32[64,128]{1,0:T(8,128)S(1)}, u32[]{:S(2)}, u32[]{:S(2)}) collective-permute-start(f32[64,128]{1,0:T(8,128)S(1)} %shard_map.70.own_ref), channel_id=1, source_target_pairs={{0,2},{1,3},{2,0},{3,1},{4,6},{5,7},{6,4},{7,5},{8,10},{9,11},{10,... | collective-permute-start | bytes 98312 | tf_op jit(solution)/shard_map/ppermute | solution.py:257
  30.0 0.5 collective-permute-start.8
  30.5 0.9 collective-permute-start.7
  31.5 0.7 collective-permute-done.9.second_ref
  32.1 0.6 collective-permute-done.8.third_ref
  32.8 2.3 %collective-permute-done.7.first_ref = f32[64,128]{1,0:T(8,128)S(1)} collective-permute-done((f32[64,128]{1,0:T(8,128)S(1)}, f32[64,128]{1,0:T(8,128)S(1)}, u32[]{:S(2)}, u32[]{:S(2)}) %collective-permute-start.7) | collective-permute-done | bytes 32800 | tf_op jit(solution)/shard_map/ppermute | solution.py:257
  35.1 5.8 %collective-permute-start.10 = (bf16[48,128]{1,0:T(8,128)(2,1)S(1)}, bf16[48,128]{1,0:T(8,128)(2,1)S(1)}, u32[]{:S(2)}, u32[]{:S(2)}) collective-permute-start(bf16[48,128]{1,0:T(8,128)(2,1)S(1)} %get-tuple-element.20), channel_id=1, source_target_pairs={{0,12},{4,16},{8,20},{12,24},{16,28},{20,32},{24,36},{28,40},{32,4... | collective-permute-start | bytes 36872 | tf_op jit(solution)/shard_map/ppermute | solution.py:242
  41.0 0.7 collective-permute-start.11
  41.6 1.1 fusion.5.local_ref
  42.8 0.0 copy-start.1
  42.8 0.0 collective-permute-done.10.many_ref
  42.8 0.0 collective-permute-done.11.few_ref
  42.8 0.2 shard_map.72.own_ref
  43.1 2.3 %collective-permute-start.14 = (f32[64,128]{1,0:T(8,128)S(1)}, f32[64,128]{1,0:T(8,128)S(1)}, u32[]{:S(2)}, u32[]{:S(2)}) collective-permute-start(f32[64,128]{1,0:T(8,128)S(1)} %shard_map.72.own_ref), channel_id=1, source_target_pairs={{0,2},{1,3},{2,0},{3,1},{4,6},{5,7},{6,4},{7,5},{8,10},{9,11},{10,... | collective-permute-start | bytes 98312 | tf_op jit(solution)/shard_map/ppermute | solution.py:257
  45.3 0.2 collective-permute-start.13
  45.5 1.3 %collective-permute-start.12 = (f32[64,128]{1,0:T(8,128)S(1)}, f32[64,128]{1,0:T(8,128)S(1)}, u32[]{:S(2)}, u32[]{:S(2)}) collective-permute-start(f32[64,128]{1,0:T(8,128)S(1)} %shard_map.72.own_ref), channel_id=1, source_target_pairs={{0,1},{1,2},{2,3},{3,0},{4,5},{5,6},{6,7},{7,4},{8,9},{9,10},{10,1... | collective-permute-start | bytes 98312 | tf_op jit(solution)/shard_map/ppermute | solution.py:257
  46.8 0.6 collective-permute-done.14.second_ref
  47.4 0.7 collective-permute-done.13.third_ref
  48.1 1.4 %collective-permute-done.12.first_ref = f32[64,128]{1,0:T(8,128)S(1)} collective-permute-done((f32[64,128]{1,0:T(8,128)S(1)}, f32[64,128]{1,0:T(8,128)S(1)}, u32[]{:S(2)}, u32[]{:S(2)}) %collective-permute-start.12) | collective-permute-done | bytes 32800 | tf_op jit(solution)/shard_map/ppermute | solution.py:257
  49.5 0.7 collective-permute-start.15
  50.2 0.9 fusion.4
  51.0 0.2 shard_map.74.packed_ref
  51.2 0.0 collective-permute-done.15.many_ref
  51.2 0.4 shard_map.75
  51.6 35.6 %all_to_all.10.gathered_ref = f32[256,1,128]{2,1,0:T(1,128)S(1)} all-to-all(f32[256,1,128]{2,1,0:T(1,128)S(1)} %shard_map.75), channel_id=1, replica_groups=mesh['tm'=64,'series'=4] {'tm','series'}, dimensions={0} | all-to-all | bytes 262144 | tf_op jit(solution)/shard_map/all_to_all | solution.py:310
  87.2 0.0 copy-done.1
  87.2 2.0 %shard_map.76 = (f32[8,128]{1,0:T(8,128)S(1)}, bf16[64,64,128]{2,1,0:T(8,128)(2,1)}) custom-call(f32[256,1,128]{2,1,0:T(1,128)S(1)} %all_to_all.10.gathered_ref, f32[64,128]{1,0:T(8,128)S(1)} %copy-done.2, f32[64,128]{1,0:T(8,128)S(1)} %get-tuple-element.15.field_ref.zero_ref, f32[64,128]{1,0:T(8,128)S(1)} %get-tuple-element.19.field_ref.one_ref, ...), custom_call_target="tpu_custom_call" | custom-call | tf_op jit(solution)/shard_map/pallas_call | solution.py:311
  89.2 4.7 %all-to-all-start.1 = ((bf16[64,64,128]{2,1,0:T(8,128)(2,1)}), bf16[64,64,128]{2,1,0:T(8,128)(2,1)S(1)}, u32[]{:S(2)}, u32[]{:S(2)}) async-start(bf16[64,64,128]{2,1,0:T(8,128)(2,1)} %get-tuple-element.27), calls=%async_computation.1 | async-start | bytes 2097152 | tf_op jit(solution)/shard_map/all_to_all | solution.py:325
  93.9 0.6 shard_map.77
  94.6 27.5 %all-to-all-done.1 = bf16[64,64,128]{2,1,0:T(8,128)(2,1)S(1)} async-done(((bf16[64,64,128]{2,1,0:T(8,128)(2,1)}), bf16[64,64,128]{2,1,0:T(8,128)(2,1)S(1)}, u32[]{:S(2)}, u32[]{:S(2)}) %all-to-all-start.1) | async-done | bytes 1048608 | tf_op jit(solution)/shard_map/all_to_all | solution.py:325
  122.1 1.0 copy.14
  (3 shorter events, 0.0 us)
Async XLA Ops:
  0.6 8.9 %copy-start = (bf16[8192,128]{1,0:T(8,128)(2,1)S(1)}, bf16[8192,128]{1,0:T(8,128)(2,1)}, u32[]{:S(2)}) copy-start(bf16[8192,128]{1,0:T(8,128)(2,1)} %factors_ref.1) | copy-start | bytes 6291460
  0.6 11.9 %collective-permute-start.1 = (f32[64,128]{1,0:T(8,128)}, f32[64,128]{1,0:T(8,128)S(1)}, u32[]{:S(2)}, u32[]{:S(2)}) collective-permute-start(f32[64,128]{1,0:T(8,128)} %start_ref.3), channel_id=1, source_target_pairs={{2,6},{6,10},{10,14},{14,18},{18,22},{22,26},{26,30},{30,34},{34,3... | collective-permute-start | bytes 98312 | tf_op jit(solution)/shard_map/ppermute | solution.py:241
  1.4 11.1 %collective-permute-start = (f32[64,128]{1,0:T(8,128)}, f32[64,128]{1,0:T(8,128)S(1)}, u32[]{:S(2)}, u32[]{:S(2)}) collective-permute-start(f32[64,128]{1,0:T(8,128)} %start_ref.3), channel_id=1, source_target_pairs={{0,12},{4,16},{8,20},{12,24},{16,28},{20,32},{24,36},{28,40},{32,4... | collective-permute-start | bytes 98312 | tf_op jit(solution)/shard_map/ppermute | solution.py:242
  9.5 1.8 %copy-start.2 = (f32[64,128]{1,0:T(8,128)S(1)}, f32[64,128]{1,0:T(8,128)}, u32[]{:S(2)}) copy-start(f32[64,128]{1,0:T(8,128)} %start_ref.3) | copy-start | bytes 98308
  11.4 1.2 copy-start.3
  12.8 5.2 %collective-permute-start.4 = (f32[64,128]{1,0:T(8,128)S(1)}, f32[64,128]{1,0:T(8,128)S(1)}, u32[]{:S(2)}, u32[]{:S(2)}) collective-permute-start(f32[64,128]{1,0:T(8,128)S(1)} %shard_map.68.own_ref), channel_id=1, source_target_pairs={{0,2},{1,3},{2,0},{3,1},{4,6},{5,7},{6,4},{7,5},{8,10},{9,11},{10,... | collective-permute-start | bytes 98312 | tf_op jit(solution)/shard_map/ppermute | solution.py:257
  16.5 3.1 %collective-permute-start.3 = (f32[64,128]{1,0:T(8,128)S(1)}, f32[64,128]{1,0:T(8,128)S(1)}, u32[]{:S(2)}, u32[]{:S(2)}) collective-permute-start(f32[64,128]{1,0:T(8,128)S(1)} %shard_map.68.own_ref), channel_id=1, source_target_pairs={{0,3},{1,0},{2,1},{3,2},{4,7},{5,4},{6,5},{7,6},{8,11},{9,8},{10,9... | collective-permute-start | bytes 98312 | tf_op jit(solution)/shard_map/ppermute | solution.py:257
  16.6 4.3 %collective-permute-start.2 = (f32[64,128]{1,0:T(8,128)S(1)}, f32[64,128]{1,0:T(8,128)S(1)}, u32[]{:S(2)}, u32[]{:S(2)}) collective-permute-start(f32[64,128]{1,0:T(8,128)S(1)} %shard_map.68.own_ref), channel_id=1, source_target_pairs={{0,1},{1,2},{2,3},{3,0},{4,5},{5,6},{6,7},{7,4},{8,9},{9,10},{10,1... | collective-permute-start | bytes 98312 | tf_op jit(solution)/shard_map/ppermute | solution.py:257
  20.9 6.6 %collective-permute-start.5 = (bf16[48,128]{1,0:T(8,128)(2,1)S(1)}, bf16[48,128]{1,0:T(8,128)(2,1)S(1)}, u32[]{:S(2)}, u32[]{:S(2)}) collective-permute-start(bf16[48,128]{1,0:T(8,128)(2,1)S(1)} %get-tuple-element.16), channel_id=1, source_target_pairs={{0,12},{4,16},{8,20},{12,24},{16,28},{20,32},{24,36},{28,40},{32,4... | collective-permute-start | bytes 36872 | tf_op jit(solution)/shard_map/ppermute | solution.py:242
  25.7 1.8 %collective-permute-start.6 = (bf16[48,128]{1,0:T(8,128)(2,1)S(1)}, bf16[48,128]{1,0:T(8,128)(2,1)S(1)}, u32[]{:S(2)}, u32[]{:S(2)}) collective-permute-start(bf16[48,128]{1,0:T(8,128)(2,1)S(1)} %get-tuple-element.17), channel_id=1, source_target_pairs={{2,6},{6,10},{10,14},{14,18},{18,22},{22,26},{26,30},{30,34},{34,3... | collective-permute-start | bytes 36872 | tf_op jit(solution)/shard_map/ppermute | solution.py:241
  27.8 4.4 %collective-permute-start.9 = (f32[64,128]{1,0:T(8,128)S(1)}, f32[64,128]{1,0:T(8,128)S(1)}, u32[]{:S(2)}, u32[]{:S(2)}) collective-permute-start(f32[64,128]{1,0:T(8,128)S(1)} %shard_map.70.own_ref), channel_id=1, source_target_pairs={{0,2},{1,3},{2,0},{3,1},{4,6},{5,7},{6,4},{7,5},{8,10},{9,11},{10,... | collective-permute-start | bytes 98312 | tf_op jit(solution)/shard_map/ppermute | solution.py:257
  30.0 2.8 %collective-permute-start.8 = (f32[64,128]{1,0:T(8,128)S(1)}, f32[64,128]{1,0:T(8,128)S(1)}, u32[]{:S(2)}, u32[]{:S(2)}) collective-permute-start(f32[64,128]{1,0:T(8,128)S(1)} %shard_map.70.own_ref), channel_id=1, source_target_pairs={{0,3},{1,0},{2,1},{3,2},{4,7},{5,4},{6,5},{7,6},{8,11},{9,8},{10,9... | collective-permute-start | bytes 98312 | tf_op jit(solution)/shard_map/ppermute | solution.py:257
  30.5 4.6 %collective-permute-start.7 = (f32[64,128]{1,0:T(8,128)S(1)}, f32[64,128]{1,0:T(8,128)S(1)}, u32[]{:S(2)}, u32[]{:S(2)}) collective-permute-start(f32[64,128]{1,0:T(8,128)S(1)} %shard_map.70.own_ref), channel_id=1, source_target_pairs={{0,1},{1,2},{2,3},{3,0},{4,5},{5,6},{6,7},{7,4},{8,9},{9,10},{10,1... | collective-permute-start | bytes 98312 | tf_op jit(solution)/shard_map/ppermute | solution.py:257
  35.1 7.7 %collective-permute-start.10 = (bf16[48,128]{1,0:T(8,128)(2,1)S(1)}, bf16[48,128]{1,0:T(8,128)(2,1)S(1)}, u32[]{:S(2)}, u32[]{:S(2)}) collective-permute-start(bf16[48,128]{1,0:T(8,128)(2,1)S(1)} %get-tuple-element.20), channel_id=1, source_target_pairs={{0,12},{4,16},{8,20},{12,24},{16,28},{20,32},{24,36},{28,40},{32,4... | collective-permute-start | bytes 36872 | tf_op jit(solution)/shard_map/ppermute | solution.py:242
  41.0 1.8 %collective-permute-start.11 = (bf16[48,128]{1,0:T(8,128)(2,1)S(1)}, bf16[48,128]{1,0:T(8,128)(2,1)S(1)}, u32[]{:S(2)}, u32[]{:S(2)}) collective-permute-start(bf16[48,128]{1,0:T(8,128)(2,1)S(1)} %get-tuple-element.21), channel_id=1, source_target_pairs={{2,6},{6,10},{10,14},{14,18},{18,22},{22,26},{26,30},{30,34},{34,3... | collective-permute-start | bytes 36872 | tf_op jit(solution)/shard_map/ppermute | solution.py:241
  42.8 44.4 %copy-start.1 = (bf16[64,8192]{1,0:T(8,128)(2,1)S(1)}, bf16[64,8192]{1,0:T(8,128)(2,1)}, u32[]{:S(2)}) copy-start(bf16[64,8192]{1,0:T(8,128)(2,1)} %values_ref.1) | copy-start | bytes 3145732
  43.1 4.4 %collective-permute-start.14 = (f32[64,128]{1,0:T(8,128)S(1)}, f32[64,128]{1,0:T(8,128)S(1)}, u32[]{:S(2)}, u32[]{:S(2)}) collective-permute-start(f32[64,128]{1,0:T(8,128)S(1)} %shard_map.72.own_ref), channel_id=1, source_target_pairs={{0,2},{1,3},{2,0},{3,1},{4,6},{5,7},{6,4},{7,5},{8,10},{9,11},{10,... | collective-permute-start | bytes 98312 | tf_op jit(solution)/shard_map/ppermute | solution.py:257
  45.3 2.8 %collective-permute-start.13 = (f32[64,128]{1,0:T(8,128)S(1)}, f32[64,128]{1,0:T(8,128)S(1)}, u32[]{:S(2)}, u32[]{:S(2)}) collective-permute-start(f32[64,128]{1,0:T(8,128)S(1)} %shard_map.72.own_ref), channel_id=1, source_target_pairs={{0,3},{1,0},{2,1},{3,2},{4,7},{5,4},{6,5},{7,6},{8,11},{9,8},{10,9... | collective-permute-start | bytes 98312 | tf_op jit(solution)/shard_map/ppermute | solution.py:257
  45.5 4.0 %collective-permute-start.12 = (f32[64,128]{1,0:T(8,128)S(1)}, f32[64,128]{1,0:T(8,128)S(1)}, u32[]{:S(2)}, u32[]{:S(2)}) collective-permute-start(f32[64,128]{1,0:T(8,128)S(1)} %shard_map.72.own_ref), channel_id=1, source_target_pairs={{0,1},{1,2},{2,3},{3,0},{4,5},{5,6},{6,7},{7,4},{8,9},{9,10},{10,1... | collective-permute-start | bytes 98312 | tf_op jit(solution)/shard_map/ppermute | solution.py:257
  49.5 1.7 %collective-permute-start.15 = (bf16[48,128]{1,0:T(8,128)(2,1)S(1)}, bf16[48,128]{1,0:T(8,128)(2,1)S(1)}, u32[]{:S(2)}, u32[]{:S(2)}) collective-permute-start(bf16[48,128]{1,0:T(8,128)(2,1)S(1)} %get-tuple-element.25), channel_id=1, source_target_pairs={{13,1},{17,5},{21,9},{25,13},{29,17},{33,21},{37,25},{41,29},{45,3... | collective-permute-start | bytes 36872 | tf_op jit(solution)/shard_map/ppermute | solution.py:292
  89.2 32.9 %all-to-all-start.1 = ((bf16[64,64,128]{2,1,0:T(8,128)(2,1)}), bf16[64,64,128]{2,1,0:T(8,128)(2,1)S(1)}, u32[]{:S(2)}, u32[]{:S(2)}) async-start(bf16[64,64,128]{2,1,0:T(8,128)(2,1)} %get-tuple-element.27), calls=%async_computation.1 | async-start | bytes 2097152 | tf_op jit(solution)/shard_map/all_to_all | solution.py:325

commit v14 on v12

--- a/solution.py
+++ b/solution.py
@@ -56,7 +56,7 @@
 
 
 def penalty_kernel(
-    scale, last_time, field_ref, many_ref, few_ref, weights_ref, local_ref,
+    scale, last_time, field_ref, few_ref, many_ref, weights_ref, local_ref,
     part_ref, window, short,
 ):
     here = lax.axis_index("series")
@@ -241,7 +241,7 @@
             out_specs=VMEM,
             scratch_shapes=lag_scratch,
             compiler_params=SMALL,
-        )(field, many, few, lag_weights, local)
+        )(field, few, many, lag_weights, local)
 
     def series_sum(scale, part, field, out_halos):
         def moved(distance):

time: 122 us -> 122 us (level)
  no operation moved by 1% of the time
where the time goes in v14:
time: 122 us
  blocking collectives  68.3 us (56%)
  starting transfers between devices  31.3 us (26%)
  waiting for transfers between devices  10.2 us (8%)
  matrix products  6.11 us (5%)
  Pallas kernels  2.27 us (2%)
  other arithmetic  1.86 us (2%)
    all_to_all x1, blocking collectives, on_device(): lax.all_to_all(spread, both, split_axis=0, concat_axis=0, tiled=True)  35.9 us
    all_to_all x1, blocking collectives, on_device(): lax.all_to_all(misfit, 'tm', split_axis=0, concat_axis=0, tiled=True)  32.4 us
    ppermute x3, starting transfers between devices, fetch(): return (lax.ppermute(many, both, many_route), few)  16.3 us
    ppermute x9, starting transfers between devices, moved(): return lax.ppermute(part, 'series', pairs)  12.3 us
    ppermute x9, waiting for transfers between devices, moved(): return lax.ppermute(part, 'series', pairs)  10.2 us
    dot_general x4, matrix products, back(): jnp.dot(rows_here, series_factors, preferred_element_type=jnp.float32)  5.25 us
  transfers between devices with their start and end apart: 16, of which 8 were waited for; matrix products, arithmetic and copies ran while one was open for 7% of the time, Pallas kernels for 0%

profile of v14, /device:TPU:1, one launch (start us, length us, event | category | flops | bytes accessed | tf_op | source)
XLA Modules:
  0.0 121.9 jit_solution(1816769669380193045)
XLA Ops:
  0.6 0.0 copy-start
  0.6 6.3 %collective-permute-start.1 = (f32[64,128]{1,0:T(8,128)}, f32[64,128]{1,0:T(8,128)S(1)}, u32[]{:S(2)}, u32[]{:S(2)}) collective-permute-start(f32[64,128]{1,0:T(8,128)} %start_ref.1), channel_id=1, source_target_pairs={{0,12},{4,16},{8,20},{12,24},{16,28},{20,32},{24,36},{28,40},{32,4... | collective-permute-start | bytes 98312 | tf_op jit(solution)/shard_map/ppermute | solution.py:234
  7.0 0.7 collective-permute-start
  7.7 1.9 %broadcast_compare_fusion = pred[64,8192]{1,0:T(32,128)(4,1)S(1)} fusion(s32[64,8192]{1,0:T(8,128)} %param.6), kind=kLoop, calls=%fused_computation.18 | loop fusion | flops 524288 | bytes 2621440 | tf_op jit(solution)/shard_map/eq | solution.py:261
  9.5 0.0 copy-done
  9.5 0.0 copy-start.2
  9.6 1.8 %fusion.12 = f32[64,128]{1,0:T(8,128)S(1)} fusion(bf16[8192,128]{1,0:T(8,128)(2,1)S(1)} %copy-done, pred[64,8192]{1,0:T(32,128)(4,1)S(1)} %broadcast_compare_fusion, bf16[64,8192]{1,0:T(8,128)(2,1)} %values_ref.1), kind=kOutput, calls=%fused_computation.16 | convolution fusion | flops 134742016 | bytes 3702784 | tf_op jit(solution)/shard_map/dot_general | solution.py:267
  11.4 0.0 copy-done.2
  11.4 0.0 copy-start.3
  11.4 1.2 fusion.8.local_ref
  12.5 0.0 collective-permute-done.1.many_ref
  12.5 0.0 collective-permute-done.few_ref
  12.6 0.0 copy-done.3
  12.6 0.2 shard_map.68.own_ref
  12.8 4.0 %collective-permute-start.4 = (f32[64,128]{1,0:T(8,128)S(1)}, f32[64,128]{1,0:T(8,128)S(1)}, u32[]{:S(2)}, u32[]{:S(2)}) collective-permute-start(f32[64,128]{1,0:T(8,128)S(1)} %shard_map.68.own_ref), channel_id=1, source_target_pairs={{0,2},{1,3},{2,0},{3,1},{4,6},{5,7},{6,4},{7,5},{8,10},{9,11},{10,... | collective-permute-start | bytes 98312 | tf_op jit(solution)/shard_map/ppermute | solution.py:249
  16.8 0.0 collective-permute-start.3
  16.8 1.5 %collective-permute-start.2 = (f32[64,128]{1,0:T(8,128)S(1)}, f32[64,128]{1,0:T(8,128)S(1)}, u32[]{:S(2)}, u32[]{:S(2)}) collective-permute-start(f32[64,128]{1,0:T(8,128)S(1)} %shard_map.68.own_ref), channel_id=1, source_target_pairs={{0,1},{1,2},{2,3},{3,0},{4,5},{5,6},{6,7},{7,4},{8,9},{9,10},{10,1... | collective-permute-start | bytes 98312 | tf_op jit(solution)/shard_map/ppermute | solution.py:249
  18.3 0.0 collective-permute-done.4.second_ref
  18.3 1.6 %collective-permute-done.3.third_ref = f32[64,128]{1,0:T(8,128)S(1)} collective-permute-done((f32[64,128]{1,0:T(8,128)S(1)}, f32[64,128]{1,0:T(8,128)S(1)}, u32[]{:S(2)}, u32[]{:S(2)}) %collective-permute-start.3) | collective-permute-done | bytes 32800 | tf_op jit(solution)/shard_map/ppermute | solution.py:249
  19.9 0.9 collective-permute-done.2.first_ref
  20.8 0.7 collective-permute-start.5
  21.5 4.7 %collective-permute-start.6 = (bf16[48,128]{1,0:T(8,128)(2,1)S(1)}, bf16[48,128]{1,0:T(8,128)(2,1)S(1)}, u32[]{:S(2)}, u32[]{:S(2)}) collective-permute-start(bf16[48,128]{1,0:T(8,128)(2,1)S(1)} %get-tuple-element.17), channel_id=1, source_target_pairs={{0,12},{4,16},{8,20},{12,24},{16,28},{20,32},{24,36},{28,40},{32,4... | collective-permute-start | bytes 36872 | tf_op jit(solution)/shard_map/ppermute | solution.py:234
  26.2 1.1 fusion.6.local_ref
  27.3 0.0 collective-permute-done.5.few_ref
  27.3 0.0 collective-permute-done.6.many_ref
  27.4 0.2 shard_map.70.own_ref
  27.6 2.1 %collective-permute-start.9 = (f32[64,128]{1,0:T(8,128)S(1)}, f32[64,128]{1,0:T(8,128)S(1)}, u32[]{:S(2)}, u32[]{:S(2)}) collective-permute-start(f32[64,128]{1,0:T(8,128)S(1)} %shard_map.70.own_ref), channel_id=1, source_target_pairs={{0,2},{1,3},{2,0},{3,1},{4,6},{5,7},{6,4},{7,5},{8,10},{9,11},{10,... | collective-permute-start | bytes 98312 | tf_op jit(solution)/shard_map/ppermute | solution.py:249
  29.6 1.4 %collective-permute-start.8 = (f32[64,128]{1,0:T(8,128)S(1)}, f32[64,128]{1,0:T(8,128)S(1)}, u32[]{:S(2)}, u32[]{:S(2)}) collective-permute-start(f32[64,128]{1,0:T(8,128)S(1)} %shard_map.70.own_ref), channel_id=1, source_target_pairs={{0,3},{1,0},{2,1},{3,2},{4,7},{5,4},{6,5},{7,6},{8,11},{9,8},{10,9... | collective-permute-start | bytes 98312 | tf_op jit(solution)/shard_map/ppermute | solution.py:249
  31.0 0.1 collective-permute-start.7
  31.1 0.9 collective-permute-done.9.second_ref
  32.0 0.4 collective-permute-done.8.third_ref
  32.4 2.6 %collective-permute-done.7.first_ref = f32[64,128]{1,0:T(8,128)S(1)} collective-permute-done((f32[64,128]{1,0:T(8,128)S(1)}, f32[64,128]{1,0:T(8,128)S(1)}, u32[]{:S(2)}, u32[]{:S(2)}) %collective-permute-start.7) | collective-permute-done | bytes 32800 | tf_op jit(solution)/shard_map/ppermute | solution.py:249
  35.0 0.7 collective-permute-start.10
  35.7 5.3 %collective-permute-start.11 = (bf16[48,128]{1,0:T(8,128)(2,1)S(1)}, bf16[48,128]{1,0:T(8,128)(2,1)S(1)}, u32[]{:S(2)}, u32[]{:S(2)}) collective-permute-start(bf16[48,128]{1,0:T(8,128)(2,1)S(1)} %get-tuple-element.21), channel_id=1, source_target_pairs={{0,12},{4,16},{8,20},{12,24},{16,28},{20,32},{24,36},{28,40},{32,4... | collective-permute-start | bytes 36872 | tf_op jit(solution)/shard_map/ppermute | solution.py:234
  41.0 1.2 fusion.5.local_ref
  42.2 0.0 copy-start.1
  42.2 0.0 collective-permute-done.10.few_ref
  42.2 0.0 collective-permute-done.11.many_ref
  42.2 0.2 shard_map.72.own_ref
  42.4 1.8 %collective-permute-start.14 = (f32[64,128]{1,0:T(8,128)S(1)}, f32[64,128]{1,0:T(8,128)S(1)}, u32[]{:S(2)}, u32[]{:S(2)}) collective-permute-start(f32[64,128]{1,0:T(8,128)S(1)} %shard_map.72.own_ref), channel_id=1, source_target_pairs={{0,2},{1,3},{2,0},{3,1},{4,6},{5,7},{6,4},{7,5},{8,10},{9,11},{10,... | collective-permute-start | bytes 98312 | tf_op jit(solution)/shard_map/ppermute | solution.py:249
  44.2 1.3 %collective-permute-start.13 = (f32[64,128]{1,0:T(8,128)S(1)}, f32[64,128]{1,0:T(8,128)S(1)}, u32[]{:S(2)}, u32[]{:S(2)}) collective-permute-start(f32[64,128]{1,0:T(8,128)S(1)} %shard_map.72.own_ref), channel_id=1, source_target_pairs={{0,3},{1,0},{2,1},{3,2},{4,7},{5,4},{6,5},{7,6},{8,11},{9,8},{10,9... | collective-permute-start | bytes 98312 | tf_op jit(solution)/shard_map/ppermute | solution.py:249
  45.5 0.2 collective-permute-start.12
  45.7 1.1 collective-permute-done.14.second_ref
  46.8 0.4 collective-permute-done.13.third_ref
  47.2 2.3 %collective-permute-done.12.first_ref = f32[64,128]{1,0:T(8,128)S(1)} collective-permute-done((f32[64,128]{1,0:T(8,128)S(1)}, f32[64,128]{1,0:T(8,128)S(1)}, u32[]{:S(2)}, u32[]{:S(2)}) %collective-permute-start.12) | collective-permute-done | bytes 32800 | tf_op jit(solution)/shard_map/ppermute | solution.py:249
  49.5 0.7 collective-permute-start.15
  50.1 0.9 fusion.4
  51.0 0.2 shard_map.74.packed_ref
  51.2 0.0 collective-permute-done.15.many_ref
  51.2 0.4 shard_map.75
  51.5 35.9 %all_to_all.10.gathered_ref = f32[256,1,128]{2,1,0:T(1,128)S(1)} all-to-all(f32[256,1,128]{2,1,0:T(1,128)S(1)} %shard_map.75), channel_id=1, replica_groups=mesh['tm'=64,'series'=4] {'tm','series'}, dimensions={0} | all-to-all | bytes 262144 | tf_op jit(solution)/shard_map/all_to_all | solution.py:302
  87.4 0.0 copy-done.1
  87.4 1.0 shard_map.76
  88.5 32.4 %all_to_all.11 = bf16[64,64,128]{2,1,0:T(8,128)(2,1)S(1)} all-to-all(bf16[64,64,128]{2,1,0:T(8,128)(2,1)S(1)} %get-tuple-element.27), channel_id=1, replica_groups=mesh['tm'=64,'series'=4] {'tm'}, dimensions={0} | all-to-all | bytes 2097152 | tf_op jit(solution)/shard_map/all_to_all | solution.py:310
  120.9 1.0 copy.14
  (3 shorter events, 0.0 us)
Async XLA Ops:
  0.6 8.9 %copy-start = (bf16[8192,128]{1,0:T(8,128)(2,1)S(1)}, bf16[8192,128]{1,0:T(8,128)(2,1)}, u32[]{:S(2)}) copy-start(bf16[8192,128]{1,0:T(8,128)(2,1)} %factors_ref.1) | copy-start | bytes 6291460
  0.6 11.9 %collective-permute-start.1 = (f32[64,128]{1,0:T(8,128)}, f32[64,128]{1,0:T(8,128)S(1)}, u32[]{:S(2)}, u32[]{:S(2)}) collective-permute-start(f32[64,128]{1,0:T(8,128)} %start_ref.1), channel_id=1, source_target_pairs={{0,12},{4,16},{8,20},{12,24},{16,28},{20,32},{24,36},{28,40},{32,4... | collective-permute-start | bytes 98312 | tf_op jit(solution)/shard_map/ppermute | solution.py:234
  7.0 5.6 %collective-permute-start = (f32[64,128]{1,0:T(8,128)}, f32[64,128]{1,0:T(8,128)S(1)}, u32[]{:S(2)}, u32[]{:S(2)}) collective-permute-start(f32[64,128]{1,0:T(8,128)} %start_ref.1), channel_id=1, source_target_pairs={{2,6},{6,10},{10,14},{14,18},{18,22},{22,26},{26,30},{30,34},{34,3... | collective-permute-start | bytes 98312 | tf_op jit(solution)/shard_map/ppermute | solution.py:233
  9.5 1.8 %copy-start.2 = (f32[64,128]{1,0:T(8,128)S(1)}, f32[64,128]{1,0:T(8,128)}, u32[]{:S(2)}) copy-start(f32[64,128]{1,0:T(8,128)} %start_ref.1) | copy-start | bytes 98308
  11.4 1.2 copy-start.3
  12.8 5.5 %collective-permute-start.4 = (f32[64,128]{1,0:T(8,128)S(1)}, f32[64,128]{1,0:T(8,128)S(1)}, u32[]{:S(2)}, u32[]{:S(2)}) collective-permute-start(f32[64,128]{1,0:T(8,128)S(1)} %shard_map.68.own_ref), channel_id=1, source_target_pairs={{0,2},{1,3},{2,0},{3,1},{4,6},{5,7},{6,4},{7,5},{8,10},{9,11},{10,... | collective-permute-start | bytes 98312 | tf_op jit(solution)/shard_map/ppermute | solution.py:249
  16.8 3.1 %collective-permute-start.3 = (f32[64,128]{1,0:T(8,128)S(1)}, f32[64,128]{1,0:T(8,128)S(1)}, u32[]{:S(2)}, u32[]{:S(2)}) collective-permute-start(f32[64,128]{1,0:T(8,128)S(1)} %shard_map.68.own_ref), channel_id=1, source_target_pairs={{0,3},{1,0},{2,1},{3,2},{4,7},{5,4},{6,5},{7,6},{8,11},{9,8},{10,9... | collective-permute-start | bytes 98312 | tf_op jit(solution)/shard_map/ppermute | solution.py:249
  16.8 4.0 %collective-permute-start.2 = (f32[64,128]{1,0:T(8,128)S(1)}, f32[64,128]{1,0:T(8,128)S(1)}, u32[]{:S(2)}, u32[]{:S(2)}) collective-permute-start(f32[64,128]{1,0:T(8,128)S(1)} %shard_map.68.own_ref), channel_id=1, source_target_pairs={{0,1},{1,2},{2,3},{3,0},{4,5},{5,6},{6,7},{7,4},{8,9},{9,10},{10,1... | collective-permute-start | bytes 98312 | tf_op jit(solution)/shard_map/ppermute | solution.py:249
  20.8 6.5 %collective-permute-start.5 = (bf16[48,128]{1,0:T(8,128)(2,1)S(1)}, bf16[48,128]{1,0:T(8,128)(2,1)S(1)}, u32[]{:S(2)}, u32[]{:S(2)}) collective-permute-start(bf16[48,128]{1,0:T(8,128)(2,1)S(1)} %get-tuple-element.16), channel_id=1, source_target_pairs={{2,6},{6,10},{10,14},{14,18},{18,22},{22,26},{26,30},{30,34},{34,3... | collective-permute-start | bytes 36872 | tf_op jit(solution)/shard_map/ppermute | solution.py:233
  21.5 5.8 %collective-permute-start.6 = (bf16[48,128]{1,0:T(8,128)(2,1)S(1)}, bf16[48,128]{1,0:T(8,128)(2,1)S(1)}, u32[]{:S(2)}, u32[]{:S(2)}) collective-permute-start(bf16[48,128]{1,0:T(8,128)(2,1)S(1)} %get-tuple-element.17), channel_id=1, source_target_pairs={{0,12},{4,16},{8,20},{12,24},{16,28},{20,32},{24,36},{28,40},{32,4... | collective-permute-start | bytes 36872 | tf_op jit(solution)/shard_map/ppermute | solution.py:234
  27.6 4.4 %collective-permute-start.9 = (f32[64,128]{1,0:T(8,128)S(1)}, f32[64,128]{1,0:T(8,128)S(1)}, u32[]{:S(2)}, u32[]{:S(2)}) collective-permute-start(f32[64,128]{1,0:T(8,128)S(1)} %shard_map.70.own_ref), channel_id=1, source_target_pairs={{0,2},{1,3},{2,0},{3,1},{4,6},{5,7},{6,4},{7,5},{8,10},{9,11},{10,... | collective-permute-start | bytes 98312 | tf_op jit(solution)/shard_map/ppermute | solution.py:249
  29.6 2.8 %collective-permute-start.8 = (f32[64,128]{1,0:T(8,128)S(1)}, f32[64,128]{1,0:T(8,128)S(1)}, u32[]{:S(2)}, u32[]{:S(2)}) collective-permute-start(f32[64,128]{1,0:T(8,128)S(1)} %shard_map.70.own_ref), channel_id=1, source_target_pairs={{0,3},{1,0},{2,1},{3,2},{4,7},{5,4},{6,5},{7,6},{8,11},{9,8},{10,9... | collective-permute-start | bytes 98312 | tf_op jit(solution)/shard_map/ppermute | solution.py:249
  31.0 4.0 %collective-permute-start.7 = (f32[64,128]{1,0:T(8,128)S(1)}, f32[64,128]{1,0:T(8,128)S(1)}, u32[]{:S(2)}, u32[]{:S(2)}) collective-permute-start(f32[64,128]{1,0:T(8,128)S(1)} %shard_map.70.own_ref), channel_id=1, source_target_pairs={{0,1},{1,2},{2,3},{3,0},{4,5},{5,6},{6,7},{7,4},{8,9},{9,10},{10,1... | collective-permute-start | bytes 98312 | tf_op jit(solution)/shard_map/ppermute | solution.py:249
  35.0 7.2 %collective-permute-start.10 = (bf16[48,128]{1,0:T(8,128)(2,1)S(1)}, bf16[48,128]{1,0:T(8,128)(2,1)S(1)}, u32[]{:S(2)}, u32[]{:S(2)}) collective-permute-start(bf16[48,128]{1,0:T(8,128)(2,1)S(1)} %get-tuple-element.20), channel_id=1, source_target_pairs={{2,6},{6,10},{10,14},{14,18},{18,22},{22,26},{26,30},{30,34},{34,3... | collective-permute-start | bytes 36872 | tf_op jit(solution)/shard_map/ppermute | solution.py:233
  35.7 6.5 %collective-permute-start.11 = (bf16[48,128]{1,0:T(8,128)(2,1)S(1)}, bf16[48,128]{1,0:T(8,128)(2,1)S(1)}, u32[]{:S(2)}, u32[]{:S(2)}) collective-permute-start(bf16[48,128]{1,0:T(8,128)(2,1)S(1)} %get-tuple-element.21), channel_id=1, source_target_pairs={{0,12},{4,16},{8,20},{12,24},{16,28},{20,32},{24,36},{28,40},{32,4... | collective-permute-start | bytes 36872 | tf_op jit(solution)/shard_map/ppermute | solution.py:234
  42.2 45.3 %copy-start.1 = (bf16[64,8192]{1,0:T(8,128)(2,1)S(1)}, bf16[64,8192]{1,0:T(8,128)(2,1)}, u32[]{:S(2)}) copy-start(bf16[64,8192]{1,0:T(8,128)(2,1)} %values_ref.1) | copy-start | bytes 3145732
  42.4 4.4 %collective-permute-start.14 = (f32[64,128]{1,0:T(8,128)S(1)}, f32[64,128]{1,0:T(8,128)S(1)}, u32[]{:S(2)}, u32[]{:S(2)}) collective-permute-start(f32[64,128]{1,0:T(8,128)S(1)} %shard_map.72.own_ref), channel_id=1, source_target_pairs={{0,2},{1,3},{2,0},{3,1},{4,6},{5,7},{6,4},{7,5},{8,10},{9,11},{10,... | collective-permute-start | bytes 98312 | tf_op jit(solution)/shard_map/ppermute | solution.py:249
  44.2 3.0 %collective-permute-start.13 = (f32[64,128]{1,0:T(8,128)S(1)}, f32[64,128]{1,0:T(8,128)S(1)}, u32[]{:S(2)}, u32[]{:S(2)}) collective-permute-start(f32[64,128]{1,0:T(8,128)S(1)} %shard_map.72.own_ref), channel_id=1, source_target_pairs={{0,3},{1,0},{2,1},{3,2},{4,7},{5,4},{6,5},{7,6},{8,11},{9,8},{10,9... | collective-permute-start | bytes 98312 | tf_op jit(solution)/shard_map/ppermute | solution.py:249
  45.5 4.0 %collective-permute-start.12 = (f32[64,128]{1,0:T(8,128)S(1)}, f32[64,128]{1,0:T(8,128)S(1)}, u32[]{:S(2)}, u32[]{:S(2)}) collective-permute-start(f32[64,128]{1,0:T(8,128)S(1)} %shard_map.72.own_ref), channel_id=1, source_target_pairs={{0,1},{1,2},{2,3},{3,0},{4,5},{5,6},{6,7},{7,4},{8,9},{9,10},{10,1... | collective-permute-start | bytes 98312 | tf_op jit(solution)/shard_map/ppermute | solution.py:249
  49.5 1.7 %collective-permute-start.15 = (bf16[48,128]{1,0:T(8,128)(2,1)S(1)}, bf16[48,128]{1,0:T(8,128)(2,1)S(1)}, u32[]{:S(2)}, u32[]{:S(2)}) collective-permute-start(bf16[48,128]{1,0:T(8,128)(2,1)S(1)} %get-tuple-element.25), channel_id=1, source_target_pairs={{13,1},{17,5},{21,9},{25,13},{29,17},{33,21},{37,25},{41,29},{45,3... | collective-permute-start | bytes 36872 | tf_op jit(solution)/shard_map/ppermute | solution.py:284

commit v15 on v12

--- a/solution.py
+++ b/solution.py
@@ -70,6 +70,10 @@
     ]
     product = lag_product(blocks, weights_ref, window, short, last_time)
     part_ref[...] = data_weight * local_ref[...] + scale * product
+
+
+def start_penalty_kernel(scale, last_time, field_ref, few_ref, many_ref, *refs):
+    penalty_kernel(scale, last_time, field_ref, many_ref, few_ref, *refs)
 
 
 def rows_for(late, field):
@@ -233,15 +237,15 @@
         few = lax.ppermute(few, both, few_route)
         return lax.ppermute(many, both, many_route), few
 
-    def penalty(scale, field, many, few, local):
+    def penalty(scale, field, first, second, local, kernel=penalty_kernel):
         return pl.pallas_call(
-            functools.partial(penalty_kernel, scale, last_time),
+            functools.partial(kernel, scale, last_time),
             out_shape=field_shape,
             in_specs=[VMEM] * 5,
             out_specs=VMEM,
             scratch_shapes=lag_scratch,
             compiler_params=SMALL,
-        )(field, many, few, lag_weights, local)
+        )(field, first, second, lag_weights, local)
 
     def series_sum(scale, part, field, out_halos):
         def moved(distance):
@@ -270,7 +274,7 @@
     many, few = fetch(time_factors, time_factors)
     kept = jnp.where(seen, series_values, jnp.zeros((), jnp.bfloat16))
     local = back(kept) - back(fit(low).astype(jnp.bfloat16))
-    part = penalty(-penalty_weight, time_factors, many, few, local)
+    part = penalty(-penalty_weight, time_factors, few, many, local, start_penalty_kernel)
     power0, low, many, few = series_sum(-ridge_weight, part, time_factors, halo_shapes)
 
     def image(field, low, many, few, out_halos):

time: 122 us -> 122 us (level)
  no operation moved by 1% of the time
where the time goes in v15:
time: 122 us; the launch traced here: 121 us
  blocking collectives  67.9 us (56%)
  starting transfers between devices  33.1 us (27%)
  waiting for transfers between devices  8.23 us (7%)
  matrix products  6.11 us (5%)
  Pallas kernels  2.28 us (2%)
  other arithmetic  1.86 us (2%)
    all_to_all x1, blocking collectives, on_device(): lax.all_to_all(spread, both, split_axis=0, concat_axis=0, tiled=True)  35.5 us
    all_to_all x1, blocking collectives, on_device(): lax.all_to_all(misfit, 'tm', split_axis=0, concat_axis=0, tiled=True)  32.4 us
    ppermute x3, starting transfers between devices, fetch(): return (lax.ppermute(many, both, many_route), few)  17.7 us
    ppermute x9, starting transfers between devices, moved(): return lax.ppermute(part, 'series', pairs)  12.8 us
    ppermute x9, waiting for transfers between devices, moved(): return lax.ppermute(part, 'series', pairs)  8.21 us
    dot_general x4, matrix products, back(): jnp.dot(rows_here, series_factors, preferred_element_type=jnp.float32)  5.25 us
  transfers between devices with their start and end apart: 16, of which 8 were waited for; matrix products, arithmetic and copies ran while one was open for 7% of the time, Pallas kernels for 0%

profile of v15, /device:TPU:1, one launch (start us, length us, event | category | flops | bytes accessed | tf_op | source)
XLA Modules:
  0.0 121.4 jit_solution(15456459763139427191)
XLA Ops:
  0.6 0.0 copy-start
  0.6 6.3 %collective-permute-start.1 = (f32[64,128]{1,0:T(8,128)}, f32[64,128]{1,0:T(8,128)S(1)}, u32[]{:S(2)}, u32[]{:S(2)}) collective-permute-start(f32[64,128]{1,0:T(8,128)} %start_ref.1), channel_id=1, source_target_pairs={{0,12},{4,16},{8,20},{12,24},{16,28},{20,32},{24,36},{28,40},{32,4... | collective-permute-start | bytes 98312 | tf_op jit(solution)/shard_map/ppermute | solution.py:238
  7.0 0.7 collective-permute-start
  7.7 1.9 %broadcast_compare_fusion = pred[64,8192]{1,0:T(32,128)(4,1)S(1)} fusion(s32[64,8192]{1,0:T(8,128)} %param.6), kind=kLoop, calls=%fused_computation.18 | loop fusion | flops 524288 | bytes 2621440 | tf_op jit(solution)/shard_map/eq | solution.py:265
  9.5 0.0 copy-done
  9.5 0.0 copy-start.2
  9.6 1.8 %fusion.12 = f32[64,128]{1,0:T(8,128)S(1)} fusion(bf16[8192,128]{1,0:T(8,128)(2,1)S(1)} %copy-done, pred[64,8192]{1,0:T(32,128)(4,1)S(1)} %broadcast_compare_fusion, bf16[64,8192]{1,0:T(8,128)(2,1)} %values_ref.1), kind=kOutput, calls=%fused_computation.16 | convolution fusion | flops 134742016 | bytes 3702784 | tf_op jit(solution)/shard_map/dot_general | solution.py:271
  11.4 0.0 copy-done.2
  11.4 0.0 copy-start.3
  11.4 1.2 fusion.8.refs_1_
  12.5 0.0 collective-permute-done.1.many_ref
  12.5 0.0 collective-permute-done.few_ref
  12.6 0.0 copy-done.3
  12.6 0.2 shard_map.68.own_ref
  12.8 4.0 %collective-permute-start.4 = (f32[64,128]{1,0:T(8,128)S(1)}, f32[64,128]{1,0:T(8,128)S(1)}, u32[]{:S(2)}, u32[]{:S(2)}) collective-permute-start(f32[64,128]{1,0:T(8,128)S(1)} %shard_map.68.own_ref), channel_id=1, source_target_pairs={{0,2},{1,3},{2,0},{3,1},{4,6},{5,7},{6,4},{7,5},{8,10},{9,11},{10,... | collective-permute-start | bytes 98312 | tf_op jit(solution)/shard_map/ppermute | solution.py:253
  16.8 0.0 collective-permute-start.3
  16.8 1.5 %collective-permute-start.2 = (f32[64,128]{1,0:T(8,128)S(1)}, f32[64,128]{1,0:T(8,128)S(1)}, u32[]{:S(2)}, u32[]{:S(2)}) collective-permute-start(f32[64,128]{1,0:T(8,128)S(1)} %shard_map.68.own_ref), channel_id=1, source_target_pairs={{0,1},{1,2},{2,3},{3,0},{4,5},{5,6},{6,7},{7,4},{8,9},{9,10},{10,1... | collective-permute-start | bytes 98312 | tf_op jit(solution)/shard_map/ppermute | solution.py:253
  18.3 0.0 collective-permute-done.4.second_ref
  18.3 1.6 %collective-permute-done.3.third_ref = f32[64,128]{1,0:T(8,128)S(1)} collective-permute-done((f32[64,128]{1,0:T(8,128)S(1)}, f32[64,128]{1,0:T(8,128)S(1)}, u32[]{:S(2)}, u32[]{:S(2)}) %collective-permute-start.3) | collective-permute-done | bytes 32800 | tf_op jit(solution)/shard_map/ppermute | solution.py:253
  19.9 0.9 collective-permute-done.2.first_ref
  20.8 4.7 %collective-permute-start.5 = (bf16[48,128]{1,0:T(8,128)(2,1)S(1)}, bf16[48,128]{1,0:T(8,128)(2,1)S(1)}, u32[]{:S(2)}, u32[]{:S(2)}) collective-permute-start(bf16[48,128]{1,0:T(8,128)(2,1)S(1)} %get-tuple-element.16), channel_id=1, source_target_pairs={{0,12},{4,16},{8,20},{12,24},{16,28},{20,32},{24,36},{28,40},{32,4... | collective-permute-start | bytes 36872 | tf_op jit(solution)/shard_map/ppermute | solution.py:238
  25.5 0.7 collective-permute-start.6
  26.2 1.1 fusion.6.local_ref
  27.3 0.0 collective-permute-done.5.many_ref
  27.3 0.0 collective-permute-done.6.few_ref
  27.4 0.2 shard_map.70.own_ref
  27.6 2.3 %collective-permute-start.9 = (f32[64,128]{1,0:T(8,128)S(1)}, f32[64,128]{1,0:T(8,128)S(1)}, u32[]{:S(2)}, u32[]{:S(2)}) collective-permute-start(f32[64,128]{1,0:T(8,128)S(1)} %shard_map.70.own_ref), channel_id=1, source_target_pairs={{0,2},{1,3},{2,0},{3,1},{4,6},{5,7},{6,4},{7,5},{8,10},{9,11},{10,... | collective-permute-start | bytes 98312 | tf_op jit(solution)/shard_map/ppermute | solution.py:253
  29.9 0.4 collective-permute-start.8
  30.3 1.1 collective-permute-start.7
  31.4 0.6 collective-permute-done.9.second_ref
  31.9 0.9 collective-permute-done.8.third_ref
  32.8 1.5 %collective-permute-done.7.first_ref = f32[64,128]{1,0:T(8,128)S(1)} collective-permute-done((f32[64,128]{1,0:T(8,128)S(1)}, f32[64,128]{1,0:T(8,128)S(1)}, u32[]{:S(2)}, u32[]{:S(2)}) %collective-permute-start.7) | collective-permute-done | bytes 32800 | tf_op jit(solution)/shard_map/ppermute | solution.py:253
  34.3 6.7 %collective-permute-start.10 = (bf16[48,128]{1,0:T(8,128)(2,1)S(1)}, bf16[48,128]{1,0:T(8,128)(2,1)S(1)}, u32[]{:S(2)}, u32[]{:S(2)}) collective-permute-start(bf16[48,128]{1,0:T(8,128)(2,1)S(1)} %get-tuple-element.20), channel_id=1, source_target_pairs={{0,12},{4,16},{8,20},{12,24},{16,28},{20,32},{24,36},{28,40},{32,4... | collective-permute-start | bytes 36872 | tf_op jit(solution)/shard_map/ppermute | solution.py:238
  41.0 0.7 collective-permute-start.11
  41.7 1.2 fusion.5.local_ref
  42.8 0.0 copy-start.1
  42.9 0.0 collective-permute-done.10.many_ref
  42.9 0.0 collective-permute-done.11.few_ref
  42.9 0.2 shard_map.72.own_ref
  43.1 2.0 %collective-permute-start.14 = (f32[64,128]{1,0:T(8,128)S(1)}, f32[64,128]{1,0:T(8,128)S(1)}, u32[]{:S(2)}, u32[]{:S(2)}) collective-permute-start(f32[64,128]{1,0:T(8,128)S(1)} %shard_map.72.own_ref), channel_id=1, source_target_pairs={{0,2},{1,3},{2,0},{3,1},{4,6},{5,7},{6,4},{7,5},{8,10},{9,11},{10,... | collective-permute-start | bytes 98312 | tf_op jit(solution)/shard_map/ppermute | solution.py:253
  45.1 0.3 collective-permute-start.13
  45.4 1.2 collective-permute-start.12
  46.6 0.8 collective-permute-done.14.second_ref
  47.5 0.7 collective-permute-done.13.third_ref
  48.2 1.2 collective-permute-done.12.first_ref
  49.4 0.7 collective-permute-start.15
  50.1 0.9 fusion.4
  50.9 0.2 shard_map.74.packed_ref
  51.1 0.0 collective-permute-done.15.many_ref
  51.1 0.4 shard_map.75
  51.5 35.5 %all_to_all.10.gathered_ref = f32[256,1,128]{2,1,0:T(1,128)S(1)} all-to-all(f32[256,1,128]{2,1,0:T(1,128)S(1)} %shard_map.75), channel_id=1, replica_groups=mesh['tm'=64,'series'=4] {'tm','series'}, dimensions={0} | all-to-all | bytes 262144 | tf_op jit(solution)/shard_map/all_to_all | solution.py:306
  86.9 0.0 copy-done.1
  86.9 1.0 shard_map.76
  88.0 32.4 %all_to_all.11 = bf16[64,64,128]{2,1,0:T(8,128)(2,1)S(1)} all-to-all(bf16[64,64,128]{2,1,0:T(8,128)(2,1)S(1)} %get-tuple-element.27), channel_id=1, replica_groups=mesh['tm'=64,'series'=4] {'tm'}, dimensions={0} | all-to-all | bytes 2097152 | tf_op jit(solution)/shard_map/all_to_all | solution.py:314
  120.4 1.0 copy.14
  (3 shorter events, 0.0 us)
Async XLA Ops:
  0.6 8.9 %copy-start = (bf16[8192,128]{1,0:T(8,128)(2,1)S(1)}, bf16[8192,128]{1,0:T(8,128)(2,1)}, u32[]{:S(2)}) copy-start(bf16[8192,128]{1,0:T(8,128)(2,1)} %factors_ref.1) | copy-start | bytes 6291460
  0.6 11.9 %collective-permute-start.1 = (f32[64,128]{1,0:T(8,128)}, f32[64,128]{1,0:T(8,128)S(1)}, u32[]{:S(2)}, u32[]{:S(2)}) collective-permute-start(f32[64,128]{1,0:T(8,128)} %start_ref.1), channel_id=1, source_target_pairs={{0,12},{4,16},{8,20},{12,24},{16,28},{20,32},{24,36},{28,40},{32,4... | collective-permute-start | bytes 98312 | tf_op jit(solution)/shard_map/ppermute | solution.py:238
  7.0 5.6 %collective-permute-start = (f32[64,128]{1,0:T(8,128)}, f32[64,128]{1,0:T(8,128)S(1)}, u32[]{:S(2)}, u32[]{:S(2)}) collective-permute-start(f32[64,128]{1,0:T(8,128)} %start_ref.1), channel_id=1, source_target_pairs={{2,6},{6,10},{10,14},{14,18},{18,22},{22,26},{26,30},{30,34},{34,3... | collective-permute-start | bytes 98312 | tf_op jit(solution)/shard_map/ppermute | solution.py:237
  9.5 1.8 %copy-start.2 = (f32[64,128]{1,0:T(8,128)S(1)}, f32[64,128]{1,0:T(8,128)}, u32[]{:S(2)}) copy-start(f32[64,128]{1,0:T(8,128)} %start_ref.1) | copy-start | bytes 98308
  11.4 1.2 copy-start.3
  12.8 5.5 %collective-permute-start.4 = (f32[64,128]{1,0:T(8,128)S(1)}, f32[64,128]{1,0:T(8,128)S(1)}, u32[]{:S(2)}, u32[]{:S(2)}) collective-permute-start(f32[64,128]{1,0:T(8,128)S(1)} %shard_map.68.own_ref), channel_id=1, source_target_pairs={{0,2},{1,3},{2,0},{3,1},{4,6},{5,7},{6,4},{7,5},{8,10},{9,11},{10,... | collective-permute-start | bytes 98312 | tf_op jit(solution)/shard_map/ppermute | solution.py:253
  16.8 3.1 %collective-permute-start.3 = (f32[64,128]{1,0:T(8,128)S(1)}, f32[64,128]{1,0:T(8,128)S(1)}, u32[]{:S(2)}, u32[]{:S(2)}) collective-permute-start(f32[64,128]{1,0:T(8,128)S(1)} %shard_map.68.own_ref), channel_id=1, source_target_pairs={{0,3},{1,0},{2,1},{3,2},{4,7},{5,4},{6,5},{7,6},{8,11},{9,8},{10,9... | collective-permute-start | bytes 98312 | tf_op jit(solution)/shard_map/ppermute | solution.py:253
  16.8 4.0 %collective-permute-start.2 = (f32[64,128]{1,0:T(8,128)S(1)}, f32[64,128]{1,0:T(8,128)S(1)}, u32[]{:S(2)}, u32[]{:S(2)}) collective-permute-start(f32[64,128]{1,0:T(8,128)S(1)} %shard_map.68.own_ref), channel_id=1, source_target_pairs={{0,1},{1,2},{2,3},{3,0},{4,5},{5,6},{6,7},{7,4},{8,9},{9,10},{10,1... | collective-permute-start | bytes 98312 | tf_op jit(solution)/shard_map/ppermute | solution.py:253
  20.8 6.5 %collective-permute-start.5 = (bf16[48,128]{1,0:T(8,128)(2,1)S(1)}, bf16[48,128]{1,0:T(8,128)(2,1)S(1)}, u32[]{:S(2)}, u32[]{:S(2)}) collective-permute-start(bf16[48,128]{1,0:T(8,128)(2,1)S(1)} %get-tuple-element.16), channel_id=1, source_target_pairs={{0,12},{4,16},{8,20},{12,24},{16,28},{20,32},{24,36},{28,40},{32,4... | collective-permute-start | bytes 36872 | tf_op jit(solution)/shard_map/ppermute | solution.py:238
  25.5 1.8 %collective-permute-start.6 = (bf16[48,128]{1,0:T(8,128)(2,1)S(1)}, bf16[48,128]{1,0:T(8,128)(2,1)S(1)}, u32[]{:S(2)}, u32[]{:S(2)}) collective-permute-start(bf16[48,128]{1,0:T(8,128)(2,1)S(1)} %get-tuple-element.17), channel_id=1, source_target_pairs={{2,6},{6,10},{10,14},{14,18},{18,22},{22,26},{26,30},{30,34},{34,3... | collective-permute-start | bytes 36872 | tf_op jit(solution)/shard_map/ppermute | solution.py:237
  27.6 4.4 %collective-permute-start.9 = (f32[64,128]{1,0:T(8,128)S(1)}, f32[64,128]{1,0:T(8,128)S(1)}, u32[]{:S(2)}, u32[]{:S(2)}) collective-permute-start(f32[64,128]{1,0:T(8,128)S(1)} %shard_map.70.own_ref), channel_id=1, source_target_pairs={{0,2},{1,3},{2,0},{3,1},{4,6},{5,7},{6,4},{7,5},{8,10},{9,11},{10,... | collective-permute-start | bytes 98312 | tf_op jit(solution)/shard_map/ppermute | solution.py:253
  29.9 2.9 %collective-permute-start.8 = (f32[64,128]{1,0:T(8,128)S(1)}, f32[64,128]{1,0:T(8,128)S(1)}, u32[]{:S(2)}, u32[]{:S(2)}) collective-permute-start(f32[64,128]{1,0:T(8,128)S(1)} %shard_map.70.own_ref), channel_id=1, source_target_pairs={{0,3},{1,0},{2,1},{3,2},{4,7},{5,4},{6,5},{7,6},{8,11},{9,8},{10,9... | collective-permute-start | bytes 98312 | tf_op jit(solution)/shard_map/ppermute | solution.py:253
  30.3 4.0 %collective-permute-start.7 = (f32[64,128]{1,0:T(8,128)S(1)}, f32[64,128]{1,0:T(8,128)S(1)}, u32[]{:S(2)}, u32[]{:S(2)}) collective-permute-start(f32[64,128]{1,0:T(8,128)S(1)} %shard_map.70.own_ref), channel_id=1, source_target_pairs={{0,1},{1,2},{2,3},{3,0},{4,5},{5,6},{6,7},{7,4},{8,9},{9,10},{10,1... | collective-permute-start | bytes 98312 | tf_op jit(solution)/shard_map/ppermute | solution.py:253
  34.3 8.5 %collective-permute-start.10 = (bf16[48,128]{1,0:T(8,128)(2,1)S(1)}, bf16[48,128]{1,0:T(8,128)(2,1)S(1)}, u32[]{:S(2)}, u32[]{:S(2)}) collective-permute-start(bf16[48,128]{1,0:T(8,128)(2,1)S(1)} %get-tuple-element.20), channel_id=1, source_target_pairs={{0,12},{4,16},{8,20},{12,24},{16,28},{20,32},{24,36},{28,40},{32,4... | collective-permute-start | bytes 36872 | tf_op jit(solution)/shard_map/ppermute | solution.py:238
  41.0 1.9 %collective-permute-start.11 = (bf16[48,128]{1,0:T(8,128)(2,1)S(1)}, bf16[48,128]{1,0:T(8,128)(2,1)S(1)}, u32[]{:S(2)}, u32[]{:S(2)}) collective-permute-start(bf16[48,128]{1,0:T(8,128)(2,1)S(1)} %get-tuple-element.21), channel_id=1, source_target_pairs={{2,6},{6,10},{10,14},{14,18},{18,22},{22,26},{26,30},{30,34},{34,3... | collective-permute-start | bytes 36872 | tf_op jit(solution)/shard_map/ppermute | solution.py:237
  42.8 44.1 %copy-start.1 = (bf16[64,8192]{1,0:T(8,128)(2,1)S(1)}, bf16[64,8192]{1,0:T(8,128)(2,1)}, u32[]{:S(2)}) copy-start(bf16[64,8192]{1,0:T(8,128)(2,1)} %values_ref.1) | copy-start | bytes 3145732
  43.1 4.4 %collective-permute-start.14 = (f32[64,128]{1,0:T(8,128)S(1)}, f32[64,128]{1,0:T(8,128)S(1)}, u32[]{:S(2)}, u32[]{:S(2)}) collective-permute-start(f32[64,128]{1,0:T(8,128)S(1)} %shard_map.72.own_ref), channel_id=1, source_target_pairs={{0,2},{1,3},{2,0},{3,1},{4,6},{5,7},{6,4},{7,5},{8,10},{9,11},{10,... | collective-permute-start | bytes 98312 | tf_op jit(solution)/shard_map/ppermute | solution.py:253
  45.1 3.1 %collective-permute-start.13 = (f32[64,128]{1,0:T(8,128)S(1)}, f32[64,128]{1,0:T(8,128)S(1)}, u32[]{:S(2)}, u32[]{:S(2)}) collective-permute-start(f32[64,128]{1,0:T(8,128)S(1)} %shard_map.72.own_ref), channel_id=1, source_target_pairs={{0,3},{1,0},{2,1},{3,2},{4,7},{5,4},{6,5},{7,6},{8,11},{9,8},{10,9... | collective-permute-start | bytes 98312 | tf_op jit(solution)/shard_map/ppermute | solution.py:253
  45.4 4.0 %collective-permute-start.12 = (f32[64,128]{1,0:T(8,128)S(1)}, f32[64,128]{1,0:T(8,128)S(1)}, u32[]{:S(2)}, u32[]{:S(2)}) collective-permute-start(f32[64,128]{1,0:T(8,128)S(1)} %shard_map.72.own_ref), channel_id=1, source_target_pairs={{0,1},{1,2},{2,3},{3,0},{4,5},{5,6},{6,7},{7,4},{8,9},{9,10},{10,1... | collective-permute-start | bytes 98312 | tf_op jit(solution)/shard_map/ppermute | solution.py:253
  49.4 1.7 %collective-permute-start.15 = (bf16[48,128]{1,0:T(8,128)(2,1)S(1)}, bf16[48,128]{1,0:T(8,128)(2,1)S(1)}, u32[]{:S(2)}, u32[]{:S(2)}) collective-permute-start(bf16[48,128]{1,0:T(8,128)(2,1)S(1)} %get-tuple-element.25), channel_id=1, source_target_pairs={{13,1},{17,5},{21,9},{25,13},{29,17},{33,21},{37,25},{41,29},{45,3... | collective-permute-start | bytes 36872 | tf_op jit(solution)/shard_map/ppermute | solution.py:288
